TPU v7x, 32 devices: a whole 2x2x4 slice. The times are simulated.
32 devices in a mesh: dp: 4 (over z), tensor: 8 (over y, x, core).
Axes of the slice: x: 2, y: 2, z: 4, core: 2. Of those that a mesh axis runs over, the one named last changes fastest.
Arguments:
- hidden_in: bfloat16 [4, 1024, 2304], P('dp', 'tensor'), may hold values from -6 to 6
- prompt_len: int32 [4], P('dp'), may hold values from 1 to 1024, 2560 in all
- start_pos: int32 [4], P('dp'), may hold values from 0 to 511
- routes: int32 [4, 1024, 2], P('dp'), may hold values from 0 to 7, as said below
- trainer_qkv: float32 [2304, 3, 2048], P(('tensor', 'dp')), may hold values from -1 to 1
- trainer_out: float32 [2048, 2304], P(('tensor', 'dp')), may hold values from -0.125 to 0.125
- trainer_gate: float32 [2304, 5760], P('tensor'), may hold values from -0.125 to 0.125
- trainer_up: float32 [2304, 5760], P('tensor'), may hold values from -0.125 to 0.125
- trainer_down: float32 [2304, 5760], P('tensor'), may hold values from -0.078125 to 0.078125
- attn_gain: float32 [2304], replicated, may hold values from 0.25 to 1.75
- moe_gain: float32 [2304], replicated, may hold values from 0.25 to 1.75
- router: bfloat16 [2304, 8], replicated, may hold values from -0.125 to 0.125
Outputs:
- server_qkv: bfloat16 [2304, 3, 2048], P(None, None, 'tensor')
- server_out: bfloat16 [2048, 2304], P('tensor')
- server_gate: bfloat16 [2304, 5760], P(None, 'tensor')
- server_up: bfloat16 [2304, 5760], P(None, 'tensor')
- server_down: bfloat16 [2304, 5760], P(None, 'tensor')
- hidden_out: bfloat16 [4, 1024, 2304], P('dp', 'tensor')
- kv_cache: bfloat16 [4, 2, 1024, 2048], P('dp', None, None, 'tensor')
Inputs may be any that keep to these rules, and one draw needn't show every extreme that they name: `routes`: each row names two different experts; expert 0 is named by at most 512 rows of each prompt and by exactly 512 rows of some prompt.
All inputs are finite; a program needn't handle non-finite values. No bound on the sum of `prompt_len` on one device may be relied on, other than what follows from the above.
Results may differ from a plain program's by a relative error of at most 0.011.
The roundings to bfloat16 on the way count: a program that leaves them out, or rounds other values in their place, can miss the bound.
Values may be sent and summed in bfloat16 or wider, within the bound.
No kernel may reach another device: no remote copies, remote signals or barrier semaphores. Data moves between devices by JAX's collectives and lax.ppermute only.
A program may use at most 256 MiB of HBM per device.

v0:
```python
import jax
import jax.numpy as jnp
from jax import lax
from jax.sharding import PartitionSpec as P

HEAD_DIM = 64


def rms_scale(values, gain_row):
    mean_sq = jnp.mean(values * values, axis=-1, keepdims=True)
    return values * lax.rsqrt(mean_sq + 1e-05) * gain_row


def rotate(head_block, positions):
    half_dim = head_block.shape[-1] // 2
    inv_freq = jnp.power(
        10000.0, jnp.arange(half_dim, dtype=jnp.float32) * (-2.0 / head_block.shape[-1])
    )
    angles = positions.astype(jnp.float32)[:, None] * inv_freq[None, :]
    cosine = jnp.cos(angles)[:, None, :]
    sine_part = jnp.sin(angles)[:, None, :]
    first_half = head_block[..., :half_dim]
    second_half = head_block[..., half_dim:]
    return jnp.concatenate(
        [
            first_half * cosine - second_half * sine_part,
            second_half * cosine + first_half * sine_part,
        ],
        axis=-1,
    )


def attend_block(query_blk, key_blk, value_blk, row_start):
    scores = jnp.einsum(
        "qhd,khd->hqk", query_blk, key_blk, preferred_element_type=jnp.float32
    ) * query_blk.shape[-1] ** (-0.5)
    row_ids = row_start + jnp.arange(query_blk.shape[0], dtype=jnp.int32)
    col_ids = jnp.arange(key_blk.shape[0], dtype=jnp.int32)
    scores = jnp.where(row_ids[None, :, None] >= col_ids[None, None, :], scores, -1e30)
    row_max = jnp.max(scores, axis=-1, keepdims=True)
    exp_scores = jnp.exp(scores - row_max)
    attn_probs = (exp_scores / jnp.sum(exp_scores, axis=-1, keepdims=True)).astype(jnp.bfloat16)
    return jnp.einsum(
        "hqk,khd->qhd", attn_probs, value_blk, preferred_element_type=jnp.float32
    ).astype(jnp.bfloat16)


def shards(
    hidden_in,
    prompt_len,
    start_pos,
    routes,
    trainer_qkv,
    trainer_out,
    trainer_gate,
    trainer_up,
    trainer_down,
    attn_gain,
    moe_gain,
    router,
):
    tensor_size = lax.axis_size("tensor")
    replica_count = lax.axis_size("dp")
    expert_mats = (
        lax.all_to_all(
            trainer_gate.astype(jnp.bfloat16), "tensor", split_axis=1, concat_axis=0, tiled=True
        ),
        lax.all_to_all(
            trainer_up.astype(jnp.bfloat16), "tensor", split_axis=1, concat_axis=0, tiled=True
        ),
        lax.all_to_all(
            trainer_down.astype(jnp.bfloat16), "tensor", split_axis=1, concat_axis=0, tiled=True
        ),
    )
    server_gate, server_up, server_down = expert_mats
    qkv_cast = trainer_qkv.astype(jnp.bfloat16)
    out_cast = trainer_out.astype(jnp.bfloat16)
    column_part = lax.all_to_all(qkv_cast, "tensor", split_axis=2, concat_axis=0, tiled=True)
    stacked, server_out = (
        lax.all_gather(column_part, "dp", axis=0, tiled=True),
        lax.all_gather(out_cast, "dp", axis=0, tiled=True),
    )
    block_rows = stacked.shape[0] // (replica_count * tensor_size)
    server_qkv = (
        stacked.reshape(replica_count, tensor_size, block_rows, 3, stacked.shape[2])
        .transpose(1, 0, 2, 3, 4)
        .reshape(stacked.shape)
    )
    rows_dev = hidden_in.shape[1]
    seq_len = rows_dev * tensor_size
    length = prompt_len[0]
    offset = start_pos[0]
    my_first = lax.axis_index("tensor") * rows_dev
    tokens = hidden_in[0].astype(jnp.float32)
    normed = rms_scale(tokens, attn_gain).astype(jnp.bfloat16)
    local_width = server_qkv.shape[2]
    heads_here = local_width // HEAD_DIM
    piece = lax.all_gather(normed, "tensor", axis=0, tiled=True)
    mixed = jnp.einsum("sd,dtc->stc", piece, server_qkv, preferred_element_type=jnp.float32)
    places = offset + jnp.arange(piece.shape[0], dtype=jnp.int32)
    query_rot = rotate(mixed[:, 0].reshape(-1, heads_here, HEAD_DIM), places).reshape(
        -1, local_width
    )
    key_rot = rotate(mixed[:, 1].reshape(-1, heads_here, HEAD_DIM), places).reshape(-1, local_width)
    qkv_rows = jnp.stack([query_rot, key_rot, mixed[:, 2]], axis=1).astype(jnp.bfloat16)
    query_all = qkv_rows[:, 0].reshape(seq_len, heads_here, HEAD_DIM)
    keys_all = qkv_rows[:, 1].reshape(seq_len, heads_here, HEAD_DIM)
    values_all = qkv_rows[:, 2].reshape(seq_len, heads_here, HEAD_DIM)
    block_len = min(512, seq_len)
    block_outs = []
    for block_id in range(seq_len // block_len):
        row_lo = block_id * block_len
        row_hi = row_lo + block_len
        query_blk = query_all[row_lo:row_hi]
        key_blk = keys_all[:row_hi]
        value_blk = values_all[:row_hi]
        block_result = attend_block(query_blk, key_blk, value_blk, row_lo)
        block_outs.append(block_result)
    attended = jnp.concatenate(block_outs, axis=0).reshape(seq_len, local_width)
    attn_sum = lax.psum_scatter(
        jnp.dot(attended, server_out, preferred_element_type=jnp.float32).astype(jnp.bfloat16),
        "tensor",
        scatter_dimension=0,
        tiled=True,
    ).astype(jnp.float32)
    middle = (tokens + attn_sum).astype(jnp.bfloat16)
    normed_moe = rms_scale(middle.astype(jnp.float32), moe_gain).astype(jnp.bfloat16)
    local_routes = lax.dynamic_slice_in_dim(routes[0], my_first, rows_dev, 0)
    local_valid = my_first + jnp.arange(rows_dev, dtype=jnp.int32) < length
    logits = jnp.dot(normed_moe, router, preferred_element_type=jnp.float32)
    expert_ids = jnp.arange(router.shape[1], dtype=jnp.int32)
    logit_first = jnp.sum(
        jnp.where(local_routes[:, 0:1] == expert_ids[None, :], logits, 0.0), axis=1
    )
    logit_second = jnp.sum(
        jnp.where(local_routes[:, 1:2] == expert_ids[None, :], logits, 0.0), axis=1
    )
    other_logit = jnp.where(local_routes[:, 0] == 0, logit_second, logit_first)
    local_routed = jnp.any(local_routes == 0, axis=1)
    route_w = jnp.where(local_routed, jax.nn.sigmoid(logits[:, 0] - other_logit), 0.0)
    gathered = lax.all_gather(normed_moe, "tensor", axis=0, tiled=True)
    seq_ids = jnp.arange(seq_len, dtype=jnp.int32)
    all_routed = jnp.any(routes[0] == 0, axis=1)
    capacity = seq_len // 2
    slot = jnp.cumsum(all_routed.astype(jnp.int32)) - 1
    slot_rows = (
        jnp.full((capacity,), seq_len, jnp.int32)
        .at[jnp.where(all_routed, slot, capacity)]
        .set(seq_ids, mode="drop")
    )
    picked = gathered[jnp.minimum(slot_rows, seq_len - 1)]
    gate_val = jnp.dot(picked, server_gate, preferred_element_type=jnp.float32)
    up_val = jnp.dot(picked, server_up, preferred_element_type=jnp.float32)
    act = (jax.nn.silu(gate_val) * up_val).astype(jnp.bfloat16)
    slot_sums = lax.dot_general(
        act, server_down, (((1,), (1,)), ((), ())), preferred_element_type=jnp.float32
    )
    terms = (
        jnp.zeros((seq_len, normed_moe.shape[1]), jnp.float32)
        .at[slot_rows]
        .add(slot_sums, mode="drop")
    )
    expert_sum = lax.psum_scatter(
        terms.astype(jnp.bfloat16), "tensor", scatter_dimension=0, tiled=True
    ).astype(jnp.float32)
    result = middle.astype(jnp.float32) + route_w[:, None] * expert_sum
    hidden_out = jnp.where(local_valid[:, None], result, 0.0).astype(jnp.bfloat16)[None]
    seq_valid = jnp.arange(seq_len, dtype=jnp.int32) < length
    cache_pair = jnp.where(
        seq_valid[None, :, None], qkv_rows[:, 1:3].transpose(1, 0, 2), jnp.zeros((), jnp.bfloat16)
    )
    return (
        server_qkv,
        server_out,
        server_gate,
        server_up,
        server_down,
        hidden_out,
        cache_pair[None],
    )


def solution(mesh):
    placed = (
        P("dp", "tensor", None),
        P("dp"),
        P("dp"),
        P("dp", None, None),
        P(("tensor", "dp"), None, None),
        P(("tensor", "dp"), None),
        P("tensor", None),
        P("tensor", None),
        P("tensor", None),
        P(),
        P(),
        P(),
    )
    return jax.shard_map(
        shards,
        mesh=mesh,
        in_specs=placed,
        out_specs=(
            P(None, None, "tensor"),
            P("tensor", None),
            P(None, "tensor"),
            P(None, "tensor"),
            P(None, "tensor"),
            P("dp", "tensor", None),
            P("dp", None, None, "tensor"),
        ),
        check_vma=False,
    )
```

profile of v0, /device:TPU:12, one launch (start us, length us, event | category | flops | bytes accessed | tf_op | source)
XLA Modules:
  0.0 507.0 jit_solution(11771919291552511364)
XLA Ops:
  16.3 16.8 %all_to_all.75 = bf16[8,2,27648]{2,1,0:T(2,128)(2,1)} all-to-all(bf16[8,2,27648]{2,1,0:T(2,128)(2,1)} %reshape.272), channel_id=1, replica_groups=mesh['dp'=4,'tensor'=8] {'tensor'}, dimensions={0} | all-to-all | bytes 1769472 | tf_op jit(solution)/shard_map/all_to_all | solution.py:78
  44.3 63.5 %all-gather.5.cloned.1.call-done = bf16[2304,3,256]{2,0,1:T(8,128)(2,1)} async-done(((bf16[576,3,256]{2,0,1:T(8,128)(2,1)}), bf16[2304,3,256]{2,0,1:T(8,128)(2,1)}) %all-gather.5.cloned.1.call-update) | async-done | bytes 3538960 | tf_op jit(solution)/shard_map/all_gather | solution.py:80
  112.0 38.1 %all-gather.9.cloned.1.call-done = bf16[1024,2304]{1,0:T(8,128)(2,1)} async-done(((bf16[128,2304]{1,0:T(8,128)(2,1)}), bf16[1024,2304]{1,0:T(8,128)(2,1)}) %all-gather.9.cloned.1.call-update) | async-done | bytes 4718608 | tf_op jit(solution)/shard_map/all_gather | solution.py:98
  150.0 6.8 %fusion.61 = (bf16[1024,3,256]{0,2,1:T(8,128)(2,1)S(1)}, f32[1024,3,256]{0,2,1:T(8,128)S(1)}) fusion(bf16[2304,3,256]{2,0,1:T(8,128)(2,1)} %bitcast.102, bf16[1024,2304]{1,0:T(8,128)(2,1)} %all-gather.9.cloned.1.call-done), kind=kOutput, calls=%fused_computation.108 | convolution fusion | flops 3624665088 | bytes 12976128 | tf_op jit(solution)/shard_map/sd,dtc->stc/dot_general | solution.py:99
  157.4 5.4 %fusion.62 = (f32[4,512]{1,0:T(4,128)S(1)}, f32[4,512,1024]{2,1,0:T(8,128)}) fusion(pred[512,1024]{1,0:T(8,128)(4,1)S(1)} %iota_compare_fusion, bf16[1024,4,32]{0,2,1:T(8,128)(2,1)S(1)} %get-tuple-element.52, bf16[1024,4,32]{0,2,1:T(8,128)(2,1)S(1)} %get-tuple-element.53, bf16[1024,4,32]{0,2,1:T(8,128)(2,1)S(1)} %get-tuple-element.49, ...), kind=kOutput, calls=%fused_computation.109 | convolution fusion | flops 278397952 | bytes 9969664 | tf_op jit(solution)/shard_map/sub | solution.py:41
  172.7 9.6 %all-gather.7.cloned.1.call-done = bf16[256,2304]{1,0:T(8,128)(2,1)} async-done(((bf16[64,2304]{1,0:T(8,128)(2,1)}), bf16[256,2304]{1,0:T(8,128)(2,1)}) %all-gather.7.cloned.1.call-update) | async-done | bytes 1179664 | tf_op jit(solution)/shard_map/all_gather | solution.py:81
  187.4 53.4 %reduce-scatter.3.cloned.1.call-done = bf16[128,2304]{1,0:T(8,128)(2,1)} async-done(((bf16[1024,2304]{1,0:T(8,128)(2,1)}), bf16[128,2304]{1,0:T(8,128)(2,1)}) %reduce-scatter.3.cloned.1.call-update) | async-done | bytes 589840 | tf_op jit(solution)/shard_map/reduce_scatter | solution.py:120
  249.3 8.5 %all_to_all.59 = bf16[288,8,720]{2,1,0:T(8,128)(2,1)} reshape(bf16[288,5760]{1,0:T(8,128)(2,1)} %convert_element_type.88) | data formatting | bytes 6635520 | tf_op jit(solution)/shard_map/all_to_all | solution.py:65
  272.3 8.5 %all_to_all.63 = bf16[288,8,720]{2,1,0:T(8,128)(2,1)} reshape(bf16[288,5760]{1,0:T(8,128)(2,1)} %convert_element_type.89) | data formatting | bytes 6635520 | tf_op jit(solution)/shard_map/all_to_all | solution.py:68
  285.3 34.4 %all-to-all-done.1 = bf16[288,8,720]{2,0,1:T(8,128)(2,1)} async-done(((bf16[288,8,720]{2,0,1:T(8,128)(2,1)}), bf16[288,8,720]{2,0,1:T(8,128)(2,1)}, u32[]{:S(2)}, u32[]{:S(2)}) %all-to-all-start.1) | async-done | bytes 3317792 | tf_op jit(solution)/shard_map/all_to_all | solution.py:65
  319.7 5.9 %all-to-all-start.2 = ((bf16[288,8,720]{2,0,1:T(8,128)(2,1)}), bf16[288,8,720]{2,0,1:T(8,128)(2,1)}, u32[]{:S(2)}, u32[]{:S(2)}) async-start(bf16[288,8,720]{2,0,1:T(8,128)(2,1)} %copy.64), calls=%async_computation.2 | async-start | bytes 7077888 | tf_op jit(solution)/shard_map/all_to_all | solution.py:68
  330.5 8.4 %all_to_all.67 = bf16[288,8,720]{2,1,0:T(8,128)(2,1)} reshape(bf16[288,5760]{1,0:T(8,128)(2,1)} %convert_element_type.90) | data formatting | bytes 6635520 | tf_op jit(solution)/shard_map/all_to_all | solution.py:71
  343.5 22.8 %all-to-all-done.2 = bf16[288,8,720]{2,0,1:T(8,128)(2,1)} async-done(((bf16[288,8,720]{2,0,1:T(8,128)(2,1)}), bf16[288,8,720]{2,0,1:T(8,128)(2,1)}, u32[]{:S(2)}, u32[]{:S(2)}) %all-to-all-start.2) | async-done | bytes 3317792 | tf_op jit(solution)/shard_map/all_to_all | solution.py:68
  366.3 5.9 %all-to-all-start.3 = ((bf16[288,8,720]{2,0,1:T(8,128)(2,1)}), bf16[288,8,720]{2,0,1:T(8,128)(2,1)}, u32[]{:S(2)}, u32[]{:S(2)}) async-start(bf16[288,8,720]{2,0,1:T(8,128)(2,1)} %copy.65), calls=%async_computation.3 | async-start | bytes 7077888 | tf_op jit(solution)/shard_map/all_to_all | solution.py:71
  377.4 7.8 %gather_fusion = bf16[512,2304]{1,0:T(8,128)(2,1)S(1)} fusion(bf16[1024,2304]{1,0:T(8,128)(2,1)} %all-gather.11.cloned.1.call-done, s32[1024]{0:T(1024)S(1)} %pad_clamp_fusion), kind=kCustom, calls=%fused_computation | custom fusion | bytes 4720640 | tf_op jit(solution)/shard_map/gather | solution.py:151
  385.3 5.0 fusion.72
  390.3 22.6 %all-to-all-done.3 = bf16[288,8,720]{2,0,1:T(8,128)(2,1)} async-done(((bf16[288,8,720]{2,0,1:T(8,128)(2,1)}), bf16[288,8,720]{2,0,1:T(8,128)(2,1)}, u32[]{:S(2)}, u32[]{:S(2)}) %all-to-all-start.3) | async-done | bytes 3317792 | tf_op jit(solution)/shard_map/all_to_all | solution.py:71
  412.9 9.9 %fusion.32 = f32[512,2304]{1,0:T(8,128)} fusion(bf16[2304,720]{1,0:T(8,128)(2,1)} %bitcast.12, f32[512,720]{0,1:T(8,128)} %fusion.72, bf16[512,2304]{1,0:T(8,128)(2,1)S(1)} %gather_fusion, bf16[2304,720]{1,0:T(8,128)(2,1)} %bitcast.10), kind=kOutput, calls=%fused_computation.51 | convolution fusion | flops 3399598080 | bytes 15187968 | tf_op jit(solution)/shard_map/dot_general | solution.py:155
  422.9 13.3 %scatter_custom_fusion.1 = f32[1024,2304]{1,0:T(8,128)} fusion(s32[512]{0:T(512)S(1)} %get-tuple-element.57, f32[512,2304]{1,0:T(8,128)} %fusion.32, f32[]{:T(128)} %constant.20.clone.1), kind=kCustom, calls=%fused_computation.12 | custom fusion | flops 1179648 | bytes 9437696 | tf_op jit(solution)/shard_map/scatter-add | solution.py:161
  436.2 6.4 %convert_element_type.109 = bf16[1024,2304]{1,0:T(8,128)(2,1)} convert(f32[1024,2304]{1,0:T(8,128)} %scatter_custom_fusion.1) | non-fusion elementwise | flops 2359296 | bytes 14155776 | tf_op jit(solution)/shard_map/convert_element_type | solution.py:164
  443.3 5.6 %copy.68 = bf16[2304,720]{0,1:T(8,128)(2,1)} copy(bf16[2304,720]{1,0:T(8,128)(2,1)} %bitcast.8) | data formatting | bytes 6635520
  448.9 5.8 %copy.69 = bf16[2304,720]{0,1:T(8,128)(2,1)} copy(bf16[2304,720]{1,0:T(8,128)(2,1)} %bitcast.10) | data formatting | bytes 6635520
  454.7 5.8 %copy.70 = bf16[2304,720]{0,1:T(8,128)(2,1)} copy(bf16[2304,720]{1,0:T(8,128)(2,1)} %bitcast.12) | data formatting | bytes 6635520
  464.2 32.4 %reduce-scatter.5.cloned.1.call-done = bf16[128,2304]{1,0:T(8,128)(2,1)} async-done(((bf16[1024,2304]{1,0:T(8,128)(2,1)}), bf16[128,2304]{1,0:T(8,128)(2,1)}) %reduce-scatter.5.cloned.1.call-update) | async-done | bytes 589840 | tf_op jit(solution)/shard_map/reduce_scatter | solution.py:163
  (99 shorter events, 88.3 us)
Async XLA Ops:
  7.2 456.8 %copy-start = (bf16[2304,8]{0,1:T(8,128)(2,1)S(1)}, bf16[2304,8]{0,1:T(8,128)(2,1)}, u32[]{:S(2)}) copy-start(bf16[2304,8]{0,1:T(8,128)(2,1)} %param.23) | copy-start | bytes 110596
  7.2 100.6 %all-gather.5.cloned.1.call-start = ((), (), s32[]{:S(2)}) async-start(), calls=%async_computation.6 | async-start | bytes 4423680 | tf_op jit(solution)/shard_map/all_gather | solution.py:80
  33.2 6.8 %copy-start.1 = (bf16[1,128,2304]{2,1,0:T(8,128)(2,1)S(1)}, bf16[1,128,2304]{2,1,0:T(8,128)(2,1)}, u32[]{:S(2)}) copy-start(bf16[1,128,2304]{2,1,0:T(8,128)(2,1)} %param.12) | copy-start | bytes 1769476
  33.2 7.0 %copy-start.10 = (f32[2304]{0:T(1024)S(1)}, f32[2304]{0:T(1024)}, u32[]{:S(2)}) copy-start(f32[2304]{0:T(1024)} %param.21) | copy-start | bytes 27652
  37.6 3.6 copy-start.9
  39.9 110.2 %all-gather.9.cloned.1.call-start = ((), (), s32[]{:S(2)}) async-start(), calls=%async_computation.8 | async-start | bytes 5308416 | tf_op jit(solution)/shard_map/all_gather | solution.py:98
  41.2 141.1 %all-gather.7.cloned.1.call-start = ((), (), s32[]{:S(2)}) async-start(), calls=%async_computation.7 | async-start | bytes 1474560 | tf_op jit(solution)/shard_map/all_gather | solution.py:81
  42.0 198.8 %reduce-scatter.3.cloned.1.call-start = ((), (), s32[]{:S(2)}) async-start(), calls=%async_computation.9 | async-start | bytes 5308416 | tf_op jit(solution)/shard_map/reduce_scatter | solution.py:120
  157.4 5.4 %copy-start.5 = (bf16[1024,4,32]{0,2,1:T(8,128)(2,1)}, bf16[1024,4,32]{0,2,1:T(8,128)(2,1)S(1)}, u32[]{:S(2)}) copy-start(bf16[1024,4,32]{0,2,1:T(8,128)(2,1)S(1)} %get-tuple-element.48) | copy-start | bytes 786436
  157.4 5.4 %copy-start.7 = (bf16[1024,4,32]{0,2,1:T(8,128)(2,1)}, bf16[1024,4,32]{0,2,1:T(8,128)(2,1)S(1)}, u32[]{:S(2)}) copy-start(bf16[1024,4,32]{0,2,1:T(8,128)(2,1)S(1)} %get-tuple-element.49) | copy-start | bytes 786436
  166.5 4.7 copy-start.13
  187.2 55.0 %copy-start.11 = (f32[2304]{0:T(1024)S(1)}, f32[2304]{0:T(1024)}, u32[]{:S(2)}) copy-start(f32[2304]{0:T(1024)} %param.22) | copy-start | bytes 27652
  187.2 190.2 %all-gather.11.cloned.1.call-start = ((), (), s32[]{:S(2)}) async-start(), calls=%async_computation.10 | async-start | bytes 5308416 | tf_op jit(solution)/shard_map/all_gather | solution.py:141
  262.3 57.4 %all-to-all-start.1 = ((bf16[288,8,720]{2,0,1:T(8,128)(2,1)}), bf16[288,8,720]{2,0,1:T(8,128)(2,1)}, u32[]{:S(2)}, u32[]{:S(2)}) async-start(bf16[288,8,720]{2,0,1:T(8,128)(2,1)} %copy.63), calls=%async_computation.1 | async-start | bytes 7077888 | tf_op jit(solution)/shard_map/all_to_all | solution.py:65
  319.7 46.6 %all-to-all-start.2 = ((bf16[288,8,720]{2,0,1:T(8,128)(2,1)}), bf16[288,8,720]{2,0,1:T(8,128)(2,1)}, u32[]{:S(2)}, u32[]{:S(2)}) async-start(bf16[288,8,720]{2,0,1:T(8,128)(2,1)} %copy.64), calls=%async_computation.2 | async-start | bytes 7077888 | tf_op jit(solution)/shard_map/all_to_all | solution.py:68
  343.5 28.7 %copy-start.12 = (s32[1,1024,2]{1,2,0:T(2,128)S(1)}, s32[1,1024,2]{1,2,0:T(2,128)}, u32[]{:S(2)}) copy-start(s32[1,1024,2]{1,2,0:T(2,128)} %param.15) | copy-start | bytes 24580
  366.3 46.6 %all-to-all-start.3 = ((bf16[288,8,720]{2,0,1:T(8,128)(2,1)}), bf16[288,8,720]{2,0,1:T(8,128)(2,1)}, u32[]{:S(2)}, u32[]{:S(2)}) async-start(bf16[288,8,720]{2,0,1:T(8,128)(2,1)} %copy.65), calls=%async_computation.3 | async-start | bytes 7077888 | tf_op jit(solution)/shard_map/all_to_all | solution.py:71
  372.2 124.4 %reduce-scatter.5.cloned.1.call-start = ((), (), s32[]{:S(2)}) async-start(), calls=%async_computation.11 | async-start | bytes 5308416 | tf_op jit(solution)/shard_map/reduce_scatter | solution.py:163
  454.7 5.8 %copy-start.6 = (bf16[1024,4,32]{0,2,1:T(8,128)(2,1)S(1)}, bf16[1024,4,32]{0,2,1:T(8,128)(2,1)}, u32[]{:S(2)}) copy-start(bf16[1024,4,32]{0,2,1:T(8,128)(2,1)} %copy-done.5) | copy-start | bytes 786436
  454.7 5.8 %copy-start.8 = (bf16[1024,4,32]{0,2,1:T(8,128)(2,1)S(1)}, bf16[1024,4,32]{0,2,1:T(8,128)(2,1)}, u32[]{:S(2)}) copy-start(bf16[1024,4,32]{0,2,1:T(8,128)(2,1)} %copy-done.7) | copy-start | bytes 786436
  460.5 3.4 copy-start.2
  460.5 36.1 %copy-start.3 = (bf16[128,2304]{1,0:T(8,128)(2,1)S(1)}, bf16[128,2304]{1,0:T(8,128)(2,1)}, u32[]{:S(2)}) copy-start(bf16[128,2304]{1,0:T(8,128)(2,1)} %reduce-scatter.3.cloned.1.call-done) | copy-start | bytes 1769476
  460.6 38.3 %copy-start.4 = (bf16[256,2304]{1,0:T(8,128)(2,1)S(1)}, bf16[256,2304]{1,0:T(8,128)(2,1)}, u32[]{:S(2)}) copy-start(bf16[256,2304]{1,0:T(8,128)(2,1)} %all-gather.7.cloned.1.call-done) | copy-start | bytes 3538948
Sparse Core Ops, SparseCore 0:
  40.0 67.7 all-gather.4
  110.3 39.7 all-gather.8
  152.2 30.1 all-gather.6
  187.3 53.4 reduce-scatter.2
  244.5 59.9 all-gather.10
  442.7 53.8 reduce-scatter.4
where the time goes:
time: 513 us; the launch traced here: 507 us
  waiting for transfers between devices  277 us (54%)
  local copies, waits for them, and re-layouts  91.6 us (18%)
  other arithmetic  47.8 us (9%)
  matrix products  40.2 us (8%)
  starting transfers between devices  17.6 us (3%)
  blocking collectives  16.8 us (3%)
  between operations  16 us (3%)
    all_gather x1, waiting for transfers between devices, shards(): lax.all_gather(column_part, 'dp', axis=0, tiled=True)  63.5 us
    reduce_scatter x1, waiting for transfers between devices, shards(): lax.psum_scatter(jnp.dot(attended, server_out, preferred_element_type=jnp...  53.4 us
    all_gather x1, waiting for transfers between devices, shards(): piece = lax.all_gather(normed, 'tensor', axis=0, tiled=True)  38.1 us
    all_to_all x1, waiting for transfers between devices, shards(): lax.all_to_all(trainer_gate.astype(jnp.bfloat16), 'tensor', split_axis=1,...  34.4 us
    reduce_scatter x1, waiting for transfers between devices, shards(): lax.psum_scatter(terms.astype(jnp.bfloat16), 'tensor', scatter_dimension=...  32.4 us
    unnamed x35, local copies, waits for them, and re-layouts  30.6 us
    all_to_all x1, waiting for transfers between devices, shards(): lax.all_to_all(trainer_up.astype(jnp.bfloat16), 'tensor', split_axis=1, c...  22.8 us
    all_to_all x1, waiting for transfers between devices, shards(): lax.all_to_all(trainer_down.astype(jnp.bfloat16), 'tensor', split_axis=1,...  22.6 us
  transfers between devices with their start and end apart: 9, of which 8 were waited for; matrix products, arithmetic and copies ran while one was open for 19% of the time, Pallas kernels for 0%

commit v1 on v0

v1 whole, which is shorter than its diff:
```python
import jax
import jax.numpy as jnp
from jax import lax
from jax.experimental import pallas as pl
from jax.experimental.pallas import tpu as pltpu
from jax.sharding import PartitionSpec as P

HEAD_DIM = 64


def swap_pairs(size, step):
    return [(i, i ^ step) for i in range(size)]


def send(block, size, step):
    return lax.ppermute(block, "tensor", swap_pairs(size, step))


def split_columns(matrix, parts):
    rows, width = matrix.shape
    part = width // parts
    chunk = rows
    for cand in (48, 32, 16):
        if rows % cand == 0:
            chunk = cand
            break

    def kernel(x_ref, o_ref):
        for t in range(parts):
            o_ref[t] = x_ref[:, t * part : (t + 1) * part].astype(jnp.bfloat16)

    return pl.pallas_call(
        kernel,
        out_shape=jax.ShapeDtypeStruct((parts, rows, part), jnp.bfloat16),
        grid=(rows // chunk,),
        in_specs=[pl.BlockSpec((chunk, width), lambda i: (i, 0))],
        out_specs=pl.BlockSpec((parts, chunk, part), lambda i: (0, i, 0)),
        name="split_columns",
    )(matrix)


def split_heads(qkv, parts):
    _, rows, width = qkv.shape
    part = width // parts

    def kernel(x_ref, o_ref):
        for t in range(parts):
            for j in range(3):
                o_ref[t, j] = x_ref[j, :, t * part : (t + 1) * part].astype(jnp.bfloat16)

    return pl.pallas_call(
        kernel,
        out_shape=jax.ShapeDtypeStruct((parts, 3, rows, part), jnp.bfloat16),
        name="split_heads",
    )(qkv)


def reorder_blocks(stacked, me):
    count, rows, width = stacked.shape

    def kernel(me_ref, x_ref, o_ref):
        o_ref[...] = x_ref[0]

    return pl.pallas_call(
        kernel,
        out_shape=jax.ShapeDtypeStruct((count * rows, width), stacked.dtype),
        grid_spec=pltpu.PrefetchScalarGridSpec(
            num_scalar_prefetch=1,
            grid=(count,),
            in_specs=[pl.BlockSpec((1, rows, width), lambda i, m: (m[0] ^ i, 0, 0))],
            out_specs=pl.BlockSpec((rows, width), lambda i, m: (i, 0)),
        ),
        name="reorder_blocks",
    )(me.reshape(1), stacked)


def rms_scale(values, gain_row):
    mean_sq = jnp.mean(values * values, axis=-1, keepdims=True)
    return values * lax.rsqrt(mean_sq + 1e-05) * gain_row


def rotate(head_block, positions):
    half_dim = head_block.shape[-1] // 2
    inv_freq = jnp.power(
        10000.0, jnp.arange(half_dim, dtype=jnp.float32) * (-2.0 / head_block.shape[-1])
    )
    angles = positions.astype(jnp.float32)[:, None] * inv_freq[None, :]
    cosine = jnp.cos(angles)[:, None, :]
    sine_part = jnp.sin(angles)[:, None, :]
    first_half = head_block[..., :half_dim]
    second_half = head_block[..., half_dim:]
    return jnp.concatenate(
        [
            first_half * cosine - second_half * sine_part,
            second_half * cosine + first_half * sine_part,
        ],
        axis=-1,
    )


def attend_block(query_blk, key_blk, value_blk, row_start):
    scores = jnp.einsum(
        "qhd,khd->hqk", query_blk, key_blk, preferred_element_type=jnp.float32
    ) * query_blk.shape[-1] ** (-0.5)
    row_ids = row_start + jnp.arange(query_blk.shape[0], dtype=jnp.int32)
    col_ids = jnp.arange(key_blk.shape[0], dtype=jnp.int32)
    scores = jnp.where(row_ids[None, :, None] >= col_ids[None, None, :], scores, -1e30)
    row_max = jnp.max(scores, axis=-1, keepdims=True)
    exp_scores = jnp.exp(scores - row_max)
    attn_probs = (exp_scores / jnp.sum(exp_scores, axis=-1, keepdims=True)).astype(jnp.bfloat16)
    return jnp.einsum(
        "hqk,khd->qhd", attn_probs, value_blk, preferred_element_type=jnp.float32
    ).astype(jnp.bfloat16)


def shards(
    hidden_in,
    prompt_len,
    start_pos,
    routes,
    trainer_qkv,
    trainer_out,
    trainer_gate,
    trainer_up,
    trainer_down,
    attn_gain,
    moe_gain,
    router,
):
    size = lax.axis_size("tensor")
    replicas = lax.axis_size("dp")
    chips = size // 2
    me = lax.axis_index("tensor").astype(jnp.int32)
    plane = lax.axis_index("dp").astype(jnp.int32)
    chip, core = me // 2, me % 2
    rows_dev, model = hidden_in.shape[1], hidden_in.shape[2]
    seq_len = rows_dev * size
    length = prompt_len[0]
    offset = start_pos[0]
    my_first = me * rows_dev

    qkv_parts = split_heads(trainer_qkv.transpose(1, 0, 2), size)
    qkv_cols = lax.all_to_all(qkv_parts, "tensor", 0, 0, tiled=True)
    out_cast = trainer_out.astype(jnp.bfloat16)

    tokens = hidden_in[0].astype(jnp.float32)
    normed = rms_scale(tokens, attn_gain).astype(jnp.bfloat16)
    same_core = jnp.stack([normed] + [send(normed, size, 2 * j) for j in range(1, chips)])
    other_core = send(same_core, size, 1)
    stacked = jnp.stack([same_core, other_core], axis=1).reshape(size, rows_dev, model)
    piece = reorder_blocks(stacked, me)

    gate_parts = split_columns(trainer_gate, size)
    up_parts = split_columns(trainer_up, size)
    down_rows = trainer_down.shape[0] // replicas
    down_quarter = lax.dynamic_slice_in_dim(trainer_down, plane * down_rows, down_rows, 0)
    down_parts = split_columns(down_quarter, size)

    server_out = lax.all_gather(out_cast, "dp", axis=0, tiled=True)
    qkv_all = lax.all_gather(qkv_cols, "dp", axis=0)
    server_gate = lax.all_to_all(gate_parts, "tensor", 0, 0, tiled=True).reshape(model, -1)
    server_up = lax.all_to_all(up_parts, "tensor", 0, 0, tiled=True).reshape(model, -1)
    down_cols = lax.all_to_all(down_parts, "tensor", 0, 0, tiled=True)
    down_all = lax.all_gather(down_cols, "dp", axis=0)
    units = server_gate.shape[1]
    down_t = down_all.transpose(3, 1, 0, 2).reshape(units, model)
    server_down = down_t.T
    local_width = trainer_qkv.shape[2] // size
    qkv_server = qkv_all.transpose(2, 1, 0, 3, 4).reshape(3, model, local_width)
    server_qkv = qkv_server.transpose(1, 0, 2)

    out_pair = jnp.concatenate([server_out, send(server_out, size, 1)], axis=0)
    gate_other = send(server_gate, size, 1)
    up_other = send(server_up, size, 1)
    down_other = send(down_t, size, 1)

    heads_here = local_width // HEAD_DIM
    mixed = jnp.einsum("sd,tdc->tsc", piece, qkv_server, preferred_element_type=jnp.float32)
    places = offset + jnp.arange(seq_len, dtype=jnp.int32)
    query_all = rotate(mixed[0].reshape(-1, heads_here, HEAD_DIM), places).astype(jnp.bfloat16)
    keys_all = rotate(mixed[1].reshape(-1, heads_here, HEAD_DIM), places).astype(jnp.bfloat16)
    values_all = mixed[2].reshape(-1, heads_here, HEAD_DIM).astype(jnp.bfloat16)
    block_len = min(512, seq_len)
    block_outs = []
    for block_id in range(seq_len // block_len):
        row_lo = block_id * block_len
        row_hi = row_lo + block_len
        block_outs.append(
            attend_block(query_all[row_lo:row_hi], keys_all[:row_hi], values_all[:row_hi], row_lo)
        )
    attended = jnp.concatenate(block_outs, axis=0).reshape(chips, 2, rows_dev, local_width)
    seq_valid = jnp.arange(seq_len, dtype=jnp.int32) < length
    cache_pair = jnp.where(
        seq_valid[None, :, None],
        jnp.stack([keys_all.reshape(seq_len, -1), values_all.reshape(seq_len, -1)]),
        jnp.zeros((), jnp.bfloat16),
    )

    att_mine = lax.dynamic_index_in_dim(attended, core, 1, keepdims=False)
    att_other = send(lax.dynamic_index_in_dim(attended, 1 - core, 1, keepdims=False), size, 1)
    att_pair = jnp.concatenate([att_mine, att_other], axis=-1)

    def attn_part(j):
        rows = lax.dynamic_index_in_dim(att_pair, chip ^ j, 0, keepdims=False)
        return jnp.dot(rows, out_pair, preferred_element_type=jnp.float32)

    got = [send(attn_part(j).astype(jnp.bfloat16), size, 2 * j) for j in range(1, chips)]
    attn_sum = attn_part(0)
    for part in got:
        attn_sum = attn_sum + part.astype(jnp.float32)
    middle = (tokens + attn_sum).astype(jnp.bfloat16)
    normed_moe = rms_scale(middle.astype(jnp.float32), moe_gain).astype(jnp.bfloat16)

    moe_rows = jnp.concatenate(
        [normed_moe] + [send(normed_moe, size, 2 * j) for j in range(1, chips)], axis=0
    )

    local_routes = lax.dynamic_slice_in_dim(routes[0], my_first, rows_dev, 0)
    local_valid = my_first + jnp.arange(rows_dev, dtype=jnp.int32) < length
    logits = jnp.dot(normed_moe, router, preferred_element_type=jnp.float32)
    expert_ids = jnp.arange(router.shape[1], dtype=jnp.int32)
    logit_first = jnp.sum(
        jnp.where(local_routes[:, 0:1] == expert_ids[None, :], logits, 0.0), axis=1
    )
    logit_second = jnp.sum(
        jnp.where(local_routes[:, 1:2] == expert_ids[None, :], logits, 0.0), axis=1
    )
    other_logit = jnp.where(local_routes[:, 0] == 0, logit_second, logit_first)
    local_routed = jnp.any(local_routes == 0, axis=1)
    route_w = jnp.where(local_routed, jax.nn.sigmoid(logits[:, 0] - other_logit), 0.0)

    def activate(gate_w, up_w):
        gate_val = jnp.dot(moe_rows, gate_w, preferred_element_type=jnp.float32)
        up_val = jnp.dot(moe_rows, up_w, preferred_element_type=jnp.float32)
        return (jax.nn.silu(gate_val) * up_val).astype(jnp.bfloat16)

    sums = jnp.dot(
        activate(server_gate, server_up), down_t, preferred_element_type=jnp.float32
    ) + jnp.dot(activate(gate_other, up_other), down_other, preferred_element_type=jnp.float32)
    sums = sums.reshape(chips, rows_dev, model)
    expert_sum = sums[0]
    for j in range(1, chips):
        expert_sum = expert_sum + send(sums[j].astype(jnp.bfloat16), size, 2 * j).astype(
            jnp.float32
        )
    expert_sum = jnp.where(local_routed[:, None], expert_sum, 0.0)
    result = middle.astype(jnp.float32) + route_w[:, None] * expert_sum
    hidden_out = jnp.where(local_valid[:, None], result, 0.0).astype(jnp.bfloat16)[None]
    return (
        server_qkv,
        server_out,
        server_gate,
        server_up,
        server_down,
        hidden_out,
        cache_pair[None],
    )


def solution(mesh):
    placed = (
        P("dp", "tensor", None),
        P("dp"),
        P("dp"),
        P("dp", None, None),
        P(("tensor", "dp"), None, None),
        P(("tensor", "dp"), None),
        P("tensor", None),
        P("tensor", None),
        P("tensor", None),
        P(),
        P(),
        P(),
    )
    return jax.shard_map(
        shards,
        mesh=mesh,
        in_specs=placed,
        out_specs=(
            P(None, None, "tensor"),
            P("tensor", None),
            P(None, "tensor"),
            P(None, "tensor"),
            P(None, "tensor"),
            P("dp", "tensor", None),
            P("dp", None, None, "tensor"),
        ),
        check_vma=False,
    )
```

time: 513 us -> 355 us (0.69)
  waiting for transfers between devices: 277 us -> 125 us
  local copies, waits for them, and re-layouts: 91.6 us -> 56.5 us
  other arithmetic: 47.8 us -> 17.4 us
  Pallas kernels: 0 us -> 25.5 us
  matrix products: 40.2 us -> 62.2 us
  starting transfers between devices: 17.6 us -> 29.1 us
    ppermute x0 -> x18, waiting for transfers between devices: none -> 121 us  [send(): return lax.ppermute(block, 'tensor', swap_pairs(size, step))]
    all_gather x4 -> x3, waiting for transfers between devices: 111 us -> 3.86 us  [the longest x1 3.82 us: shards(): qkv_all = lax.all_gather(qkv_cols, 'dp', axis=0)]
    reduce_scatter x2 -> x0, waiting for transfers between devices: 85.8 us -> none  [the longest x1 53.4 us: shards(): lax.psum_scatter(jnp.dot(attended, server_out, preferred_element_type=jnp...]
    all_to_all x3, waiting for transfers between devices: 79.8 us -> 0.01 us  [the longest x1 0.01 us: shards(): down_cols = lax.all_to_all(down_parts, 'tensor', 0, 0, tiled=True)]
    all_to_all x7 -> x0, local copies, waits for them, and re-layouts: 41.2 us -> none  [the longest x2 13 us: shards(): lax.all_to_all(trainer_gate.astype(jnp.bfloat16), 'tensor', split_axis=1,...]
    pallas_call x0 -> x5, Pallas kernels: none -> 25.5 us  [the longest x3 16.1 us: split_columns(): pl.pallas_call(kernel, out_shape=jax.ShapeDtypeStruct((parts, rows, part)...]
    convert_element_type x6 -> x1, other arithmetic: 23.8 us -> 0.03 us  [shards(): rotate(mixed[1].reshape(-1, heads_here, HEAD_DIM), places)]
    dot_general x4 -> x9, matrix products: 26.7 us -> 43.9 us  [the longest x1 11.7 us: shards(): jnp.dot(activate(gate_other, up_other), down_other, preferred_element_typ...]
  transfers between devices with their start and end apart: 9 -> 24, of which waited for: 8 -> 9; matrix products, arithmetic and copies ran while one was open for 19% -> 32% of each run, Pallas kernels for 0% -> 7%
where the time goes in v1:
time: 355 us; the launch traced here: 348 us
  waiting for transfers between devices  125 us (35%)
  matrix products  62.2 us (18%)
  local copies, waits for them, and re-layouts  56.5 us (16%)
  starting transfers between devices  29.1 us (8%)
  Pallas kernels  25.5 us (7%)
  other arithmetic  17.4 us (5%)
  blocking collectives  16.8 us (5%)
  between operations  15.4 us (4%)
    ppermute x18, waiting for transfers between devices, send(): return lax.ppermute(block, 'tensor', swap_pairs(size, step))  121 us
    unnamed x48, local copies, waits for them, and re-layouts  28.6 us
    all_to_all x1, blocking collectives, shards(): qkv_cols = lax.all_to_all(qkv_parts, 'tensor', 0, 0, tiled=True)  16.8 us
    pallas_call x3, Pallas kernels, split_columns(): pl.pallas_call(kernel, out_shape=jax.ShapeDtypeStruct((parts, rows, part)...  16.1 us
    ppermute x18, starting transfers between devices, send(): return lax.ppermute(block, 'tensor', swap_pairs(size, step))  15.3 us
    sub x2, matrix products, attend_block(): exp_scores = jnp.exp(scores - row_max)  12.6 us
    dot_general x1, matrix products, shards(): jnp.dot(activate(gate_other, up_other), down_other, preferred_element_typ...  11.7 us
    dot_general x2, matrix products, activate(): up_val = jnp.dot(moe_rows, up_w, preferred_element_type=jnp.float32)  11.5 us
  transfers between devices with their start and end apart: 24, of which 9 were waited for; matrix products, arithmetic and copies ran while one was open for 32% of the time, Pallas kernels for 7%

profile of v1, /device:TPU:12, one launch (start us, length us, event | category | flops | bytes accessed | tf_op | source)
XLA Modules:
  0.0 348.1 jit_solution(1295927051155685337)
XLA Ops:
  11.7 16.8 %all_to_all.20 = bf16[8,3,72,256]{3,2,1,0:T(8,128)(2,1)} all-to-all(bf16[8,3,72,256]{3,2,1,0:T(8,128)(2,1)} %split_heads.1), channel_id=1, replica_groups=mesh['dp'=4,'tensor'=8] {'tensor'}, dimensions={0} | all-to-all | bytes 1769472 | tf_op jit(solution)/shard_map/all_to_all | solution.py:143
  32.8 12.5 %collective-permute-done = bf16[128,2304]{1,0:T(8,128)(2,1)S(1)} collective-permute-done((bf16[128,2304]{1,0:T(8,128)(2,1)S(1)}, bf16[128,2304]{1,0:T(8,128)(2,1)S(1)}, u32[]{:S(2)}, u32[]{:S(2)}) %collective-permute-start) | collective-permute-done | bytes 589856 | tf_op jit(solution)/shard_map/ppermute | solution.py:16
  45.3 10.8 %collective-permute-done.1 = bf16[128,2304]{1,0:T(8,128)(2,1)S(1)} collective-permute-done((bf16[128,2304]{1,0:T(8,128)(2,1)S(1)}, bf16[128,2304]{1,0:T(8,128)(2,1)S(1)}, u32[]{:S(2)}, u32[]{:S(2)}) %collective-permute-start.1) | collective-permute-done | bytes 589856 | tf_op jit(solution)/shard_map/ppermute | solution.py:16
  65.5 4.3 %all-to-all-start.3 = ((bf16[8,72,720]{2,1,0:T(8,128)(2,1)}), bf16[8,72,720]{2,1,0:T(8,128)(2,1)S(1)}, u32[]{:S(2)}, u32[]{:S(2)}) async-start(bf16[8,72,720]{2,1,0:T(8,128)(2,1)} %split_columns.5), calls=%async_computation.3 | async-start | bytes 1769472 | tf_op jit(solution)/shard_map/all_to_all | solution.py:163
  70.5 6.7 %split_columns.4 = bf16[8,288,720]{2,1,0:T(8,128)(2,1)} custom-call(f32[288,5760]{1,0:T(8,128)} %x_ref.3), custom_call_target="tpu_custom_call" | custom-call | tf_op jit(solution)/shard_map/split_columns/pallas_call | solution.py:32
  77.2 6.7 %split_columns.3 = bf16[8,288,720]{2,1,0:T(8,128)(2,1)} custom-call(f32[288,5760]{1,0:T(8,128)} %x_ref.2), custom_call_target="tpu_custom_call" | custom-call | tf_op jit(solution)/shard_map/split_columns/pallas_call | solution.py:32
  87.3 4.5 %all-to-all-start.2 = ((bf16[8,288,720]{2,1,0:T(8,128)(2,1)}), bf16[8,288,720]{2,1,0:T(8,128)(2,1)}, u32[]{:S(2)}, u32[]{:S(2)}) async-start(bf16[8,288,720]{2,1,0:T(8,128)(2,1)} %split_columns.4), calls=%async_computation.2 | async-start | bytes 7077888 | tf_op jit(solution)/shard_map/all_to_all | solution.py:162
  99.4 6.9 %reorder_blocks.1 = bf16[1024,2304]{1,0:T(8,128)(2,1)} custom-call(s32[1]{0:T(128)} %bitcast.13.me_ref, bf16[8,128,2304]{2,1,0:T(8,128)(2,1)} %bitcast.123), custom_call_target="tpu_custom_call" | custom-call | tf_op jit(solution)/shard_map/reorder_blocks/pallas_call | solution.py:64
  121.1 7.8 %fusion.102 = (f32[4,512]{1,0:T(4,128)S(1)}, f32[4,512,1024]{2,1,0:T(8,128)}) fusion(pred[512,1024]{1,0:T(8,128)(4,1)} %iota_compare_fusion, bf16[1024,4,32]{0,2,1:T(8,128)(2,1)} %get-tuple-element.47, bf16[1024,4,32]{0,2,1:T(8,128)(2,1)} %get-tuple-element.46, bf16[1024,4,32]{0,2,1:T(8,128)(2,1)} %copy-done.16, bf16[1024,4,32]{0,2,1:T(8,128)(2,1)} %copy-done.15), kind=kOutput, calls=%fused_computation.149 | convolution fusion | flops 278397952 | bytes 9969664 | tf_op jit(solution)/shard_map/sub | solution.py:109
  128.9 4.7 %fusion.103 = (f32[4,512]{1,0:T(4,128)S(1)}, f32[4,512,512]{1,2,0:T(8,128)}) fusion(pred[512,512]{0,1:T(8,128)(4,1)} %iota_compare_fusion.1, bf16[1024,4,64]{0,2,1:T(8,128)(2,1)S(1)} %maximum_convert_fusion, bf16[1024,4,32]{0,2,1:T(8,128)(2,1)} %get-tuple-element.46, bf16[1024,4,32]{0,2,1:T(8,128)(2,1)} %get-tuple-element.47), kind=kOutput, calls=%fused_computation.150 | convolution fusion | flops 138936832 | bytes 5251072 | tf_op jit(solution)/shard_map/sub | solution.py:109
  151.8 4.9 %all-to-all-start.1 = ((bf16[8,288,720]{2,1,0:T(8,128)(2,1)}), bf16[8,288,720]{2,1,0:T(8,128)(2,1)}, u32[]{:S(2)}, u32[]{:S(2)}) async-start(bf16[8,288,720]{2,1,0:T(8,128)(2,1)} %split_columns.3), calls=%async_computation.1 | async-start | bytes 7077888 | tf_op jit(solution)/shard_map/all_to_all | solution.py:161
  162.3 5.7 %copy.62 = bf16[2304,720]{0,1:T(8,128)(2,1)} copy(bf16[2304,720]{1,0:T(8,128)(2,1)} %bitcast.6) | data formatting | bytes 6635520
  168.0 53.6 %collective-permute-done.7 = bf16[128,2304]{1,0:T(8,128)(2,1)} collective-permute-done((bf16[128,2304]{1,0:T(8,128)(2,1)}, bf16[128,2304]{1,0:T(8,128)(2,1)}, u32[]{:S(2)}, u32[]{:S(2)}) %collective-permute-start.7) | collective-permute-done | bytes 589856 | tf_op jit(solution)/shard_map/ppermute | solution.py:16
  232.6 5.2 %copy.52 = bf16[4,8,72,720]{3,2,0,1:T(8,128)(2,1)} copy(bf16[4,8,72,720]{3,2,1,0:T(8,128)(2,1)} %bitcast.133) | data formatting | bytes 6635520 | tf_op jit(solution)/shard_map/all_gather | solution.py:164
  237.8 5.7 %copy.60 = bf16[720,2304]{1,0:T(8,128)(2,1)} copy(bf16[720,2304]{0,1:T(8,128)(2,1)} %bitcast.120) | data formatting | bytes 6635520 | tf_op jit(solution)/shard_map/reshape | solution.py:166
  246.1 5.6 %copy.63 = bf16[2304,720]{0,1:T(8,128)(2,1)} copy(bf16[2304,720]{1,0:T(8,128)(2,1)} %bitcast.121) | data formatting | bytes 6635520
  253.8 7.8 %collective-permute-done.11 = bf16[128,2304]{1,0:T(8,128)(2,1)} collective-permute-done((bf16[128,2304]{1,0:T(8,128)(2,1)}, bf16[128,2304]{1,0:T(8,128)(2,1)}, u32[]{:S(2)}, u32[]{:S(2)}) %collective-permute-start.11) | collective-permute-done | bytes 589856 | tf_op jit(solution)/shard_map/ppermute | solution.py:16
  261.6 11.1 %collective-permute-done.9 = bf16[128,2304]{1,0:T(8,128)(2,1)} collective-permute-done((bf16[128,2304]{1,0:T(8,128)(2,1)}, bf16[128,2304]{1,0:T(8,128)(2,1)}, u32[]{:S(2)}, u32[]{:S(2)}) %collective-permute-start.9) | collective-permute-done | bytes 589856 | tf_op jit(solution)/shard_map/ppermute | solution.py:16
  272.8 5.8 %fusion.97 = f32[512,720]{0,1:T(8,128)} fusion(bf16[2304,720]{1,0:T(8,128)(2,1)} %bitcast.6, bf16[128,2304]{1,0:T(8,128)(2,1)} %collective-permute-done.11, bf16[128,2304]{1,0:T(8,128)(2,1)} %collective-permute-done.10, bf16[128,2304]{1,0:T(8,128)(2,1)} %collective-permute-done.9, bf16[128,2304]{1,0:T(8,128)(2,1)} %multiply_convert_fusion.2), kind=kOutput, calls=%fused_computation.145 | convolution fusion | flops 1708130304 | bytes 7151616 | tf_op jit(solution)/shard_map/dot_general | solution.py:234
  278.5 5.7 %fusion.95 = f32[512,720]{0,1:T(8,128)} fusion(bf16[2304,720]{0,1:T(8,128)(2,1)} %collective-permute-done.13, bf16[128,2304]{1,0:T(8,128)(2,1)} %collective-permute-done.11, bf16[128,2304]{1,0:T(8,128)(2,1)} %collective-permute-done.10, bf16[128,2304]{1,0:T(8,128)(2,1)} %collective-permute-done.9, bf16[128,2304]{1,0:T(8,128)(2,1)} %multiply_convert_fusion.2), kind=kOutput, calls=%fused_computation.143 | convolution fusion | flops 1708130304 | bytes 7151616 | tf_op jit(solution)/shard_map/dot_general | solution.py:234
  284.3 10.6 %fusion.42 = f32[512,2304]{1,0:T(8,128)} fusion(bf16[720,2304]{0,1:T(8,128)(2,1)} %bitcast.122, f32[512,720]{0,1:T(8,128)} %fusion.97, bf16[2304,720]{1,0:T(8,128)(2,1)} %bitcast.5, bf16[128,2304]{1,0:T(8,128)(2,1)} %collective-permute-done.11, bf16[128,2304]{1,0:T(8,128)(2,1)} %collective-permute-done.10, bf16[128,2304]{1,0:T(8,128)(2,1)} %collective-permute-done.9, ...), kind=kOutput, calls=%fused_computation.65 | convolution fusion | flops 3409035264 | bytes 15187968 | tf_op jit(solution)/shard_map/dot_general | solution.py:237
  294.9 11.7 %fusion.112 = (bf16[512,2304]{1,0:T(8,128)(2,1)S(1)}, f32[512,2304]{1,0:T(8,128)}) fusion(f32[512,2304]{1,0:T(8,128)} %fusion.42, bf16[720,2304]{1,0:T(8,128)(2,1)} %collective-permute-done.14, f32[512,720]{0,1:T(8,128)} %fusion.95, bf16[2304,720]{0,1:T(8,128)(2,1)} %collective-permute-done.12, bf16[128,2304]{1,0:T(8,128)(2,1)} %collective-permute-done.11, ...), kind=kOutput, calls=%fused_computation.151 | convolution fusion | flops 3411394560 | bytes 22265856 | tf_op jit(solution)/shard_map/dot_general | solution.py:239
  314.1 10.3 %collective-permute-done.15 = bf16[128,2304]{1,0:T(8,128)(2,1)} collective-permute-done((bf16[128,2304]{1,0:T(8,128)(2,1)}, bf16[128,2304]{1,0:T(8,128)(2,1)}, u32[]{:S(2)}, u32[]{:S(2)}) %collective-permute-start.15) | collective-permute-done | bytes 589856 | tf_op jit(solution)/shard_map/ppermute | solution.py:16
  324.4 12.8 %collective-permute-done.16 = bf16[128,2304]{1,0:T(8,128)(2,1)} collective-permute-done((bf16[128,2304]{1,0:T(8,128)(2,1)}, bf16[128,2304]{1,0:T(8,128)(2,1)}, u32[]{:S(2)}, u32[]{:S(2)}) %collective-permute-start.16) | collective-permute-done | bytes 589856 | tf_op jit(solution)/shard_map/ppermute | solution.py:16
  (134 shorter events, 94.2 us)
Async XLA Ops:
  7.2 85.3 %all-gather.6.cloned.1.call-start = ((), (), s32[]{:S(2)}) async-start(), calls=%async_computation.4 | async-start | bytes 1474560 | tf_op jit(solution)/shard_map/all_gather | solution.py:159
  9.1 101.0 %all-gather.8.cloned.1.call-start = ((), (), s32[]{:S(2)}) async-start(), calls=%async_computation.5 | async-start | bytes 4423680 | tf_op jit(solution)/shard_map/all_gather | solution.py:160
  29.0 16.3 %collective-permute-start = (bf16[128,2304]{1,0:T(8,128)(2,1)S(1)}, bf16[128,2304]{1,0:T(8,128)(2,1)S(1)}, u32[]{:S(2)}, u32[]{:S(2)}) collective-permute-start(bf16[128,2304]{1,0:T(8,128)(2,1)S(1)} %fusion.28), channel_id=1, source_target_pairs={{0,2},{1,3},{2,0},{3,1},{4,6},{5,7},{6,4},{7,5},{8,10},{9,11},{10,... | collective-permute-start | bytes 1769480 | tf_op jit(solution)/shard_map/ppermute | solution.py:16
  29.6 26.5 %collective-permute-start.1 = (bf16[128,2304]{1,0:T(8,128)(2,1)S(1)}, bf16[128,2304]{1,0:T(8,128)(2,1)S(1)}, u32[]{:S(2)}, u32[]{:S(2)}) collective-permute-start(bf16[128,2304]{1,0:T(8,128)(2,1)S(1)} %fusion.28), channel_id=1, source_target_pairs={{0,4},{1,5},{2,6},{3,7},{4,0},{5,1},{6,2},{7,3},{8,12},{9,13},{10,... | collective-permute-start | bytes 1769480 | tf_op jit(solution)/shard_map/ppermute | solution.py:16
  31.1 26.6 %collective-permute-start.2 = (bf16[128,2304]{1,0:T(8,128)(2,1)S(1)}, bf16[128,2304]{1,0:T(8,128)(2,1)S(1)}, u32[]{:S(2)}, u32[]{:S(2)}) collective-permute-start(bf16[128,2304]{1,0:T(8,128)(2,1)S(1)} %fusion.28), channel_id=1, source_target_pairs={{0,6},{1,7},{2,4},{3,5},{4,2},{5,3},{6,0},{7,1},{8,14},{9,15},{10,... | collective-permute-start | bytes 1769480 | tf_op jit(solution)/shard_map/ppermute | solution.py:16
  60.1 34.0 %collective-permute-start.3 = (bf16[4,128,2304]{2,1,0:T(8,128)(2,1)}, bf16[4,128,2304]{2,1,0:T(8,128)(2,1)}, u32[]{:S(2)}, u32[]{:S(2)}) collective-permute-start(bf16[4,128,2304]{2,1,0:T(8,128)(2,1)} %get-tuple-element.45), channel_id=1, source_target_pairs={{0,1},{1,0},{2,3},{3,2},{4,5},{5,4},{6,7},{7,6},{8,9},{9,8},{10,11... | collective-permute-start | bytes 7077896 | tf_op jit(solution)/shard_map/ppermute | solution.py:16
  65.5 20.9 %all-to-all-start.3 = ((bf16[8,72,720]{2,1,0:T(8,128)(2,1)}), bf16[8,72,720]{2,1,0:T(8,128)(2,1)S(1)}, u32[]{:S(2)}, u32[]{:S(2)}) async-start(bf16[8,72,720]{2,1,0:T(8,128)(2,1)} %split_columns.5), calls=%async_computation.3 | async-start | bytes 1769472 | tf_op jit(solution)/shard_map/all_to_all | solution.py:163
  87.3 64.5 %all-to-all-start.2 = ((bf16[8,288,720]{2,1,0:T(8,128)(2,1)}), bf16[8,288,720]{2,1,0:T(8,128)(2,1)}, u32[]{:S(2)}, u32[]{:S(2)}) async-start(bf16[8,288,720]{2,1,0:T(8,128)(2,1)} %split_columns.4), calls=%async_computation.2 | async-start | bytes 7077888 | tf_op jit(solution)/shard_map/all_to_all | solution.py:162
  91.8 140.8 %all-gather.10.cloned.1.call-start = ((), (), s32[]{:S(2)}) async-start(), calls=%async_computation.6 | async-start | bytes 4423680 | tf_op jit(solution)/shard_map/all_gather | solution.py:164
  92.5 53.9 %collective-permute-start.5 = (bf16[256,2304]{1,0:T(8,128)(2,1)}, bf16[256,2304]{1,0:T(8,128)(2,1)}, u32[]{:S(2)}, u32[]{:S(2)}) collective-permute-start(bf16[256,2304]{1,0:T(8,128)(2,1)} %all-gather.6.cloned.1.call-done), channel_id=1, source_target_pairs={{0,1},{1,0},{2,3},{3,2},{4,5},{5,4},{6,7},{7,6},{8,9},{9,8},{10,11... | collective-permute-start | bytes 3538952 | tf_op jit(solution)/shard_map/ppermute | solution.py:16
  146.4 2.6 collective-permute-start.4
  150.4 17.6 %collective-permute-start.6 = (bf16[128,2304]{1,0:T(8,128)(2,1)}, bf16[128,2304]{1,0:T(8,128)(2,1)}, u32[]{:S(2)}, u32[]{:S(2)}) collective-permute-start(bf16[128,2304]{1,0:T(8,128)(2,1)} %convolution_convert_fusion.2), channel_id=1, source_target_pairs={{0,2},{1,3},{2,0},{3,1},{4,6},{5,7},{6,4},{7,5},{8,10},{9,11},{10,... | collective-permute-start | bytes 1769480 | tf_op jit(solution)/shard_map/ppermute | solution.py:16
  151.8 76.3 %all-to-all-start.1 = ((bf16[8,288,720]{2,1,0:T(8,128)(2,1)}), bf16[8,288,720]{2,1,0:T(8,128)(2,1)}, u32[]{:S(2)}, u32[]{:S(2)}) async-start(bf16[8,288,720]{2,1,0:T(8,128)(2,1)} %split_columns.3), calls=%async_computation.1 | async-start | bytes 7077888 | tf_op jit(solution)/shard_map/all_to_all | solution.py:161
  158.1 63.5 %collective-permute-start.7 = (bf16[128,2304]{1,0:T(8,128)(2,1)}, bf16[128,2304]{1,0:T(8,128)(2,1)}, u32[]{:S(2)}, u32[]{:S(2)}) collective-permute-start(bf16[128,2304]{1,0:T(8,128)(2,1)} %convolution_convert_fusion.1), channel_id=1, source_target_pairs={{0,4},{1,5},{2,6},{3,7},{4,0},{5,1},{6,2},{7,3},{8,12},{9,13},{10,... | collective-permute-start | bytes 1769480 | tf_op jit(solution)/shard_map/ppermute | solution.py:16
  159.5 62.1 %collective-permute-start.8 = (bf16[128,2304]{1,0:T(8,128)(2,1)}, bf16[128,2304]{1,0:T(8,128)(2,1)}, u32[]{:S(2)}, u32[]{:S(2)}) collective-permute-start(bf16[128,2304]{1,0:T(8,128)(2,1)} %convolution_convert_fusion), channel_id=1, source_target_pairs={{0,6},{1,7},{2,4},{3,5},{4,2},{5,3},{6,0},{7,1},{8,14},{9,15},{10,... | collective-permute-start | bytes 1769480 | tf_op jit(solution)/shard_map/ppermute | solution.py:16
  168.0 110.6 %collective-permute-start.13 = (bf16[2304,720]{0,1:T(8,128)(2,1)}, bf16[2304,720]{0,1:T(8,128)(2,1)}, u32[]{:S(2)}, u32[]{:S(2)}) collective-permute-start(bf16[2304,720]{0,1:T(8,128)(2,1)} %copy.62), channel_id=1, source_target_pairs={{0,1},{1,0},{2,3},{3,2},{4,5},{5,4},{6,7},{7,6},{8,9},{9,8},{10,11... | collective-permute-start | bytes 9953288 | tf_op jit(solution)/shard_map/ppermute | solution.py:16
  225.8 19.9 %collective-permute-start.10 = (bf16[128,2304]{1,0:T(8,128)(2,1)}, bf16[128,2304]{1,0:T(8,128)(2,1)}, u32[]{:S(2)}, u32[]{:S(2)}) collective-permute-start(bf16[128,2304]{1,0:T(8,128)(2,1)} %multiply_convert_fusion.2), channel_id=1, source_target_pairs={{0,4},{1,5},{2,6},{3,7},{4,0},{5,1},{6,2},{7,3},{8,12},{9,13},{10,... | collective-permute-start | bytes 1769480 | tf_op jit(solution)/shard_map/ppermute | solution.py:16
  232.5 62.4 %collective-permute-start.12 = (bf16[2304,720]{0,1:T(8,128)(2,1)S(1)}, bf16[2304,720]{0,1:T(8,128)(2,1)}, u32[]{:S(2)}, u32[]{:S(2)}) collective-permute-start(bf16[2304,720]{0,1:T(8,128)(2,1)S(1)} %copy.61), channel_id=1, source_target_pairs={{0,1},{1,0},{2,3},{3,2},{4,5},{5,4},{6,7},{7,6},{8,9},{9,8},{10,11... | collective-permute-start | bytes 9953288 | tf_op jit(solution)/shard_map/ppermute | solution.py:16
  243.5 51.3 %collective-permute-start.14 = (bf16[720,2304]{1,0:T(8,128)(2,1)}, bf16[720,2304]{1,0:T(8,128)(2,1)}, u32[]{:S(2)}, u32[]{:S(2)}) collective-permute-start(bf16[720,2304]{1,0:T(8,128)(2,1)} %copy.60), channel_id=1, source_target_pairs={{0,1},{1,0},{2,3},{3,2},{4,5},{5,4},{6,7},{7,6},{8,9},{9,8},{10,11... | collective-permute-start | bytes 9953288 | tf_op jit(solution)/shard_map/ppermute | solution.py:16
  244.2 17.4 %collective-permute-start.11 = (bf16[128,2304]{1,0:T(8,128)(2,1)}, bf16[128,2304]{1,0:T(8,128)(2,1)}, u32[]{:S(2)}, u32[]{:S(2)}) collective-permute-start(bf16[128,2304]{1,0:T(8,128)(2,1)} %multiply_convert_fusion.2), channel_id=1, source_target_pairs={{0,6},{1,7},{2,4},{3,5},{4,2},{5,3},{6,0},{7,1},{8,14},{9,15},{10,... | collective-permute-start | bytes 1769480 | tf_op jit(solution)/shard_map/ppermute | solution.py:16
  245.7 27.0 %collective-permute-start.9 = (bf16[128,2304]{1,0:T(8,128)(2,1)}, bf16[128,2304]{1,0:T(8,128)(2,1)}, u32[]{:S(2)}, u32[]{:S(2)}) collective-permute-start(bf16[128,2304]{1,0:T(8,128)(2,1)} %multiply_convert_fusion.2), channel_id=1, source_target_pairs={{0,2},{1,3},{2,0},{3,1},{4,6},{5,7},{6,4},{7,5},{8,10},{9,11},{10,... | collective-permute-start | bytes 1769480 | tf_op jit(solution)/shard_map/ppermute | solution.py:16
  307.8 16.6 %collective-permute-start.15 = (bf16[128,2304]{1,0:T(8,128)(2,1)}, bf16[128,2304]{1,0:T(8,128)(2,1)}, u32[]{:S(2)}, u32[]{:S(2)}) collective-permute-start(bf16[128,2304]{1,0:T(8,128)(2,1)} %get-tuple-element.41), channel_id=1, source_target_pairs={{0,2},{1,3},{2,0},{3,1},{4,6},{5,7},{6,4},{7,5},{8,10},{9,11},{10,... | collective-permute-start | bytes 1769480 | tf_op jit(solution)/shard_map/ppermute | solution.py:16
  309.5 27.6 %collective-permute-start.16 = (bf16[128,2304]{1,0:T(8,128)(2,1)}, bf16[128,2304]{1,0:T(8,128)(2,1)}, u32[]{:S(2)}, u32[]{:S(2)}) collective-permute-start(bf16[128,2304]{1,0:T(8,128)(2,1)} %get-tuple-element.43), channel_id=1, source_target_pairs={{0,4},{1,5},{2,6},{3,7},{4,0},{5,1},{6,2},{7,3},{8,12},{9,13},{10,... | collective-permute-start | bytes 1769480 | tf_op jit(solution)/shard_map/ppermute | solution.py:16
  311.0 26.2 %collective-permute-start.17 = (bf16[128,2304]{1,0:T(8,128)(2,1)S(1)}, bf16[128,2304]{1,0:T(8,128)(2,1)}, u32[]{:S(2)}, u32[]{:S(2)}) collective-permute-start(bf16[128,2304]{1,0:T(8,128)(2,1)S(1)} %get-tuple-element.42), channel_id=1, source_target_pairs={{0,6},{1,7},{2,4},{3,5},{4,2},{5,3},{6,0},{7,1},{8,14},{9,15},{10,... | collective-permute-start | bytes 1769480 | tf_op jit(solution)/shard_map/ppermute | solution.py:16
  (20 other events, 478.5 us)
Sparse Core Ops, SparseCore 0:
  10.2 31.0 all-gather.5
  42.8 67.2 all-gather.7
  112.2 68.5 all-gather.9

commit v2 on v1

v2 whole, which is shorter than its diff:
```python
import jax
import jax.numpy as jnp
from jax import lax
from jax.experimental import pallas as pl
from jax.experimental.pallas import tpu as pltpu
from jax.sharding import PartitionSpec as P

HEAD_DIM = 64


def swap_pairs(size, step):
    return [(i, i ^ step) for i in range(size)]


def send(block, size, step):
    return lax.ppermute(block, "tensor", swap_pairs(size, step))


def gather_line(block, count, plane):
    rows = block.shape[0]
    below, above = [], []
    up = down = block
    for step in range(1, count):
        up = lax.ppermute(up, "dp", [(i, i + 1) for i in range(step - 1, count - 1)])
        down = lax.ppermute(down, "dp", [(i, i - 1) for i in range(1, count - step + 1)])
        below.insert(0, up)
        above.append(down)
    line = jnp.concatenate(below + [block] + above, axis=0)
    return lax.dynamic_slice_in_dim(line, (count - 1 - plane) * rows, count * rows, 0)


def split_stacked(matrix, parts):
    rows, width = matrix.shape
    part = width // parts
    chunk = rows
    for cand in (48, 32, 16):
        if rows % cand == 0:
            chunk = cand
            break

    def kernel(x_ref, o_ref):
        for t in range(parts):
            o_ref[t] = x_ref[:, t * part : (t + 1) * part].astype(jnp.bfloat16)

    return pl.pallas_call(
        kernel,
        out_shape=jax.ShapeDtypeStruct((parts, rows, part), jnp.bfloat16),
        grid=(rows // chunk,),
        in_specs=[pl.BlockSpec((chunk, width), lambda i: (i, 0))],
        out_specs=pl.BlockSpec((parts, chunk, part), lambda i: (0, i, 0)),
        name="split_stacked",
    )(matrix)


def split_heads(qkv, parts):
    _, rows, width = qkv.shape
    part = width // parts

    def kernel(x_ref, o_ref):
        for t in range(parts):
            for j in range(3):
                o_ref[t, j] = x_ref[j, :, t * part : (t + 1) * part].astype(jnp.bfloat16)

    return pl.pallas_call(
        kernel,
        out_shape=jax.ShapeDtypeStruct((parts, 3, rows, part), jnp.bfloat16),
        name="split_heads",
    )(qkv)


def join_rows(blocks, me):
    count = len(blocks)
    many, rows, width = blocks[0].shape

    def kernel(me_ref, *refs):
        ins, o_ref, sem = refs[:count], refs[count], refs[count + 1]
        copies = []
        for k in range(count):
            place = pl.multiple_of((me_ref[0] ^ k) * rows, 16)
            copies.append(
                pltpu.make_async_copy(
                    ins[k].at[pl.program_id(0)], o_ref.at[0, pl.ds(place, rows), :], sem.at[k]
                )
            )
        for copy in copies:
            copy.start()
        for copy in copies:
            copy.wait()

    return pl.pallas_call(
        kernel,
        out_shape=jax.ShapeDtypeStruct((many, count * rows, width), blocks[0].dtype),
        grid_spec=pltpu.PrefetchScalarGridSpec(
            num_scalar_prefetch=1,
            grid=(many,),
            in_specs=[pl.BlockSpec(memory_space=pl.ANY)] * count,
            out_specs=pl.BlockSpec((1, count * rows, width), lambda i, m: (i, 0, 0)),
            scratch_shapes=[pltpu.SemaphoreType.DMA((count,))],
        ),
        compiler_params=pltpu.CompilerParams(vmem_limit_bytes=32 * 1024 * 1024),
        name="join_rows",
    )(me.reshape(1), *blocks)


def split_columns(first, second, parts, me):
    rows, width = first.shape
    part = width // parts
    window = min(width, (part + 127) // 128 * 128 + 128)
    chunk = rows
    for cand in (48, 32, 16):
        if rows % cand == 0:
            chunk = cand
            break

    def kernel(me_ref, first_ref, second_ref, *o_refs):
        for k in range(parts):
            left = (me_ref[0] ^ k) * part
            base = jnp.minimum(lax.div(left, 128) * 128, width - window)
            for i, x_ref in enumerate((first_ref, second_ref)):
                cols = x_ref[:, pl.ds(pl.multiple_of(base, 128), window)]
                cols = pltpu.roll(cols, window - (left - base), 1)
                o_refs[k][i] = cols[:, :part].astype(jnp.bfloat16)

    return pl.pallas_call(
        kernel,
        out_shape=[jax.ShapeDtypeStruct((2, rows, part), jnp.bfloat16)] * parts,
        grid_spec=pltpu.PrefetchScalarGridSpec(
            num_scalar_prefetch=1,
            grid=(rows // chunk,),
            in_specs=[pl.BlockSpec((chunk, width), lambda i, m: (i, 0))] * 2,
            out_specs=[pl.BlockSpec((2, chunk, part), lambda i, m: (0, i, 0))] * parts,
        ),
        name="split_columns",
    )(me.reshape(1), first, second)


def dot_nt(a, b):
    return lax.dot_general(a, b, (((1,), (1,)), ((), ())), preferred_element_type=jnp.float32)


def attention(tokens, weights, cosine, sine, scalars, rows_dev):
    seq, model = tokens.shape
    width = weights.shape[2]
    heads = width // HEAD_DIM
    block = min(256, seq)
    steps = seq // block
    half = HEAD_DIM // 2

    def kernel(s_ref, x_ref, w_ref, cos_ref, sin_ref, kv_ref, att_ref, k_all, v_all):
        step = pl.program_id(0)
        lane = lax.broadcasted_iota(jnp.int32, (block, width), 1)
        low = lax.rem(lane, HEAD_DIM) < half
        head_of = lax.div(lane, HEAD_DIM)
        x = x_ref[...]

        def rotated(j):
            m = jnp.dot(x, w_ref[j], preferred_element_type=jnp.float32)
            turned = jnp.where(
                low, -pltpu.roll(m, width - half, 1), pltpu.roll(m, half, 1)
            )
            return m * cos_ref[...] + turned * sin_ref[...]

        row = step * block + lax.broadcasted_iota(jnp.int32, (block, width), 0)
        valid = row < s_ref[0]
        start = pl.multiple_of(step * block, block)
        key = rotated(1)
        k_all[pl.ds(start, block), :] = key.astype(jnp.bfloat16)
        kv_ref[0] = jnp.where(valid, key, 0.0).astype(jnp.bfloat16)
        value = jnp.dot(x, w_ref[2], preferred_element_type=jnp.float32)
        v_all[pl.ds(start, block), :] = value.astype(jnp.bfloat16)
        kv_ref[1] = jnp.where(valid, value, 0.0).astype(jnp.bfloat16)
        query = rotated(0).astype(jnp.bfloat16).astype(jnp.float32) * HEAD_DIM ** (-0.5)

        for here in range(steps):

            @pl.when(step == here)
            def _():
                lo = here * block
                causal = lax.broadcasted_iota(
                    jnp.int32, (block, block), 0
                ) >= lax.broadcasted_iota(jnp.int32, (block, block), 1)
                out = jnp.zeros((block, width), jnp.float32)
                for h in range(heads):
                    q = jnp.where(head_of == h, query, 0.0).astype(jnp.bfloat16)
                    diag = jnp.where(causal, dot_nt(q, k_all[lo : lo + block, :]), -1e30)
                    top = jnp.max(diag, axis=-1, keepdims=True)
                    if lo:
                        past = dot_nt(q, k_all[:lo, :])
                        top = jnp.maximum(top, jnp.max(past, axis=-1, keepdims=True))
                        past = jnp.exp(past - top)
                    diag = jnp.exp(diag - top)
                    total = jnp.sum(diag, axis=-1, keepdims=True)
                    if lo:
                        total = total + jnp.sum(past, axis=-1, keepdims=True)
                    inv = 1.0 / total
                    res = jnp.dot(
                        (diag * inv).astype(jnp.bfloat16),
                        v_all[lo : lo + block, :],
                        preferred_element_type=jnp.float32,
                    )
                    if lo:
                        res = res + jnp.dot(
                            (past * inv).astype(jnp.bfloat16),
                            v_all[:lo, :],
                            preferred_element_type=jnp.float32,
                        )
                    out = jnp.where(head_of == h, res, out)
                out = out.astype(jnp.bfloat16)
                for piece in range(block // rows_dev):
                    dev = here * (block // rows_dev) + piece
                    slot = jnp.where(s_ref[1] == dev % 2, 0, 1)
                    att_ref[slot, (dev // 2) * rows_dev : (dev // 2 + 1) * rows_dev, :] = out[
                        piece * rows_dev : (piece + 1) * rows_dev
                    ]

    return pl.pallas_call(
        kernel,
        out_shape=(
            jax.ShapeDtypeStruct((2, seq, width), jnp.bfloat16),
            jax.ShapeDtypeStruct((2, seq // 2, width), jnp.bfloat16),
        ),
        grid_spec=pltpu.PrefetchScalarGridSpec(
            num_scalar_prefetch=1,
            grid=(steps,),
            in_specs=[
                pl.BlockSpec((block, model), lambda i, s: (i, 0)),
                pl.BlockSpec((3, model, width), lambda i, s: (0, 0, 0)),
                pl.BlockSpec((block, width), lambda i, s: (i, 0)),
                pl.BlockSpec((block, width), lambda i, s: (i, 0)),
            ],
            out_specs=(
                pl.BlockSpec((2, block, width), lambda i, s: (0, i, 0)),
                pl.BlockSpec((2, seq // 2, width), lambda i, s: (0, 0, 0)),
            ),
            scratch_shapes=[
                pltpu.VMEM((seq, width), jnp.bfloat16),
                pltpu.VMEM((seq, width), jnp.bfloat16),
            ],
        ),
        compiler_params=pltpu.CompilerParams(vmem_limit_bytes=48 * 1024 * 1024),
        name="attention",
    )(scalars, tokens, weights, cosine, sine)


def expert(blocks, own, other):
    count = len(blocks)
    rows, model = blocks[0].shape
    units = own[0].shape[0]

    def kernel(*refs):
        x_in, w_in = refs[:count], refs[count : count + 6]
        outs = refs[count + 6 : 2 * count + 6]
        x_all, w_all, total, x_sem, w_sem = refs[2 * count + 6 :]
        x_copies = [
            pltpu.make_async_copy(x_in[j], x_all.at[pl.ds(j * rows, rows), :], x_sem.at[j])
            for j in range(count)
        ]
        w_copies = [
            pltpu.make_async_copy(w_in[j], w_all.at[j], w_sem.at[j]) for j in range(6)
        ]
        for copy in x_copies + w_copies:
            copy.start()
        for copy in x_copies:
            copy.wait()
        x = x_all[...]
        for half in range(2):
            w_copies[3 * half].wait()
            gate = dot_nt(x, w_all[3 * half])
            w_copies[3 * half + 1].wait()
            up = dot_nt(x, w_all[3 * half + 1])
            act = (gate / (1.0 + jnp.exp(-gate)) * up).astype(jnp.bfloat16)
            w_copies[3 * half + 2].wait()
            part = jnp.dot(act, w_all[3 * half + 2], preferred_element_type=jnp.float32)
            if half == 0:
                total[...] = part
            else:
                part = (total[...] + part).astype(jnp.bfloat16)
                for j in range(count):
                    outs[j][...] = part[j * rows : (j + 1) * rows]

    return pl.pallas_call(
        kernel,
        out_shape=[jax.ShapeDtypeStruct((rows, model), jnp.bfloat16)] * count,
        in_specs=[pl.BlockSpec(memory_space=pl.ANY)] * (count + 6),
        out_specs=[pl.BlockSpec(memory_space=pltpu.VMEM)] * count,
        scratch_shapes=[
            pltpu.VMEM((count * rows, model), jnp.bfloat16),
            pltpu.VMEM((6, units, model), jnp.bfloat16),
            pltpu.VMEM((count * rows, model), jnp.float32),
            pltpu.SemaphoreType.DMA((count,)),
            pltpu.SemaphoreType.DMA((6,)),
        ],
        compiler_params=pltpu.CompilerParams(vmem_limit_bytes=56 * 1024 * 1024),
        name="expert",
    )(*blocks, *own, *other)


def rms_scale(values, gain_row):
    mean_sq = jnp.mean(values * values, axis=-1, keepdims=True)
    return values * lax.rsqrt(mean_sq + 1e-05) * gain_row


def shards(
    hidden_in,
    prompt_len,
    start_pos,
    routes,
    trainer_qkv,
    trainer_out,
    trainer_gate,
    trainer_up,
    trainer_down,
    attn_gain,
    moe_gain,
    router,
):
    size = lax.axis_size("tensor")
    replicas = lax.axis_size("dp")
    chips = size // 2
    me = lax.axis_index("tensor").astype(jnp.int32)
    plane = lax.axis_index("dp").astype(jnp.int32)
    chip, core = me // 2, me % 2
    rows_dev, model = hidden_in.shape[1], hidden_in.shape[2]
    seq_len = rows_dev * size
    length = prompt_len[0]
    offset = start_pos[0]
    my_first = me * rows_dev

    local_width = trainer_qkv.shape[2] // size
    qkv_parts = split_heads(trainer_qkv.transpose(1, 0, 2), size)
    qkv_cols = lax.all_to_all(qkv_parts, "tensor", 0, 0, tiled=True)
    qkv_all = lax.all_gather(qkv_cols, "dp", axis=0)
    qkv_server = qkv_all.transpose(2, 1, 0, 3, 4).reshape(3, model, local_width)
    server_qkv = qkv_server.transpose(1, 0, 2)
    server_out = gather_line(trainer_out.astype(jnp.bfloat16), replicas, plane)

    tokens = hidden_in[0].astype(jnp.float32)
    normed = rms_scale(tokens, attn_gain).astype(jnp.bfloat16)
    blocks = []
    for j in range(chips):
        block = send(normed, size, 2 * j) if j else normed
        blocks += [block[None], send(block, size, 1)[None]]
    piece = join_rows(blocks, me)[0]

    down_rows = trainer_down.shape[0] // replicas
    down_quarter = lax.dynamic_slice_in_dim(trainer_down, plane * down_rows, down_rows, 0)
    down_cols = lax.all_to_all(split_stacked(down_quarter, size), "tensor", 0, 0, tiled=True)
    down_all = lax.all_gather(down_cols, "dp", axis=0)

    parts = split_columns(trainer_gate, trainer_up, size, me)
    early = [send(parts[k], size, k) for k in [1] + list(range(2, size, 2))]
    late = list(lax.optimization_barrier((*parts[3::2], *early)))[: chips - 1]
    late = [send(block, size, 2 * j + 3) for j, block in enumerate(late)]
    joined = [parts[0], early[0]]
    for j in range(1, chips):
        joined += [early[j], late[j - 1]]


    out_pair = jnp.concatenate([server_out, send(server_out, size, 1)], axis=0)

    half_dim = HEAD_DIM // 2
    inv_freq = jnp.power(
        10000.0, jnp.arange(half_dim, dtype=jnp.float32) * (-2.0 / HEAD_DIM)
    )
    places = offset + jnp.arange(seq_len, dtype=jnp.int32)
    angles = places.astype(jnp.float32)[:, None] * inv_freq[None, :]
    repeats = local_width // half_dim
    cosine = jnp.tile(jnp.cos(angles), (1, repeats))
    sine_part = jnp.tile(jnp.sin(angles), (1, repeats))
    scalars = jnp.stack([length, core])
    cache_pair, attended = attention(
        piece, qkv_server, cosine, sine_part, scalars, rows_dev
    )

    att_pair = jnp.concatenate([attended[0], send(attended[1], size, 1)], axis=-1)
    att_pair = att_pair.reshape(chips, rows_dev, 2 * local_width)

    def attn_part(j):
        rows = lax.dynamic_index_in_dim(att_pair, chip ^ j, 0, keepdims=False)
        return jnp.dot(rows, out_pair, preferred_element_type=jnp.float32)

    partial = [attn_part(j) for j in range(chips)]
    sent = [part.astype(jnp.bfloat16) for part in partial[1:]]
    got = [send(block, size, 2 * j + 2) for j, block in enumerate(sent)]
    joined = list(lax.optimization_barrier((*joined, *sent)))[:size]
    gate_up = join_rows(joined, me)
    gate_t, up_t = gate_up[0].T, gate_up[1].T
    gate_other = send(gate_t, size, 1)
    up_other = send(up_t, size, 1)
    attn_sum = partial[0]
    for block in got:
        attn_sum = attn_sum + block.astype(jnp.float32)
    middle = (tokens + attn_sum).astype(jnp.bfloat16)
    normed_moe = rms_scale(middle.astype(jnp.float32), moe_gain).astype(jnp.bfloat16)

    moe_rows = [normed_moe] + [send(normed_moe, size, 2 * j) for j in range(1, chips)]
    down_late, _ = lax.optimization_barrier((down_all, moe_rows[1]))
    down_t = down_late.transpose(3, 1, 0, 2).reshape(-1, model)
    down_other = send(down_t, size, 1)

    local_routes = lax.dynamic_slice_in_dim(routes[0], my_first, rows_dev, 0)
    local_valid = my_first + jnp.arange(rows_dev, dtype=jnp.int32) < length
    logits = jnp.dot(normed_moe, router, preferred_element_type=jnp.float32)
    expert_ids = jnp.arange(router.shape[1], dtype=jnp.int32)
    logit_first = jnp.sum(
        jnp.where(local_routes[:, 0:1] == expert_ids[None, :], logits, 0.0), axis=1
    )
    logit_second = jnp.sum(
        jnp.where(local_routes[:, 1:2] == expert_ids[None, :], logits, 0.0), axis=1
    )
    other_logit = jnp.where(local_routes[:, 0] == 0, logit_second, logit_first)
    local_routed = jnp.any(local_routes == 0, axis=1)
    route_w = jnp.where(local_routed, jax.nn.sigmoid(logits[:, 0] - other_logit), 0.0)

    sums = expert(
        moe_rows, (gate_t, up_t, down_t), (gate_other, up_other, down_other)
    )
    expert_sum = sums[0].astype(jnp.float32)
    for j in range(1, chips):
        expert_sum = expert_sum + send(sums[j], size, 2 * j).astype(jnp.float32)
    expert_sum = jnp.where(local_routed[:, None], expert_sum, 0.0)
    result = middle.astype(jnp.float32) + route_w[:, None] * expert_sum
    hidden_out = jnp.where(local_valid[:, None], result, 0.0).astype(jnp.bfloat16)[None]
    return (
        server_qkv,
        server_out,
        gate_t.T,
        up_t.T,
        down_t.T,
        hidden_out,
        cache_pair[None],
    )


def solution(mesh):
    placed = (
        P("dp", "tensor", None),
        P("dp"),
        P("dp"),
        P("dp", None, None),
        P(("tensor", "dp"), None, None),
        P(("tensor", "dp"), None),
        P("tensor", None),
        P("tensor", None),
        P("tensor", None),
        P(),
        P(),
        P(),
    )
    return jax.shard_map(
        shards,
        mesh=mesh,
        in_specs=placed,
        out_specs=(
            P(None, None, "tensor"),
            P("tensor", None),
            P(None, "tensor"),
            P(None, "tensor"),
            P(None, "tensor"),
            P("dp", "tensor", None),
            P("dp", None, None, "tensor"),
        ),
        check_vma=False,
    )
```

time: 355 us -> 379 us (1.068); the launches traced: 348 us -> 377 us
  matrix products: 62.2 us -> 13.1 us
  waiting for transfers between devices: 125 us -> 168 us
  Pallas kernels: 25.5 us -> 58.5 us
  starting transfers between devices: 29.1 us -> 47.1 us
  other arithmetic: 17.4 us -> 6.5 us
  local copies, waits for them, and re-layouts: 56.5 us -> 51.1 us
    ppermute x0 -> x6, waiting for transfers between devices: none -> 56.6 us  [the longest x3 47 us: gather_line(): lax.ppermute(down, 'dp', [(i, i - 1) for i in range(1, count - step + 1)])]
    dot_general x7 -> x0, matrix products: 42.2 us -> none  [the longest x1 11.7 us: shards(): jnp.dot(activate(gate_other, up_other), down_other, preferred_element_typ...]
    pallas_call x4 -> x6, Pallas kernels: 23 us -> 55.9 us  [the longest x1 22.3 us: expert(): pl.pallas_call(kernel, out_shape=[jax.ShapeDtypeStruct((rows, model), jnp...]
    ppermute x0 -> x6, starting transfers between devices: none -> 14.6 us  [the longest x3 9.04 us: gather_line(): lax.ppermute(up, 'dp', [(i, i + 1) for i in range(step - 1, count - 1)])]
    sub x2 -> x0, matrix products: 12.6 us -> none  [attend_block(): exp_scores = jnp.exp(scores - row_max)]
    ppermute x18 -> x28, starting transfers between devices: 15.3 us -> 26.7 us  [send(): return lax.ppermute(block, 'tensor', swap_pairs(size, step))]
    ppermute x18 -> x28, waiting for transfers between devices: 121 us -> 112 us  [send(): return lax.ppermute(block, 'tensor', swap_pairs(size, step))]
    all_to_all x3 -> x1, starting transfers between devices: 13.7 us -> 5.72 us  [shards(): lax.all_to_all(split_stacked(down_quarter, size), 'tensor', 0, 0, tiled=T...]
  transfers between devices with their start and end apart: 24 -> 37, of which waited for: 9 -> 12; matrix products, arithmetic and copies ran while one was open for 32% -> 16% of each run, Pallas kernels for 7% -> 9%
where the time goes in v2:
time: 379 us; the launch traced here: 377 us
  waiting for transfers between devices  168 us (44%)
  Pallas kernels  58.5 us (15%)
  local copies, waits for them, and re-layouts  51.1 us (13%)
  starting transfers between devices  47.1 us (12%)
  blocking collectives  16.9 us (4%)
  between operations  15.8 us (4%)
  matrix products  13.1 us (3%)
  other arithmetic  6.5 us (2%)
    ppermute x28, waiting for transfers between devices, send(): return lax.ppermute(block, 'tensor', swap_pairs(size, step))  112 us
    ppermute x3, waiting for transfers between devices, gather_line(): lax.ppermute(down, 'dp', [(i, i - 1) for i in range(1, count - step + 1)])  47 us
    unnamed x60, local copies, waits for them, and re-layouts  28.3 us
    ppermute x28, starting transfers between devices, send(): return lax.ppermute(block, 'tensor', swap_pairs(size, step))  26.7 us
    pallas_call x1, Pallas kernels, expert(): pl.pallas_call(kernel, out_shape=[jax.ShapeDtypeStruct((rows, model), jnp...  22.3 us
    all_to_all x1, blocking collectives, shards(): qkv_cols = lax.all_to_all(qkv_parts, 'tensor', 0, 0, tiled=True)  16.9 us
    pallas_call x1, Pallas kernels, attention(): pl.pallas_call(kernel, out_shape=(jax.ShapeDtypeStruct((2, seq, width), j...  14.2 us
    dot_general x4, matrix products, attn_part(): return jnp.dot(rows, out_pair, preferred_element_type=jnp.float32)  11.8 us
  transfers between devices with their start and end apart: 37, of which 12 were waited for; matrix products, arithmetic and copies ran while one was open for 16% of the time, Pallas kernels for 9%

profile of v2, /device:TPU:12, one launch (start us, length us, event | category | flops | bytes accessed | tf_op | source)
XLA Modules:
  0.0 377.2 jit_solution(5404045801806350173)
XLA Ops:
  9.8 16.9 %all_to_all.10 = bf16[8,3,72,256]{3,2,1,0:T(8,128)(2,1)} all-to-all(bf16[8,3,72,256]{3,2,1,0:T(8,128)(2,1)} %split_heads.1), channel_id=1, replica_groups=mesh['dp'=4,'tensor'=8] {'tensor'}, dimensions={0} | all-to-all | bytes 1769472 | tf_op jit(solution)/shard_map/all_to_all | solution.py:331
  26.7 3.5 collective-permute-start
  38.2 5.7 %all-to-all-start.1 = ((bf16[8,72,720]{2,1,0:T(8,128)(2,1)}), bf16[8,72,720]{2,1,0:T(8,128)(2,1)}, u32[]{:S(2)}, u32[]{:S(2)}) async-start(bf16[8,72,720]{2,1,0:T(8,128)(2,1)} %split_stacked.1), calls=%async_computation.1 | async-start | bytes 1769472 | tf_op jit(solution)/shard_map/all_to_all | solution.py:347
  44.2 4.2 %collective-permute-start.1 = (bf16[64,2304]{1,0:T(8,128)(2,1)S(1)}, bf16[64,2304]{1,0:T(8,128)(2,1)}, u32[]{:S(2)}, u32[]{:S(2)}) collective-permute-start(bf16[64,2304]{1,0:T(8,128)(2,1)S(1)} %collective-permute-done), channel_id=1, source_target_pairs={{8,16},{16,24},{9,17},{17,25},{10,18},{18,26},{11,19},{19,27},{12,... | collective-permute-start | bytes 884744 | tf_op jit(solution)/shard_map/ppermute | solution.py:24
  51.4 10.3 %split_columns.1 = (bf16[2,288,720]{2,1,0:T(8,128)(2,1)}, bf16[2,288,720]{2,1,0:T(8,128)(2,1)}, bf16[2,288,720]{2,1,0:T(8,128)(2,1)}, bf16[2,288,720]{2,1,0:T(8,...) custom-call(s32[1]{0:T(128)} %bitcast.5.me_ref, ...), custom_call_target="tpu_custom_call" | custom-call | tf_op jit(solution)/shard_map/split_columns/pallas_call | solution.py:124
  63.1 9.6 %collective-permute-done.1 = bf16[64,2304]{1,0:T(8,128)(2,1)} collective-permute-done((bf16[64,2304]{1,0:T(8,128)(2,1)S(1)}, bf16[64,2304]{1,0:T(8,128)(2,1)}, u32[]{:S(2)}, u32[]{:S(2)}) %collective-permute-start.1) | collective-permute-done | bytes 294944 | tf_op jit(solution)/shard_map/ppermute | solution.py:24
  85.3 28.5 %collective-permute-done.4 = bf16[64,2304]{1,0:T(8,128)(2,1)S(1)} collective-permute-done((bf16[64,2304]{1,0:T(8,128)(2,1)}, bf16[64,2304]{1,0:T(8,128)(2,1)S(1)}, u32[]{:S(2)}, u32[]{:S(2)}) %collective-permute-start.4) | collective-permute-done | bytes 294944 | tf_op jit(solution)/shard_map/ppermute | solution.py:25
  117.6 18.5 %collective-permute-done.5 = bf16[64,2304]{1,0:T(8,128)(2,1)S(1)} collective-permute-done((bf16[64,2304]{1,0:T(8,128)(2,1)S(1)}, bf16[64,2304]{1,0:T(8,128)(2,1)S(1)}, u32[]{:S(2)}, u32[]{:S(2)}) %collective-permute-start.5) | collective-permute-done | bytes 294944 | tf_op jit(solution)/shard_map/ppermute | solution.py:25
  136.1 5.1 %collective-permute-start.18 = (bf16[128,2304]{1,0:T(8,128)(2,1)}, bf16[128,2304]{1,0:T(8,128)(2,1)S(1)}, u32[]{:S(2)}, u32[]{:S(2)}) collective-permute-start(bf16[128,2304]{1,0:T(8,128)(2,1)} %fusion.9), channel_id=1, source_target_pairs={{0,6},{1,7},{2,4},{3,5},{4,2},{5,3},{6,0},{7,1},{8,14},{9,15},{10,... | collective-permute-start | bytes 1769480 | tf_op jit(solution)/shard_map/ppermute | solution.py:16
  142.3 7.0 %collective-permute-done.18 = bf16[128,2304]{1,0:T(8,128)(2,1)S(1)} collective-permute-done((bf16[128,2304]{1,0:T(8,128)(2,1)}, bf16[128,2304]{1,0:T(8,128)(2,1)S(1)}, u32[]{:S(2)}, u32[]{:S(2)}) %collective-permute-start.18) | collective-permute-done | bytes 589856 | tf_op jit(solution)/shard_map/ppermute | solution.py:16
  150.0 15.9 %collective-permute-done.8.refs_4_ = bf16[2,288,720]{2,1,0:T(8,128)(2,1)S(1)} collective-permute-done((bf16[2,288,720]{2,1,0:T(8,128)(2,1)S(1)}, bf16[2,288,720]{2,1,0:T(8,128)(2,1)S(1)}, u32[]{:S(2)}, u32[]{:S(2)}) %collective-permute-start.8) | collective-permute-done | bytes 829472 | tf_op jit(solution)/shard_map/ppermute | solution.py:16
  174.9 14.2 %attention.1 = (bf16[2,1024,256]{2,1,0:T(8,128)(2,1)}, bf16[2,512,256]{2,1,0:T(8,128)(2,1)S(1)}) custom-call(s32[2]{0:T(128)S(1)} %pad_add_fusion.s_ref, bf16[1024,2304]{1,0:T(8,128)(2,1)} %bitcast.97, bf16[3,2304,256]{2,1,0:T(8,128)(2,1)S(1)} %bitcast.98, f32[1024,256]{1,0:T(8,128)S(1)} %copy.33.cos_ref, f32[1024,256]{1,0:T(8,128)S(1)} %copy.34.sin_ref), custom_call_target="tpu_custom_call" | custom-call | tf_op jit(solution)/shard_map/attention/pallas_call | solution.py:216
  205.2 37.9 %collective-permute-done.11.refs_5_ = bf16[2,288,720]{2,1,0:T(8,128)(2,1)} collective-permute-done((bf16[2,288,720]{2,1,0:T(8,128)(2,1)}, bf16[2,288,720]{2,1,0:T(8,128)(2,1)}, u32[]{:S(2)}, u32[]{:S(2)}) %collective-permute-start.11) | collective-permute-done | bytes 829472 | tf_op jit(solution)/shard_map/ppermute | solution.py:16
  245.5 4.7 %join_rows.3 = bf16[2,2304,720]{2,1,0:T(8,128)(2,1)S(1)} custom-call(s32[1]{0:T(128)} %bitcast.5.me_ref, bf16[2,288,720]{2,1,0:T(8,128)(2,1)S(1)} %copy-done.3, bf16[2,288,720]{2,1,0:T(8,128)(2,1)S(1)} %collective-permute-done.6.refs_1_, bf16[2,288,720]{2,1,0:T(8,128)(2,1)S(1)} %copy-done.5, bf16[2,288,720]{2,1,0:T(8,128)(2,1)} %collective-permute-done.10.refs_3_, ...), custom_call_target="tpu_custom_call" | custom-call | tf_op jit(solution)/shard_map/join_rows/pallas_call | solution.py:90
  250.2 5.8 %collective-permute-done.23 = bf16[128,2304]{1,0:T(8,128)(2,1)} collective-permute-done((bf16[128,2304]{1,0:T(8,128)(2,1)}, bf16[128,2304]{1,0:T(8,128)(2,1)}, u32[]{:S(2)}, u32[]{:S(2)}) %collective-permute-start.23) | collective-permute-done | bytes 589856 | tf_op jit(solution)/shard_map/ppermute | solution.py:16
  264.8 5.6 %copy.41 = bf16[1,2304,720]{1,2,0:T(8,128)(2,1)} copy(bf16[1,2304,720]{2,1,0:T(8,128)(2,1)} %get-tuple-element.78) | data formatting | bytes 6635520
  270.4 5.6 %copy.42 = bf16[1,2304,720]{1,2,0:T(8,128)(2,1)} copy(bf16[1,2304,720]{2,1,0:T(8,128)(2,1)} %get-tuple-element.77) | data formatting | bytes 6635520
  276.6 4.3 %copy.37 = bf16[4,8,72,720]{3,2,0,1:T(8,128)(2,1)} copy(bf16[4,8,72,720]{3,2,1,0:T(8,128)(2,1)} %bitcast.115) | data formatting | bytes 6635520 | tf_op jit(solution)/shard_map/optimization_barrier | solution.py:397
  280.9 5.6 %copy.39.refs_6_ = bf16[720,2304]{1,0:T(8,128)(2,1)} copy(bf16[720,2304]{0,1:T(8,128)(2,1)} %bitcast.105) | data formatting | bytes 6635520 | tf_op jit(solution)/shard_map/reshape | solution.py:398
  289.1 26.1 %collective-permute-done.26.refs_2_ = bf16[128,2304]{1,0:T(8,128)(2,1)S(1)} collective-permute-done((bf16[128,2304]{1,0:T(8,128)(2,1)}, bf16[128,2304]{1,0:T(8,128)(2,1)S(1)}, u32[]{:S(2)}, u32[]{:S(2)}) %collective-permute-start.26) | collective-permute-done | bytes 589856 | tf_op jit(solution)/shard_map/ppermute | solution.py:16
  316.2 22.3 %expert.1 = (bf16[128,2304]{1,0:T(8,128)(2,1)}, bf16[128,2304]{1,0:T(8,128)(2,1)}, bf16[128,2304]{1,0:T(8,128)(2,1)}, bf16[128,2304]{1,0:T(8,128)(2,1)}) custom-call(bf16[128,2304]{1,0:T(8,128)(2,1)} %multiply_convert_fusion.refs_0_, bf16[128,2304]{1,0:T(8,128)(2,1)} %copy-done.15, bf16[128,2304]{1,0:T(8,128)(2,1)} %copy-done.17, ...), custom_call_target="tpu_custom_call" | custom-call | tf_op jit(solution)/shard_map/expert/pallas_call | solution.py:281
  343.5 5.7 %copy.40 = bf16[2304,720]{0,1:T(8,128)(2,1)} copy(bf16[2304,720]{1,0:T(8,128)(2,1)} %bitcast.106) | data formatting | bytes 6635520
  349.2 6.8 %collective-permute-done.33 = bf16[128,2304]{1,0:T(8,128)(2,1)S(1)} collective-permute-done((bf16[128,2304]{1,0:T(8,128)(2,1)}, bf16[128,2304]{1,0:T(8,128)(2,1)S(1)}, u32[]{:S(2)}, u32[]{:S(2)}) %collective-permute-start.33) | collective-permute-done | bytes 589856 | tf_op jit(solution)/shard_map/ppermute | solution.py:16
  356.0 11.3 %collective-permute-done.32 = bf16[128,2304]{1,0:T(8,128)(2,1)S(1)} collective-permute-done((bf16[128,2304]{1,0:T(8,128)(2,1)}, bf16[128,2304]{1,0:T(8,128)(2,1)S(1)}, u32[]{:S(2)}, u32[]{:S(2)}) %collective-permute-start.32) | collective-permute-done | bytes 589856 | tf_op jit(solution)/shard_map/ppermute | solution.py:16
  (154 shorter events, 80.1 us)
Async XLA Ops:
  7.2 165.3 %all-gather.5.cloned.1.call-start = ((), (), s32[]{:S(2)}) async-start(), calls=%async_computation.2 | async-start | bytes 4423680 | tf_op jit(solution)/shard_map/all_gather | solution.py:332
  30.2 47.7 %collective-permute-start.3 = (bf16[64,2304]{1,0:T(8,128)(2,1)S(1)}, bf16[64,2304]{1,0:T(8,128)(2,1)}, u32[]{:S(2)}, u32[]{:S(2)}) collective-permute-start(bf16[64,2304]{1,0:T(8,128)(2,1)S(1)} %convert_element_type.68), channel_id=1, source_target_pairs={{8,0},{16,8},{24,16},{9,1},{17,9},{25,17},{10,2},{18,10},{26,18},{... | collective-permute-start | bytes 884744 | tf_op jit(solution)/shard_map/ppermute | solution.py:25
  38.2 39.6 %all-to-all-start.1 = ((bf16[8,72,720]{2,1,0:T(8,128)(2,1)}), bf16[8,72,720]{2,1,0:T(8,128)(2,1)}, u32[]{:S(2)}, u32[]{:S(2)}) async-start(bf16[8,72,720]{2,1,0:T(8,128)(2,1)} %split_stacked.1), calls=%async_computation.1 | async-start | bytes 1769472 | tf_op jit(solution)/shard_map/all_to_all | solution.py:347
  44.0 232.6 %all-gather.7.cloned.1.call-start = ((), (), s32[]{:S(2)}) async-start(), calls=%async_computation.3 | async-start | bytes 4423680 | tf_op jit(solution)/shard_map/all_gather | solution.py:348
  44.2 28.5 %collective-permute-start.1 = (bf16[64,2304]{1,0:T(8,128)(2,1)S(1)}, bf16[64,2304]{1,0:T(8,128)(2,1)}, u32[]{:S(2)}, u32[]{:S(2)}) collective-permute-start(bf16[64,2304]{1,0:T(8,128)(2,1)S(1)} %collective-permute-done), channel_id=1, source_target_pairs={{8,16},{16,24},{9,17},{17,25},{10,18},{18,26},{11,19},{19,27},{12,... | collective-permute-start | bytes 884744 | tf_op jit(solution)/shard_map/ppermute | solution.py:24
  49.4 66.1 %collective-permute-start.14 = (bf16[128,2304]{1,0:T(8,128)(2,1)}, bf16[128,2304]{1,0:T(8,128)(2,1)}, u32[]{:S(2)}, u32[]{:S(2)}) collective-permute-start(bf16[128,2304]{1,0:T(8,128)(2,1)} %fusion.9), channel_id=1, source_target_pairs={{0,2},{1,3},{2,0},{3,1},{4,6},{5,7},{6,4},{7,5},{8,10},{9,11},{10,... | collective-permute-start | bytes 1769480 | tf_op jit(solution)/shard_map/ppermute | solution.py:16
  50.9 65.3 %collective-permute-start.16 = (bf16[128,2304]{1,0:T(8,128)(2,1)}, bf16[128,2304]{1,0:T(8,128)(2,1)}, u32[]{:S(2)}, u32[]{:S(2)}) collective-permute-start(bf16[128,2304]{1,0:T(8,128)(2,1)} %fusion.9), channel_id=1, source_target_pairs={{0,4},{1,5},{2,6},{3,7},{4,0},{5,1},{6,2},{7,3},{8,12},{9,13},{10,... | collective-permute-start | bytes 1769480 | tf_op jit(solution)/shard_map/ppermute | solution.py:16
  61.7 87.7 %collective-permute-start.6 = (bf16[2,288,720]{2,1,0:T(8,128)(2,1)}, bf16[2,288,720]{2,1,0:T(8,128)(2,1)S(1)}, u32[]{:S(2)}, u32[]{:S(2)}) collective-permute-start(bf16[2,288,720]{2,1,0:T(8,128)(2,1)} %get-tuple-element.34), channel_id=1, source_target_pairs={{0,1},{1,0},{2,3},{3,2},{4,5},{5,4},{6,7},{7,6},{8,9},{9,8},{10,11... | collective-permute-start | bytes 2488328 | tf_op jit(solution)/shard_map/ppermute | solution.py:16
  77.9 72.0 %collective-permute-start.7 = (bf16[2,288,720]{2,1,0:T(8,128)(2,1)}, bf16[2,288,720]{2,1,0:T(8,128)(2,1)S(1)}, u32[]{:S(2)}, u32[]{:S(2)}) collective-permute-start(bf16[2,288,720]{2,1,0:T(8,128)(2,1)} %get-tuple-element.35), channel_id=1, source_target_pairs={{0,2},{1,3},{2,0},{3,1},{4,6},{5,7},{6,4},{7,5},{8,10},{9,11},{10,... | collective-permute-start | bytes 2488328 | tf_op jit(solution)/shard_map/ppermute | solution.py:16
  79.3 34.5 %collective-permute-start.4 = (bf16[64,2304]{1,0:T(8,128)(2,1)}, bf16[64,2304]{1,0:T(8,128)(2,1)S(1)}, u32[]{:S(2)}, u32[]{:S(2)}) collective-permute-start(bf16[64,2304]{1,0:T(8,128)(2,1)} %collective-permute-done.3), channel_id=1, source_target_pairs={{8,0},{16,8},{9,1},{17,9},{10,2},{18,10},{11,3},{19,11},{12,4},{20... | collective-permute-start | bytes 884744 | tf_op jit(solution)/shard_map/ppermute | solution.py:25
  113.8 52.1 %collective-permute-start.8 = (bf16[2,288,720]{2,1,0:T(8,128)(2,1)S(1)}, bf16[2,288,720]{2,1,0:T(8,128)(2,1)S(1)}, u32[]{:S(2)}, u32[]{:S(2)}) collective-permute-start(bf16[2,288,720]{2,1,0:T(8,128)(2,1)S(1)} %copy-done.23), channel_id=1, source_target_pairs={{0,4},{1,5},{2,6},{3,7},{4,0},{5,1},{6,2},{7,3},{8,12},{9,13},{10,... | collective-permute-start | bytes 2488328 | tf_op jit(solution)/shard_map/ppermute | solution.py:16
  115.5 51.3 %collective-permute-start.9 = (bf16[2,288,720]{2,1,0:T(8,128)(2,1)S(1)}, bf16[2,288,720]{2,1,0:T(8,128)(2,1)S(1)}, u32[]{:S(2)}, u32[]{:S(2)}) collective-permute-start(bf16[2,288,720]{2,1,0:T(8,128)(2,1)S(1)} %copy-done.22), channel_id=1, source_target_pairs={{0,6},{1,7},{2,4},{3,5},{4,2},{5,3},{6,0},{7,1},{8,14},{9,15},{10,... | collective-permute-start | bytes 2488328 | tf_op jit(solution)/shard_map/ppermute | solution.py:16
  168.4 35.0 %collective-permute-start.10 = (bf16[2,288,720]{2,1,0:T(8,128)(2,1)}, bf16[2,288,720]{2,1,0:T(8,128)(2,1)}, u32[]{:S(2)}, u32[]{:S(2)}) collective-permute-start(bf16[2,288,720]{2,1,0:T(8,128)(2,1)} %get-tuple-element.41), channel_id=1, source_target_pairs={{0,3},{1,2},{2,1},{3,0},{4,7},{5,6},{6,5},{7,4},{8,11},{9,10},{10,... | collective-permute-start | bytes 2488328 | tf_op jit(solution)/shard_map/ppermute | solution.py:16
  189.5 53.6 %collective-permute-start.11 = (bf16[2,288,720]{2,1,0:T(8,128)(2,1)}, bf16[2,288,720]{2,1,0:T(8,128)(2,1)}, u32[]{:S(2)}, u32[]{:S(2)}) collective-permute-start(bf16[2,288,720]{2,1,0:T(8,128)(2,1)} %get-tuple-element.42), channel_id=1, source_target_pairs={{0,5},{1,4},{2,7},{3,6},{4,1},{5,0},{6,3},{7,2},{8,13},{9,12},{10,... | collective-permute-start | bytes 2488328 | tf_op jit(solution)/shard_map/ppermute | solution.py:16
  191.0 52.1 %collective-permute-start.12 = (bf16[2,288,720]{2,1,0:T(8,128)(2,1)}, bf16[2,288,720]{2,1,0:T(8,128)(2,1)}, u32[]{:S(2)}, u32[]{:S(2)}) collective-permute-start(bf16[2,288,720]{2,1,0:T(8,128)(2,1)} %get-tuple-element.43), channel_id=1, source_target_pairs={{0,7},{1,6},{2,5},{3,4},{4,3},{5,2},{6,1},{7,0},{8,15},{9,14},{10,... | collective-permute-start | bytes 2488328 | tf_op jit(solution)/shard_map/ppermute | solution.py:16
  195.5 54.7 %collective-permute-start.24 = (bf16[128,2304]{1,0:T(8,128)(2,1)}, bf16[128,2304]{1,0:T(8,128)(2,1)S(1)}, u32[]{:S(2)}, u32[]{:S(2)}) collective-permute-start(bf16[128,2304]{1,0:T(8,128)(2,1)} %convolution_convert_fusion), channel_id=1, source_target_pairs={{0,6},{1,7},{2,4},{3,5},{4,2},{5,3},{6,0},{7,1},{8,14},{9,15},{10,... | collective-permute-start | bytes 1769480 | tf_op jit(solution)/shard_map/ppermute | solution.py:16
  199.8 56.2 %collective-permute-start.23 = (bf16[128,2304]{1,0:T(8,128)(2,1)}, bf16[128,2304]{1,0:T(8,128)(2,1)}, u32[]{:S(2)}, u32[]{:S(2)}) collective-permute-start(bf16[128,2304]{1,0:T(8,128)(2,1)} %convolution_convert_fusion.1), channel_id=1, source_target_pairs={{0,4},{1,5},{2,6},{3,7},{4,0},{5,1},{6,2},{7,3},{8,12},{9,13},{10,... | collective-permute-start | bytes 1769480 | tf_op jit(solution)/shard_map/ppermute | solution.py:16
  203.4 52.7 %collective-permute-start.22 = (bf16[128,2304]{1,0:T(8,128)(2,1)}, bf16[128,2304]{1,0:T(8,128)(2,1)}, u32[]{:S(2)}, u32[]{:S(2)}) collective-permute-start(bf16[128,2304]{1,0:T(8,128)(2,1)} %convolution_convert_fusion.2), channel_id=1, source_target_pairs={{0,2},{1,3},{2,0},{3,1},{4,6},{5,7},{6,4},{7,5},{8,10},{9,11},{10,... | collective-permute-start | bytes 1769480 | tf_op jit(solution)/shard_map/ppermute | solution.py:16
  276.1 39.1 %collective-permute-start.28 = (bf16[720,2304]{1,0:T(8,128)(2,1)}, bf16[720,2304]{1,0:T(8,128)(2,1)}, u32[]{:S(2)}, u32[]{:S(2)}) collective-permute-start(bf16[720,2304]{1,0:T(8,128)(2,1)} %bitcast.107), channel_id=1, source_target_pairs={{0,1},{1,0},{2,3},{3,2},{4,5},{5,4},{6,7},{7,6},{8,9},{9,8},{10,11... | collective-permute-start | bytes 9953288 | tf_op jit(solution)/shard_map/ppermute | solution.py:16
  276.1 39.1 %collective-permute-start.29 = (bf16[720,2304]{1,0:T(8,128)(2,1)}, bf16[720,2304]{1,0:T(8,128)(2,1)}, u32[]{:S(2)}, u32[]{:S(2)}) collective-permute-start(bf16[720,2304]{1,0:T(8,128)(2,1)} %bitcast.110), channel_id=1, source_target_pairs={{0,1},{1,0},{2,3},{3,2},{4,5},{5,4},{6,7},{7,6},{8,9},{9,8},{10,11... | collective-permute-start | bytes 9953288 | tf_op jit(solution)/shard_map/ppermute | solution.py:16
  286.6 28.6 %collective-permute-start.30 = (bf16[720,2304]{1,0:T(8,128)(2,1)}, bf16[720,2304]{1,0:T(8,128)(2,1)}, u32[]{:S(2)}, u32[]{:S(2)}) collective-permute-start(bf16[720,2304]{1,0:T(8,128)(2,1)} %copy.39.refs_6_), channel_id=1, source_target_pairs={{0,1},{1,0},{2,3},{3,2},{4,5},{5,4},{6,7},{7,6},{8,9},{9,8},{10,11... | collective-permute-start | bytes 9953288 | tf_op jit(solution)/shard_map/ppermute | solution.py:16
  286.6 28.6 %collective-permute-start.26 = (bf16[128,2304]{1,0:T(8,128)(2,1)}, bf16[128,2304]{1,0:T(8,128)(2,1)S(1)}, u32[]{:S(2)}, u32[]{:S(2)}) collective-permute-start(bf16[128,2304]{1,0:T(8,128)(2,1)} %multiply_convert_fusion.refs_0_), channel_id=1, source_target_pairs={{0,4},{1,5},{2,6},{3,7},{4,0},{5,1},{6,2},{7,3},{8,12},{9,13},{10,... | collective-permute-start | bytes 1769480 | tf_op jit(solution)/shard_map/ppermute | solution.py:16
  339.9 27.3 %collective-permute-start.32 = (bf16[128,2304]{1,0:T(8,128)(2,1)}, bf16[128,2304]{1,0:T(8,128)(2,1)S(1)}, u32[]{:S(2)}, u32[]{:S(2)}) collective-permute-start(bf16[128,2304]{1,0:T(8,128)(2,1)} %get-tuple-element.56), channel_id=1, source_target_pairs={{0,4},{1,5},{2,6},{3,7},{4,0},{5,1},{6,2},{7,3},{8,12},{9,13},{10,... | collective-permute-start | bytes 1769480 | tf_op jit(solution)/shard_map/ppermute | solution.py:16
  340.4 27.3 %collective-permute-start.31 = (bf16[128,2304]{1,0:T(8,128)(2,1)}, bf16[128,2304]{1,0:T(8,128)(2,1)}, u32[]{:S(2)}, u32[]{:S(2)}) collective-permute-start(bf16[128,2304]{1,0:T(8,128)(2,1)} %get-tuple-element.55), channel_id=1, source_target_pairs={{0,2},{1,3},{2,0},{3,1},{4,6},{5,7},{6,4},{7,5},{8,10},{9,11},{10,... | collective-permute-start | bytes 1769480 | tf_op jit(solution)/shard_map/ppermute | solution.py:16
  (39 other events, 953.0 us)
Sparse Core Ops, SparseCore 0:
  26.8 74.9 all-gather.4
  103.3 75.7 all-gather.6

commit v3 on v2

v3 whole, which is shorter than its diff:
```python
import jax
import jax.numpy as jnp
from jax import lax
from jax.experimental import pallas as pl
from jax.experimental.pallas import tpu as pltpu
from jax.sharding import PartitionSpec as P

HEAD_DIM = 64


def swap_pairs(size, step):
    return [(i, i ^ step) for i in range(size)]


def send(block, size, step):
    return lax.ppermute(block, "tensor", swap_pairs(size, step))


def split_heads(qkv, parts):
    _, rows, width = qkv.shape
    part = width // parts

    def kernel(x_ref, o_ref):
        for t in range(parts):
            for j in range(3):
                o_ref[t, j] = x_ref[j, :, t * part : (t + 1) * part].astype(jnp.bfloat16)

    return pl.pallas_call(
        kernel,
        out_shape=jax.ShapeDtypeStruct((parts, 3, rows, part), jnp.bfloat16),
        name="split_heads",
    )(qkv)


def split_rows(matrix, parts, plane, rows):
    width = matrix.shape[1]
    part = width // parts

    def kernel(p_ref, x_ref, o_ref):
        for t in range(parts):
            o_ref[t] = x_ref[:, t * part : (t + 1) * part].astype(jnp.bfloat16)

    return pl.pallas_call(
        kernel,
        out_shape=jax.ShapeDtypeStruct((parts, rows, part), jnp.bfloat16),
        grid_spec=pltpu.PrefetchScalarGridSpec(
            num_scalar_prefetch=1,
            grid=(1,),
            in_specs=[pl.BlockSpec((rows, width), lambda i, p: (p[0], 0))],
            out_specs=pl.BlockSpec((parts, rows, part), lambda i, p: (0, 0, 0)),
        ),
        compiler_params=pltpu.CompilerParams(vmem_limit_bytes=32 * 1024 * 1024),
        name="split_rows",
    )(plane.reshape(1), matrix)


def split_columns(gate, up, down_tail, parts, me):
    rows, width = gate.shape
    tail = down_tail.shape[0]
    part = width // parts
    window = min(width, (part + 127) // 128 * 128 + 128)
    chunk = 48 if rows % 48 == 0 else 16

    def kernel(me_ref, gate_ref, up_ref, tail_ref, *o_refs):
        step = pl.program_id(0)
        groups = chunk // 16

        def columns(x_ref, k):
            left = (me_ref[0] ^ k) * part
            base = jnp.minimum(lax.div(left, 128) * 128, width - window)
            cols = x_ref[:, pl.ds(pl.multiple_of(base, 128), window)]
            cols = pltpu.roll(cols, window - (left - base), 1)[:, :part]
            return cols.astype(jnp.bfloat16).reshape(-1, 16, part)

        for k in range(parts):
            o_refs[k][pl.ds(step * groups, groups)] = columns(gate_ref, k)
            o_refs[k][pl.ds(step * groups + rows // 16, groups)] = columns(up_ref, k)

        @pl.when(step == 0)
        def _():
            for k in range(parts):
                o_refs[k][rows // 8 : (2 * rows + tail) // 16] = columns(tail_ref, k)

    return pl.pallas_call(
        kernel,
        out_shape=[jax.ShapeDtypeStruct(((2 * rows + tail) // 16, 16, part), jnp.bfloat16)]
        * parts,
        grid_spec=pltpu.PrefetchScalarGridSpec(
            num_scalar_prefetch=1,
            grid=(rows // chunk,),
            in_specs=[pl.BlockSpec((chunk, width), lambda i, m: (i, 0))] * 2
            + [pl.BlockSpec((tail, width), lambda i, m: (0, 0))],
            out_specs=[
                pl.BlockSpec(((2 * rows + tail) // 16, 16, part), lambda i, m: (0, 0, 0))
            ]
            * parts,
        ),
        compiler_params=pltpu.CompilerParams(vmem_limit_bytes=40 * 1024 * 1024),
        name="split_columns",
    )(me.reshape(1), gate, up, down_tail)


def copy_rows(moves, outs_shape, sources, me, name):
    count = len(sources)
    outs = len(outs_shape)

    def kernel(me_ref, *refs):
        ins, o_refs, sem = refs[:count], refs[count : count + outs], refs[count + outs]
        copies = [
            pltpu.make_async_copy(source, o_refs[out].at[pl.ds(first, groups)], sem.at[i])
            for i, (source, out, first, groups) in enumerate(moves(me_ref[0], ins))
        ]
        for copy in copies:
            copy.start()
        for copy in copies:
            copy.wait()

    return pl.pallas_call(
        kernel,
        out_shape=[jax.ShapeDtypeStruct(shape, jnp.bfloat16) for shape in outs_shape],
        grid_spec=pltpu.PrefetchScalarGridSpec(
            num_scalar_prefetch=1,
            grid=(1,),
            in_specs=[pl.BlockSpec(memory_space=pl.ANY)] * count,
            out_specs=[pl.BlockSpec(shape, lambda i, m: (0, 0, 0)) for shape in outs_shape],
            scratch_shapes=[pltpu.SemaphoreType.DMA((160,))],
        ),
        compiler_params=pltpu.CompilerParams(vmem_limit_bytes=40 * 1024 * 1024),
        name=name,
    )(me.reshape(1), *sources)


def join_blocks(blocks, me):
    rows, width = blocks[0].shape
    groups = rows // 16

    def moves(index, ins):
        return [(ref, 0, (index ^ k) * groups, groups) for k, ref in enumerate(ins)]

    blocks = [block.reshape(groups, 16, width) for block in blocks]
    shape = (len(blocks) * groups, 16, width)
    return copy_rows(moves, [shape], blocks, me, "join_blocks")[0].reshape(-1, width)


def join_gate_up(blocks, me, rows):
    width = blocks[0].shape[2]
    groups = rows // 16

    def moves(index, ins):
        return [
            (ref.at[pl.ds(i * groups, groups)], i, (index ^ k) * groups, groups)
            for i in range(2)
            for k, ref in enumerate(ins)
        ]

    shape = (len(blocks) * groups, 16, width)
    joined = copy_rows(moves, [shape, shape], blocks, me, "join_gate_up")
    return [matrix.reshape(-1, width) for matrix in joined]


def join_down(gathered, blocks, me, rows):
    planes, count, part_rows, width = gathered.shape
    groups, part_groups = rows // 16, part_rows // 16
    rest = groups - planes * part_groups
    gathered = gathered.reshape(planes, count, part_groups, 16, width)

    def moves(index, ins):
        found = [
            (ins[0].at[p, t], 0, t * groups + p * part_groups, part_groups)
            for p in range(planes)
            for t in range(count)
        ]
        return found + [
            (
                ref.at[pl.ds(2 * groups, rest)],
                0,
                (index ^ k) * groups + planes * part_groups,
                rest,
            )
            for k, ref in enumerate(ins[1:])
        ]

    shape = (count * groups, 16, width)
    return copy_rows(moves, [shape], [gathered, *blocks], me, "join_down")[0].reshape(-1, width)


def expert(blocks, gate_w, up_w, down_w):
    count = len(blocks)
    rows, model = blocks[0].shape
    units = gate_w.shape[1]

    def kernel(*refs):
        x_in, w_in = refs[:count], refs[count : count + 3]
        outs = refs[count + 3 : 2 * count + 3]
        x_all, w_all, x_sem, w_sem = refs[2 * count + 3 :]
        x_copies = [
            pltpu.make_async_copy(x_in[j], x_all.at[pl.ds(j * rows, rows), :], x_sem.at[j])
            for j in range(count)
        ]
        w_copies = [pltpu.make_async_copy(w_in[j], w_all.at[j], w_sem.at[j]) for j in range(3)]
        for copy in x_copies + w_copies:
            copy.start()
        for copy in x_copies:
            copy.wait()
        x = x_all[...]
        w_copies[0].wait()
        gate = jnp.dot(x, w_all[0], preferred_element_type=jnp.float32)
        w_copies[1].wait()
        up = jnp.dot(x, w_all[1], preferred_element_type=jnp.float32)
        act = (gate / (1.0 + jnp.exp(-gate)) * up).astype(jnp.bfloat16)
        w_copies[2].wait()
        for j in range(count):
            outs[j][...] = dot_nt(act[j * rows : (j + 1) * rows], w_all[2]).astype(jnp.bfloat16)

    return pl.pallas_call(
        kernel,
        out_shape=[jax.ShapeDtypeStruct((rows, model), jnp.bfloat16)] * count,
        in_specs=[pl.BlockSpec(memory_space=pl.ANY)] * (count + 3),
        out_specs=[pl.BlockSpec(memory_space=pltpu.VMEM)] * count,
        scratch_shapes=[
            pltpu.VMEM((count * rows, model), jnp.bfloat16),
            pltpu.VMEM((3, model, units), jnp.bfloat16),
            pltpu.SemaphoreType.DMA((count,)),
            pltpu.SemaphoreType.DMA((3,)),
        ],
        compiler_params=pltpu.CompilerParams(vmem_limit_bytes=56 * 1024 * 1024),
        cost_estimate=pl.CostEstimate(
            flops=6 * count * rows * model * units,
            bytes_accessed=6 * model * units,
            transcendentals=count * rows * units,
        ),
        name="expert",
    )(*blocks, gate_w, up_w, down_w)


def dot_nt(a, b):
    return lax.dot_general(a, b, (((1,), (1,)), ((), ())), preferred_element_type=jnp.float32)


def attention(tokens, weights, cosine, sine, scalars, rows_dev):
    seq, model = tokens.shape
    width = weights.shape[2]
    heads = width // HEAD_DIM
    block = min(256, seq)
    steps = seq // block
    half = HEAD_DIM // 2

    def kernel(s_ref, x_ref, w_ref, cos_ref, sin_ref, kv_ref, att_ref, k_all, v_all):
        step = pl.program_id(0)
        lane = lax.broadcasted_iota(jnp.int32, (block, width), 1)
        low = lax.rem(lane, HEAD_DIM) < half
        head_of = lax.div(lane, HEAD_DIM)
        x = x_ref[...]

        def rotated(j):
            m = jnp.dot(x, w_ref[j], preferred_element_type=jnp.float32)
            turned = jnp.where(
                low, -pltpu.roll(m, width - half, 1), pltpu.roll(m, half, 1)
            )
            return m * cos_ref[...] + turned * sin_ref[...]

        row = step * block + lax.broadcasted_iota(jnp.int32, (block, width), 0)
        valid = row < s_ref[0]
        start = pl.multiple_of(step * block, block)
        key = rotated(1)
        k_all[pl.ds(start, block), :] = key.astype(jnp.bfloat16)
        kv_ref[0] = jnp.where(valid, key, 0.0).astype(jnp.bfloat16)
        value = jnp.dot(x, w_ref[2], preferred_element_type=jnp.float32)
        v_all[pl.ds(start, block), :] = value.astype(jnp.bfloat16)
        kv_ref[1] = jnp.where(valid, value, 0.0).astype(jnp.bfloat16)
        query = rotated(0).astype(jnp.bfloat16).astype(jnp.float32) * HEAD_DIM ** (-0.5)

        for here in range(steps):

            @pl.when(step == here)
            def _():
                lo = here * block
                causal = lax.broadcasted_iota(
                    jnp.int32, (block, block), 0
                ) >= lax.broadcasted_iota(jnp.int32, (block, block), 1)
                out = jnp.zeros((block, width), jnp.float32)
                for h in range(heads):
                    q = jnp.where(head_of == h, query, 0.0).astype(jnp.bfloat16)
                    diag = jnp.where(causal, dot_nt(q, k_all[lo : lo + block, :]), -1e30)
                    top = jnp.max(diag, axis=-1, keepdims=True)
                    if lo:
                        past = dot_nt(q, k_all[:lo, :])
                        top = jnp.maximum(top, jnp.max(past, axis=-1, keepdims=True))
                        past = jnp.exp(past - top)
                    diag = jnp.exp(diag - top)
                    total = jnp.sum(diag, axis=-1, keepdims=True)
                    if lo:
                        total = total + jnp.sum(past, axis=-1, keepdims=True)
                    inv = 1.0 / total
                    res = jnp.dot(
                        (diag * inv).astype(jnp.bfloat16),
                        v_all[lo : lo + block, :],
                        preferred_element_type=jnp.float32,
                    )
                    if lo:
                        res = res + jnp.dot(
                            (past * inv).astype(jnp.bfloat16),
                            v_all[:lo, :],
                            preferred_element_type=jnp.float32,
                        )
                    out = jnp.where(head_of == h, res, out)
                out = out.astype(jnp.bfloat16)
                for piece in range(block // rows_dev):
                    dev = here * (block // rows_dev) + piece
                    slot = jnp.where(s_ref[1] == dev % 2, 0, 1)
                    att_ref[slot, (dev // 2) * rows_dev : (dev // 2 + 1) * rows_dev, :] = out[
                        piece * rows_dev : (piece + 1) * rows_dev
                    ]

    return pl.pallas_call(
        kernel,
        out_shape=(
            jax.ShapeDtypeStruct((2, seq, width), jnp.bfloat16),
            jax.ShapeDtypeStruct((2, seq // 2, width), jnp.bfloat16),
        ),
        grid_spec=pltpu.PrefetchScalarGridSpec(
            num_scalar_prefetch=1,
            grid=(steps,),
            in_specs=[
                pl.BlockSpec((block, model), lambda i, s: (i, 0)),
                pl.BlockSpec((3, model, width), lambda i, s: (0, 0, 0)),
                pl.BlockSpec((block, width), lambda i, s: (i, 0)),
                pl.BlockSpec((block, width), lambda i, s: (i, 0)),
            ],
            out_specs=(
                pl.BlockSpec((2, block, width), lambda i, s: (0, i, 0)),
                pl.BlockSpec((2, seq // 2, width), lambda i, s: (0, 0, 0)),
            ),
            scratch_shapes=[
                pltpu.VMEM((seq, width), jnp.bfloat16),
                pltpu.VMEM((seq, width), jnp.bfloat16),
            ],
        ),
        compiler_params=pltpu.CompilerParams(vmem_limit_bytes=48 * 1024 * 1024),
        cost_estimate=pl.CostEstimate(
            flops=6 * seq * model * width + 4 * seq * seq * width,
            bytes_accessed=2 * (seq * model + 3 * model * width),
            transcendentals=seq * seq * heads,
        ),
        name="attention",
    )(scalars, tokens, weights, cosine, sine)


def rms_scale(values, gain_row):
    mean_sq = jnp.mean(values * values, axis=-1, keepdims=True)
    return values * lax.rsqrt(mean_sq + 1e-05) * gain_row


def shards(
    hidden_in,
    prompt_len,
    start_pos,
    routes,
    trainer_qkv,
    trainer_out,
    trainer_gate,
    trainer_up,
    trainer_down,
    attn_gain,
    moe_gain,
    router,
):
    size = lax.axis_size("tensor")
    replicas = lax.axis_size("dp")
    chips = size // 2
    me = lax.axis_index("tensor").astype(jnp.int32)
    plane = lax.axis_index("dp").astype(jnp.int32)
    chip, core = me // 2, me % 2
    rows_dev, model = hidden_in.shape[1], hidden_in.shape[2]
    seq_len = rows_dev * size
    length = prompt_len[0]
    offset = start_pos[0]
    my_first = me * rows_dev

    mat_rows = trainer_down.shape[0]
    part_rows = mat_rows // (16 * replicas) * 16
    local_width = trainer_qkv.shape[2] // size
    qkv_parts = split_heads(trainer_qkv.transpose(1, 0, 2), size)
    qkv_cols = lax.all_to_all(qkv_parts, "tensor", 0, 0, tiled=True)
    parts = split_columns(
        trainer_gate, trainer_up, trainer_down[part_rows * replicas :], size, me
    )
    tokens = hidden_in[0].astype(jnp.float32)
    normed = rms_scale(tokens, attn_gain).astype(jnp.bfloat16)
    qkv_cols, normed, *parts = lax.optimization_barrier((qkv_cols, normed, *parts))
    qkv_all = lax.all_gather(qkv_cols, "dp", axis=0)
    qkv_server = qkv_all.transpose(2, 1, 0, 3, 4).reshape(3, model, local_width)
    server_qkv = qkv_server.transpose(1, 0, 2)
    down_parts = split_rows(trainer_down, size, plane, part_rows)
    down_cols = lax.all_to_all(down_parts, "tensor", 0, 0, tiled=True)
    down_all = lax.all_gather(down_cols, "dp", axis=0)

    same_core = [normed] + [send(normed, size, 2 * j) for j in range(1, chips)]
    out_cast, _ = lax.optimization_barrier((trainer_out.astype(jnp.bfloat16), same_core[1]))
    server_out = lax.all_gather(out_cast, "dp", axis=0, tiled=True)
    other_core = send(jnp.stack(same_core), size, 1)
    blocks = []
    for j in range(chips):
        blocks += [same_core[j], other_core[j]]
    piece = join_blocks(blocks, me)

    even, odd = list(range(2, size, 2)), list(range(1, size, 2))
    early = [send(parts[k], size, k) for k in even]
    late = list(lax.optimization_barrier((*[parts[k] for k in odd], *early)))
    early = late[len(odd) :]
    late = [send(block, size, k) for block, k in zip(late, odd)]

    out_pair = jnp.concatenate([server_out, send(server_out, size, 1)], axis=0)

    half_dim = HEAD_DIM // 2
    inv_freq = jnp.power(
        10000.0, jnp.arange(half_dim, dtype=jnp.float32) * (-2.0 / HEAD_DIM)
    )
    places = offset + jnp.arange(seq_len, dtype=jnp.int32)
    angles = places.astype(jnp.float32)[:, None] * inv_freq[None, :]
    repeats = local_width // half_dim
    cosine = jnp.tile(jnp.cos(angles), (1, repeats))
    sine_part = jnp.tile(jnp.sin(angles), (1, repeats))
    scalars = jnp.stack([length, core])
    qkv_here, _, *early = lax.optimization_barrier((qkv_server, down_cols, *early))
    cache_pair, attended = attention(
        piece, qkv_here, cosine, sine_part, scalars, rows_dev
    )

    att_pair = jnp.concatenate([attended[0], send(attended[1], size, 1)], axis=-1)
    att_pair, *late = lax.optimization_barrier((att_pair, *late))
    att_pair = att_pair.reshape(chips, rows_dev, 2 * local_width)
    joined = [parts[0]] * size
    for block, k in zip(early + late, even + odd):
        joined[k] = block

    def attn_part(j):
        rows = lax.dynamic_index_in_dim(att_pair, chip ^ j, 0, keepdims=False)
        return jnp.dot(rows, out_pair, preferred_element_type=jnp.float32)

    partial = [attn_part(j) for j in range(chips)]
    sent = [part.astype(jnp.bfloat16) for part in partial[1:]]
    got = [send(block, size, 2 * j + 2) for j, block in enumerate(sent)]
    attn_sum = partial[0]
    for block in got:
        attn_sum = attn_sum + block.astype(jnp.float32)
    middle = (tokens + attn_sum).astype(jnp.bfloat16)
    normed_moe = rms_scale(middle.astype(jnp.float32), moe_gain).astype(jnp.bfloat16)

    moe_rows = [normed_moe] + [send(normed_moe, size, 2 * j) for j in range(1, chips)]
    moe_other = send(jnp.stack(moe_rows), size, 1)
    gate, up = join_gate_up(joined, me, mat_rows)
    down = join_down(down_all, joined, me, mat_rows)

    local_routes = lax.dynamic_slice_in_dim(routes[0], my_first, rows_dev, 0)
    local_valid = my_first + jnp.arange(rows_dev, dtype=jnp.int32) < length
    logits = jnp.dot(normed_moe, router, preferred_element_type=jnp.float32)
    expert_ids = jnp.arange(router.shape[1], dtype=jnp.int32)
    logit_first = jnp.sum(
        jnp.where(local_routes[:, 0:1] == expert_ids[None, :], logits, 0.0), axis=1
    )
    logit_second = jnp.sum(
        jnp.where(local_routes[:, 1:2] == expert_ids[None, :], logits, 0.0), axis=1
    )
    other_logit = jnp.where(local_routes[:, 0] == 0, logit_second, logit_first)
    local_routed = jnp.any(local_routes == 0, axis=1)
    route_w = jnp.where(local_routed, jax.nn.sigmoid(logits[:, 0] - other_logit), 0.0)

    sums_mine = expert(moe_rows, gate, up, down)
    sums_other = expert([moe_other[j] for j in range(chips)], gate, up, down)
    from_other = send(jnp.stack(sums_other), size, 1)
    sums = [
        block.astype(jnp.float32) + from_other[j].astype(jnp.float32)
        for j, block in enumerate(sums_mine)
    ]
    expert_sum = sums[0]
    for j in range(1, chips):
        expert_sum = expert_sum + send(sums[j].astype(jnp.bfloat16), size, 2 * j).astype(
            jnp.float32
        )
    expert_sum = jnp.where(local_routed[:, None], expert_sum, 0.0)
    result = middle.astype(jnp.float32) + route_w[:, None] * expert_sum
    hidden_out = jnp.where(local_valid[:, None], result, 0.0).astype(jnp.bfloat16)[None]
    return (
        server_qkv,
        server_out,
        gate,
        up,
        down,
        hidden_out,
        cache_pair[None],
    )


def solution(mesh):
    placed = (
        P("dp", "tensor", None),
        P("dp"),
        P("dp"),
        P("dp", None, None),
        P(("tensor", "dp"), None, None),
        P(("tensor", "dp"), None),
        P("tensor", None),
        P("tensor", None),
        P("tensor", None),
        P(),
        P(),
        P(),
    )
    return jax.shard_map(
        shards,
        mesh=mesh,
        in_specs=placed,
        out_specs=(
            P(None, None, "tensor"),
            P("tensor", None),
            P(None, "tensor"),
            P(None, "tensor"),
            P(None, "tensor"),
            P("dp", "tensor", None),
            P("dp", None, None, "tensor"),
        ),
        check_vma=False,
    )
```

time: 379 us -> 341 us (0.90); the launches traced: 377 us -> 334 us
  waiting for transfers between devices: 168 us -> 130 us
  blocking collectives: 16.9 us -> 0 us
  starting transfers between devices: 47.1 us -> 33.9 us
  local copies, waits for them, and re-layouts: 51.1 us -> 62.2 us
  Pallas kernels: 58.5 us -> 68.7 us
  other arithmetic: 6.5 us -> 16.7 us
  matrix products: 13.1 us -> 7.26 us
    ppermute x6 -> x0, waiting for transfers between devices: 56.6 us -> none  [the longest x3 47 us: gather_line(): lax.ppermute(down, 'dp', [(i, i - 1) for i in range(1, count - step + 1)])]
    all_to_all x1 -> x0, blocking collectives: 16.9 us -> none  [shards(): qkv_cols = lax.all_to_all(qkv_parts, 'tensor', 0, 0, tiled=True)]
    ppermute x6 -> x0, starting transfers between devices: 14.6 us -> none  [the longest x3 9.04 us: gather_line(): lax.ppermute(up, 'dp', [(i, i + 1) for i in range(step - 1, count - 1)])]
    unnamed x60 -> x79, local copies, waits for them, and re-layouts: 28.3 us -> 41.3 us
    all_gather x1, waiting for transfers between devices: 0.01 us -> 10.6 us  [shards(): qkv_all = lax.all_gather(qkv_cols, 'dp', axis=0)]
    ppermute x28 -> x24, waiting for transfers between devices: 112 us -> 119 us  [send(): return lax.ppermute(block, 'tensor', swap_pairs(size, step))]
    pallas_call x1 -> x2, Pallas kernels: 22.3 us -> 28.8 us  [expert(): pl.pallas_call(kernel, out_shape=[jax.ShapeDtypeStruct((rows, model), jnp...]
    reshape x1 -> x0, local copies, waits for them, and re-layouts: 5.64 us -> none  [shards(): down_t = down_late.transpose(3, 1, 0, 2).reshape(-1, model)]
  transfers between devices with their start and end apart: 37 -> 29, of which waited for: 12 -> 13; matrix products, arithmetic and copies ran while one was open for 16% -> 14% of each run, Pallas kernels for 9% -> 15%
where the time goes in v3:
time: 341 us; the launch traced here: 334 us
  waiting for transfers between devices  130 us (38%)
  Pallas kernels  68.7 us (20%)
  local copies, waits for them, and re-layouts  62.2 us (18%)
  starting transfers between devices  33.9 us (10%)
  other arithmetic  16.7 us (5%)
  between operations  15.5 us (5%)
  matrix products  7.26 us (2%)
    ppermute x24, waiting for transfers between devices, send(): return lax.ppermute(block, 'tensor', swap_pairs(size, step))  119 us
    unnamed x79, local copies, waits for them, and re-layouts  41.3 us
    pallas_call x2, Pallas kernels, expert(): pl.pallas_call(kernel, out_shape=[jax.ShapeDtypeStruct((rows, model), jnp...  28.8 us
    ppermute x24, starting transfers between devices, send(): return lax.ppermute(block, 'tensor', swap_pairs(size, step))  24.6 us
    pallas_call x3, Pallas kernels, copy_rows(): pl.pallas_call(kernel, out_shape=[jax.ShapeDtypeStruct(shape, jnp.bfloat1...  13.8 us
    pallas_call x1, Pallas kernels, attention(): pl.pallas_call(kernel, out_shape=(jax.ShapeDtypeStruct((2, seq, width), j...  13.6 us
    all_gather x1, waiting for transfers between devices, shards(): qkv_all = lax.all_gather(qkv_cols, 'dp', axis=0)  10.6 us
    pallas_call x1, Pallas kernels, split_columns(): pl.pallas_call(kernel, out_shape=[jax.ShapeDtypeStruct(((2 * rows + tail)...  9.67 us
  transfers between devices with their start and end apart: 29, of which 13 were waited for; matrix products, arithmetic and copies ran while one was open for 14% of the time, Pallas kernels for 15%

profile of v3, /device:TPU:12, one launch (start us, length us, event | category | flops | bytes accessed | tf_op | source)
XLA Modules:
  0.0 334.3 jit_solution(15156734856578489405)
XLA Ops:
  9.7 4.6 %all-to-all-start = ((bf16[8,3,72,256]{3,2,1,0:T(8,128)(2,1)}), bf16[8,3,72,256]{3,2,1,0:T(8,128)(2,1)}, u32[]{:S(2)}, u32[]{:S(2)}) async-start(bf16[8,3,72,256]{3,2,1,0:T(8,128)(2,1)} %split_heads.1), calls=%async_computation | async-start | bytes 1769472 | tf_op jit(solution)/shard_map/all_to_all | solution.py:384
  15.8 9.7 %split_columns.1 = (bf16[38,16,720]{2,1,0:T(8,128)(2,1)S(1)}, bf16[38,16,720]{2,1,0:T(8,128)(2,1)S(1)}, bf16[38,16,720]{2,1,0:T(8,128)(2,1)}, bf16[38,16,720]{2,...) custom-call(s32[1]{0:T(128)} %bitcast.3.me_ref, ...), custom_call_target="tpu_custom_call" | custom-call | tf_op jit(solution)/shard_map/split_columns/pallas_call | solution.py:84
  32.5 12.1 %collective-permute-done = bf16[128,2304]{1,0:T(8,128)(2,1)S(1)} collective-permute-done((bf16[128,2304]{1,0:T(8,128)(2,1)S(1)}, bf16[128,2304]{1,0:T(8,128)(2,1)S(1)}, u32[]{:S(2)}, u32[]{:S(2)}) %collective-permute-start) | collective-permute-done | bytes 589856 | tf_op jit(solution)/shard_map/ppermute | solution.py:16
  48.4 12.6 %collective-permute-done.2 = bf16[128,2304]{1,0:T(8,128)(2,1)S(1)} collective-permute-done((bf16[128,2304]{1,0:T(8,128)(2,1)S(1)}, bf16[128,2304]{1,0:T(8,128)(2,1)S(1)}, u32[]{:S(2)}, u32[]{:S(2)}) %collective-permute-start.2) | collective-permute-done | bytes 589856 | tf_op jit(solution)/shard_map/ppermute | solution.py:16
  61.0 12.5 %collective-permute-done.1 = bf16[128,2304]{1,0:T(8,128)(2,1)S(1)} collective-permute-done((bf16[128,2304]{1,0:T(8,128)(2,1)S(1)}, bf16[128,2304]{1,0:T(8,128)(2,1)S(1)}, u32[]{:S(2)}, u32[]{:S(2)}) %collective-permute-start.1) | collective-permute-done | bytes 589856 | tf_op jit(solution)/shard_map/ppermute | solution.py:16
  83.1 4.7 %all-to-all-start.1 = ((bf16[8,64,720]{2,1,0:T(8,128)(2,1)}), bf16[8,64,720]{2,1,0:T(8,128)(2,1)}, u32[]{:S(2)}, u32[]{:S(2)}) async-start(bf16[8,64,720]{2,1,0:T(8,128)(2,1)} %copy-done.8), calls=%async_computation.1 | async-start | bytes 1572864 | tf_op jit(solution)/shard_map/all_to_all | solution.py:395
  99.2 20.8 %collective-permute-done.5.refs_4_.refs_5_ = bf16[38,16,720]{2,1,0:T(8,128)(2,1)S(1)} collective-permute-done((bf16[38,16,720]{2,1,0:T(8,128)(2,1)}, bf16[38,16,720]{2,1,0:T(8,128)(2,1)S(1)}, u32[]{:S(2)}, u32[]{:S(2)}) %collective-permute-start.5) | collective-permute-done | bytes 875552 | tf_op jit(solution)/shard_map/ppermute | solution.py:16
  134.1 10.6 %all-gather.8.cloned.1.call-done = bf16[32,3,72,256]{3,2,1,0:T(8,128)(2,1)} async-done(((bf16[8,3,72,256]{3,2,1,0:T(8,128)(2,1)}), bf16[32,3,72,256]{3,2,1,0:T(8,128)(2,1)}) %all-gather.8.cloned.1.call-update) | async-done | bytes 3538960 | tf_op jit(solution)/shard_map/all_gather | solution.py:391
  144.7 4.2 %copy.29 = bf16[4,8,3,72,256]{4,3,0,1,2:T(8,128)(2,1)} copy(bf16[4,8,3,72,256]{4,3,2,1,0:T(8,128)(2,1)} %bitcast.155) | data formatting | bytes 7077888 | tf_op jit(solution)/shard_map/all_gather | solution.py:391
  153.4 13.6 %attention.1 = (bf16[2,1024,256]{2,1,0:T(8,128)(2,1)}, bf16[2,512,256]{2,1,0:T(8,128)(2,1)S(1)}) custom-call(s32[2]{0:T(128)S(1)} %pad_add_fusion.s_ref, bf16[1024,2304]{1,0:T(8,128)(2,1)} %bitcast.133, bf16[3,2304,256]{2,1,0:T(8,128)(2,1)S(1)} %bitcast.135, f32[1024,256]{1,0:T(8,128)S(1)} %copy-done.16, f32[1024,256]{1,0:T(8,128)S(1)} %copy-done.15), custom_call_target="tpu_custom_call" | custom-call | flops 4697620480 | bytes 8257536 | tf_op jit(solution)/shard_map/attention/pallas_call | solution.py:315
  176.4 12.9 %collective-permute-done.13 = bf16[128,2304]{1,0:T(8,128)(2,1)} collective-permute-done((bf16[128,2304]{1,0:T(8,128)(2,1)}, bf16[128,2304]{1,0:T(8,128)(2,1)}, u32[]{:S(2)}, u32[]{:S(2)}) %collective-permute-start.13) | collective-permute-done | bytes 589856 | tf_op jit(solution)/shard_map/ppermute | solution.py:16
  189.3 13.4 %collective-permute-done.14 = bf16[128,2304]{1,0:T(8,128)(2,1)} collective-permute-done((bf16[128,2304]{1,0:T(8,128)(2,1)}, bf16[128,2304]{1,0:T(8,128)(2,1)}, u32[]{:S(2)}, u32[]{:S(2)}) %collective-permute-start.14) | collective-permute-done | bytes 589856 | tf_op jit(solution)/shard_map/ppermute | solution.py:16
  209.6 13.5 %collective-permute-done.18.refs_3_ = bf16[128,2304]{1,0:T(8,128)(2,1)S(1)} collective-permute-done((bf16[128,2304]{1,0:T(8,128)(2,1)S(1)}, bf16[128,2304]{1,0:T(8,128)(2,1)S(1)}, u32[]{:S(2)}, u32[]{:S(2)}) %collective-permute-start.18) | collective-permute-done | bytes 589856 | tf_op jit(solution)/shard_map/ppermute | solution.py:16
  223.2 10.9 %collective-permute-done.17.refs_2_ = bf16[128,2304]{1,0:T(8,128)(2,1)S(1)} collective-permute-done((bf16[128,2304]{1,0:T(8,128)(2,1)S(1)}, bf16[128,2304]{1,0:T(8,128)(2,1)S(1)}, u32[]{:S(2)}, u32[]{:S(2)}) %collective-permute-start.17) | collective-permute-done | bytes 589856 | tf_op jit(solution)/shard_map/ppermute | solution.py:16
  236.1 4.4 %join_gate_up.1 = (bf16[144,16,720]{2,1,0:T(8,128)(2,1)S(1)}, bf16[144,16,720]{2,1,0:T(8,128)(2,1)S(1)}) custom-call(s32[1]{0:T(128)} %bitcast.3.me_ref, bf16[38,16,720]{2,1,0:T(8,128)(2,1)S(1)} %get-tuple-element.65.refs_0_.refs_1_, bf16[38,16,720]{2,1,0:T(8,128)(2,1)} %collective-permute-done.8.refs_1_.refs_2_, ...), custom_call_target="tpu_custom_call" | custom-call | tf_op jit(solution)/shard_map/join_gate_up/pallas_call | solution.py:118
  245.9 6.7 %join_down.1 = bf16[144,16,720]{2,1,0:T(8,128)(2,1)S(1)} custom-call(s32[1]{0:T(128)} %bitcast.3.me_ref, bf16[4,8,4,16,720]{4,3,2,1,0:T(8,128)(2,1)S(1)} %bitcast.142, bf16[38,16,720]{2,1,0:T(8,128)(2,1)S(1)} %get-tuple-element.65.refs_0_.refs_1_, bf16[38,16,720]{2,1,0:T(8,128)(2,1)} %collective-permute-done.8.refs_1_.refs_2_, ...), custom_call_target="tpu_custom_call" | custom-call | tf_op jit(solution)/shard_map/join_down/pallas_call | solution.py:118
  252.7 4.3 %slice_bitcast_fusion.4 = (bf16[128,2304]{1,0:T(8,128)(2,1)}, bf16[128,2304]{1,0:T(8,128)(2,1)}, bf16[128,2304]{1,0:T(8,128)(2,1)}, bf16[128,2304]{1,0:T(8,128)(2,1)}) fusion(bf16[4,128,2304]{2,1,0:T(8,128)(2,1)} %collective-permute-done.19), kind=kLoop, calls=%fused_computation.39 | loop fusion | bytes 4718592 | tf_op jit(solution)/shard_map/squeeze | solution.py:470
  257.0 14.4 %expert.3 = (bf16[128,2304]{1,0:T(8,128)(2,1)}, bf16[128,2304]{1,0:T(8,128)(2,1)}, bf16[128,2304]{1,0:T(8,128)(2,1)}, bf16[128,2304]{1,0:T(8,128)(2,1)}) custom-call(bf16[128,2304]{1,0:T(8,128)(2,1)} %get-tuple-element.132.refs_0_, bf16[128,2304]{1,0:T(8,128)(2,1)} %get-tuple-element.131.refs_1_, bf16[128,2304]{1,0:T(8,128)(2,1)} %get-tuple-element.130.refs_2_, ...), custom_call_target="tpu_custom_call" | custom-call | flops 5096079360 | bytes 9953280 | tf_op jit(solution)/shard_map/expert/pallas_call | solution.py:215
  274.5 14.4 %expert.2 = (bf16[128,2304]{1,0:T(8,128)(2,1)}, bf16[128,2304]{1,0:T(8,128)(2,1)}, bf16[128,2304]{1,0:T(8,128)(2,1)}, bf16[128,2304]{1,0:T(8,128)(2,1)}) custom-call(bf16[128,2304]{1,0:T(8,128)(2,1)} %copy-done.28, bf16[128,2304]{1,0:T(8,128)(2,1)} %copy-done.33, bf16[128,2304]{1,0:T(8,128)(2,1)} %copy-done.32, bf16[128,2304]{1,0:T(8,128)(2,1)} %copy-done.31, ...), custom_call_target="tpu_custom_call" | custom-call | flops 5096079360 | bytes 9953280 | tf_op jit(solution)/shard_map/expert/pallas_call | solution.py:215
  288.9 3.6 %fusion.10 = (bf16[128,2304]{1,0:T(8,128)(2,1)}, bf16[128,2304]{1,0:T(8,128)(2,1)}, bf16[128,2304]{1,0:T(8,128)(2,1)}) fusion(bf16[128,2304]{1,0:T(8,128)(2,1)} %get-tuple-element.97, bf16[4,128,2304]{2,1,0:T(8,128)(2,1)} %collective-permute-done.20, bf16[128,2304]{1,0:T(8,128)(2,1)} %get-tuple-element.99, bf16[128,2304]{1,0:T(8,128)(2,1)} %get-tuple-element.98), kind=kLoop, calls=%fused_computation.22 | loop fusion | flops 3538944 | bytes 5308416 | tf_op jit(solution)/shard_map/convert_element_type | solution.py:478
  296.0 5.6 %copy.34 = bf16[2304,720]{0,1:T(8,128)(2,1)} copy(bf16[2304,720]{1,0:T(8,128)(2,1)} %bitcast.130) | data formatting | bytes 6635520
  301.7 5.6 %copy.33 = bf16[2304,720]{0,1:T(8,128)(2,1)} copy(bf16[2304,720]{1,0:T(8,128)(2,1)} %bitcast.141) | data formatting | bytes 6635520
  307.3 5.8 %copy.32 = bf16[2304,720]{0,1:T(8,128)(2,1)} copy(bf16[2304,720]{1,0:T(8,128)(2,1)} %bitcast.138) | data formatting | bytes 6635520
  313.4 7.6 %collective-permute-done.23 = bf16[128,2304]{1,0:T(8,128)(2,1)} collective-permute-done((bf16[128,2304]{1,0:T(8,128)(2,1)}, bf16[128,2304]{1,0:T(8,128)(2,1)}, u32[]{:S(2)}, u32[]{:S(2)}) %collective-permute-start.23) | collective-permute-done | bytes 589856 | tf_op jit(solution)/shard_map/ppermute | solution.py:16
  (161 shorter events, 90.1 us)
Async XLA Ops:
  9.7 18.8 %all-to-all-start = ((bf16[8,3,72,256]{3,2,1,0:T(8,128)(2,1)}), bf16[8,3,72,256]{3,2,1,0:T(8,128)(2,1)}, u32[]{:S(2)}, u32[]{:S(2)}) async-start(bf16[8,3,72,256]{3,2,1,0:T(8,128)(2,1)} %split_heads.1), calls=%async_computation | async-start | bytes 1769472 | tf_op jit(solution)/shard_map/all_to_all | solution.py:384
  14.4 110.3 %all-gather.6.cloned.1.call-start = ((), (), s32[]{:S(2)}) async-start(), calls=%async_computation.2 | async-start | bytes 1474560 | tf_op jit(solution)/shard_map/all_gather | solution.py:400
  44.7 100.0 %all-gather.8.cloned.1.call-start = ((), (), s32[]{:S(2)}) async-start(), calls=%async_computation.3 | async-start | bytes 4423680 | tf_op jit(solution)/shard_map/all_gather | solution.py:391
  46.9 26.6 %collective-permute-start.1 = (bf16[128,2304]{1,0:T(8,128)(2,1)S(1)}, bf16[128,2304]{1,0:T(8,128)(2,1)S(1)}, u32[]{:S(2)}, u32[]{:S(2)}) collective-permute-start(bf16[128,2304]{1,0:T(8,128)(2,1)S(1)} %fusion.7), channel_id=1, source_target_pairs={{0,4},{1,5},{2,6},{3,7},{4,0},{5,1},{6,2},{7,3},{8,12},{9,13},{10,... | collective-permute-start | bytes 1769480 | tf_op jit(solution)/shard_map/ppermute | solution.py:16
  75.3 51.8 %collective-permute-start.3 = (bf16[4,128,2304]{2,1,0:T(8,128)(2,1)}, bf16[4,128,2304]{2,1,0:T(8,128)(2,1)}, u32[]{:S(2)}, u32[]{:S(2)}) collective-permute-start(bf16[4,128,2304]{2,1,0:T(8,128)(2,1)} %pad_maximum_fusion), channel_id=1, source_target_pairs={{0,1},{1,0},{2,3},{3,2},{4,5},{5,4},{6,7},{7,6},{8,9},{9,8},{10,11... | collective-permute-start | bytes 7077896 | tf_op jit(solution)/shard_map/ppermute | solution.py:16
  75.5 23.8 %collective-permute-start.4 = (bf16[38,16,720]{2,1,0:T(8,128)(2,1)}, bf16[38,16,720]{2,1,0:T(8,128)(2,1)S(1)}, u32[]{:S(2)}, u32[]{:S(2)}) collective-permute-start(bf16[38,16,720]{2,1,0:T(8,128)(2,1)} %get-tuple-element.70), channel_id=1, source_target_pairs={{0,2},{1,3},{2,0},{3,1},{4,6},{5,7},{6,4},{7,5},{8,10},{9,11},{10,... | collective-permute-start | bytes 2626568 | tf_op jit(solution)/shard_map/ppermute | solution.py:16
  76.2 43.8 %collective-permute-start.5 = (bf16[38,16,720]{2,1,0:T(8,128)(2,1)}, bf16[38,16,720]{2,1,0:T(8,128)(2,1)S(1)}, u32[]{:S(2)}, u32[]{:S(2)}) collective-permute-start(bf16[38,16,720]{2,1,0:T(8,128)(2,1)} %get-tuple-element.71), channel_id=1, source_target_pairs={{0,4},{1,5},{2,6},{3,7},{4,0},{5,1},{6,2},{7,3},{8,12},{9,13},{10,... | collective-permute-start | bytes 2626568 | tf_op jit(solution)/shard_map/ppermute | solution.py:16
  77.5 42.5 %collective-permute-start.6 = (bf16[38,16,720]{2,1,0:T(8,128)(2,1)}, bf16[38,16,720]{2,1,0:T(8,128)(2,1)}, u32[]{:S(2)}, u32[]{:S(2)}) collective-permute-start(bf16[38,16,720]{2,1,0:T(8,128)(2,1)} %get-tuple-element.72), channel_id=1, source_target_pairs={{0,6},{1,7},{2,4},{3,5},{4,2},{5,3},{6,0},{7,1},{8,14},{9,15},{10,... | collective-permute-start | bytes 2626568 | tf_op jit(solution)/shard_map/ppermute | solution.py:16
  83.1 65.8 %all-to-all-start.1 = ((bf16[8,64,720]{2,1,0:T(8,128)(2,1)}), bf16[8,64,720]{2,1,0:T(8,128)(2,1)}, u32[]{:S(2)}, u32[]{:S(2)}) async-start(bf16[8,64,720]{2,1,0:T(8,128)(2,1)} %copy-done.8), calls=%async_computation.1 | async-start | bytes 1572864 | tf_op jit(solution)/shard_map/all_to_all | solution.py:395
  87.7 156.4 %all-gather.10.cloned.1.call-start = ((), (), s32[]{:S(2)}) async-start(), calls=%async_computation.4 | async-start | bytes 3932160 | tf_op jit(solution)/shard_map/all_gather | solution.py:396
  120.0 48.7 %collective-permute-start.8 = (bf16[38,16,720]{2,1,0:T(8,128)(2,1)}, bf16[38,16,720]{2,1,0:T(8,128)(2,1)}, u32[]{:S(2)}, u32[]{:S(2)}) collective-permute-start(bf16[38,16,720]{2,1,0:T(8,128)(2,1)} %copy-done.20), channel_id=1, source_target_pairs={{0,1},{1,0},{2,3},{3,2},{4,5},{5,4},{6,7},{7,6},{8,9},{9,8},{10,11... | collective-permute-start | bytes 2626568 | tf_op jit(solution)/shard_map/ppermute | solution.py:16
  120.0 48.7 %collective-permute-start.9 = (bf16[38,16,720]{2,1,0:T(8,128)(2,1)}, bf16[38,16,720]{2,1,0:T(8,128)(2,1)}, u32[]{:S(2)}, u32[]{:S(2)}) collective-permute-start(bf16[38,16,720]{2,1,0:T(8,128)(2,1)} %copy-done.19), channel_id=1, source_target_pairs={{0,3},{1,2},{2,1},{3,0},{4,7},{5,6},{6,5},{7,4},{8,11},{9,10},{10,... | collective-permute-start | bytes 2626568 | tf_op jit(solution)/shard_map/ppermute | solution.py:16
  123.5 45.2 %collective-permute-start.10 = (bf16[38,16,720]{2,1,0:T(8,128)(2,1)}, bf16[38,16,720]{2,1,0:T(8,128)(2,1)}, u32[]{:S(2)}, u32[]{:S(2)}) collective-permute-start(bf16[38,16,720]{2,1,0:T(8,128)(2,1)} %copy-done.18), channel_id=1, source_target_pairs={{0,5},{1,4},{2,7},{3,6},{4,1},{5,0},{6,3},{7,2},{8,13},{9,12},{10,... | collective-permute-start | bytes 2626568 | tf_op jit(solution)/shard_map/ppermute | solution.py:16
  123.7 45.1 %collective-permute-start.11 = (bf16[38,16,720]{2,1,0:T(8,128)(2,1)}, bf16[38,16,720]{2,1,0:T(8,128)(2,1)}, u32[]{:S(2)}, u32[]{:S(2)}) collective-permute-start(bf16[38,16,720]{2,1,0:T(8,128)(2,1)} %copy-done.17), channel_id=1, source_target_pairs={{0,7},{1,6},{2,5},{3,4},{4,3},{5,2},{6,1},{7,0},{8,15},{9,14},{10,... | collective-permute-start | bytes 2626568 | tf_op jit(solution)/shard_map/ppermute | solution.py:16
  127.0 40.0 %collective-permute-start.12 = (bf16[256,2304]{1,0:T(8,128)(2,1)}, bf16[256,2304]{1,0:T(8,128)(2,1)}, u32[]{:S(2)}, u32[]{:S(2)}) collective-permute-start(bf16[256,2304]{1,0:T(8,128)(2,1)} %all-gather.6.cloned.1.call-done), channel_id=1, source_target_pairs={{0,1},{1,0},{2,3},{3,2},{4,5},{5,4},{6,7},{7,6},{8,9},{9,8},{10,11... | collective-permute-start | bytes 3538952 | tf_op jit(solution)/shard_map/ppermute | solution.py:16
  174.4 28.4 %collective-permute-start.14 = (bf16[128,2304]{1,0:T(8,128)(2,1)}, bf16[128,2304]{1,0:T(8,128)(2,1)}, u32[]{:S(2)}, u32[]{:S(2)}) collective-permute-start(bf16[128,2304]{1,0:T(8,128)(2,1)} %convolution_convert_fusion.1), channel_id=1, source_target_pairs={{0,4},{1,5},{2,6},{3,7},{4,0},{5,1},{6,2},{7,3},{8,12},{9,13},{10,... | collective-permute-start | bytes 1769480 | tf_op jit(solution)/shard_map/ppermute | solution.py:16
  174.9 27.9 %collective-permute-start.15 = (bf16[128,2304]{1,0:T(8,128)(2,1)}, bf16[128,2304]{1,0:T(8,128)(2,1)}, u32[]{:S(2)}, u32[]{:S(2)}) collective-permute-start(bf16[128,2304]{1,0:T(8,128)(2,1)} %convolution_convert_fusion), channel_id=1, source_target_pairs={{0,6},{1,7},{2,4},{3,5},{4,2},{5,3},{6,0},{7,1},{8,14},{9,15},{10,... | collective-permute-start | bytes 1769480 | tf_op jit(solution)/shard_map/ppermute | solution.py:16
  205.9 17.3 %collective-permute-start.18 = (bf16[128,2304]{1,0:T(8,128)(2,1)S(1)}, bf16[128,2304]{1,0:T(8,128)(2,1)S(1)}, u32[]{:S(2)}, u32[]{:S(2)}) collective-permute-start(bf16[128,2304]{1,0:T(8,128)(2,1)S(1)} %multiply_convert_fusion.refs_0_), channel_id=1, source_target_pairs={{0,6},{1,7},{2,4},{3,5},{4,2},{5,3},{6,0},{7,1},{8,14},{9,15},{10,... | collective-permute-start | bytes 1769480 | tf_op jit(solution)/shard_map/ppermute | solution.py:16
  207.1 27.0 %collective-permute-start.17 = (bf16[128,2304]{1,0:T(8,128)(2,1)S(1)}, bf16[128,2304]{1,0:T(8,128)(2,1)S(1)}, u32[]{:S(2)}, u32[]{:S(2)}) collective-permute-start(bf16[128,2304]{1,0:T(8,128)(2,1)S(1)} %multiply_convert_fusion.refs_0_), channel_id=1, source_target_pairs={{0,4},{1,5},{2,6},{3,7},{4,0},{5,1},{6,2},{7,3},{8,12},{9,13},{10,... | collective-permute-start | bytes 1769480 | tf_op jit(solution)/shard_map/ppermute | solution.py:16
  208.0 26.2 %collective-permute-start.16 = (bf16[128,2304]{1,0:T(8,128)(2,1)S(1)}, bf16[128,2304]{1,0:T(8,128)(2,1)S(1)}, u32[]{:S(2)}, u32[]{:S(2)}) collective-permute-start(bf16[128,2304]{1,0:T(8,128)(2,1)S(1)} %multiply_convert_fusion.refs_0_), channel_id=1, source_target_pairs={{0,2},{1,3},{2,0},{3,1},{4,6},{5,7},{6,4},{7,5},{8,10},{9,11},{10,... | collective-permute-start | bytes 1769480 | tf_op jit(solution)/shard_map/ppermute | solution.py:16
  235.9 16.8 %collective-permute-start.19 = (bf16[4,128,2304]{2,1,0:T(8,128)(2,1)}, bf16[4,128,2304]{2,1,0:T(8,128)(2,1)}, u32[]{:S(2)}, u32[]{:S(2)}) collective-permute-start(bf16[4,128,2304]{2,1,0:T(8,128)(2,1)} %pad_maximum_fusion.1), channel_id=1, source_target_pairs={{0,1},{1,0},{2,3},{3,2},{4,5},{5,4},{6,7},{7,6},{8,9},{9,8},{10,11... | collective-permute-start | bytes 7077896 | tf_op jit(solution)/shard_map/ppermute | solution.py:16
  292.5 20.9 %collective-permute-start.21 = (bf16[128,2304]{1,0:T(8,128)(2,1)}, bf16[128,2304]{1,0:T(8,128)(2,1)S(1)}, u32[]{:S(2)}, u32[]{:S(2)}) collective-permute-start(bf16[128,2304]{1,0:T(8,128)(2,1)} %get-tuple-element.126), channel_id=1, source_target_pairs={{0,2},{1,3},{2,0},{3,1},{4,6},{5,7},{6,4},{7,5},{8,10},{9,11},{10,... | collective-permute-start | bytes 1769480 | tf_op jit(solution)/shard_map/ppermute | solution.py:16
  293.1 27.8 %collective-permute-start.23 = (bf16[128,2304]{1,0:T(8,128)(2,1)}, bf16[128,2304]{1,0:T(8,128)(2,1)}, u32[]{:S(2)}, u32[]{:S(2)}) collective-permute-start(bf16[128,2304]{1,0:T(8,128)(2,1)} %get-tuple-element.127), channel_id=1, source_target_pairs={{0,6},{1,7},{2,4},{3,5},{4,2},{5,3},{6,0},{7,1},{8,14},{9,15},{10,... | collective-permute-start | bytes 1769480 | tf_op jit(solution)/shard_map/ppermute | solution.py:16
  294.6 27.7 %collective-permute-start.22 = (bf16[128,2304]{1,0:T(8,128)(2,1)}, bf16[128,2304]{1,0:T(8,128)(2,1)}, u32[]{:S(2)}, u32[]{:S(2)}) collective-permute-start(bf16[128,2304]{1,0:T(8,128)(2,1)} %get-tuple-element.128), channel_id=1, source_target_pairs={{0,4},{1,5},{2,6},{3,7},{4,0},{5,1},{6,2},{7,3},{8,12},{9,13},{10,... | collective-permute-start | bytes 1769480 | tf_op jit(solution)/shard_map/ppermute | solution.py:16
  (42 other events, 646.8 us)
Sparse Core Ops, SparseCore 0:
  44.8 31.0 all-gather.5
  77.4 67.2 all-gather.7
  176.5 62.1 all-gather.9

commit v4 on v3

--- a/solution.py
+++ b/solution.py
@@ -184,53 +184,56 @@
     return copy_rows(moves, [shape], [gathered, *blocks], me, "join_down")[0].reshape(-1, width)
 
 
-def expert(blocks, gate_w, up_w, down_w):
-    count = len(blocks)
-    rows, model = blocks[0].shape
+def expert(mine, other, gate_w, up_w, down_w):
+    rows, model = mine.shape
     units = gate_w.shape[1]
-
-    def kernel(*refs):
-        x_in, w_in = refs[:count], refs[count : count + 3]
-        outs = refs[count + 3 : 2 * count + 3]
-        x_all, w_all, x_sem, w_sem = refs[2 * count + 3 :]
+    block = min(512, rows)
+
+    def kernel(mine_in, other_in, gate_in, up_in, down_in, mine_out, other_out, x_all, w_all, sem):
         x_copies = [
-            pltpu.make_async_copy(x_in[j], x_all.at[pl.ds(j * rows, rows), :], x_sem.at[j])
-            for j in range(count)
+            pltpu.make_async_copy(mine_in, x_all.at[0], sem.at[0]),
+            pltpu.make_async_copy(other_in, x_all.at[1], sem.at[1]),
         ]
-        w_copies = [pltpu.make_async_copy(w_in[j], w_all.at[j], w_sem.at[j]) for j in range(3)]
-        for copy in x_copies + w_copies:
+        w_copies = [
+            pltpu.make_async_copy(w_in, w_all.at[j], sem.at[2 + j])
+            for j, w_in in enumerate((gate_in, up_in, down_in))
+        ]
+        for copy in [x_copies[1], w_copies[0], w_copies[1], w_copies[2], x_copies[0]]:
             copy.start()
-        for copy in x_copies:
-            copy.wait()
-        x = x_all[...]
-        w_copies[0].wait()
-        gate = jnp.dot(x, w_all[0], preferred_element_type=jnp.float32)
-        w_copies[1].wait()
-        up = jnp.dot(x, w_all[1], preferred_element_type=jnp.float32)
-        act = (gate / (1.0 + jnp.exp(-gate)) * up).astype(jnp.bfloat16)
-        w_copies[2].wait()
-        for j in range(count):
-            outs[j][...] = dot_nt(act[j * rows : (j + 1) * rows], w_all[2]).astype(jnp.bfloat16)
+        for step, side in enumerate((1, 0)):
+            out = (mine_out, other_out)[side]
+            x_copies[side].wait()
+            for first in range(0, rows, block):
+                x = x_all[side, first : first + block]
+                if step == 0 and first == 0:
+                    w_copies[0].wait()
+                gate = jnp.dot(x, w_all[0], preferred_element_type=jnp.float32)
+                if step == 0 and first == 0:
+                    w_copies[1].wait()
+                up = jnp.dot(x, w_all[1], preferred_element_type=jnp.float32)
+                act = (gate / (1.0 + jnp.exp(-gate)) * up).astype(jnp.bfloat16)
+                if step == 0 and first == 0:
+                    w_copies[2].wait()
+                out[first : first + block] = dot_nt(act, w_all[2]).astype(jnp.bfloat16)
 
     return pl.pallas_call(
         kernel,
-        out_shape=[jax.ShapeDtypeStruct((rows, model), jnp.bfloat16)] * count,
-        in_specs=[pl.BlockSpec(memory_space=pl.ANY)] * (count + 3),
-        out_specs=[pl.BlockSpec(memory_space=pltpu.VMEM)] * count,
+        out_shape=[jax.ShapeDtypeStruct((rows, model), jnp.bfloat16)] * 2,
+        in_specs=[pl.BlockSpec(memory_space=pl.ANY)] * 5,
+        out_specs=[pl.BlockSpec(memory_space=pltpu.VMEM)] * 2,
         scratch_shapes=[
-            pltpu.VMEM((count * rows, model), jnp.bfloat16),
+            pltpu.VMEM((2, rows, model), jnp.bfloat16),
             pltpu.VMEM((3, model, units), jnp.bfloat16),
-            pltpu.SemaphoreType.DMA((count,)),
-            pltpu.SemaphoreType.DMA((3,)),
+            pltpu.SemaphoreType.DMA((5,)),
         ],
         compiler_params=pltpu.CompilerParams(vmem_limit_bytes=56 * 1024 * 1024),
         cost_estimate=pl.CostEstimate(
-            flops=6 * count * rows * model * units,
+            flops=12 * rows * model * units,
             bytes_accessed=6 * model * units,
-            transcendentals=count * rows * units,
+            transcendentals=2 * rows * units,
         ),
         name="expert",
-    )(*blocks, gate_w, up_w, down_w)
+    )(mine, other, gate_w, up_w, down_w)
 
 
 def dot_nt(a, b):
@@ -389,15 +392,9 @@
     normed = rms_scale(tokens, attn_gain).astype(jnp.bfloat16)
     qkv_cols, normed, *parts = lax.optimization_barrier((qkv_cols, normed, *parts))
     qkv_all = lax.all_gather(qkv_cols, "dp", axis=0)
-    qkv_server = qkv_all.transpose(2, 1, 0, 3, 4).reshape(3, model, local_width)
-    server_qkv = qkv_server.transpose(1, 0, 2)
     down_parts = split_rows(trainer_down, size, plane, part_rows)
     down_cols = lax.all_to_all(down_parts, "tensor", 0, 0, tiled=True)
-    down_all = lax.all_gather(down_cols, "dp", axis=0)
-
     same_core = [normed] + [send(normed, size, 2 * j) for j in range(1, chips)]
-    out_cast, _ = lax.optimization_barrier((trainer_out.astype(jnp.bfloat16), same_core[1]))
-    server_out = lax.all_gather(out_cast, "dp", axis=0, tiled=True)
     other_core = send(jnp.stack(same_core), size, 1)
     blocks = []
     for j in range(chips):
@@ -410,25 +407,32 @@
     early = late[len(odd) :]
     late = [send(block, size, k) for block, k in zip(late, odd)]
 
-    out_pair = jnp.concatenate([server_out, send(server_out, size, 1)], axis=0)
-
     half_dim = HEAD_DIM // 2
     inv_freq = jnp.power(
         10000.0, jnp.arange(half_dim, dtype=jnp.float32) * (-2.0 / HEAD_DIM)
     )
     places = offset + jnp.arange(seq_len, dtype=jnp.int32)
-    angles = places.astype(jnp.float32)[:, None] * inv_freq[None, :]
-    repeats = local_width // half_dim
-    cosine = jnp.tile(jnp.cos(angles), (1, repeats))
-    sine_part = jnp.tile(jnp.sin(angles), (1, repeats))
+    angles = places.astype(jnp.float32)[:, None] * jnp.tile(inv_freq, local_width // half_dim)
+    cosine, sine_part = jnp.cos(angles), jnp.sin(angles)
+    out_cast = trainer_out.astype(jnp.bfloat16)
+    qkv_all, out_cast, piece, cosine, sine_part, down_cols, *early = lax.optimization_barrier(
+        (qkv_all, out_cast, piece, cosine, sine_part, down_cols, *early)
+    )
+    server_out = lax.all_gather(out_cast, "dp", axis=0, tiled=True)
+    qkv_server = qkv_all.transpose(2, 1, 0, 3, 4).reshape(3, model, local_width)
+    server_qkv = qkv_server.transpose(1, 0, 2)
     scalars = jnp.stack([length, core])
-    qkv_here, _, *early = lax.optimization_barrier((qkv_server, down_cols, *early))
     cache_pair, attended = attention(
-        piece, qkv_here, cosine, sine_part, scalars, rows_dev
-    )
+        piece, qkv_server, cosine, sine_part, scalars, rows_dev
+    )
+    attended, down_cols, server_out = lax.optimization_barrier(
+        (attended, down_cols, server_out)
+    )
+    down_all = lax.all_gather(down_cols, "dp", axis=0)
+    attended, *late = lax.optimization_barrier((attended, *late))
+    out_pair = jnp.concatenate([server_out, send(server_out, size, 1)], axis=0)
 
     att_pair = jnp.concatenate([attended[0], send(attended[1], size, 1)], axis=-1)
-    att_pair, *late = lax.optimization_barrier((att_pair, *late))
     att_pair = att_pair.reshape(chips, rows_dev, 2 * local_width)
     joined = [parts[0]] * size
     for block, k in zip(early + late, even + odd):
@@ -448,9 +452,11 @@
     normed_moe = rms_scale(middle.astype(jnp.float32), moe_gain).astype(jnp.bfloat16)
 
     moe_rows = [normed_moe] + [send(normed_moe, size, 2 * j) for j in range(1, chips)]
-    moe_other = send(jnp.stack(moe_rows), size, 1)
     gate, up = join_gate_up(joined, me, mat_rows)
     down = join_down(down_all, joined, me, mat_rows)
+    *moe_rows, gate, up, down = lax.optimization_barrier((*moe_rows, gate, up, down))
+    moe_mine = jnp.stack(moe_rows)
+    moe_other = send(moe_mine, size, 1)
 
     local_routes = lax.dynamic_slice_in_dim(routes[0], my_first, rows_dev, 0)
     local_valid = my_first + jnp.arange(rows_dev, dtype=jnp.int32) < length
@@ -466,12 +472,14 @@
     local_routed = jnp.any(local_routes == 0, axis=1)
     route_w = jnp.where(local_routed, jax.nn.sigmoid(logits[:, 0] - other_logit), 0.0)
 
-    sums_mine = expert(moe_rows, gate, up, down)
-    sums_other = expert([moe_other[j] for j in range(chips)], gate, up, down)
-    from_other = send(jnp.stack(sums_other), size, 1)
+    sums_mine, sums_other = expert(
+        moe_mine.reshape(-1, model), moe_other.reshape(-1, model), gate, up, down
+    )
+    from_other = send(sums_other, size, 1)
     sums = [
-        block.astype(jnp.float32) + from_other[j].astype(jnp.float32)
-        for j, block in enumerate(sums_mine)
+        sums_mine[j * rows_dev : (j + 1) * rows_dev].astype(jnp.float32)
+        + from_other[j * rows_dev : (j + 1) * rows_dev].astype(jnp.float32)
+        for j in range(chips)
     ]
     expert_sum = sums[0]
     for j in range(1, chips):

time: 341 us -> 305 us (0.89)
  local copies, waits for them, and re-layouts: 62.2 us -> 45.5 us
  Pallas kernels: 68.7 us -> 57 us
  waiting for transfers between devices: 130 us -> 126 us
    pallas_call x2 -> x1, Pallas kernels: 28.8 us -> 17.4 us  [expert(): pl.pallas_call(kernel, out_shape=[jax.ShapeDtypeStruct((rows, model), jnp...]
    all_gather x1, waiting for transfers between devices: 10.6 us -> 0.01 us  [shards(): qkv_all = lax.all_gather(qkv_cols, 'dp', axis=0)]
    all_gather x1, waiting for transfers between devices: 0.01 us -> 9.68 us  [shards(): server_out = lax.all_gather(out_cast, 'dp', axis=0, tiled=True)]
    another operation x4 -> x1, local copies, waits for them, and re-layouts: 8.14 us -> 0.01 us  [shards(): jnp.tile(inv_freq, local_width // half_dim)]
    squeeze x2 -> x1, local copies, waits for them, and re-layouts: 4.35 us -> 0.03 us  [shards(): attended[1]]
    sin x1, other arithmetic: 1.19 us -> 5.5 us  [shards(): cosine, sine_part = (jnp.cos(angles), jnp.sin(angles))]
    all_gather x1 -> x0, local copies, waits for them, and re-layouts: 4.19 us -> none  [shards(): qkv_all = lax.all_gather(qkv_cols, 'dp', axis=0)]
    ppermute x24, waiting for transfers between devices: 119 us -> 115 us  [send(): return lax.ppermute(block, 'tensor', swap_pairs(size, step))]
  transfers between devices with their start and end apart: 29 -> 29, of which waited for: 13 -> 15; matrix products, arithmetic and copies ran while one was open for 14% -> 14% of each run, Pallas kernels for 15% -> 12%
where the time goes in v4:
time: 305 us; the launch traced here: 301 us
  waiting for transfers between devices  126 us (41%)
  Pallas kernels  57 us (19%)
  local copies, waits for them, and re-layouts  45.5 us (15%)
  starting transfers between devices  31 us (10%)
  other arithmetic  19.1 us (6%)
  between operations  15.5 us (5%)
  matrix products  7.43 us (2%)
    ppermute x24, waiting for transfers between devices, send(): return lax.ppermute(block, 'tensor', swap_pairs(size, step))  115 us
    unnamed x75, local copies, waits for them, and re-layouts  38.7 us
    ppermute x24, starting transfers between devices, send(): return lax.ppermute(block, 'tensor', swap_pairs(size, step))  22 us
    pallas_call x1, Pallas kernels, expert(): pl.pallas_call(kernel, out_shape=[jax.ShapeDtypeStruct((rows, model), jnp...  17.4 us
    pallas_call x3, Pallas kernels, copy_rows(): pl.pallas_call(kernel, out_shape=[jax.ShapeDtypeStruct(shape, jnp.bfloat1...  13.6 us
    pallas_call x1, Pallas kernels, attention(): pl.pallas_call(kernel, out_shape=(jax.ShapeDtypeStruct((2, seq, width), j...  13.5 us
    all_gather x1, waiting for transfers between devices, shards(): server_out = lax.all_gather(out_cast, 'dp', axis=0, tiled=True)  9.68 us
    pallas_call x1, Pallas kernels, split_columns(): pl.pallas_call(kernel, out_shape=[jax.ShapeDtypeStruct(((2 * rows + tail)...  9.61 us
  transfers between devices with their start and end apart: 29, of which 15 were waited for; matrix products, arithmetic and copies ran while one was open for 14% of the time, Pallas kernels for 12%

profile of v4, /device:TPU:12, one launch (start us, length us, event | category | flops | bytes accessed | tf_op | source)
XLA Modules:
  0.0 301.3 jit_solution(7098079630437202075)
XLA Ops:
  9.7 4.2 %all-to-all-start = ((bf16[8,3,72,256]{3,2,1,0:T(8,128)(2,1)}), bf16[8,3,72,256]{3,2,1,0:T(8,128)(2,1)S(1)}, u32[]{:S(2)}, u32[]{:S(2)}) async-start(bf16[8,3,72,256]{3,2,1,0:T(8,128)(2,1)} %split_heads.1), calls=%async_computation | async-start | bytes 1769472 | tf_op jit(solution)/shard_map/all_to_all | solution.py:387
  15.4 9.6 %split_columns.1 = (bf16[38,16,720]{2,1,0:T(8,128)(2,1)S(1)}, bf16[38,16,720]{2,1,0:T(8,128)(2,1)S(1)}, bf16[38,16,720]{2,1,0:T(8,128)(2,1)}, bf16[38,16,720]{2,...) custom-call(s32[1]{0:T(128)} %bitcast.3.me_ref, ...), custom_call_target="tpu_custom_call" | custom-call | tf_op jit(solution)/shard_map/split_columns/pallas_call | solution.py:84
  33.5 13.6 %collective-permute-done.2 = bf16[128,2304]{1,0:T(8,128)(2,1)S(1)} collective-permute-done((bf16[128,2304]{1,0:T(8,128)(2,1)S(1)}, bf16[128,2304]{1,0:T(8,128)(2,1)S(1)}, u32[]{:S(2)}, u32[]{:S(2)}) %collective-permute-start.2) | collective-permute-done | bytes 589856 | tf_op jit(solution)/shard_map/ppermute | solution.py:16
  47.1 11.8 %collective-permute-done.1 = bf16[128,2304]{1,0:T(8,128)(2,1)S(1)} collective-permute-done((bf16[128,2304]{1,0:T(8,128)(2,1)S(1)}, bf16[128,2304]{1,0:T(8,128)(2,1)S(1)}, u32[]{:S(2)}, u32[]{:S(2)}) %collective-permute-start.1) | collective-permute-done | bytes 589856 | tf_op jit(solution)/shard_map/ppermute | solution.py:16
  68.5 4.6 %all-to-all-start.1 = ((bf16[8,64,720]{2,1,0:T(8,128)(2,1)}), bf16[8,64,720]{2,1,0:T(8,128)(2,1)}, u32[]{:S(2)}, u32[]{:S(2)}) async-start(bf16[8,64,720]{2,1,0:T(8,128)(2,1)} %copy-done.8), calls=%async_computation.1 | async-start | bytes 1572864 | tf_op jit(solution)/shard_map/all_to_all | solution.py:396
  75.7 5.5 %multiply_sine_fusion = (f32[1024,256]{1,0:T(8,128)}, f32[1024,256]{1,0:T(8,128)}) fusion(f32[256]{0:T(256)S(1)} %mul.84, f32[1024]{0:T(1024)S(1)} %add_convert_fusion.3), kind=kLoop, calls=%fused_computation.13 | loop fusion | flops 262144 | bytes 2102272 | tf_op jit(solution)/shard_map/sin | solution.py:416
  81.2 3.5 %collective-permute-done.4.refs_2_.refs_3_ = bf16[38,16,720]{2,1,0:T(8,128)(2,1)S(1)} collective-permute-done((bf16[38,16,720]{2,1,0:T(8,128)(2,1)}, bf16[38,16,720]{2,1,0:T(8,128)(2,1)S(1)}, u32[]{:S(2)}, u32[]{:S(2)}) %collective-permute-start.4) | collective-permute-done | bytes 875552 | tf_op jit(solution)/shard_map/ppermute | solution.py:16
  84.7 20.6 %collective-permute-done.5.refs_4_.refs_5_ = bf16[38,16,720]{2,1,0:T(8,128)(2,1)S(1)} collective-permute-done((bf16[38,16,720]{2,1,0:T(8,128)(2,1)}, bf16[38,16,720]{2,1,0:T(8,128)(2,1)S(1)}, u32[]{:S(2)}, u32[]{:S(2)}) %collective-permute-start.5) | collective-permute-done | bytes 875552 | tf_op jit(solution)/shard_map/ppermute | solution.py:16
  120.0 13.5 %attention.1 = (bf16[2,1024,256]{2,1,0:T(8,128)(2,1)}, bf16[2,512,256]{2,1,0:T(8,128)(2,1)S(1)}) custom-call(s32[2]{0:T(128)S(1)} %pad_add_fusion.s_ref, bf16[1024,2304]{1,0:T(8,128)(2,1)} %bitcast.98, bf16[3,2304,256]{2,1,0:T(8,128)(2,1)S(1)} %bitcast.99, f32[1024,256]{1,0:T(8,128)S(1)} %copy-done.16, f32[1024,256]{1,0:T(8,128)S(1)} %copy-done.15), custom_call_target="tpu_custom_call" | custom-call | flops 4697620480 | bytes 8257536 | tf_op jit(solution)/shard_map/attention/pallas_call | solution.py:318
  135.3 9.7 %all-gather.6.cloned.1.call-done = bf16[256,2304]{1,0:T(8,128)(2,1)} async-done(((bf16[64,2304]{1,0:T(8,128)(2,1)}), bf16[256,2304]{1,0:T(8,128)(2,1)}) %all-gather.6.cloned.1.call-update) | async-done | bytes 1179664 | tf_op jit(solution)/shard_map/all_gather | solution.py:421
  145.0 14.4 %collective-permute-done.9.refs_5_.refs_6_ = bf16[38,16,720]{2,1,0:T(8,128)(2,1)} collective-permute-done((bf16[38,16,720]{2,1,0:T(8,128)(2,1)}, bf16[38,16,720]{2,1,0:T(8,128)(2,1)}, u32[]{:S(2)}, u32[]{:S(2)}) %collective-permute-start.9) | collective-permute-done | bytes 875552 | tf_op jit(solution)/shard_map/ppermute | solution.py:16
  170.4 13.0 %collective-permute-done.13 = bf16[128,2304]{1,0:T(8,128)(2,1)} collective-permute-done((bf16[128,2304]{1,0:T(8,128)(2,1)}, bf16[128,2304]{1,0:T(8,128)(2,1)}, u32[]{:S(2)}, u32[]{:S(2)}) %collective-permute-start.13) | collective-permute-done | bytes 589856 | tf_op jit(solution)/shard_map/ppermute | solution.py:16
  183.4 11.8 %collective-permute-done.14 = bf16[128,2304]{1,0:T(8,128)(2,1)} collective-permute-done((bf16[128,2304]{1,0:T(8,128)(2,1)}, bf16[128,2304]{1,0:T(8,128)(2,1)}, u32[]{:S(2)}, u32[]{:S(2)}) %collective-permute-start.14) | collective-permute-done | bytes 589856 | tf_op jit(solution)/shard_map/ppermute | solution.py:16
  202.0 4.4 %join_gate_up.1 = (bf16[144,16,720]{2,1,0:T(8,128)(2,1)S(1)}, bf16[144,16,720]{2,1,0:T(8,128)(2,1)S(1)}) custom-call(s32[1]{0:T(128)} %bitcast.3.me_ref, bf16[38,16,720]{2,1,0:T(8,128)(2,1)S(1)} %get-tuple-element.96.refs_0_.refs_1_, bf16[38,16,720]{2,1,0:T(8,128)(2,1)} %collective-permute-done.7.refs_1_.refs_2_, ...), custom_call_target="tpu_custom_call" | custom-call | tf_op jit(solution)/shard_map/join_gate_up/pallas_call | solution.py:118
  211.9 6.7 %join_down.1 = bf16[144,16,720]{2,1,0:T(8,128)(2,1)S(1)} custom-call(s32[1]{0:T(128)} %bitcast.3.me_ref, bf16[4,8,4,16,720]{4,3,2,1,0:T(8,128)(2,1)S(1)} %bitcast.105, bf16[38,16,720]{2,1,0:T(8,128)(2,1)S(1)} %get-tuple-element.96.refs_0_.refs_1_, bf16[38,16,720]{2,1,0:T(8,128)(2,1)} %collective-permute-done.7.refs_1_.refs_2_, ...), custom_call_target="tpu_custom_call" | custom-call | tf_op jit(solution)/shard_map/join_down/pallas_call | solution.py:118
  218.6 7.9 %collective-permute-done.17 = bf16[128,2304]{1,0:T(8,128)(2,1)} collective-permute-done((bf16[128,2304]{1,0:T(8,128)(2,1)S(1)}, bf16[128,2304]{1,0:T(8,128)(2,1)}, u32[]{:S(2)}, u32[]{:S(2)}) %collective-permute-start.17) | collective-permute-done | bytes 589856 | tf_op jit(solution)/shard_map/ppermute | solution.py:16
  228.5 4.5 %collective-permute-done.19 = bf16[4,128,2304]{2,1,0:T(8,128)(2,1)S(1)} collective-permute-done((bf16[4,128,2304]{2,1,0:T(8,128)(2,1)S(1)}, bf16[4,128,2304]{2,1,0:T(8,128)(2,1)S(1)}, u32[]{:S(2)}, u32[]{:S(2)}) %collective-permute-start.19) | collective-permute-done | bytes 2359328 | tf_op jit(solution)/shard_map/ppermute | solution.py:16
  234.5 17.4 %expert.1 = (bf16[512,2304]{1,0:T(8,128)(2,1)}, bf16[512,2304]{1,0:T(8,128)(2,1)}) custom-call(bf16[512,2304]{1,0:T(8,128)(2,1)} %bitcast.126, bf16[512,2304]{1,0:T(8,128)(2,1)} %bitcast.128, bf16[2304,720]{1,0:T(8,128)(2,1)} %bitcast.101, bf16[2304,720]{1,0:T(8,128)(2,1)} %bitcast.103, bf16[2304,720]{1,0:T(8,128)(2,1)} %bitcast.94), custom_call_target="tpu_custom_call" | custom-call | flops 10192158720 | bytes 9953280 | tf_op jit(solution)/shard_map/expert/pallas_call | solution.py:219
  252.8 3.9 %collective-permute-done.20 = bf16[512,2304]{1,0:T(8,128)(2,1)S(1)} collective-permute-done((bf16[512,2304]{1,0:T(8,128)(2,1)}, bf16[512,2304]{1,0:T(8,128)(2,1)S(1)}, u32[]{:S(2)}, u32[]{:S(2)}) %collective-permute-start.20) | collective-permute-done | bytes 2359328 | tf_op jit(solution)/shard_map/ppermute | solution.py:16
  256.7 3.8 %add_convert_fusion.2 = (bf16[128,2304]{1,0:T(8,128)(2,1)}, bf16[128,2304]{1,0:T(8,128)(2,1)}, bf16[128,2304]{1,0:T(8,128)(2,1)}) fusion(bf16[512,2304]{1,0:T(8,128)(2,1)S(1)} %collective-permute-done.20, bf16[512,2304]{1,0:T(8,128)(2,1)} %get-tuple-element.114), kind=kLoop, calls=%fused_computation.21 | loop fusion | flops 3538944 | bytes 5308416 | tf_op jit(solution)/shard_map/convert_element_type | solution.py:486
  264.3 5.7 %copy.26 = bf16[2304,720]{0,1:T(8,128)(2,1)} copy(bf16[2304,720]{1,0:T(8,128)(2,1)} %bitcast.95) | data formatting | bytes 6635520
  270.0 5.6 %copy.25 = bf16[2304,720]{0,1:T(8,128)(2,1)} copy(bf16[2304,720]{1,0:T(8,128)(2,1)} %bitcast.104) | data formatting | bytes 6635520
  275.6 5.7 %copy.24 = bf16[2304,720]{0,1:T(8,128)(2,1)} copy(bf16[2304,720]{1,0:T(8,128)(2,1)} %bitcast.102) | data formatting | bytes 6635520
  281.4 7.8 %collective-permute-done.23 = bf16[128,2304]{1,0:T(8,128)(2,1)S(1)} collective-permute-done((bf16[128,2304]{1,0:T(8,128)(2,1)}, bf16[128,2304]{1,0:T(8,128)(2,1)S(1)}, u32[]{:S(2)}, u32[]{:S(2)}) %collective-permute-start.23) | collective-permute-done | bytes 589856 | tf_op jit(solution)/shard_map/ppermute | solution.py:16
  (150 shorter events, 76.4 us)
Async XLA Ops:
  9.7 19.2 %all-to-all-start = ((bf16[8,3,72,256]{3,2,1,0:T(8,128)(2,1)}), bf16[8,3,72,256]{3,2,1,0:T(8,128)(2,1)S(1)}, u32[]{:S(2)}, u32[]{:S(2)}) async-start(bf16[8,3,72,256]{3,2,1,0:T(8,128)(2,1)} %split_heads.1), calls=%async_computation | async-start | bytes 1769472 | tf_op jit(solution)/shard_map/all_to_all | solution.py:387
  14.0 99.1 %all-gather.8.cloned.1.call-start = ((), (), s32[]{:S(2)}) async-start(), calls=%async_computation.3 | async-start | bytes 4423680 | tf_op jit(solution)/shard_map/all_gather | solution.py:394
  29.9 17.2 %collective-permute-start.2 = (bf16[128,2304]{1,0:T(8,128)(2,1)S(1)}, bf16[128,2304]{1,0:T(8,128)(2,1)S(1)}, u32[]{:S(2)}, u32[]{:S(2)}) collective-permute-start(bf16[128,2304]{1,0:T(8,128)(2,1)S(1)} %fusion.7), channel_id=1, source_target_pairs={{0,6},{1,7},{2,4},{3,5},{4,2},{5,3},{6,0},{7,1},{8,14},{9,15},{10,... | collective-permute-start | bytes 1769480 | tf_op jit(solution)/shard_map/ppermute | solution.py:16
  31.5 27.5 %collective-permute-start.1 = (bf16[128,2304]{1,0:T(8,128)(2,1)S(1)}, bf16[128,2304]{1,0:T(8,128)(2,1)S(1)}, u32[]{:S(2)}, u32[]{:S(2)}) collective-permute-start(bf16[128,2304]{1,0:T(8,128)(2,1)S(1)} %fusion.7), channel_id=1, source_target_pairs={{0,4},{1,5},{2,6},{3,7},{4,0},{5,1},{6,2},{7,3},{8,12},{9,13},{10,... | collective-permute-start | bytes 1769480 | tf_op jit(solution)/shard_map/ppermute | solution.py:16
  32.9 26.0 %collective-permute-start = (bf16[128,2304]{1,0:T(8,128)(2,1)S(1)}, bf16[128,2304]{1,0:T(8,128)(2,1)S(1)}, u32[]{:S(2)}, u32[]{:S(2)}) collective-permute-start(bf16[128,2304]{1,0:T(8,128)(2,1)S(1)} %fusion.7), channel_id=1, source_target_pairs={{0,2},{1,3},{2,0},{3,1},{4,6},{5,7},{6,4},{7,5},{8,10},{9,11},{10,... | collective-permute-start | bytes 1769480 | tf_op jit(solution)/shard_map/ppermute | solution.py:16
  60.7 44.6 %collective-permute-start.3 = (bf16[4,128,2304]{2,1,0:T(8,128)(2,1)}, bf16[4,128,2304]{2,1,0:T(8,128)(2,1)}, u32[]{:S(2)}, u32[]{:S(2)}) collective-permute-start(bf16[4,128,2304]{2,1,0:T(8,128)(2,1)} %pad_maximum_fusion), channel_id=1, source_target_pairs={{0,1},{1,0},{2,3},{3,2},{4,5},{5,4},{6,7},{7,6},{8,9},{9,8},{10,11... | collective-permute-start | bytes 7077896 | tf_op jit(solution)/shard_map/ppermute | solution.py:16
  60.9 23.8 %collective-permute-start.4 = (bf16[38,16,720]{2,1,0:T(8,128)(2,1)}, bf16[38,16,720]{2,1,0:T(8,128)(2,1)S(1)}, u32[]{:S(2)}, u32[]{:S(2)}) collective-permute-start(bf16[38,16,720]{2,1,0:T(8,128)(2,1)} %get-tuple-element.76), channel_id=1, source_target_pairs={{0,2},{1,3},{2,0},{3,1},{4,6},{5,7},{6,4},{7,5},{8,10},{9,11},{10,... | collective-permute-start | bytes 2626568 | tf_op jit(solution)/shard_map/ppermute | solution.py:16
  61.5 43.8 %collective-permute-start.5 = (bf16[38,16,720]{2,1,0:T(8,128)(2,1)}, bf16[38,16,720]{2,1,0:T(8,128)(2,1)S(1)}, u32[]{:S(2)}, u32[]{:S(2)}) collective-permute-start(bf16[38,16,720]{2,1,0:T(8,128)(2,1)} %get-tuple-element.77), channel_id=1, source_target_pairs={{0,4},{1,5},{2,6},{3,7},{4,0},{5,1},{6,2},{7,3},{8,12},{9,13},{10,... | collective-permute-start | bytes 2626568 | tf_op jit(solution)/shard_map/ppermute | solution.py:16
  63.0 42.3 %collective-permute-start.6 = (bf16[38,16,720]{2,1,0:T(8,128)(2,1)}, bf16[38,16,720]{2,1,0:T(8,128)(2,1)}, u32[]{:S(2)}, u32[]{:S(2)}) collective-permute-start(bf16[38,16,720]{2,1,0:T(8,128)(2,1)} %get-tuple-element.78), channel_id=1, source_target_pairs={{0,6},{1,7},{2,4},{3,5},{4,2},{5,3},{6,0},{7,1},{8,14},{9,15},{10,... | collective-permute-start | bytes 2626568 | tf_op jit(solution)/shard_map/ppermute | solution.py:16
  68.5 44.5 %all-to-all-start.1 = ((bf16[8,64,720]{2,1,0:T(8,128)(2,1)}), bf16[8,64,720]{2,1,0:T(8,128)(2,1)}, u32[]{:S(2)}, u32[]{:S(2)}) async-start(bf16[8,64,720]{2,1,0:T(8,128)(2,1)} %copy-done.8), calls=%async_computation.1 | async-start | bytes 1572864 | tf_op jit(solution)/shard_map/all_to_all | solution.py:396
  73.1 71.8 %all-gather.6.cloned.1.call-start = ((), (), s32[]{:S(2)}) async-start(), calls=%async_computation.2 | async-start | bytes 1474560 | tf_op jit(solution)/shard_map/all_gather | solution.py:421
  113.1 96.9 %all-gather.10.cloned.1.call-start = ((), (), s32[]{:S(2)}) async-start(), calls=%async_computation.4 | async-start | bytes 3932160 | tf_op jit(solution)/shard_map/all_gather | solution.py:431
  114.0 31.0 %collective-permute-start.7 = (bf16[38,16,720]{2,1,0:T(8,128)(2,1)}, bf16[38,16,720]{2,1,0:T(8,128)(2,1)}, u32[]{:S(2)}, u32[]{:S(2)}) collective-permute-start(bf16[38,16,720]{2,1,0:T(8,128)(2,1)} %copy-done.20), channel_id=1, source_target_pairs={{0,1},{1,0},{2,3},{3,2},{4,5},{5,4},{6,7},{7,6},{8,9},{9,8},{10,11... | collective-permute-start | bytes 2626568 | tf_op jit(solution)/shard_map/ppermute | solution.py:16
  114.1 30.9 %collective-permute-start.8 = (bf16[38,16,720]{2,1,0:T(8,128)(2,1)}, bf16[38,16,720]{2,1,0:T(8,128)(2,1)}, u32[]{:S(2)}, u32[]{:S(2)}) collective-permute-start(bf16[38,16,720]{2,1,0:T(8,128)(2,1)} %copy-done.19), channel_id=1, source_target_pairs={{0,3},{1,2},{2,1},{3,0},{4,7},{5,6},{6,5},{7,4},{8,11},{9,10},{10,... | collective-permute-start | bytes 2626568 | tf_op jit(solution)/shard_map/ppermute | solution.py:16
  116.3 43.1 %collective-permute-start.9 = (bf16[38,16,720]{2,1,0:T(8,128)(2,1)}, bf16[38,16,720]{2,1,0:T(8,128)(2,1)}, u32[]{:S(2)}, u32[]{:S(2)}) collective-permute-start(bf16[38,16,720]{2,1,0:T(8,128)(2,1)} %copy-done.18), channel_id=1, source_target_pairs={{0,5},{1,4},{2,7},{3,6},{4,1},{5,0},{6,3},{7,2},{8,13},{9,12},{10,... | collective-permute-start | bytes 2626568 | tf_op jit(solution)/shard_map/ppermute | solution.py:16
  116.4 43.0 %collective-permute-start.10 = (bf16[38,16,720]{2,1,0:T(8,128)(2,1)}, bf16[38,16,720]{2,1,0:T(8,128)(2,1)}, u32[]{:S(2)}, u32[]{:S(2)}) collective-permute-start(bf16[38,16,720]{2,1,0:T(8,128)(2,1)} %copy-done.17), channel_id=1, source_target_pairs={{0,7},{1,6},{2,5},{3,4},{4,3},{5,2},{6,1},{7,0},{8,15},{9,14},{10,... | collective-permute-start | bytes 2626568 | tf_op jit(solution)/shard_map/ppermute | solution.py:16
  166.9 28.3 %collective-permute-start.14 = (bf16[128,2304]{1,0:T(8,128)(2,1)}, bf16[128,2304]{1,0:T(8,128)(2,1)}, u32[]{:S(2)}, u32[]{:S(2)}) collective-permute-start(bf16[128,2304]{1,0:T(8,128)(2,1)} %convolution_convert_fusion.1), channel_id=1, source_target_pairs={{0,4},{1,5},{2,6},{3,7},{4,0},{5,1},{6,2},{7,3},{8,12},{9,13},{10,... | collective-permute-start | bytes 1769480 | tf_op jit(solution)/shard_map/ppermute | solution.py:16
  168.3 26.9 %collective-permute-start.15 = (bf16[128,2304]{1,0:T(8,128)(2,1)}, bf16[128,2304]{1,0:T(8,128)(2,1)}, u32[]{:S(2)}, u32[]{:S(2)}) collective-permute-start(bf16[128,2304]{1,0:T(8,128)(2,1)} %convolution_convert_fusion), channel_id=1, source_target_pairs={{0,6},{1,7},{2,4},{3,5},{4,2},{5,3},{6,0},{7,1},{8,14},{9,15},{10,... | collective-permute-start | bytes 1769480 | tf_op jit(solution)/shard_map/ppermute | solution.py:16
  198.4 20.2 %collective-permute-start.18 = (bf16[128,2304]{1,0:T(8,128)(2,1)S(1)}, bf16[128,2304]{1,0:T(8,128)(2,1)}, u32[]{:S(2)}, u32[]{:S(2)}) collective-permute-start(bf16[128,2304]{1,0:T(8,128)(2,1)S(1)} %multiply_convert_fusion), channel_id=1, source_target_pairs={{0,6},{1,7},{2,4},{3,5},{4,2},{5,3},{6,0},{7,1},{8,14},{9,15},{10,... | collective-permute-start | bytes 1769480 | tf_op jit(solution)/shard_map/ppermute | solution.py:16
  200.1 26.5 %collective-permute-start.17 = (bf16[128,2304]{1,0:T(8,128)(2,1)S(1)}, bf16[128,2304]{1,0:T(8,128)(2,1)}, u32[]{:S(2)}, u32[]{:S(2)}) collective-permute-start(bf16[128,2304]{1,0:T(8,128)(2,1)S(1)} %multiply_convert_fusion), channel_id=1, source_target_pairs={{0,4},{1,5},{2,6},{3,7},{4,0},{5,1},{6,2},{7,3},{8,12},{9,13},{10,... | collective-permute-start | bytes 1769480 | tf_op jit(solution)/shard_map/ppermute | solution.py:16
  201.7 25.0 %collective-permute-start.16 = (bf16[128,2304]{1,0:T(8,128)(2,1)S(1)}, bf16[128,2304]{1,0:T(8,128)(2,1)}, u32[]{:S(2)}, u32[]{:S(2)}) collective-permute-start(bf16[128,2304]{1,0:T(8,128)(2,1)S(1)} %multiply_convert_fusion), channel_id=1, source_target_pairs={{0,2},{1,3},{2,0},{3,1},{4,6},{5,7},{6,4},{7,5},{8,10},{9,11},{10,... | collective-permute-start | bytes 1769480 | tf_op jit(solution)/shard_map/ppermute | solution.py:16
  260.5 20.9 %collective-permute-start.21 = (bf16[128,2304]{1,0:T(8,128)(2,1)}, bf16[128,2304]{1,0:T(8,128)(2,1)S(1)}, u32[]{:S(2)}, u32[]{:S(2)}) collective-permute-start(bf16[128,2304]{1,0:T(8,128)(2,1)} %get-tuple-element.135), channel_id=1, source_target_pairs={{0,2},{1,3},{2,0},{3,1},{4,6},{5,7},{6,4},{7,5},{8,10},{9,11},{10,... | collective-permute-start | bytes 1769480 | tf_op jit(solution)/shard_map/ppermute | solution.py:16
  261.2 28.0 %collective-permute-start.23 = (bf16[128,2304]{1,0:T(8,128)(2,1)}, bf16[128,2304]{1,0:T(8,128)(2,1)S(1)}, u32[]{:S(2)}, u32[]{:S(2)}) collective-permute-start(bf16[128,2304]{1,0:T(8,128)(2,1)} %get-tuple-element.136), channel_id=1, source_target_pairs={{0,6},{1,7},{2,4},{3,5},{4,2},{5,3},{6,0},{7,1},{8,14},{9,15},{10,... | collective-permute-start | bytes 1769480 | tf_op jit(solution)/shard_map/ppermute | solution.py:16
  262.9 27.8 %collective-permute-start.22 = (bf16[128,2304]{1,0:T(8,128)(2,1)}, bf16[128,2304]{1,0:T(8,128)(2,1)}, u32[]{:S(2)}, u32[]{:S(2)}) collective-permute-start(bf16[128,2304]{1,0:T(8,128)(2,1)} %get-tuple-element.137), channel_id=1, source_target_pairs={{0,4},{1,5},{2,6},{3,7},{4,0},{5,1},{6,2},{7,3},{8,12},{9,13},{10,... | collective-permute-start | bytes 1769480 | tf_op jit(solution)/shard_map/ppermute | solution.py:16
  (40 other events, 567.1 us)
Sparse Core Ops, SparseCore 0:
  30.1 68.6 all-gather.7
  113.2 31.6 all-gather.5
  146.5 60.8 all-gather.9

commit v5 on v4

--- a/solution.py
+++ b/solution.py
@@ -401,11 +401,12 @@
         blocks += [same_core[j], other_core[j]]
     piece = join_blocks(blocks, me)
 
-    even, odd = list(range(2, size, 2)), list(range(1, size, 2))
-    early = [send(parts[k], size, k) for k in even]
-    late = list(lax.optimization_barrier((*[parts[k] for k in odd], *early)))
-    early = late[len(odd) :]
-    late = [send(block, size, k) for block, k in zip(late, odd)]
+    first = [1, 2, 4][: size.bit_length() - 1]
+    rest = [k for k in range(3, size) if k not in first]
+    early = [send(parts[k], size, k) for k in first]
+    late = list(lax.optimization_barrier((*[parts[k] for k in rest], *early)))
+    early = late[len(rest) :]
+    late = [send(block, size, k) for block, k in zip(late, rest)]
 
     half_dim = HEAD_DIM // 2
     inv_freq = jnp.power(
@@ -414,28 +415,27 @@
     places = offset + jnp.arange(seq_len, dtype=jnp.int32)
     angles = places.astype(jnp.float32)[:, None] * jnp.tile(inv_freq, local_width // half_dim)
     cosine, sine_part = jnp.cos(angles), jnp.sin(angles)
-    out_cast = trainer_out.astype(jnp.bfloat16)
-    qkv_all, out_cast, piece, cosine, sine_part, down_cols, *early = lax.optimization_barrier(
-        (qkv_all, out_cast, piece, cosine, sine_part, down_cols, *early)
-    )
-    server_out = lax.all_gather(out_cast, "dp", axis=0, tiled=True)
+    server_out = lax.all_gather(trainer_out.astype(jnp.bfloat16), "dp", axis=0, tiled=True)
+    qkv_all, down_cols = lax.optimization_barrier((qkv_all, down_cols))
+    down_all = lax.all_gather(down_cols, "dp", axis=0)
+    qkv_all, piece, cosine, sine_part, *early = lax.optimization_barrier(
+        (qkv_all, piece, cosine, sine_part, *early)
+    )
     qkv_server = qkv_all.transpose(2, 1, 0, 3, 4).reshape(3, model, local_width)
     server_qkv = qkv_server.transpose(1, 0, 2)
     scalars = jnp.stack([length, core])
     cache_pair, attended = attention(
         piece, qkv_server, cosine, sine_part, scalars, rows_dev
     )
-    attended, down_cols, server_out = lax.optimization_barrier(
-        (attended, down_cols, server_out)
-    )
-    down_all = lax.all_gather(down_cols, "dp", axis=0)
-    attended, *late = lax.optimization_barrier((attended, *late))
+    half = len(late) // 2
+    attended, *late[:half] = lax.optimization_barrier((attended, *late[:half]))
     out_pair = jnp.concatenate([server_out, send(server_out, size, 1)], axis=0)
 
     att_pair = jnp.concatenate([attended[0], send(attended[1], size, 1)], axis=-1)
+    att_pair, *late[half:] = lax.optimization_barrier((att_pair, *late[half:]))
     att_pair = att_pair.reshape(chips, rows_dev, 2 * local_width)
     joined = [parts[0]] * size
-    for block, k in zip(early + late, even + odd):
+    for block, k in zip(early + late, first + rest):
         joined[k] = block
 
     def attn_part(j):

time: 305 us -> 295 us (0.967)
  waiting for transfers between devices: 126 us -> 110 us
    ppermute x24, waiting for transfers between devices: 115 us -> 101 us  [send(): return lax.ppermute(block, 'tensor', swap_pairs(size, step))]
    all_gather x1, waiting for transfers between devices: 9.68 us -> 0.01 us  [shards(): lax.all_gather(trainer_out.astype(jnp.bfloat16), 'dp', axis=0, tiled=True)]
    all_gather x1, waiting for transfers between devices: 0.01 us -> 8.7 us  [shards(): qkv_all = lax.all_gather(qkv_cols, 'dp', axis=0)]
    unnamed x75 -> x63, local copies, waits for them, and re-layouts: 38.7 us -> 39.9 us
  transfers between devices with their start and end apart: 29 -> 29, of which waited for: 15 -> 14; matrix products, arithmetic and copies ran while one was open for 14% -> 15% of each run, Pallas kernels for 12% -> 14%
where the time goes in v5:
time: 295 us; the launch traced here: 292 us
  waiting for transfers between devices  110 us (37%)
  Pallas kernels  58.9 us (20%)
  local copies, waits for them, and re-layouts  48.5 us (16%)
  starting transfers between devices  33.3 us (11%)
  other arithmetic  18.7 us (6%)
  between operations  15.4 us (5%)
  matrix products  7.42 us (3%)
    ppermute x24, waiting for transfers between devices, send(): return lax.ppermute(block, 'tensor', swap_pairs(size, step))  101 us
    unnamed x63, local copies, waits for them, and re-layouts  39.9 us
    ppermute x24, starting transfers between devices, send(): return lax.ppermute(block, 'tensor', swap_pairs(size, step))  23.6 us
    pallas_call x1, Pallas kernels, expert(): pl.pallas_call(kernel, out_shape=[jax.ShapeDtypeStruct((rows, model), jnp...  17.6 us
    pallas_call x3, Pallas kernels, copy_rows(): pl.pallas_call(kernel, out_shape=[jax.ShapeDtypeStruct(shape, jnp.bfloat1...  13.9 us
    pallas_call x1, Pallas kernels, attention(): pl.pallas_call(kernel, out_shape=(jax.ShapeDtypeStruct((2, seq, width), j...  13.6 us
    pallas_call x1, Pallas kernels, split_columns(): pl.pallas_call(kernel, out_shape=[jax.ShapeDtypeStruct(((2 * rows + tail)...  11 us
    all_gather x1, waiting for transfers between devices, shards(): qkv_all = lax.all_gather(qkv_cols, 'dp', axis=0)  8.7 us
  transfers between devices with their start and end apart: 29, of which 14 were waited for; matrix products, arithmetic and copies ran while one was open for 15% of the time, Pallas kernels for 14%

profile of v5, /device:TPU:12, one launch (start us, length us, event | category | flops | bytes accessed | tf_op | source)
XLA Modules:
  0.0 291.9 jit_solution(12975923340071645422)
XLA Ops:
  11.6 4.2 %all-to-all-start = ((bf16[8,3,72,256]{3,2,1,0:T(8,128)(2,1)}), bf16[8,3,72,256]{3,2,1,0:T(8,128)(2,1)S(1)}, u32[]{:S(2)}, u32[]{:S(2)}) async-start(bf16[8,3,72,256]{3,2,1,0:T(8,128)(2,1)} %split_heads.1), calls=%async_computation | async-start | bytes 1769472 | tf_op jit(solution)/shard_map/all_to_all | solution.py:387
  17.3 11.0 %split_columns.1 = (bf16[38,16,720]{2,1,0:T(8,128)(2,1)S(1)}, bf16[38,16,720]{2,1,0:T(8,128)(2,1)}, bf16[38,16,720]{2,1,0:T(8,128)(2,1)}, bf16[38,16,720]{2,1,0:...) custom-call(s32[1]{0:T(128)} %bitcast.3.me_ref, ...), custom_call_target="tpu_custom_call" | custom-call | tf_op jit(solution)/shard_map/split_columns/pallas_call | solution.py:84
  33.0 13.6 %collective-permute-done.2 = bf16[128,2304]{1,0:T(8,128)(2,1)S(1)} collective-permute-done((bf16[128,2304]{1,0:T(8,128)(2,1)S(1)}, bf16[128,2304]{1,0:T(8,128)(2,1)S(1)}, u32[]{:S(2)}, u32[]{:S(2)}) %collective-permute-start.2) | collective-permute-done | bytes 589856 | tf_op jit(solution)/shard_map/ppermute | solution.py:16
  46.6 10.7 %collective-permute-done = bf16[128,2304]{1,0:T(8,128)(2,1)S(1)} collective-permute-done((bf16[128,2304]{1,0:T(8,128)(2,1)S(1)}, bf16[128,2304]{1,0:T(8,128)(2,1)S(1)}, u32[]{:S(2)}, u32[]{:S(2)}) %collective-permute-start) | collective-permute-done | bytes 589856 | tf_op jit(solution)/shard_map/ppermute | solution.py:16
  66.9 5.4 %all-to-all-start.1 = ((bf16[8,64,720]{2,1,0:T(8,128)(2,1)}), bf16[8,64,720]{2,1,0:T(8,128)(2,1)}, u32[]{:S(2)}, u32[]{:S(2)}) async-start(bf16[8,64,720]{2,1,0:T(8,128)(2,1)} %copy-done.8), calls=%async_computation.1 | async-start | bytes 1572864 | tf_op jit(solution)/shard_map/all_to_all | solution.py:396
  73.9 5.5 %multiply_sine_fusion = (f32[1024,256]{1,0:T(8,128)}, f32[1024,256]{1,0:T(8,128)}) fusion(f32[256]{0:T(256)S(1)} %mul.84, f32[1024]{0:T(1024)S(1)} %add_convert_fusion.3), kind=kLoop, calls=%fused_computation.13 | loop fusion | flops 262144 | bytes 2102272 | tf_op jit(solution)/shard_map/sin | solution.py:417
  79.4 5.1 %collective-permute-done.5.refs_2_.refs_3_ = bf16[38,16,720]{2,1,0:T(8,128)(2,1)S(1)} collective-permute-done((bf16[38,16,720]{2,1,0:T(8,128)(2,1)}, bf16[38,16,720]{2,1,0:T(8,128)(2,1)S(1)}, u32[]{:S(2)}, u32[]{:S(2)}) %collective-permute-start.5) | collective-permute-done | bytes 875552 | tf_op jit(solution)/shard_map/ppermute | solution.py:16
  100.8 8.7 %all-gather.8.cloned.1.call-done = bf16[32,3,72,256]{3,2,1,0:T(8,128)(2,1)} async-done(((bf16[8,3,72,256]{3,2,1,0:T(8,128)(2,1)}), bf16[32,3,72,256]{3,2,1,0:T(8,128)(2,1)}) %all-gather.8.cloned.1.call-update) | async-done | bytes 3538960 | tf_op jit(solution)/shard_map/all_gather | solution.py:394
  109.5 4.2 %copy.23 = bf16[4,8,3,72,256]{4,3,0,1,2:T(8,128)(2,1)} copy(bf16[4,8,3,72,256]{4,3,2,1,0:T(8,128)(2,1)} %bitcast.118) | data formatting | bytes 7077888 | tf_op jit(solution)/shard_map/optimization_barrier | solution.py:421
  118.2 13.6 %attention.1 = (bf16[2,1024,256]{2,1,0:T(8,128)(2,1)}, bf16[2,512,256]{2,1,0:T(8,128)(2,1)S(1)}) custom-call(s32[2]{0:T(128)S(1)} %pad_add_fusion.s_ref, bf16[1024,2304]{1,0:T(8,128)(2,1)} %bitcast.99, bf16[3,2304,256]{2,1,0:T(8,128)(2,1)S(1)} %bitcast.101, f32[1024,256]{1,0:T(8,128)S(1)} %copy-done.16, f32[1024,256]{1,0:T(8,128)S(1)} %copy-done.15), custom_call_target="tpu_custom_call" | custom-call | flops 4697620480 | bytes 8257536 | tf_op jit(solution)/shard_map/attention/pallas_call | solution.py:318
  131.8 19.7 %collective-permute-done.8.refs_5_.refs_6_ = bf16[38,16,720]{2,1,0:T(8,128)(2,1)} collective-permute-done((bf16[38,16,720]{2,1,0:T(8,128)(2,1)}, bf16[38,16,720]{2,1,0:T(8,128)(2,1)}, u32[]{:S(2)}, u32[]{:S(2)}) %collective-permute-start.8) | collective-permute-done | bytes 875552 | tf_op jit(solution)/shard_map/ppermute | solution.py:16
  162.8 10.4 %collective-permute-done.13 = bf16[128,2304]{1,0:T(8,128)(2,1)} collective-permute-done((bf16[128,2304]{1,0:T(8,128)(2,1)}, bf16[128,2304]{1,0:T(8,128)(2,1)}, u32[]{:S(2)}, u32[]{:S(2)}) %collective-permute-start.13) | collective-permute-done | bytes 589856 | tf_op jit(solution)/shard_map/ppermute | solution.py:16
  173.2 13.3 %collective-permute-done.14 = bf16[128,2304]{1,0:T(8,128)(2,1)} collective-permute-done((bf16[128,2304]{1,0:T(8,128)(2,1)}, bf16[128,2304]{1,0:T(8,128)(2,1)}, u32[]{:S(2)}, u32[]{:S(2)}) %collective-permute-start.14) | collective-permute-done | bytes 589856 | tf_op jit(solution)/shard_map/ppermute | solution.py:16
  193.1 4.7 %join_gate_up.1 = (bf16[144,16,720]{2,1,0:T(8,128)(2,1)S(1)}, bf16[144,16,720]{2,1,0:T(8,128)(2,1)S(1)}) custom-call(s32[1]{0:T(128)} %bitcast.3.me_ref, bf16[38,16,720]{2,1,0:T(8,128)(2,1)S(1)} %get-tuple-element.92.refs_0_.refs_1_, bf16[38,16,720]{2,1,0:T(8,128)(2,1)S(1)} %collective-permute-done.4.refs_1_.refs_2_, ...), custom_call_target="tpu_custom_call" | custom-call | tf_op jit(solution)/shard_map/join_gate_up/pallas_call | solution.py:118
  203.2 6.8 %join_down.1 = bf16[144,16,720]{2,1,0:T(8,128)(2,1)S(1)} custom-call(s32[1]{0:T(128)} %bitcast.3.me_ref, bf16[4,8,4,16,720]{4,3,2,1,0:T(8,128)(2,1)S(1)} %bitcast.106, bf16[38,16,720]{2,1,0:T(8,128)(2,1)S(1)} %get-tuple-element.92.refs_0_.refs_1_, bf16[38,16,720]{2,1,0:T(8,128)(2,1)S(1)} %collective-permute-done.4.refs_1_.refs_2_, ...), custom_call_target="tpu_custom_call" | custom-call | tf_op jit(solution)/shard_map/join_down/pallas_call | solution.py:118
  210.0 7.7 %collective-permute-done.17 = bf16[128,2304]{1,0:T(8,128)(2,1)} collective-permute-done((bf16[128,2304]{1,0:T(8,128)(2,1)S(1)}, bf16[128,2304]{1,0:T(8,128)(2,1)}, u32[]{:S(2)}, u32[]{:S(2)}) %collective-permute-start.17) | collective-permute-done | bytes 589856 | tf_op jit(solution)/shard_map/ppermute | solution.py:16
  219.5 4.5 %collective-permute-done.19 = bf16[4,128,2304]{2,1,0:T(8,128)(2,1)S(1)} collective-permute-done((bf16[4,128,2304]{2,1,0:T(8,128)(2,1)S(1)}, bf16[4,128,2304]{2,1,0:T(8,128)(2,1)S(1)}, u32[]{:S(2)}, u32[]{:S(2)}) %collective-permute-start.19) | collective-permute-done | bytes 2359328 | tf_op jit(solution)/shard_map/ppermute | solution.py:16
  225.4 17.6 %expert.1 = (bf16[512,2304]{1,0:T(8,128)(2,1)}, bf16[512,2304]{1,0:T(8,128)(2,1)}) custom-call(bf16[512,2304]{1,0:T(8,128)(2,1)} %bitcast.119, bf16[512,2304]{1,0:T(8,128)(2,1)} %bitcast.125, bf16[2304,720]{1,0:T(8,128)(2,1)} %bitcast.104, bf16[2304,720]{1,0:T(8,128)(2,1)} %bitcast.102, bf16[2304,720]{1,0:T(8,128)(2,1)} %bitcast.95), custom_call_target="tpu_custom_call" | custom-call | flops 10192158720 | bytes 9953280 | tf_op jit(solution)/shard_map/expert/pallas_call | solution.py:219
  243.9 4.0 %collective-permute-done.20 = bf16[512,2304]{1,0:T(8,128)(2,1)} collective-permute-done((bf16[512,2304]{1,0:T(8,128)(2,1)}, bf16[512,2304]{1,0:T(8,128)(2,1)}, u32[]{:S(2)}, u32[]{:S(2)}) %collective-permute-start.20) | collective-permute-done | bytes 2359328 | tf_op jit(solution)/shard_map/ppermute | solution.py:16
  248.0 3.4 %add_convert_fusion.2 = (bf16[128,2304]{1,0:T(8,128)(2,1)}, bf16[128,2304]{1,0:T(8,128)(2,1)}, bf16[128,2304]{1,0:T(8,128)(2,1)}) fusion(bf16[512,2304]{1,0:T(8,128)(2,1)} %collective-permute-done.20, bf16[512,2304]{1,0:T(8,128)(2,1)} %get-tuple-element.110), kind=kLoop, calls=%fused_computation.21 | loop fusion | flops 3538944 | bytes 5308416 | tf_op jit(solution)/shard_map/convert_element_type | solution.py:486
  255.1 5.7 %copy.24 = bf16[2304,720]{0,1:T(8,128)(2,1)} copy(bf16[2304,720]{1,0:T(8,128)(2,1)} %bitcast.105) | data formatting | bytes 6635520
  260.8 5.6 %copy.25 = bf16[2304,720]{0,1:T(8,128)(2,1)} copy(bf16[2304,720]{1,0:T(8,128)(2,1)} %bitcast.103) | data formatting | bytes 6635520
  266.4 5.7 %copy.26 = bf16[2304,720]{0,1:T(8,128)(2,1)} copy(bf16[2304,720]{1,0:T(8,128)(2,1)} %bitcast.96) | data formatting | bytes 6635520
  272.2 7.6 %collective-permute-done.22 = bf16[128,2304]{1,0:T(8,128)(2,1)S(1)} collective-permute-done((bf16[128,2304]{1,0:T(8,128)(2,1)}, bf16[128,2304]{1,0:T(8,128)(2,1)S(1)}, u32[]{:S(2)}, u32[]{:S(2)}) %collective-permute-start.22) | collective-permute-done | bytes 589856 | tf_op jit(solution)/shard_map/ppermute | solution.py:16
  (139 shorter events, 77.7 us)
Async XLA Ops:
  7.2 84.0 %all-gather.6.cloned.1.call-start = ((), (), s32[]{:S(2)}) async-start(), calls=%async_computation.2 | async-start | bytes 1474560 | tf_op jit(solution)/shard_map/all_gather | solution.py:418
  15.9 93.6 %all-gather.8.cloned.1.call-start = ((), (), s32[]{:S(2)}) async-start(), calls=%async_computation.3 | async-start | bytes 4423680 | tf_op jit(solution)/shard_map/all_gather | solution.py:394
  29.4 17.2 %collective-permute-start.2 = (bf16[128,2304]{1,0:T(8,128)(2,1)S(1)}, bf16[128,2304]{1,0:T(8,128)(2,1)S(1)}, u32[]{:S(2)}, u32[]{:S(2)}) collective-permute-start(bf16[128,2304]{1,0:T(8,128)(2,1)S(1)} %fusion.7), channel_id=1, source_target_pairs={{0,6},{1,7},{2,4},{3,5},{4,2},{5,3},{6,0},{7,1},{8,14},{9,15},{10,... | collective-permute-start | bytes 1769480 | tf_op jit(solution)/shard_map/ppermute | solution.py:16
  31.0 26.4 %collective-permute-start = (bf16[128,2304]{1,0:T(8,128)(2,1)S(1)}, bf16[128,2304]{1,0:T(8,128)(2,1)S(1)}, u32[]{:S(2)}, u32[]{:S(2)}) collective-permute-start(bf16[128,2304]{1,0:T(8,128)(2,1)S(1)} %fusion.7), channel_id=1, source_target_pairs={{0,2},{1,3},{2,0},{3,1},{4,6},{5,7},{6,4},{7,5},{8,10},{9,11},{10,... | collective-permute-start | bytes 1769480 | tf_op jit(solution)/shard_map/ppermute | solution.py:16
  32.0 26.4 %collective-permute-start.1 = (bf16[128,2304]{1,0:T(8,128)(2,1)S(1)}, bf16[128,2304]{1,0:T(8,128)(2,1)S(1)}, u32[]{:S(2)}, u32[]{:S(2)}) collective-permute-start(bf16[128,2304]{1,0:T(8,128)(2,1)S(1)} %fusion.7), channel_id=1, source_target_pairs={{0,4},{1,5},{2,6},{3,7},{4,0},{5,1},{6,2},{7,3},{8,12},{9,13},{10,... | collective-permute-start | bytes 1769480 | tf_op jit(solution)/shard_map/ppermute | solution.py:16
  60.1 33.5 %collective-permute-start.3 = (bf16[4,128,2304]{2,1,0:T(8,128)(2,1)}, bf16[4,128,2304]{2,1,0:T(8,128)(2,1)}, u32[]{:S(2)}, u32[]{:S(2)}) collective-permute-start(bf16[4,128,2304]{2,1,0:T(8,128)(2,1)} %pad_maximum_fusion), channel_id=1, source_target_pairs={{0,1},{1,0},{2,3},{3,2},{4,5},{5,4},{6,7},{7,6},{8,9},{9,8},{10,11... | collective-permute-start | bytes 7077896 | tf_op jit(solution)/shard_map/ppermute | solution.py:16
  60.2 19.2 %collective-permute-start.4 = (bf16[38,16,720]{2,1,0:T(8,128)(2,1)}, bf16[38,16,720]{2,1,0:T(8,128)(2,1)S(1)}, u32[]{:S(2)}, u32[]{:S(2)}) collective-permute-start(bf16[38,16,720]{2,1,0:T(8,128)(2,1)} %get-tuple-element.75), channel_id=1, source_target_pairs={{0,1},{1,0},{2,3},{3,2},{4,5},{5,4},{6,7},{7,6},{8,9},{9,8},{10,11... | collective-permute-start | bytes 2626568 | tf_op jit(solution)/shard_map/ppermute | solution.py:16
  60.7 23.8 %collective-permute-start.5 = (bf16[38,16,720]{2,1,0:T(8,128)(2,1)}, bf16[38,16,720]{2,1,0:T(8,128)(2,1)S(1)}, u32[]{:S(2)}, u32[]{:S(2)}) collective-permute-start(bf16[38,16,720]{2,1,0:T(8,128)(2,1)} %get-tuple-element.76), channel_id=1, source_target_pairs={{0,2},{1,3},{2,0},{3,1},{4,6},{5,7},{6,4},{7,5},{8,10},{9,11},{10,... | collective-permute-start | bytes 2626568 | tf_op jit(solution)/shard_map/ppermute | solution.py:16
  62.1 25.3 %collective-permute-start.6 = (bf16[38,16,720]{2,1,0:T(8,128)(2,1)}, bf16[38,16,720]{2,1,0:T(8,128)(2,1)}, u32[]{:S(2)}, u32[]{:S(2)}) collective-permute-start(bf16[38,16,720]{2,1,0:T(8,128)(2,1)} %get-tuple-element.77), channel_id=1, source_target_pairs={{0,4},{1,5},{2,6},{3,7},{4,0},{5,1},{6,2},{7,3},{8,12},{9,13},{10,... | collective-permute-start | bytes 2626568 | tf_op jit(solution)/shard_map/ppermute | solution.py:16
  66.9 33.9 %all-to-all-start.1 = ((bf16[8,64,720]{2,1,0:T(8,128)(2,1)}), bf16[8,64,720]{2,1,0:T(8,128)(2,1)}, u32[]{:S(2)}, u32[]{:S(2)}) async-start(bf16[8,64,720]{2,1,0:T(8,128)(2,1)} %copy-done.8), calls=%async_computation.1 | async-start | bytes 1572864 | tf_op jit(solution)/shard_map/all_to_all | solution.py:396
  72.4 129.0 %all-gather.10.cloned.1.call-start = ((), (), s32[]{:S(2)}) async-start(), calls=%async_computation.4 | async-start | bytes 3932160 | tf_op jit(solution)/shard_map/all_gather | solution.py:420
  87.4 44.4 %collective-permute-start.7 = (bf16[38,16,720]{2,1,0:T(8,128)(2,1)}, bf16[38,16,720]{2,1,0:T(8,128)(2,1)}, u32[]{:S(2)}, u32[]{:S(2)}) collective-permute-start(bf16[38,16,720]{2,1,0:T(8,128)(2,1)} %get-tuple-element.86), channel_id=1, source_target_pairs={{0,3},{1,2},{2,1},{3,0},{4,7},{5,6},{6,5},{7,4},{8,11},{9,10},{10,... | collective-permute-start | bytes 2626568 | tf_op jit(solution)/shard_map/ppermute | solution.py:16
  87.4 64.1 %collective-permute-start.8 = (bf16[38,16,720]{2,1,0:T(8,128)(2,1)}, bf16[38,16,720]{2,1,0:T(8,128)(2,1)}, u32[]{:S(2)}, u32[]{:S(2)}) collective-permute-start(bf16[38,16,720]{2,1,0:T(8,128)(2,1)} %get-tuple-element.87), channel_id=1, source_target_pairs={{0,5},{1,4},{2,7},{3,6},{4,1},{5,0},{6,3},{7,2},{8,13},{9,12},{10,... | collective-permute-start | bytes 2626568 | tf_op jit(solution)/shard_map/ppermute | solution.py:16
  88.9 66.0 %collective-permute-start.10 = (bf16[38,16,720]{2,1,0:T(8,128)(2,1)}, bf16[38,16,720]{2,1,0:T(8,128)(2,1)}, u32[]{:S(2)}, u32[]{:S(2)}) collective-permute-start(bf16[38,16,720]{2,1,0:T(8,128)(2,1)} %get-tuple-element.89), channel_id=1, source_target_pairs={{0,6},{1,7},{2,4},{3,5},{4,2},{5,3},{6,0},{7,1},{8,14},{9,15},{10,... | collective-permute-start | bytes 2626568 | tf_op jit(solution)/shard_map/ppermute | solution.py:16
  90.6 64.4 %collective-permute-start.11 = (bf16[38,16,720]{2,1,0:T(8,128)(2,1)}, bf16[38,16,720]{2,1,0:T(8,128)(2,1)}, u32[]{:S(2)}, u32[]{:S(2)}) collective-permute-start(bf16[38,16,720]{2,1,0:T(8,128)(2,1)} %get-tuple-element.90), channel_id=1, source_target_pairs={{0,7},{1,6},{2,5},{3,4},{4,3},{5,2},{6,1},{7,0},{8,15},{9,14},{10,... | collective-permute-start | bytes 2626568 | tf_op jit(solution)/shard_map/ppermute | solution.py:16
  93.6 60.0 %collective-permute-start.12 = (bf16[256,2304]{1,0:T(8,128)(2,1)}, bf16[256,2304]{1,0:T(8,128)(2,1)}, u32[]{:S(2)}, u32[]{:S(2)}) collective-permute-start(bf16[256,2304]{1,0:T(8,128)(2,1)} %all-gather.6.cloned.1.call-done), channel_id=1, source_target_pairs={{0,1},{1,0},{2,3},{3,2},{4,5},{5,4},{6,7},{7,6},{8,9},{9,8},{10,11... | collective-permute-start | bytes 3538952 | tf_op jit(solution)/shard_map/ppermute | solution.py:16
  158.5 27.9 %collective-permute-start.14 = (bf16[128,2304]{1,0:T(8,128)(2,1)}, bf16[128,2304]{1,0:T(8,128)(2,1)}, u32[]{:S(2)}, u32[]{:S(2)}) collective-permute-start(bf16[128,2304]{1,0:T(8,128)(2,1)} %convolution_convert_fusion.1), channel_id=1, source_target_pairs={{0,4},{1,5},{2,6},{3,7},{4,0},{5,1},{6,2},{7,3},{8,12},{9,13},{10,... | collective-permute-start | bytes 1769480 | tf_op jit(solution)/shard_map/ppermute | solution.py:16
  160.0 26.5 %collective-permute-start.15 = (bf16[128,2304]{1,0:T(8,128)(2,1)}, bf16[128,2304]{1,0:T(8,128)(2,1)}, u32[]{:S(2)}, u32[]{:S(2)}) collective-permute-start(bf16[128,2304]{1,0:T(8,128)(2,1)} %convolution_convert_fusion), channel_id=1, source_target_pairs={{0,6},{1,7},{2,4},{3,5},{4,2},{5,3},{6,0},{7,1},{8,14},{9,15},{10,... | collective-permute-start | bytes 1769480 | tf_op jit(solution)/shard_map/ppermute | solution.py:16
  189.6 20.4 %collective-permute-start.16 = (bf16[128,2304]{1,0:T(8,128)(2,1)S(1)}, bf16[128,2304]{1,0:T(8,128)(2,1)}, u32[]{:S(2)}, u32[]{:S(2)}) collective-permute-start(bf16[128,2304]{1,0:T(8,128)(2,1)S(1)} %multiply_convert_fusion), channel_id=1, source_target_pairs={{0,2},{1,3},{2,0},{3,1},{4,6},{5,7},{6,4},{7,5},{8,10},{9,11},{10,... | collective-permute-start | bytes 1769480 | tf_op jit(solution)/shard_map/ppermute | solution.py:16
  191.1 26.6 %collective-permute-start.17 = (bf16[128,2304]{1,0:T(8,128)(2,1)S(1)}, bf16[128,2304]{1,0:T(8,128)(2,1)}, u32[]{:S(2)}, u32[]{:S(2)}) collective-permute-start(bf16[128,2304]{1,0:T(8,128)(2,1)S(1)} %multiply_convert_fusion), channel_id=1, source_target_pairs={{0,4},{1,5},{2,6},{3,7},{4,0},{5,1},{6,2},{7,3},{8,12},{9,13},{10,... | collective-permute-start | bytes 1769480 | tf_op jit(solution)/shard_map/ppermute | solution.py:16
  191.8 25.9 %collective-permute-start.18 = (bf16[128,2304]{1,0:T(8,128)(2,1)S(1)}, bf16[128,2304]{1,0:T(8,128)(2,1)}, u32[]{:S(2)}, u32[]{:S(2)}) collective-permute-start(bf16[128,2304]{1,0:T(8,128)(2,1)S(1)} %multiply_convert_fusion), channel_id=1, source_target_pairs={{0,6},{1,7},{2,4},{3,5},{4,2},{5,3},{6,0},{7,1},{8,14},{9,15},{10,... | collective-permute-start | bytes 1769480 | tf_op jit(solution)/shard_map/ppermute | solution.py:16
  251.3 20.8 %collective-permute-start.21 = (bf16[128,2304]{1,0:T(8,128)(2,1)}, bf16[128,2304]{1,0:T(8,128)(2,1)S(1)}, u32[]{:S(2)}, u32[]{:S(2)}) collective-permute-start(bf16[128,2304]{1,0:T(8,128)(2,1)} %get-tuple-element.131), channel_id=1, source_target_pairs={{0,2},{1,3},{2,0},{3,1},{4,6},{5,7},{6,4},{7,5},{8,10},{9,11},{10,... | collective-permute-start | bytes 1769480 | tf_op jit(solution)/shard_map/ppermute | solution.py:16
  251.9 27.9 %collective-permute-start.22 = (bf16[128,2304]{1,0:T(8,128)(2,1)}, bf16[128,2304]{1,0:T(8,128)(2,1)S(1)}, u32[]{:S(2)}, u32[]{:S(2)}) collective-permute-start(bf16[128,2304]{1,0:T(8,128)(2,1)} %get-tuple-element.133), channel_id=1, source_target_pairs={{0,4},{1,5},{2,6},{3,7},{4,0},{5,1},{6,2},{7,3},{8,12},{9,13},{10,... | collective-permute-start | bytes 1769480 | tf_op jit(solution)/shard_map/ppermute | solution.py:16
  253.1 26.8 %collective-permute-start.23 = (bf16[128,2304]{1,0:T(8,128)(2,1)}, bf16[128,2304]{1,0:T(8,128)(2,1)}, u32[]{:S(2)}, u32[]{:S(2)}) collective-permute-start(bf16[128,2304]{1,0:T(8,128)(2,1)} %get-tuple-element.132), channel_id=1, source_target_pairs={{0,6},{1,7},{2,4},{3,5},{4,2},{5,3},{6,0},{7,1},{8,14},{9,15},{10,... | collective-permute-start | bytes 1769480 | tf_op jit(solution)/shard_map/ppermute | solution.py:16
  (34 other events, 483.0 us)
Sparse Core Ops, SparseCore 0:
  9.6 31.0 all-gather.5
  42.2 67.2 all-gather.7
  113.8 62.1 all-gather.9

commit v6 on v5

--- a/solution.py
+++ b/solution.py
@@ -2,6 +2,7 @@
 import jax.numpy as jnp
 from jax import lax
 from jax.experimental import pallas as pl
+from jax.experimental.layout import Layout, with_layout_constraint
 from jax.experimental.pallas import tpu as pltpu
 from jax.sharding import PartitionSpec as P
 
@@ -14,6 +15,12 @@
 
 def send(block, size, step):
     return lax.ppermute(block, "tensor", swap_pairs(size, step))
+
+
+def add_up(total, blocks):
+    for block in blocks:
+        total = total + block.astype(jnp.float32)
+    return total
 
 
 def split_heads(qkv, parts):
@@ -187,34 +194,44 @@
 def expert(mine, other, gate_w, up_w, down_w):
     rows, model = mine.shape
     units = gate_w.shape[1]
-    block = min(512, rows)
+    block = min(512, 2 * rows)
 
     def kernel(mine_in, other_in, gate_in, up_in, down_in, mine_out, other_out, x_all, w_all, sem):
-        x_copies = [
-            pltpu.make_async_copy(mine_in, x_all.at[0], sem.at[0]),
-            pltpu.make_async_copy(other_in, x_all.at[1], sem.at[1]),
+        copies = [
+            pltpu.make_async_copy(source, place, sem.at[i])
+            for i, (source, place) in enumerate(
+                (
+                    (other_in, x_all.at[pl.ds(0, rows), :]),
+                    (mine_in, x_all.at[pl.ds(rows, rows), :]),
+                    (gate_in, w_all.at[0]),
+                    (up_in, w_all.at[1]),
+                    (down_in, w_all.at[2]),
+                )
+            )
         ]
-        w_copies = [
-            pltpu.make_async_copy(w_in, w_all.at[j], sem.at[2 + j])
-            for j, w_in in enumerate((gate_in, up_in, down_in))
-        ]
-        for copy in [x_copies[1], w_copies[0], w_copies[1], w_copies[2], x_copies[0]]:
+        for copy in copies:
             copy.start()
-        for step, side in enumerate((1, 0)):
-            out = (mine_out, other_out)[side]
-            x_copies[side].wait()
-            for first in range(0, rows, block):
-                x = x_all[side, first : first + block]
-                if step == 0 and first == 0:
-                    w_copies[0].wait()
-                gate = jnp.dot(x, w_all[0], preferred_element_type=jnp.float32)
-                if step == 0 and first == 0:
-                    w_copies[1].wait()
-                up = jnp.dot(x, w_all[1], preferred_element_type=jnp.float32)
-                act = (gate / (1.0 + jnp.exp(-gate)) * up).astype(jnp.bfloat16)
-                if step == 0 and first == 0:
-                    w_copies[2].wait()
-                out[first : first + block] = dot_nt(act, w_all[2]).astype(jnp.bfloat16)
+        copies[0].wait()
+        copies[1].wait()
+        for place in range(0, 2 * rows, block):
+            x = x_all[place : place + block]
+            if place == 0:
+                copies[2].wait()
+            gate = jnp.dot(x, w_all[0], preferred_element_type=jnp.float32)
+            if place == 0:
+                copies[3].wait()
+            up = jnp.dot(x, w_all[1], preferred_element_type=jnp.float32)
+            act = (gate / (1.0 + jnp.exp(-gate)) * up).astype(jnp.bfloat16)
+            if place == 0:
+                copies[4].wait()
+            res = dot_nt(act, w_all[2]).astype(jnp.bfloat16)
+            if block == 2 * rows:
+                other_out[...] = res[:rows]
+                mine_out[...] = res[rows:]
+            elif place < rows:
+                other_out[place : place + block] = res
+            else:
+                mine_out[place - rows : place - rows + block] = res
 
     return pl.pallas_call(
         kernel,
@@ -222,7 +239,7 @@
         in_specs=[pl.BlockSpec(memory_space=pl.ANY)] * 5,
         out_specs=[pl.BlockSpec(memory_space=pltpu.VMEM)] * 2,
         scratch_shapes=[
-            pltpu.VMEM((2, rows, model), jnp.bfloat16),
+            pltpu.VMEM((2 * rows, model), jnp.bfloat16),
             pltpu.VMEM((3, model, units), jnp.bfloat16),
             pltpu.SemaphoreType.DMA((5,)),
         ],
@@ -433,30 +450,46 @@
 
     att_pair = jnp.concatenate([attended[0], send(attended[1], size, 1)], axis=-1)
     att_pair, *late[half:] = lax.optimization_barrier((att_pair, *late[half:]))
-    att_pair = att_pair.reshape(chips, rows_dev, 2 * local_width)
     joined = [parts[0]] * size
     for block, k in zip(early + late, first + rest):
         joined[k] = block
 
-    def attn_part(j):
-        rows = lax.dynamic_index_in_dim(att_pair, chip ^ j, 0, keepdims=False)
-        return jnp.dot(rows, out_pair, preferred_element_type=jnp.float32)
-
-    partial = [attn_part(j) for j in range(chips)]
-    sent = [part.astype(jnp.bfloat16) for part in partial[1:]]
-    got = [send(block, size, 2 * j + 2) for j, block in enumerate(sent)]
-    attn_sum = partial[0]
-    for block in got:
-        attn_sum = attn_sum + block.astype(jnp.float32)
-    middle = (tokens + attn_sum).astype(jnp.bfloat16)
-    normed_moe = rms_scale(middle.astype(jnp.float32), moe_gain).astype(jnp.bfloat16)
-
-    moe_rows = [normed_moe] + [send(normed_moe, size, 2 * j) for j in range(1, chips)]
+    pieces = 2
+    rows = rows_dev // pieces
+    att_pair = att_pair.reshape(chips, pieces, rows, 2 * local_width)
+
+    def attn_part(j, h):
+        here = lax.dynamic_index_in_dim(att_pair, chip ^ j, 0, keepdims=False)[h]
+        return jnp.dot(here, out_pair, preferred_element_type=jnp.float32)
+
     gate, up = join_gate_up(joined, me, mat_rows)
-    down = join_down(down_all, joined, me, mat_rows)
-    *moe_rows, gate, up, down = lax.optimization_barrier((*moe_rows, gate, up, down))
-    moe_mine = jnp.stack(moe_rows)
-    moe_other = send(moe_mine, size, 1)
+    flipped = [gate, up]
+    middles, normed_moes, moe_rows = [], [], []
+    got = []
+    for h in range(pieces):
+        sent = [attn_part(j, h).astype(jnp.bfloat16) for j in range(1, chips)]
+        if h:
+            sent = list(lax.optimization_barrier((*sent, *got)))[: chips - 1]
+            flipped[h], *normed_moes = lax.optimization_barrier((flipped[h], *normed_moes))
+        got = [send(block, size, 2 * j + 2) for j, block in enumerate(sent)]
+        attn_sum = add_up(attn_part(0, h), got)
+        flipped[h] = with_layout_constraint(flipped[h], Layout((1, 0)))
+        attn_sum, flipped[h], *normed_moes = lax.optimization_barrier(
+            (attn_sum, flipped[h], *normed_moes)
+        )
+        middles.append((tokens[h * rows : (h + 1) * rows] + attn_sum).astype(jnp.bfloat16))
+        normed = rms_scale(middles[h].astype(jnp.float32), moe_gain).astype(jnp.bfloat16)
+        normed_moes.append(normed)
+        if h:
+            normed, *moe_rows[h - 1] = lax.optimization_barrier((normed, *moe_rows[h - 1]))
+        moe_rows.append([normed] + [send(normed, size, 2 * j) for j in range(1, chips)])
+        if h == 0:
+            down = join_down(down_all, joined, me, mat_rows)
+            *moe_rows[0], gate, up, down = lax.optimization_barrier(
+                (*moe_rows[0], gate, up, down)
+            )
+    middle = jnp.concatenate(middles, axis=0)
+    normed_moe = jnp.concatenate(normed_moes, axis=0)
 
     local_routes = lax.dynamic_slice_in_dim(routes[0], my_first, rows_dev, 0)
     local_valid = my_first + jnp.arange(rows_dev, dtype=jnp.int32) < length
@@ -472,29 +505,38 @@
     local_routed = jnp.any(local_routes == 0, axis=1)
     route_w = jnp.where(local_routed, jax.nn.sigmoid(logits[:, 0] - other_logit), 0.0)
 
-    sums_mine, sums_other = expert(
-        moe_mine.reshape(-1, model), moe_other.reshape(-1, model), gate, up, down
-    )
-    from_other = send(sums_other, size, 1)
-    sums = [
-        sums_mine[j * rows_dev : (j + 1) * rows_dev].astype(jnp.float32)
-        + from_other[j * rows_dev : (j + 1) * rows_dev].astype(jnp.float32)
-        for j in range(chips)
-    ]
-    expert_sum = sums[0]
-    for j in range(1, chips):
-        expert_sum = expert_sum + send(sums[j].astype(jnp.bfloat16), size, 2 * j).astype(
-            jnp.float32
+    expert_sums, back = [], []
+    for h in range(pieces):
+        moe_mine = jnp.stack(moe_rows[h])
+        moe_other = send(moe_mine, size, 1)
+        sums_mine, sums_other = expert(
+            moe_mine.reshape(-1, model), moe_other.reshape(-1, model), gate, up, down
         )
+        if h:
+            sums_other, *back = lax.optimization_barrier((sums_other, *back))
+            expert_sums.append(add_up(total, back))
+        else:
+            sums_other, *moe_rows[1] = lax.optimization_barrier((sums_other, *moe_rows[1]))
+        from_other = send(sums_other, size, 1)
+        sums = [
+            sums_mine[j * rows : (j + 1) * rows].astype(jnp.float32)
+            + from_other[j * rows : (j + 1) * rows].astype(jnp.float32)
+            for j in range(chips)
+        ]
+        total = sums[0]
+        sent = [block.astype(jnp.bfloat16) for block in sums[1:]]
+        back = [send(block, size, 2 * j + 2) for j, block in enumerate(sent)]
+    expert_sums.append(add_up(total, back))
+    down_late, _ = lax.optimization_barrier((down, sent[0]))
+    expert_sum = jnp.concatenate(expert_sums, axis=0)
     expert_sum = jnp.where(local_routed[:, None], expert_sum, 0.0)
     result = middle.astype(jnp.float32) + route_w[:, None] * expert_sum
     hidden_out = jnp.where(local_valid[:, None], result, 0.0).astype(jnp.bfloat16)[None]
     return (
         server_qkv,
         server_out,
-        gate,
-        up,
-        down,
+        *flipped,
+        down_late,
         hidden_out,
         cache_pair[None],
     )

time: 295 us -> 307 us (1.041)
  waiting for transfers between devices: 110 us -> 80.9 us
  matrix products: 7.42 us -> 23.9 us
  starting transfers between devices: 33.3 us -> 44.5 us
  Pallas kernels: 58.9 us -> 64.5 us
  other arithmetic: 18.7 us -> 23.9 us
    ppermute x24 -> x35, waiting for transfers between devices: 101 us -> 72.4 us  [send(): return lax.ppermute(block, 'tensor', swap_pairs(size, step))]
    dot_general x4 -> x8, matrix products: 7.18 us -> 22.7 us  [attn_part(): return jnp.dot(here, out_pair, preferred_element_type=jnp.float32)]
    ppermute x24 -> x35, starting transfers between devices: 23.6 us -> 35.3 us  [send(): return lax.ppermute(block, 'tensor', swap_pairs(size, step))]
    unnamed x63 -> x67, local copies, waits for them, and re-layouts: 39.9 us -> 28.6 us
    reshape x0 -> x1, local copies, waits for them, and re-layouts: none -> 5.65 us  [join_gate_up(): return [matrix.reshape(-1, width) for matrix in joined]]
    optimization_barrier x0 -> x1, local copies, waits for them, and re-layouts: none -> 5.64 us  [shards(): lax.optimization_barrier((flipped[h], *normed_moes))]
    pallas_call x1 -> x2, Pallas kernels: 17.6 us -> 22.7 us  [expert(): pl.pallas_call(kernel, out_shape=[jax.ShapeDtypeStruct((rows, model), jnp...]
    convert_element_type x2 -> x6, other arithmetic: 3.52 us -> 7.82 us  [the longest x2 2.62 us: shards(): sent = [block.astype(jnp.bfloat16) for block in sums[1:]]]
  transfers between devices with their start and end apart: 29 -> 40, of which waited for: 14 -> 13; matrix products, arithmetic and copies ran while one was open for 15% -> 22% of each run, Pallas kernels for 14% -> 21%
where the time goes in v6:
time: 307 us; the launch traced here: 302 us
  waiting for transfers between devices  80.9 us (26%)
  Pallas kernels  64.5 us (21%)
  local copies, waits for them, and re-layouts  48.6 us (16%)
  starting transfers between devices  44.5 us (14%)
  other arithmetic  23.9 us (8%)
  matrix products  23.9 us (8%)
  between operations  15.5 us (5%)
    ppermute x35, waiting for transfers between devices, send(): return lax.ppermute(block, 'tensor', swap_pairs(size, step))  72.4 us
    ppermute x35, starting transfers between devices, send(): return lax.ppermute(block, 'tensor', swap_pairs(size, step))  35.3 us
    unnamed x67, local copies, waits for them, and re-layouts  28.6 us
    dot_general x8, matrix products, attn_part(): return jnp.dot(here, out_pair, preferred_element_type=jnp.float32)  22.7 us
    pallas_call x2, Pallas kernels, expert(): pl.pallas_call(kernel, out_shape=[jax.ShapeDtypeStruct((rows, model), jnp...  22.7 us
    pallas_call x1, Pallas kernels, attention(): pl.pallas_call(kernel, out_shape=(jax.ShapeDtypeStruct((2, seq, width), j...  14.1 us
    pallas_call x3, Pallas kernels, copy_rows(): pl.pallas_call(kernel, out_shape=[jax.ShapeDtypeStruct(shape, jnp.bfloat1...  13.9 us
    pallas_call x1, Pallas kernels, split_columns(): pl.pallas_call(kernel, out_shape=[jax.ShapeDtypeStruct(((2 * rows + tail)...  11 us
  transfers between devices with their start and end apart: 40, of which 13 were waited for; matrix products, arithmetic and copies ran while one was open for 22% of the time, Pallas kernels for 21%

profile of v6, /device:TPU:12, one launch (start us, length us, event | category | flops | bytes accessed | tf_op | source)
XLA Modules:
  0.0 301.6 jit_solution(12919396019409784764)
XLA Ops:
  11.6 4.4 %all-to-all-start = ((bf16[8,3,72,256]{3,2,1,0:T(8,128)(2,1)}), bf16[8,3,72,256]{3,2,1,0:T(8,128)(2,1)S(1)}, u32[]{:S(2)}, u32[]{:S(2)}) async-start(bf16[8,3,72,256]{3,2,1,0:T(8,128)(2,1)} %split_heads.1), calls=%async_computation | async-start | bytes 1769472 | tf_op jit(solution)/shard_map/all_to_all | solution.py:404
  17.3 11.0 %split_columns.1 = (bf16[38,16,720]{2,1,0:T(8,128)(2,1)S(1)}, bf16[38,16,720]{2,1,0:T(8,128)(2,1)}, bf16[38,16,720]{2,1,0:T(8,128)(2,1)}, bf16[38,16,720]{2,1,0:...) custom-call(s32[1]{0:T(128)} %bitcast.2.me_ref, ...), custom_call_target="tpu_custom_call" | custom-call | tf_op jit(solution)/shard_map/split_columns/pallas_call | solution.py:91
  33.0 13.6 %collective-permute-done.2 = bf16[128,2304]{1,0:T(8,128)(2,1)S(1)} collective-permute-done((bf16[128,2304]{1,0:T(8,128)(2,1)S(1)}, bf16[128,2304]{1,0:T(8,128)(2,1)S(1)}, u32[]{:S(2)}, u32[]{:S(2)}) %collective-permute-start.2) | collective-permute-done | bytes 589856 | tf_op jit(solution)/shard_map/ppermute | solution.py:17
  46.6 11.8 %collective-permute-done.1 = bf16[128,2304]{1,0:T(8,128)(2,1)S(1)} collective-permute-done((bf16[128,2304]{1,0:T(8,128)(2,1)S(1)}, bf16[128,2304]{1,0:T(8,128)(2,1)S(1)}, u32[]{:S(2)}, u32[]{:S(2)}) %collective-permute-start.1) | collective-permute-done | bytes 589856 | tf_op jit(solution)/shard_map/ppermute | solution.py:17
  66.9 4.7 %all-to-all-start.1 = ((bf16[8,64,720]{2,1,0:T(8,128)(2,1)}), bf16[8,64,720]{2,1,0:T(8,128)(2,1)}, u32[]{:S(2)}, u32[]{:S(2)}) async-start(bf16[8,64,720]{2,1,0:T(8,128)(2,1)} %copy-done.8), calls=%async_computation.1 | async-start | bytes 1572864 | tf_op jit(solution)/shard_map/all_to_all | solution.py:413
  75.3 5.5 %multiply_sine_fusion = (f32[1024,256]{1,0:T(8,128)}, f32[1024,256]{1,0:T(8,128)}) fusion(f32[256]{0:T(256)S(1)} %mul.108, f32[1024]{0:T(1024)S(1)} %add_convert_fusion.6), kind=kLoop, calls=%fused_computation.13 | loop fusion | flops 262144 | bytes 2102272 | tf_op jit(solution)/shard_map/sin | solution.py:434
  80.8 3.7 %collective-permute-done.5.refs_2_.refs_3_ = bf16[38,16,720]{2,1,0:T(8,128)(2,1)S(1)} collective-permute-done((bf16[38,16,720]{2,1,0:T(8,128)(2,1)}, bf16[38,16,720]{2,1,0:T(8,128)(2,1)S(1)}, u32[]{:S(2)}, u32[]{:S(2)}) %collective-permute-start.5) | collective-permute-done | bytes 875552 | tf_op jit(solution)/shard_map/ppermute | solution.py:17
  85.7 3.4 %collective-permute-start.8 = (bf16[38,16,720]{2,1,0:T(8,128)(2,1)}, bf16[38,16,720]{2,1,0:T(8,128)(2,1)}, u32[]{:S(2)}, u32[]{:S(2)}) collective-permute-start(bf16[38,16,720]{2,1,0:T(8,128)(2,1)} %get-tuple-element.114), channel_id=1, source_target_pairs={{0,5},{1,4},{2,7},{3,6},{4,1},{5,0},{6,3},{7,2},{8,13},{9,12},{10,... | collective-permute-start | bytes 2626568 | tf_op jit(solution)/shard_map/ppermute | solution.py:17
  101.0 8.5 %all-gather.8.cloned.1.call-done = bf16[32,3,72,256]{3,2,1,0:T(8,128)(2,1)} async-done(((bf16[8,3,72,256]{3,2,1,0:T(8,128)(2,1)}), bf16[32,3,72,256]{3,2,1,0:T(8,128)(2,1)}) %all-gather.8.cloned.1.call-update) | async-done | bytes 3538960 | tf_op jit(solution)/shard_map/all_gather | solution.py:411
  112.1 14.1 %attention.1 = (bf16[2,1024,256]{2,1,0:T(8,128)(2,1)}, bf16[2,512,256]{2,1,0:T(8,128)(2,1)S(1)}) custom-call(s32[2]{0:T(128)S(1)} %pad_add_fusion.s_ref, bf16[1024,2304]{1,0:T(8,128)(2,1)} %bitcast.141, bf16[3,2304,256]{2,1,0:T(8,128)(2,1)S(1)} %bitcast.142, f32[1024,256]{1,0:T(8,128)S(1)} %copy-done.16, f32[1024,256]{1,0:T(8,128)S(1)} %copy-done.15), custom_call_target="tpu_custom_call" | custom-call | flops 4697620480 | bytes 8257536 | tf_op jit(solution)/shard_map/attention/pallas_call | solution.py:335
  126.3 25.3 %collective-permute-done.8.refs_5_.refs_6_ = bf16[38,16,720]{2,1,0:T(8,128)(2,1)} collective-permute-done((bf16[38,16,720]{2,1,0:T(8,128)(2,1)}, bf16[38,16,720]{2,1,0:T(8,128)(2,1)}, u32[]{:S(2)}, u32[]{:S(2)}) %collective-permute-start.8) | collective-permute-done | bytes 875552 | tf_op jit(solution)/shard_map/ppermute | solution.py:17
  157.4 3.1 %convolution_convert_fusion.5 = bf16[64,2304]{1,0:T(8,128)(2,1)} fusion(bf16[512,2304]{1,0:T(8,128)(2,1)} %constant_dynamic-update-slice_fusion, bf16[4,2,64,512]{3,2,1,0:T(8,128)(2,1)S(1)} %bitcast.164, s32[]{:T(128)S(6)} %select_n.72), kind=kOutput, calls=%fused_computation.11 | convolution fusion | flops 151142400 | bytes 2719748 | tf_op jit(solution)/shard_map/dot_general | solution.py:463
  165.3 3.1 %convolution_convert_fusion.3 = bf16[64,2304]{1,0:T(8,128)(2,1)} fusion(bf16[512,2304]{1,0:T(8,128)(2,1)} %constant_dynamic-update-slice_fusion, bf16[4,2,64,512]{3,2,1,0:T(8,128)(2,1)S(1)} %bitcast.166, s32[]{:T(128)S(6)} %select_n.74), kind=kOutput, calls=%fused_computation.9 | convolution fusion | flops 151142400 | bytes 2719748 | tf_op jit(solution)/shard_map/dot_general | solution.py:463
  172.9 2.9 convolution_convert_fusion.1
  175.9 4.7 %join_gate_up.1 = (bf16[144,16,720]{2,1,0:T(8,128)(2,1)S(1)}, bf16[144,16,720]{2,1,0:T(8,128)(2,1)S(1)}) custom-call(s32[1]{0:T(128)} %bitcast.2.me_ref, bf16[38,16,720]{2,1,0:T(8,128)(2,1)S(1)} %get-tuple-element.119.refs_0_.refs_1_, bf16[38,16,720]{2,1,0:T(8,128)(2,1)S(1)} %collective-permute-done.4.refs_1_.refs_2_, ...), custom_call_target="tpu_custom_call" | custom-call | tf_op jit(solution)/shard_map/join_gate_up/pallas_call | solution.py:125
  184.1 5.7 %copy.24 = bf16[2304,720]{0,1:T(8,128)(2,1)} copy(bf16[2304,720]{1,0:T(8,128)(2,1)} %bitcast.144) | data formatting | bytes 6635520 | tf_op jit(solution)/shard_map/reshape | solution.py:165
  189.8 2.9 convolution_convert_fusion.2
  203.0 5.6 %copy.25 = bf16[2304,720]{0,1:T(8,128)(2,1)} copy(bf16[2304,720]{1,0:T(8,128)(2,1)} %bitcast.147) | data formatting | bytes 6635520 | tf_op jit(solution)/shard_map/optimization_barrier | solution.py:473
  209.4 5.9 %collective-permute-done.17 = bf16[64,2304]{1,0:T(8,128)(2,1)} collective-permute-done((bf16[64,2304]{1,0:T(8,128)(2,1)}, bf16[64,2304]{1,0:T(8,128)(2,1)}, u32[]{:S(2)}, u32[]{:S(2)}) %collective-permute-start.17) | collective-permute-done | bytes 294944 | tf_op jit(solution)/shard_map/ppermute | solution.py:17
  220.7 6.8 %join_down.1 = bf16[144,16,720]{2,1,0:T(8,128)(2,1)S(1)} custom-call(s32[1]{0:T(128)} %bitcast.2.me_ref, bf16[4,8,4,16,720]{4,3,2,1,0:T(8,128)(2,1)S(1)} %bitcast.150, bf16[38,16,720]{2,1,0:T(8,128)(2,1)S(1)} %get-tuple-element.119.refs_0_.refs_1_, bf16[38,16,720]{2,1,0:T(8,128)(2,1)S(1)} %collective-permute-done.4.refs_1_.refs_2_, ...), custom_call_target="tpu_custom_call" | custom-call | tf_op jit(solution)/shard_map/join_down/pallas_call | solution.py:125
  235.5 11.3 %expert.2 = (bf16[256,2304]{1,0:T(8,128)(2,1)}, bf16[256,2304]{1,0:T(8,128)(2,1)}) custom-call(bf16[256,2304]{1,0:T(8,128)(2,1)} %bitcast.175, bf16[256,2304]{1,0:T(8,128)(2,1)} %bitcast.180, bf16[2304,720]{1,0:T(8,128)(2,1)} %bitcast.145, bf16[2304,720]{1,0:T(8,128)(2,1)} %bitcast.148, bf16[2304,720]{1,0:T(8,128)(2,1)} %bitcast.136), custom_call_target="tpu_custom_call" | custom-call | flops 5096079360 | bytes 9953280 | tf_op jit(solution)/shard_map/expert/pallas_call | solution.py:236
  255.7 11.4 %expert.3 = (bf16[256,2304]{1,0:T(8,128)(2,1)}, bf16[256,2304]{1,0:T(8,128)(2,1)}) custom-call(bf16[256,2304]{1,0:T(8,128)(2,1)} %bitcast.174, bf16[256,2304]{1,0:T(8,128)(2,1)} %bitcast.179, bf16[2304,720]{1,0:T(8,128)(2,1)} %bitcast.146, bf16[2304,720]{1,0:T(8,128)(2,1)} %bitcast.149, bf16[2304,720]{1,0:T(8,128)(2,1)} %bitcast.137), custom_call_target="tpu_custom_call" | custom-call | flops 5096079360 | bytes 9953280 | tf_op jit(solution)/shard_map/expert/pallas_call | solution.py:236
  277.7 5.6 %copy.26 = bf16[2304,720]{0,1:T(8,128)(2,1)} copy(bf16[2304,720]{1,0:T(8,128)(2,1)} %bitcast.138) | data formatting | bytes 6635520
  283.3 5.4 %collective-permute-done.33 = bf16[64,2304]{1,0:T(8,128)(2,1)} collective-permute-done((bf16[64,2304]{1,0:T(8,128)(2,1)}, bf16[64,2304]{1,0:T(8,128)(2,1)}, u32[]{:S(2)}, u32[]{:S(2)}) %collective-permute-start.33) | collective-permute-done | bytes 294944 | tf_op jit(solution)/shard_map/ppermute | solution.py:17
  (181 shorter events, 105.6 us)
Async XLA Ops:
  7.2 84.3 %all-gather.6.cloned.1.call-start = ((), (), s32[]{:S(2)}) async-start(), calls=%async_computation.2 | async-start | bytes 1474560 | tf_op jit(solution)/shard_map/all_gather | solution.py:435
  15.9 93.6 %all-gather.8.cloned.1.call-start = ((), (), s32[]{:S(2)}) async-start(), calls=%async_computation.3 | async-start | bytes 4423680 | tf_op jit(solution)/shard_map/all_gather | solution.py:411
  29.5 17.2 %collective-permute-start.2 = (bf16[128,2304]{1,0:T(8,128)(2,1)S(1)}, bf16[128,2304]{1,0:T(8,128)(2,1)S(1)}, u32[]{:S(2)}, u32[]{:S(2)}) collective-permute-start(bf16[128,2304]{1,0:T(8,128)(2,1)S(1)} %fusion.10), channel_id=1, source_target_pairs={{0,6},{1,7},{2,4},{3,5},{4,2},{5,3},{6,0},{7,1},{8,14},{9,15},{10,... | collective-permute-start | bytes 1769480 | tf_op jit(solution)/shard_map/ppermute | solution.py:17
  31.0 27.4 %collective-permute-start.1 = (bf16[128,2304]{1,0:T(8,128)(2,1)S(1)}, bf16[128,2304]{1,0:T(8,128)(2,1)S(1)}, u32[]{:S(2)}, u32[]{:S(2)}) collective-permute-start(bf16[128,2304]{1,0:T(8,128)(2,1)S(1)} %fusion.10), channel_id=1, source_target_pairs={{0,4},{1,5},{2,6},{3,7},{4,0},{5,1},{6,2},{7,3},{8,12},{9,13},{10,... | collective-permute-start | bytes 1769480 | tf_op jit(solution)/shard_map/ppermute | solution.py:17
  32.5 26.0 %collective-permute-start = (bf16[128,2304]{1,0:T(8,128)(2,1)S(1)}, bf16[128,2304]{1,0:T(8,128)(2,1)S(1)}, u32[]{:S(2)}, u32[]{:S(2)}) collective-permute-start(bf16[128,2304]{1,0:T(8,128)(2,1)S(1)} %fusion.10), channel_id=1, source_target_pairs={{0,2},{1,3},{2,0},{3,1},{4,6},{5,7},{6,4},{7,5},{8,10},{9,11},{10,... | collective-permute-start | bytes 1769480 | tf_op jit(solution)/shard_map/ppermute | solution.py:17
  60.2 33.6 %collective-permute-start.3 = (bf16[4,128,2304]{2,1,0:T(8,128)(2,1)}, bf16[4,128,2304]{2,1,0:T(8,128)(2,1)}, u32[]{:S(2)}, u32[]{:S(2)}) collective-permute-start(bf16[4,128,2304]{2,1,0:T(8,128)(2,1)} %pad_maximum_fusion), channel_id=1, source_target_pairs={{0,1},{1,0},{2,3},{3,2},{4,5},{5,4},{6,7},{7,6},{8,9},{9,8},{10,11... | collective-permute-start | bytes 7077896 | tf_op jit(solution)/shard_map/ppermute | solution.py:17
  60.3 20.5 %collective-permute-start.4 = (bf16[38,16,720]{2,1,0:T(8,128)(2,1)}, bf16[38,16,720]{2,1,0:T(8,128)(2,1)S(1)}, u32[]{:S(2)}, u32[]{:S(2)}) collective-permute-start(bf16[38,16,720]{2,1,0:T(8,128)(2,1)} %get-tuple-element.102), channel_id=1, source_target_pairs={{0,1},{1,0},{2,3},{3,2},{4,5},{5,4},{6,7},{7,6},{8,9},{9,8},{10,11... | collective-permute-start | bytes 2626568 | tf_op jit(solution)/shard_map/ppermute | solution.py:17
  60.8 23.8 %collective-permute-start.5 = (bf16[38,16,720]{2,1,0:T(8,128)(2,1)}, bf16[38,16,720]{2,1,0:T(8,128)(2,1)S(1)}, u32[]{:S(2)}, u32[]{:S(2)}) collective-permute-start(bf16[38,16,720]{2,1,0:T(8,128)(2,1)} %get-tuple-element.103), channel_id=1, source_target_pairs={{0,2},{1,3},{2,0},{3,1},{4,6},{5,7},{6,4},{7,5},{8,10},{9,11},{10,... | collective-permute-start | bytes 2626568 | tf_op jit(solution)/shard_map/ppermute | solution.py:17
  61.4 24.3 %collective-permute-start.6 = (bf16[38,16,720]{2,1,0:T(8,128)(2,1)}, bf16[38,16,720]{2,1,0:T(8,128)(2,1)}, u32[]{:S(2)}, u32[]{:S(2)}) collective-permute-start(bf16[38,16,720]{2,1,0:T(8,128)(2,1)} %get-tuple-element.104), channel_id=1, source_target_pairs={{0,4},{1,5},{2,6},{3,7},{4,0},{5,1},{6,2},{7,3},{8,12},{9,13},{10,... | collective-permute-start | bytes 2626568 | tf_op jit(solution)/shard_map/ppermute | solution.py:17
  66.9 34.1 %all-to-all-start.1 = ((bf16[8,64,720]{2,1,0:T(8,128)(2,1)}), bf16[8,64,720]{2,1,0:T(8,128)(2,1)}, u32[]{:S(2)}, u32[]{:S(2)}) async-start(bf16[8,64,720]{2,1,0:T(8,128)(2,1)} %copy-done.8), calls=%async_computation.1 | async-start | bytes 1572864 | tf_op jit(solution)/shard_map/all_to_all | solution.py:413
  71.7 147.1 %all-gather.10.cloned.1.call-start = ((), (), s32[]{:S(2)}) async-start(), calls=%async_computation.4 | async-start | bytes 3932160 | tf_op jit(solution)/shard_map/all_gather | solution.py:437
  85.7 40.5 %collective-permute-start.7 = (bf16[38,16,720]{2,1,0:T(8,128)(2,1)}, bf16[38,16,720]{2,1,0:T(8,128)(2,1)}, u32[]{:S(2)}, u32[]{:S(2)}) collective-permute-start(bf16[38,16,720]{2,1,0:T(8,128)(2,1)} %get-tuple-element.113), channel_id=1, source_target_pairs={{0,3},{1,2},{2,1},{3,0},{4,7},{5,6},{6,5},{7,4},{8,11},{9,10},{10,... | collective-permute-start | bytes 2626568 | tf_op jit(solution)/shard_map/ppermute | solution.py:17
  85.7 65.8 %collective-permute-start.8 = (bf16[38,16,720]{2,1,0:T(8,128)(2,1)}, bf16[38,16,720]{2,1,0:T(8,128)(2,1)}, u32[]{:S(2)}, u32[]{:S(2)}) collective-permute-start(bf16[38,16,720]{2,1,0:T(8,128)(2,1)} %get-tuple-element.114), channel_id=1, source_target_pairs={{0,5},{1,4},{2,7},{3,6},{4,1},{5,0},{6,3},{7,2},{8,13},{9,12},{10,... | collective-permute-start | bytes 2626568 | tf_op jit(solution)/shard_map/ppermute | solution.py:17
  89.2 68.2 %collective-permute-start.10 = (bf16[38,16,720]{2,1,0:T(8,128)(2,1)}, bf16[38,16,720]{2,1,0:T(8,128)(2,1)}, u32[]{:S(2)}, u32[]{:S(2)}) collective-permute-start(bf16[38,16,720]{2,1,0:T(8,128)(2,1)} %get-tuple-element.116), channel_id=1, source_target_pairs={{0,6},{1,7},{2,4},{3,5},{4,2},{5,3},{6,0},{7,1},{8,14},{9,15},{10,... | collective-permute-start | bytes 2626568 | tf_op jit(solution)/shard_map/ppermute | solution.py:17
  89.2 68.2 %collective-permute-start.11 = (bf16[38,16,720]{2,1,0:T(8,128)(2,1)}, bf16[38,16,720]{2,1,0:T(8,128)(2,1)}, u32[]{:S(2)}, u32[]{:S(2)}) collective-permute-start(bf16[38,16,720]{2,1,0:T(8,128)(2,1)} %get-tuple-element.117), channel_id=1, source_target_pairs={{0,7},{1,6},{2,5},{3,4},{4,3},{5,2},{6,1},{7,0},{8,15},{9,14},{10,... | collective-permute-start | bytes 2626568 | tf_op jit(solution)/shard_map/ppermute | solution.py:17
  93.8 59.4 %collective-permute-start.12 = (bf16[256,2304]{1,0:T(8,128)(2,1)}, bf16[256,2304]{1,0:T(8,128)(2,1)}, u32[]{:S(2)}, u32[]{:S(2)}) collective-permute-start(bf16[256,2304]{1,0:T(8,128)(2,1)} %all-gather.6.cloned.1.call-done), channel_id=1, source_target_pairs={{0,1},{1,0},{2,3},{3,2},{4,5},{5,4},{6,7},{7,6},{8,9},{9,8},{10,11... | collective-permute-start | bytes 3538952 | tf_op jit(solution)/shard_map/ppermute | solution.py:17
  160.5 32.2 %collective-permute-start.13 = (bf16[64,2304]{1,0:T(8,128)(2,1)}, bf16[64,2304]{1,0:T(8,128)(2,1)}, u32[]{:S(2)}, u32[]{:S(2)}) collective-permute-start(bf16[64,2304]{1,0:T(8,128)(2,1)} %convolution_convert_fusion.5), channel_id=1, source_target_pairs={{0,2},{1,3},{2,0},{3,1},{4,6},{5,7},{6,4},{7,5},{8,10},{9,11},{10,... | collective-permute-start | bytes 884744 | tf_op jit(solution)/shard_map/ppermute | solution.py:17
  164.8 27.9 %collective-permute-start.14 = (bf16[64,2304]{1,0:T(8,128)(2,1)}, bf16[64,2304]{1,0:T(8,128)(2,1)}, u32[]{:S(2)}, u32[]{:S(2)}) collective-permute-start(bf16[64,2304]{1,0:T(8,128)(2,1)} %convolution_convert_fusion.4), channel_id=1, source_target_pairs={{0,4},{1,5},{2,6},{3,7},{4,0},{5,1},{6,2},{7,3},{8,12},{9,13},{10,... | collective-permute-start | bytes 884744 | tf_op jit(solution)/shard_map/ppermute | solution.py:17
  168.4 24.3 %collective-permute-start.15 = (bf16[64,2304]{1,0:T(8,128)(2,1)}, bf16[64,2304]{1,0:T(8,128)(2,1)}, u32[]{:S(2)}, u32[]{:S(2)}) collective-permute-start(bf16[64,2304]{1,0:T(8,128)(2,1)} %convolution_convert_fusion.3), channel_id=1, source_target_pairs={{0,6},{1,7},{2,4},{3,5},{4,2},{5,3},{6,0},{7,1},{8,14},{9,15},{10,... | collective-permute-start | bytes 884744 | tf_op jit(solution)/shard_map/ppermute | solution.py:17
  194.0 21.3 %collective-permute-start.17 = (bf16[64,2304]{1,0:T(8,128)(2,1)}, bf16[64,2304]{1,0:T(8,128)(2,1)}, u32[]{:S(2)}, u32[]{:S(2)}) collective-permute-start(bf16[64,2304]{1,0:T(8,128)(2,1)} %convolution_convert_fusion.1), channel_id=1, source_target_pairs={{0,4},{1,5},{2,6},{3,7},{4,0},{5,1},{6,2},{7,3},{8,12},{9,13},{10,... | collective-permute-start | bytes 884744 | tf_op jit(solution)/shard_map/ppermute | solution.py:17
  194.6 20.7 %collective-permute-start.18 = (bf16[64,2304]{1,0:T(8,128)(2,1)}, bf16[64,2304]{1,0:T(8,128)(2,1)}, u32[]{:S(2)}, u32[]{:S(2)}) collective-permute-start(bf16[64,2304]{1,0:T(8,128)(2,1)} %convolution_convert_fusion), channel_id=1, source_target_pairs={{0,6},{1,7},{2,4},{3,5},{4,2},{5,3},{6,0},{7,1},{8,14},{9,15},{10,... | collective-permute-start | bytes 884744 | tf_op jit(solution)/shard_map/ppermute | solution.py:17
  200.3 29.0 %collective-permute-start.21 = (bf16[64,2304]{1,0:T(8,128)(2,1)}, bf16[64,2304]{1,0:T(8,128)(2,1)}, u32[]{:S(2)}, u32[]{:S(2)}) collective-permute-start(bf16[64,2304]{1,0:T(8,128)(2,1)} %fusion.13), channel_id=1, source_target_pairs={{0,6},{1,7},{2,4},{3,5},{4,2},{5,3},{6,0},{7,1},{8,14},{9,15},{10,... | collective-permute-start | bytes 884744 | tf_op jit(solution)/shard_map/ppermute | solution.py:17
  201.6 27.8 %collective-permute-start.20 = (bf16[64,2304]{1,0:T(8,128)(2,1)}, bf16[64,2304]{1,0:T(8,128)(2,1)}, u32[]{:S(2)}, u32[]{:S(2)}) collective-permute-start(bf16[64,2304]{1,0:T(8,128)(2,1)} %fusion.13), channel_id=1, source_target_pairs={{0,4},{1,5},{2,6},{3,7},{4,0},{5,1},{6,2},{7,3},{8,12},{9,13},{10,... | collective-permute-start | bytes 884744 | tf_op jit(solution)/shard_map/ppermute | solution.py:17
  208.6 20.7 %collective-permute-start.19 = (bf16[64,2304]{1,0:T(8,128)(2,1)}, bf16[64,2304]{1,0:T(8,128)(2,1)}, u32[]{:S(2)}, u32[]{:S(2)}) collective-permute-start(bf16[64,2304]{1,0:T(8,128)(2,1)} %fusion.13), channel_id=1, source_target_pairs={{0,2},{1,3},{2,0},{3,1},{4,6},{5,7},{6,4},{7,5},{8,10},{9,11},{10,... | collective-permute-start | bytes 884744 | tf_op jit(solution)/shard_map/ppermute | solution.py:17
  (48 other events, 593.0 us)
Sparse Core Ops, SparseCore 0:
  9.6 31.0 all-gather.5
  42.2 67.2 all-gather.7
  155.7 62.2 all-gather.9

commit v7 on v6

--- a/solution.py
+++ b/solution.py
@@ -189,6 +189,57 @@
 
     shape = (count * groups, 16, width)
     return copy_rows(moves, [shape], [gathered, *blocks], me, "join_down")[0].reshape(-1, width)
+
+
+def project(mine, other, own_w, other_w, chip, rows_dev, pieces):
+    total, width = mine.shape
+    chips = total // rows_dev
+    model = own_w.shape[1]
+    rows = rows_dev // pieces
+
+    def kernel(chip_ref, mine_ref, other_ref, own_ref, other_w_ref, *outs):
+        def ordered(ref):
+            places = [
+                pl.multiple_of((chip_ref[0] ^ j) * rows_dev, rows_dev) for j in range(chips)
+            ]
+            return jnp.concatenate([ref[pl.ds(place, rows_dev), :] for place in places], axis=0)
+
+        res = jnp.dot(ordered(mine_ref), own_ref[...], preferred_element_type=jnp.float32)
+        res = res + jnp.dot(
+            ordered(other_ref), other_w_ref[...], preferred_element_type=jnp.float32
+        )
+        for h in range(pieces):
+            outs[h][...] = res[h * rows : (h + 1) * rows]
+            for j in range(1, chips):
+                first = j * rows_dev + h * rows
+                outs[pieces + h * (chips - 1) + j - 1][...] = res[first : first + rows].astype(
+                    jnp.bfloat16
+                )
+        outs[-1][...] = own_ref[...]
+
+    whole = [
+        pl.BlockSpec(shape, lambda i, c: (0, 0))
+        for shape in (mine.shape, other.shape, own_w.shape, other_w.shape)
+    ]
+    sent = [(rows, model)] * (pieces * (chips - 1))
+    res = pl.pallas_call(
+        kernel,
+        out_shape=[jax.ShapeDtypeStruct((rows, model), jnp.float32)] * pieces
+        + [jax.ShapeDtypeStruct(shape, jnp.bfloat16) for shape in sent + [own_w.shape]],
+        grid_spec=pltpu.PrefetchScalarGridSpec(
+            num_scalar_prefetch=1,
+            grid=(1,),
+            in_specs=whole,
+            out_specs=[
+                pl.BlockSpec(shape, lambda i, c: (0, 0))
+                for shape in [(rows, model)] * pieces + sent + [own_w.shape]
+            ],
+        ),
+        compiler_params=pltpu.CompilerParams(vmem_limit_bytes=56 * 1024 * 1024),
+        name="project",
+    )(chip.reshape(1), mine, other, own_w, other_w)
+    sent = [res[pieces + h * (chips - 1) :][: chips - 1] for h in range(pieces)]
+    return res[:pieces], sent, res[-1]
 
 
 def expert(mine, other, gate_w, up_w, down_w):
@@ -446,48 +497,45 @@
     )
     half = len(late) // 2
     attended, *late[:half] = lax.optimization_barrier((attended, *late[:half]))
-    out_pair = jnp.concatenate([server_out, send(server_out, size, 1)], axis=0)
-
-    att_pair = jnp.concatenate([attended[0], send(attended[1], size, 1)], axis=-1)
-    att_pair, *late[half:] = lax.optimization_barrier((att_pair, *late[half:]))
+    pieces = 2
+    rows = rows_dev // pieces
+    out_other = send(server_out, size, 1)
+    att_other = send(attended[1], size, 1)
+    att_other, *late[half:] = lax.optimization_barrier((att_other, *late[half:]))
+    own_part, partial, server_out = project(
+        attended[0], att_other, server_out, out_other, chip, rows_dev, pieces
+    )
     joined = [parts[0]] * size
     for block, k in zip(early + late, first + rest):
         joined[k] = block
 
-    pieces = 2
-    rows = rows_dev // pieces
-    att_pair = att_pair.reshape(chips, pieces, rows, 2 * local_width)
-
-    def attn_part(j, h):
-        here = lax.dynamic_index_in_dim(att_pair, chip ^ j, 0, keepdims=False)[h]
-        return jnp.dot(here, out_pair, preferred_element_type=jnp.float32)
-
     gate, up = join_gate_up(joined, me, mat_rows)
+    down = join_down(down_all, joined, me, mat_rows)
     flipped = [gate, up]
     middles, normed_moes, moe_rows = [], [], []
     got = []
     for h in range(pieces):
-        sent = [attn_part(j, h).astype(jnp.bfloat16) for j in range(1, chips)]
+        sent = partial[h]
         if h:
             sent = list(lax.optimization_barrier((*sent, *got)))[: chips - 1]
-            flipped[h], *normed_moes = lax.optimization_barrier((flipped[h], *normed_moes))
         got = [send(block, size, 2 * j + 2) for j, block in enumerate(sent)]
-        attn_sum = add_up(attn_part(0, h), got)
-        flipped[h] = with_layout_constraint(flipped[h], Layout((1, 0)))
-        attn_sum, flipped[h], *normed_moes = lax.optimization_barrier(
-            (attn_sum, flipped[h], *normed_moes)
-        )
+        if h:
+            *got, down, normed_moes[0] = lax.optimization_barrier((*got, down, normed_moes[0]))
+        attn_sum = add_up(own_part[h], got)
+        if h:
+            flipped[1], *normed_moes = lax.optimization_barrier((flipped[1], *normed_moes))
+            flipped[1] = with_layout_constraint(flipped[1], Layout((1, 0)))
+            *moe_rows[0], flipped[1] = lax.optimization_barrier((*moe_rows[0], flipped[1]))
+        else:
+            flipped[0] = with_layout_constraint(flipped[0], Layout((1, 0)))
+            attn_sum, flipped[0] = lax.optimization_barrier((attn_sum, flipped[0]))
         middles.append((tokens[h * rows : (h + 1) * rows] + attn_sum).astype(jnp.bfloat16))
         normed = rms_scale(middles[h].astype(jnp.float32), moe_gain).astype(jnp.bfloat16)
         normed_moes.append(normed)
         if h:
-            normed, *moe_rows[h - 1] = lax.optimization_barrier((normed, *moe_rows[h - 1]))
+            normed, *moe_rows[0] = lax.optimization_barrier((normed, *moe_rows[0]))
         moe_rows.append([normed] + [send(normed, size, 2 * j) for j in range(1, chips)])
-        if h == 0:
-            down = join_down(down_all, joined, me, mat_rows)
-            *moe_rows[0], gate, up, down = lax.optimization_barrier(
-                (*moe_rows[0], gate, up, down)
-            )
+    *moe_rows[0], gate, up, down = lax.optimization_barrier((*moe_rows[0], gate, up, down))
     middle = jnp.concatenate(middles, axis=0)
     normed_moe = jnp.concatenate(normed_moes, axis=0)
 

time: 307 us -> 300 us (0.977)
  waiting for transfers between devices: 80.9 us -> 106 us
  matrix products: 23.9 us -> 0.24 us
  local copies, waits for them, and re-layouts: 48.6 us -> 41.2 us
  Pallas kernels: 64.5 us -> 69.1 us
  starting transfers between devices: 44.5 us -> 41.3 us
    all_gather x1, waiting for transfers between devices: 0.01 us -> 22.8 us  [shards(): lax.all_gather(trainer_out.astype(jnp.bfloat16), 'dp', axis=0, tiled=True)]
    dot_general x8 -> x0, matrix products: 22.7 us -> none  [attn_part(): return jnp.dot(here, out_pair, preferred_element_type=jnp.float32)]
    ppermute x35, waiting for transfers between devices: 72.4 us -> 57.9 us  [send(): return lax.ppermute(block, 'tensor', swap_pairs(size, step))]
    all_gather x1, waiting for transfers between devices: 8.47 us -> 16.7 us  [shards(): qkv_all = lax.all_gather(qkv_cols, 'dp', axis=0)]
    all_to_all x1, waiting for transfers between devices: 0.01 us -> 8.17 us  [shards(): down_cols = lax.all_to_all(down_parts, 'tensor', 0, 0, tiled=True)]
    pallas_call x0 -> x1, Pallas kernels: none -> 5.12 us  [project(): pl.pallas_call(kernel, out_shape=[jax.ShapeDtypeStruct((rows, model), jnp...]
    unnamed x67 -> x75, local copies, waits for them, and re-layouts: 28.6 us -> 25.6 us
  transfers between devices with their start and end apart: 40 -> 40, of which waited for: 13 -> 14; matrix products, arithmetic and copies ran while one was open for 22% -> 12% of each run, Pallas kernels for 21% -> 23%
where the time goes in v7:
time: 300 us; the launch traced here: 295 us
  waiting for transfers between devices  106 us (35%)
  Pallas kernels  69.1 us (23%)
  starting transfers between devices  41.3 us (14%)
  local copies, waits for them, and re-layouts  41.2 us (14%)
  other arithmetic  21.6 us (7%)
  between operations  15.5 us (5%)
    ppermute x35, waiting for transfers between devices, send(): return lax.ppermute(block, 'tensor', swap_pairs(size, step))  57.9 us
    ppermute x35, starting transfers between devices, send(): return lax.ppermute(block, 'tensor', swap_pairs(size, step))  32.3 us
    unnamed x75, local copies, waits for them, and re-layouts  25.6 us
    all_gather x1, waiting for transfers between devices, shards(): lax.all_gather(trainer_out.astype(jnp.bfloat16), 'dp', axis=0, tiled=True)  22.8 us
    pallas_call x2, Pallas kernels, expert(): pl.pallas_call(kernel, out_shape=[jax.ShapeDtypeStruct((rows, model), jnp...  22.7 us
    all_gather x1, waiting for transfers between devices, shards(): qkv_all = lax.all_gather(qkv_cols, 'dp', axis=0)  16.7 us
    pallas_call x1, Pallas kernels, attention(): pl.pallas_call(kernel, out_shape=(jax.ShapeDtypeStruct((2, seq, width), j...  13.7 us
    pallas_call x3, Pallas kernels, copy_rows(): pl.pallas_call(kernel, out_shape=[jax.ShapeDtypeStruct(shape, jnp.bfloat1...  13.7 us
  transfers between devices with their start and end apart: 40, of which 14 were waited for; matrix products, arithmetic and copies ran while one was open for 12% of the time, Pallas kernels for 23%

profile of v7, /device:TPU:12, one launch (start us, length us, event | category | flops | bytes accessed | tf_op | source)
XLA Modules:
  0.0 294.6 jit_solution(6486502957606067663)
XLA Ops:
  9.7 4.4 %all-to-all-start = ((bf16[8,3,72,256]{3,2,1,0:T(8,128)(2,1)}), bf16[8,3,72,256]{3,2,1,0:T(8,128)(2,1)S(1)}, u32[]{:S(2)}, u32[]{:S(2)}) async-start(bf16[8,3,72,256]{3,2,1,0:T(8,128)(2,1)} %split_heads.1), calls=%async_computation | async-start | bytes 1769472 | tf_op jit(solution)/shard_map/all_to_all | solution.py:455
  15.4 10.3 %split_columns.1 = (bf16[38,16,720]{2,1,0:T(8,128)(2,1)S(1)}, bf16[38,16,720]{2,1,0:T(8,128)(2,1)}, bf16[38,16,720]{2,1,0:T(8,128)(2,1)S(1)}, bf16[38,16,720]{2,...) custom-call(s32[1]{0:T(128)} %bitcast.2.me_ref, ...), custom_call_target="tpu_custom_call" | custom-call | tf_op jit(solution)/shard_map/split_columns/pallas_call | solution.py:91
  32.3 13.6 %collective-permute-done.2 = bf16[128,2304]{1,0:T(8,128)(2,1)S(1)} collective-permute-done((bf16[128,2304]{1,0:T(8,128)(2,1)S(1)}, bf16[128,2304]{1,0:T(8,128)(2,1)S(1)}, u32[]{:S(2)}, u32[]{:S(2)}) %collective-permute-start.2) | collective-permute-done | bytes 589856 | tf_op jit(solution)/shard_map/ppermute | solution.py:17
  45.9 11.8 %collective-permute-done.1 = bf16[128,2304]{1,0:T(8,128)(2,1)S(1)} collective-permute-done((bf16[128,2304]{1,0:T(8,128)(2,1)S(1)}, bf16[128,2304]{1,0:T(8,128)(2,1)S(1)}, u32[]{:S(2)}, u32[]{:S(2)}) %collective-permute-start.1) | collective-permute-done | bytes 589856 | tf_op jit(solution)/shard_map/ppermute | solution.py:17
  60.5 2.9 copy-done.2
  64.5 4.6 %all-to-all-start.1 = ((bf16[8,64,720]{2,1,0:T(8,128)(2,1)}), bf16[8,64,720]{2,1,0:T(8,128)(2,1)}, u32[]{:S(2)}, u32[]{:S(2)}) async-start(bf16[8,64,720]{2,1,0:T(8,128)(2,1)} %split_rows.1), calls=%async_computation.1 | async-start | bytes 1572864 | tf_op jit(solution)/shard_map/all_to_all | solution.py:464
  72.7 8.2 %all-to-all-done.1 = bf16[8,64,720]{2,1,0:T(8,128)(2,1)} async-done(((bf16[8,64,720]{2,1,0:T(8,128)(2,1)}), bf16[8,64,720]{2,1,0:T(8,128)(2,1)}, u32[]{:S(2)}, u32[]{:S(2)}) %all-to-all-start.1) | async-done | bytes 737312 | tf_op jit(solution)/shard_map/all_to_all | solution.py:464
  80.8 16.7 %all-gather.8.cloned.1.call-done = bf16[32,3,72,256]{3,2,1,0:T(8,128)(2,1)} async-done(((bf16[8,3,72,256]{3,2,1,0:T(8,128)(2,1)}), bf16[32,3,72,256]{3,2,1,0:T(8,128)(2,1)}) %all-gather.8.cloned.1.call-update) | async-done | bytes 3538960 | tf_op jit(solution)/shard_map/all_gather | solution.py:462
  97.7 5.6 %multiply_sine_fusion = (f32[1024,256]{1,0:T(8,128)}, f32[1024,256]{1,0:T(8,128)}) fusion(f32[256]{0:T(256)S(1)} %mul.108, f32[1024]{0:T(1024)S(1)} %add_convert_fusion.6), kind=kLoop, calls=%fused_computation.1 | loop fusion | flops 262144 | bytes 2102272 | tf_op jit(solution)/shard_map/sin | solution.py:485
  107.2 22.8 %all-gather.6.cloned.1.call-done.own_ref = bf16[256,2304]{1,0:T(8,128)(2,1)} async-done(((bf16[64,2304]{1,0:T(8,128)(2,1)}), bf16[256,2304]{1,0:T(8,128)(2,1)}) %all-gather.6.cloned.1.call-update) | async-done | bytes 1179664 | tf_op jit(solution)/shard_map/all_gather | solution.py:486
  137.8 13.7 %attention.1 = (bf16[2,1024,256]{2,1,0:T(8,128)(2,1)}, bf16[2,512,256]{2,1,0:T(8,128)(2,1)S(1)}) custom-call(s32[2]{0:T(128)S(1)} %pad_add_fusion.s_ref, bf16[1024,2304]{1,0:T(8,128)(2,1)} %bitcast.109, bf16[3,2304,256]{2,1,0:T(8,128)(2,1)S(1)} %bitcast.110, f32[1024,256]{1,0:T(8,128)S(1)} %copy-done.15, f32[1024,256]{1,0:T(8,128)S(1)} %copy-done.14), custom_call_target="tpu_custom_call" | custom-call | flops 4697620480 | bytes 8257536 | tf_op jit(solution)/shard_map/attention/pallas_call | solution.py:386
  151.5 15.2 %collective-permute-done.8.refs_5_.refs_6_ = bf16[38,16,720]{2,1,0:T(8,128)(2,1)} collective-permute-done((bf16[38,16,720]{2,1,0:T(8,128)(2,1)}, bf16[38,16,720]{2,1,0:T(8,128)(2,1)}, u32[]{:S(2)}, u32[]{:S(2)}) %collective-permute-start.8) | collective-permute-done | bytes 875552 | tf_op jit(solution)/shard_map/ppermute | solution.py:17
  170.0 5.1 %project.1 = (f32[64,2304]{1,0:T(8,128)}, f32[64,2304]{1,0:T(8,128)}, bf16[64,2304]{1,0:T(8,128)(2,1)}, bf16[64,2304]{1,0:T(8,128)(2,1)}, bf16[64,2304]{1,0:T(8,...) custom-call(s32[1]{0:T(128)} %bitcast.22.chip_ref, ...), custom_call_target="tpu_custom_call" | custom-call | tf_op jit(solution)/shard_map/project/pallas_call | solution.py:225
  176.2 2.5 collective-permute-start.15
  179.7 4.7 %join_gate_up.1 = (bf16[144,16,720]{2,1,0:T(8,128)(2,1)S(1)}, bf16[144,16,720]{2,1,0:T(8,128)(2,1)S(1)}) custom-call(s32[1]{0:T(128)} %bitcast.2.me_ref, bf16[38,16,720]{2,1,0:T(8,128)(2,1)S(1)} %get-tuple-element.140.refs_0_.refs_1_, bf16[38,16,720]{2,1,0:T(8,128)(2,1)S(1)} %collective-permute-done.4.refs_1_.refs_2_, ...), custom_call_target="tpu_custom_call" | custom-call | tf_op jit(solution)/shard_map/join_gate_up/pallas_call | solution.py:125
  188.0 5.7 %copy.24 = bf16[2304,720]{0,1:T(8,128)(2,1)} copy(bf16[2304,720]{1,0:T(8,128)(2,1)} %bitcast.112) | data formatting | bytes 6635520 | tf_op jit(solution)/shard_map/reshape | solution.py:165
  194.8 2.5 collective-permute-start.21
  203.8 6.6 %join_down.1 = bf16[144,16,720]{2,1,0:T(8,128)(2,1)S(1)} custom-call(s32[1]{0:T(128)} %bitcast.2.me_ref, bf16[4,8,4,16,720]{4,3,2,1,0:T(8,128)(2,1)S(1)} %bitcast.118, bf16[38,16,720]{2,1,0:T(8,128)(2,1)S(1)} %get-tuple-element.140.refs_0_.refs_1_, bf16[38,16,720]{2,1,0:T(8,128)(2,1)S(1)} %collective-permute-done.4.refs_1_.refs_2_, ...), custom_call_target="tpu_custom_call" | custom-call | tf_op jit(solution)/shard_map/join_down/pallas_call | solution.py:125
  213.2 4.4 %collective-permute-done.20 = bf16[64,2304]{1,0:T(8,128)(2,1)} collective-permute-done((bf16[64,2304]{1,0:T(8,128)(2,1)}, bf16[64,2304]{1,0:T(8,128)(2,1)}, u32[]{:S(2)}, u32[]{:S(2)}) %collective-permute-start.20) | collective-permute-done | bytes 294944 | tf_op jit(solution)/shard_map/ppermute | solution.py:17
  219.1 5.6 %copy.25 = bf16[2304,720]{0,1:T(8,128)(2,1)} copy(bf16[2304,720]{1,0:T(8,128)(2,1)} %bitcast.115) | data formatting | bytes 6635520 | tf_op jit(solution)/shard_map/optimization_barrier | solution.py:526
  230.8 11.4 %expert.2 = (bf16[256,2304]{1,0:T(8,128)(2,1)}, bf16[256,2304]{1,0:T(8,128)(2,1)}) custom-call(bf16[256,2304]{1,0:T(8,128)(2,1)} %bitcast.136, bf16[256,2304]{1,0:T(8,128)(2,1)} %bitcast.142, bf16[2304,720]{1,0:T(8,128)(2,1)} %bitcast.113, bf16[2304,720]{1,0:T(8,128)(2,1)} %bitcast.116, bf16[2304,720]{1,0:T(8,128)(2,1)} %bitcast.104), custom_call_target="tpu_custom_call" | custom-call | flops 5096079360 | bytes 9953280 | tf_op jit(solution)/shard_map/expert/pallas_call | solution.py:287
  251.1 11.4 %expert.3 = (bf16[256,2304]{1,0:T(8,128)(2,1)}, bf16[256,2304]{1,0:T(8,128)(2,1)}) custom-call(bf16[256,2304]{1,0:T(8,128)(2,1)} %bitcast.135, bf16[256,2304]{1,0:T(8,128)(2,1)} %bitcast.141, bf16[2304,720]{1,0:T(8,128)(2,1)} %bitcast.114, bf16[2304,720]{1,0:T(8,128)(2,1)} %bitcast.117, bf16[2304,720]{1,0:T(8,128)(2,1)} %bitcast.105), custom_call_target="tpu_custom_call" | custom-call | flops 5096079360 | bytes 9953280 | tf_op jit(solution)/shard_map/expert/pallas_call | solution.py:287
  273.2 5.6 %copy.26 = bf16[2304,720]{0,1:T(8,128)(2,1)} copy(bf16[2304,720]{1,0:T(8,128)(2,1)} %bitcast.106) | data formatting | bytes 6635520
  278.8 5.2 %collective-permute-done.33 = bf16[64,2304]{1,0:T(8,128)(2,1)S(1)} collective-permute-done((bf16[64,2304]{1,0:T(8,128)(2,1)}, bf16[64,2304]{1,0:T(8,128)(2,1)S(1)}, u32[]{:S(2)}, u32[]{:S(2)}) %collective-permute-start.33) | collective-permute-done | bytes 294944 | tf_op jit(solution)/shard_map/ppermute | solution.py:17
  (181 shorter events, 78.6 us)
Async XLA Ops:
  9.7 18.1 %all-to-all-start = ((bf16[8,3,72,256]{3,2,1,0:T(8,128)(2,1)}), bf16[8,3,72,256]{3,2,1,0:T(8,128)(2,1)S(1)}, u32[]{:S(2)}, u32[]{:S(2)}) async-start(bf16[8,3,72,256]{3,2,1,0:T(8,128)(2,1)} %split_heads.1), calls=%async_computation | async-start | bytes 1769472 | tf_op jit(solution)/shard_map/all_to_all | solution.py:455
  14.0 83.5 %all-gather.8.cloned.1.call-start = ((), (), s32[]{:S(2)}) async-start(), calls=%async_computation.3 | async-start | bytes 4423680 | tf_op jit(solution)/shard_map/all_gather | solution.py:462
  28.7 101.4 %all-gather.6.cloned.1.call-start = ((), (), s32[]{:S(2)}) async-start(), calls=%async_computation.2 | async-start | bytes 1474560 | tf_op jit(solution)/shard_map/all_gather | solution.py:486
  28.8 17.2 %collective-permute-start.2 = (bf16[128,2304]{1,0:T(8,128)(2,1)S(1)}, bf16[128,2304]{1,0:T(8,128)(2,1)S(1)}, u32[]{:S(2)}, u32[]{:S(2)}) collective-permute-start(bf16[128,2304]{1,0:T(8,128)(2,1)S(1)} %fusion.6), channel_id=1, source_target_pairs={{0,6},{1,7},{2,4},{3,5},{4,2},{5,3},{6,0},{7,1},{8,14},{9,15},{10,... | collective-permute-start | bytes 1769480 | tf_op jit(solution)/shard_map/ppermute | solution.py:17
  30.3 27.5 %collective-permute-start.1 = (bf16[128,2304]{1,0:T(8,128)(2,1)S(1)}, bf16[128,2304]{1,0:T(8,128)(2,1)S(1)}, u32[]{:S(2)}, u32[]{:S(2)}) collective-permute-start(bf16[128,2304]{1,0:T(8,128)(2,1)S(1)} %fusion.6), channel_id=1, source_target_pairs={{0,4},{1,5},{2,6},{3,7},{4,0},{5,1},{6,2},{7,3},{8,12},{9,13},{10,... | collective-permute-start | bytes 1769480 | tf_op jit(solution)/shard_map/ppermute | solution.py:17
  31.8 26.0 %collective-permute-start = (bf16[128,2304]{1,0:T(8,128)(2,1)S(1)}, bf16[128,2304]{1,0:T(8,128)(2,1)S(1)}, u32[]{:S(2)}, u32[]{:S(2)}) collective-permute-start(bf16[128,2304]{1,0:T(8,128)(2,1)S(1)} %fusion.6), channel_id=1, source_target_pairs={{0,2},{1,3},{2,0},{3,1},{4,6},{5,7},{6,4},{7,5},{8,10},{9,11},{10,... | collective-permute-start | bytes 1769480 | tf_op jit(solution)/shard_map/ppermute | solution.py:17
  59.5 70.6 %collective-permute-start.3 = (bf16[4,128,2304]{2,1,0:T(8,128)(2,1)}, bf16[4,128,2304]{2,1,0:T(8,128)(2,1)}, u32[]{:S(2)}, u32[]{:S(2)}) collective-permute-start(bf16[4,128,2304]{2,1,0:T(8,128)(2,1)} %pad_maximum_fusion), channel_id=1, source_target_pairs={{0,1},{1,0},{2,3},{3,2},{4,5},{5,4},{6,7},{7,6},{8,9},{9,8},{10,11... | collective-permute-start | bytes 7077896 | tf_op jit(solution)/shard_map/ppermute | solution.py:17
  69.1 132.8 %all-gather.10.cloned.1.call-start = ((), (), s32[]{:S(2)}) async-start(), calls=%async_computation.4 | async-start | bytes 3932160 | tf_op jit(solution)/shard_map/all_gather | solution.py:488
  69.1 34.2 %collective-permute-start.4 = (bf16[38,16,720]{2,1,0:T(8,128)(2,1)}, bf16[38,16,720]{2,1,0:T(8,128)(2,1)S(1)}, u32[]{:S(2)}, u32[]{:S(2)}) collective-permute-start(bf16[38,16,720]{2,1,0:T(8,128)(2,1)} %get-tuple-element.118), channel_id=1, source_target_pairs={{0,1},{1,0},{2,3},{3,2},{4,5},{5,4},{6,7},{7,6},{8,9},{9,8},{10,11... | collective-permute-start | bytes 2626568 | tf_op jit(solution)/shard_map/ppermute | solution.py:17
  69.2 34.1 %collective-permute-start.5 = (bf16[38,16,720]{2,1,0:T(8,128)(2,1)}, bf16[38,16,720]{2,1,0:T(8,128)(2,1)S(1)}, u32[]{:S(2)}, u32[]{:S(2)}) collective-permute-start(bf16[38,16,720]{2,1,0:T(8,128)(2,1)} %copy-done.17), channel_id=1, source_target_pairs={{0,2},{1,3},{2,0},{3,1},{4,6},{5,7},{6,4},{7,5},{8,10},{9,11},{10,... | collective-permute-start | bytes 2626568 | tf_op jit(solution)/shard_map/ppermute | solution.py:17
  70.7 32.6 %collective-permute-start.6 = (bf16[38,16,720]{2,1,0:T(8,128)(2,1)}, bf16[38,16,720]{2,1,0:T(8,128)(2,1)}, u32[]{:S(2)}, u32[]{:S(2)}) collective-permute-start(bf16[38,16,720]{2,1,0:T(8,128)(2,1)} %copy-done.16), channel_id=1, source_target_pairs={{0,4},{1,5},{2,6},{3,7},{4,0},{5,1},{6,2},{7,3},{8,12},{9,13},{10,... | collective-permute-start | bytes 2626568 | tf_op jit(solution)/shard_map/ppermute | solution.py:17
  103.3 48.2 %collective-permute-start.7 = (bf16[38,16,720]{2,1,0:T(8,128)(2,1)}, bf16[38,16,720]{2,1,0:T(8,128)(2,1)}, u32[]{:S(2)}, u32[]{:S(2)}) collective-permute-start(bf16[38,16,720]{2,1,0:T(8,128)(2,1)} %get-tuple-element.129), channel_id=1, source_target_pairs={{0,3},{1,2},{2,1},{3,0},{4,7},{5,6},{6,5},{7,4},{8,11},{9,10},{10,... | collective-permute-start | bytes 2626568 | tf_op jit(solution)/shard_map/ppermute | solution.py:17
  104.3 62.5 %collective-permute-start.8 = (bf16[38,16,720]{2,1,0:T(8,128)(2,1)}, bf16[38,16,720]{2,1,0:T(8,128)(2,1)}, u32[]{:S(2)}, u32[]{:S(2)}) collective-permute-start(bf16[38,16,720]{2,1,0:T(8,128)(2,1)} %get-tuple-element.130), channel_id=1, source_target_pairs={{0,5},{1,4},{2,7},{3,6},{4,1},{5,0},{6,3},{7,2},{8,13},{9,12},{10,... | collective-permute-start | bytes 2626568 | tf_op jit(solution)/shard_map/ppermute | solution.py:17
  105.1 63.0 %collective-permute-start.10 = (bf16[38,16,720]{2,1,0:T(8,128)(2,1)}, bf16[38,16,720]{2,1,0:T(8,128)(2,1)}, u32[]{:S(2)}, u32[]{:S(2)}) collective-permute-start(bf16[38,16,720]{2,1,0:T(8,128)(2,1)} %get-tuple-element.132), channel_id=1, source_target_pairs={{0,6},{1,7},{2,4},{3,5},{4,2},{5,3},{6,0},{7,1},{8,14},{9,15},{10,... | collective-permute-start | bytes 2626568 | tf_op jit(solution)/shard_map/ppermute | solution.py:17
  106.6 61.6 %collective-permute-start.11 = (bf16[38,16,720]{2,1,0:T(8,128)(2,1)}, bf16[38,16,720]{2,1,0:T(8,128)(2,1)}, u32[]{:S(2)}, u32[]{:S(2)}) collective-permute-start(bf16[38,16,720]{2,1,0:T(8,128)(2,1)} %get-tuple-element.133), channel_id=1, source_target_pairs={{0,7},{1,6},{2,5},{3,4},{4,3},{5,2},{6,1},{7,0},{8,15},{9,14},{10,... | collective-permute-start | bytes 2626568 | tf_op jit(solution)/shard_map/ppermute | solution.py:17
  130.1 39.2 %collective-permute-start.12 = (bf16[256,2304]{1,0:T(8,128)(2,1)}, bf16[256,2304]{1,0:T(8,128)(2,1)}, u32[]{:S(2)}, u32[]{:S(2)}) collective-permute-start(bf16[256,2304]{1,0:T(8,128)(2,1)} %all-gather.6.cloned.1.call-done.own_ref), channel_id=1, source_target_pairs={{0,1},{1,0},{2,3},{3,2},{4,5},{5,4},{6,7},{7,6},{8,9},{9,8},{10,11... | collective-permute-start | bytes 3538952 | tf_op jit(solution)/shard_map/ppermute | solution.py:17
  175.2 18.5 %collective-permute-start.13 = (bf16[64,2304]{1,0:T(8,128)(2,1)}, bf16[64,2304]{1,0:T(8,128)(2,1)}, u32[]{:S(2)}, u32[]{:S(2)}) collective-permute-start(bf16[64,2304]{1,0:T(8,128)(2,1)} %get-tuple-element.137), channel_id=1, source_target_pairs={{0,2},{1,3},{2,0},{3,1},{4,6},{5,7},{6,4},{7,5},{8,10},{9,11},{10,... | collective-permute-start | bytes 884744 | tf_op jit(solution)/shard_map/ppermute | solution.py:17
  176.1 17.5 %collective-permute-start.14 = (bf16[64,2304]{1,0:T(8,128)(2,1)}, bf16[64,2304]{1,0:T(8,128)(2,1)}, u32[]{:S(2)}, u32[]{:S(2)}) collective-permute-start(bf16[64,2304]{1,0:T(8,128)(2,1)} %get-tuple-element.138), channel_id=1, source_target_pairs={{0,4},{1,5},{2,6},{3,7},{4,0},{5,1},{6,2},{7,3},{8,12},{9,13},{10,... | collective-permute-start | bytes 884744 | tf_op jit(solution)/shard_map/ppermute | solution.py:17
  176.2 17.5 %collective-permute-start.15 = (bf16[64,2304]{1,0:T(8,128)(2,1)}, bf16[64,2304]{1,0:T(8,128)(2,1)}, u32[]{:S(2)}, u32[]{:S(2)}) collective-permute-start(bf16[64,2304]{1,0:T(8,128)(2,1)} %get-tuple-element.139), channel_id=1, source_target_pairs={{0,6},{1,7},{2,4},{3,5},{4,2},{5,3},{6,0},{7,1},{8,14},{9,15},{10,... | collective-permute-start | bytes 884744 | tf_op jit(solution)/shard_map/ppermute | solution.py:17
  193.7 18.5 %collective-permute-start.19 = (bf16[64,2304]{1,0:T(8,128)(2,1)}, bf16[64,2304]{1,0:T(8,128)(2,1)}, u32[]{:S(2)}, u32[]{:S(2)}) collective-permute-start(bf16[64,2304]{1,0:T(8,128)(2,1)} %get-tuple-element.155), channel_id=1, source_target_pairs={{0,2},{1,3},{2,0},{3,1},{4,6},{5,7},{6,4},{7,5},{8,10},{9,11},{10,... | collective-permute-start | bytes 884744 | tf_op jit(solution)/shard_map/ppermute | solution.py:17
  194.8 22.9 %collective-permute-start.20 = (bf16[64,2304]{1,0:T(8,128)(2,1)}, bf16[64,2304]{1,0:T(8,128)(2,1)}, u32[]{:S(2)}, u32[]{:S(2)}) collective-permute-start(bf16[64,2304]{1,0:T(8,128)(2,1)} %get-tuple-element.156), channel_id=1, source_target_pairs={{0,4},{1,5},{2,6},{3,7},{4,0},{5,1},{6,2},{7,3},{8,12},{9,13},{10,... | collective-permute-start | bytes 884744 | tf_op jit(solution)/shard_map/ppermute | solution.py:17
  194.8 22.9 %collective-permute-start.21 = (bf16[64,2304]{1,0:T(8,128)(2,1)}, bf16[64,2304]{1,0:T(8,128)(2,1)}, u32[]{:S(2)}, u32[]{:S(2)}) collective-permute-start(bf16[64,2304]{1,0:T(8,128)(2,1)} %get-tuple-element.157), channel_id=1, source_target_pairs={{0,6},{1,7},{2,4},{3,5},{4,2},{5,3},{6,0},{7,1},{8,14},{9,15},{10,... | collective-permute-start | bytes 884744 | tf_op jit(solution)/shard_map/ppermute | solution.py:17
  199.4 25.4 %collective-permute-start.18 = (bf16[64,2304]{1,0:T(8,128)(2,1)S(1)}, bf16[64,2304]{1,0:T(8,128)(2,1)}, u32[]{:S(2)}, u32[]{:S(2)}) collective-permute-start(bf16[64,2304]{1,0:T(8,128)(2,1)S(1)} %fusion.9), channel_id=1, source_target_pairs={{0,6},{1,7},{2,4},{3,5},{4,2},{5,3},{6,0},{7,1},{8,14},{9,15},{10,... | collective-permute-start | bytes 884744 | tf_op jit(solution)/shard_map/ppermute | solution.py:17
  199.9 24.9 %collective-permute-start.17 = (bf16[64,2304]{1,0:T(8,128)(2,1)S(1)}, bf16[64,2304]{1,0:T(8,128)(2,1)}, u32[]{:S(2)}, u32[]{:S(2)}) collective-permute-start(bf16[64,2304]{1,0:T(8,128)(2,1)S(1)} %fusion.9), channel_id=1, source_target_pairs={{0,4},{1,5},{2,6},{3,7},{4,0},{5,1},{6,2},{7,3},{8,12},{9,13},{10,... | collective-permute-start | bytes 884744 | tf_op jit(solution)/shard_map/ppermute | solution.py:17
  (53 other events, 588.9 us)
Sparse Core Ops, SparseCore 0:
  28.8 68.6 all-gather.7
  99.1 30.8 all-gather.5
  131.7 60.8 all-gather.9

commit v8 on v7

--- a/solution.py
+++ b/solution.py
@@ -484,11 +484,10 @@
     angles = places.astype(jnp.float32)[:, None] * jnp.tile(inv_freq, local_width // half_dim)
     cosine, sine_part = jnp.cos(angles), jnp.sin(angles)
     server_out = lax.all_gather(trainer_out.astype(jnp.bfloat16), "dp", axis=0, tiled=True)
-    qkv_all, down_cols = lax.optimization_barrier((qkv_all, down_cols))
+    qkv_all, server_out, down_cols, piece, cosine, sine_part, *early = lax.optimization_barrier(
+        (qkv_all, server_out, down_cols, piece, cosine, sine_part, *early)
+    )
     down_all = lax.all_gather(down_cols, "dp", axis=0)
-    qkv_all, piece, cosine, sine_part, *early = lax.optimization_barrier(
-        (qkv_all, piece, cosine, sine_part, *early)
-    )
     qkv_server = qkv_all.transpose(2, 1, 0, 3, 4).reshape(3, model, local_width)
     server_qkv = qkv_server.transpose(1, 0, 2)
     scalars = jnp.stack([length, core])
@@ -527,8 +526,7 @@
             flipped[1] = with_layout_constraint(flipped[1], Layout((1, 0)))
             *moe_rows[0], flipped[1] = lax.optimization_barrier((*moe_rows[0], flipped[1]))
         else:
-            flipped[0] = with_layout_constraint(flipped[0], Layout((1, 0)))
-            attn_sum, flipped[0] = lax.optimization_barrier((attn_sum, flipped[0]))
+            attn_sum, gate, up = lax.optimization_barrier((attn_sum, gate, up))
         middles.append((tokens[h * rows : (h + 1) * rows] + attn_sum).astype(jnp.bfloat16))
         normed = rms_scale(middles[h].astype(jnp.float32), moe_gain).astype(jnp.bfloat16)
         normed_moes.append(normed)
@@ -575,7 +573,7 @@
         sent = [block.astype(jnp.bfloat16) for block in sums[1:]]
         back = [send(block, size, 2 * j + 2) for j, block in enumerate(sent)]
     expert_sums.append(add_up(total, back))
-    down_late, _ = lax.optimization_barrier((down, sent[0]))
+    down_late, gate_late, _ = lax.optimization_barrier((down, gate, sent[0]))
     expert_sum = jnp.concatenate(expert_sums, axis=0)
     expert_sum = jnp.where(local_routed[:, None], expert_sum, 0.0)
     result = middle.astype(jnp.float32) + route_w[:, None] * expert_sum
@@ -583,7 +581,8 @@
     return (
         server_qkv,
         server_out,
-        *flipped,
+        gate_late,
+        flipped[1],
         down_late,
         hidden_out,
         cache_pair[None],

time: 300 us -> 305 us (1.017)
  waiting for transfers between devices: 106 us -> 110 us
    ppermute x35, waiting for transfers between devices: 57.9 us -> 94.8 us  [send(): return lax.ppermute(block, 'tensor', swap_pairs(size, step))]
    all_gather x1, waiting for transfers between devices: 22.8 us -> 0.01 us  [shards(): lax.all_gather(trainer_out.astype(jnp.bfloat16), 'dp', axis=0, tiled=True)]
    all_to_all x1, waiting for transfers between devices: 8.17 us -> 0.45 us  [shards(): down_cols = lax.all_to_all(down_parts, 'tensor', 0, 0, tiled=True)]
    reshape x1 -> x0, local copies, waits for them, and re-layouts: 5.7 us -> none  [join_gate_up(): return [matrix.reshape(-1, width) for matrix in joined]]
    unnamed x75 -> x78, local copies, waits for them, and re-layouts: 25.6 us -> 31.1 us
  transfers between devices with their start and end apart: 40 -> 40, of which waited for: 14 -> 16; matrix products, arithmetic and copies ran while one was open for 12% -> 12% of each run, Pallas kernels for 23% -> 23%
where the time goes in v8:
time: 305 us; the launch traced here: 299 us
  waiting for transfers between devices  110 us (36%)
  Pallas kernels  68.3 us (22%)
  local copies, waits for them, and re-layouts  42.9 us (14%)
  starting transfers between devices  42.4 us (14%)
  other arithmetic  20.5 us (7%)
  between operations  15.5 us (5%)
    ppermute x35, waiting for transfers between devices, send(): return lax.ppermute(block, 'tensor', swap_pairs(size, step))  94.8 us
    ppermute x35, starting transfers between devices, send(): return lax.ppermute(block, 'tensor', swap_pairs(size, step))  33.3 us
    unnamed x78, local copies, waits for them, and re-layouts  31.1 us
    pallas_call x2, Pallas kernels, expert(): pl.pallas_call(kernel, out_shape=[jax.ShapeDtypeStruct((rows, model), jnp...  22.7 us
    all_gather x1, waiting for transfers between devices, shards(): qkv_all = lax.all_gather(qkv_cols, 'dp', axis=0)  14.3 us
    pallas_call x1, Pallas kernels, attention(): pl.pallas_call(kernel, out_shape=(jax.ShapeDtypeStruct((2, seq, width), j...  14.2 us
    pallas_call x3, Pallas kernels, copy_rows(): pl.pallas_call(kernel, out_shape=[jax.ShapeDtypeStruct(shape, jnp.bfloat1...  13.7 us
    pallas_call x1, Pallas kernels, split_columns(): pl.pallas_call(kernel, out_shape=[jax.ShapeDtypeStruct(((2 * rows + tail)...  9.73 us
  transfers between devices with their start and end apart: 40, of which 16 were waited for; matrix products, arithmetic and copies ran while one was open for 12% of the time, Pallas kernels for 23%

profile of v8, /device:TPU:12, one launch (start us, length us, event | category | flops | bytes accessed | tf_op | source)
XLA Modules:
  0.0 299.4 jit_solution(16457357206106242056)
XLA Ops:
  9.1 2.5 split_heads.1
  11.6 4.4 %all-to-all-start = ((bf16[8,3,72,256]{3,2,1,0:T(8,128)(2,1)}), bf16[8,3,72,256]{3,2,1,0:T(8,128)(2,1)S(1)}, u32[]{:S(2)}, u32[]{:S(2)}) async-start(bf16[8,3,72,256]{3,2,1,0:T(8,128)(2,1)} %split_heads.1), calls=%async_computation | async-start | bytes 1769472 | tf_op jit(solution)/shard_map/all_to_all | solution.py:455
  17.3 9.7 %split_columns.1 = (bf16[38,16,720]{2,1,0:T(8,128)(2,1)S(1)}, bf16[38,16,720]{2,1,0:T(8,128)(2,1)}, bf16[38,16,720]{2,1,0:T(8,128)(2,1)}, bf16[38,16,720]{2,1,0:...) custom-call(s32[1]{0:T(128)} %bitcast.2.me_ref, ...), custom_call_target="tpu_custom_call" | custom-call | tf_op jit(solution)/shard_map/split_columns/pallas_call | solution.py:91
  35.6 13.6 %collective-permute-done.2 = bf16[128,2304]{1,0:T(8,128)(2,1)S(1)} collective-permute-done((bf16[128,2304]{1,0:T(8,128)(2,1)S(1)}, bf16[128,2304]{1,0:T(8,128)(2,1)S(1)}, u32[]{:S(2)}, u32[]{:S(2)}) %collective-permute-start.2) | collective-permute-done | bytes 589856 | tf_op jit(solution)/shard_map/ppermute | solution.py:17
  49.2 11.8 %collective-permute-done.1 = bf16[128,2304]{1,0:T(8,128)(2,1)S(1)} collective-permute-done((bf16[128,2304]{1,0:T(8,128)(2,1)S(1)}, bf16[128,2304]{1,0:T(8,128)(2,1)S(1)}, u32[]{:S(2)}, u32[]{:S(2)}) %collective-permute-start.1) | collective-permute-done | bytes 589856 | tf_op jit(solution)/shard_map/ppermute | solution.py:17
  65.4 2.9 copy-done.2
  69.5 4.8 %all-to-all-start.1 = ((bf16[8,64,720]{2,1,0:T(8,128)(2,1)}), bf16[8,64,720]{2,1,0:T(8,128)(2,1)}, u32[]{:S(2)}, u32[]{:S(2)}) async-start(bf16[8,64,720]{2,1,0:T(8,128)(2,1)} %copy-done.8), calls=%async_computation.1 | async-start | bytes 1572864 | tf_op jit(solution)/shard_map/all_to_all | solution.py:464
  75.0 5.5 %multiply_sine_fusion = (f32[1024,256]{1,0:T(8,128)}, f32[1024,256]{1,0:T(8,128)}) fusion(f32[256]{0:T(256)S(1)} %mul.108, f32[1024]{0:T(1024)S(1)} %add_convert_fusion.6), kind=kLoop, calls=%fused_computation.1 | loop fusion | flops 262144 | bytes 2102272 | tf_op jit(solution)/shard_map/sin | solution.py:485
  80.6 6.6 %collective-permute-done.5.refs_3_.refs_2_ = bf16[38,16,720]{2,1,0:T(8,128)(2,1)S(1)} collective-permute-done((bf16[38,16,720]{2,1,0:T(8,128)(2,1)}, bf16[38,16,720]{2,1,0:T(8,128)(2,1)S(1)}, u32[]{:S(2)}, u32[]{:S(2)}) %collective-permute-start.5) | collective-permute-done | bytes 875552 | tf_op jit(solution)/shard_map/ppermute | solution.py:17
  95.2 14.3 %all-gather.8.cloned.1.call-done = bf16[32,3,72,256]{3,2,1,0:T(8,128)(2,1)} async-done(((bf16[8,3,72,256]{3,2,1,0:T(8,128)(2,1)}), bf16[32,3,72,256]{3,2,1,0:T(8,128)(2,1)}) %all-gather.8.cloned.1.call-update) | async-done | bytes 3538960 | tf_op jit(solution)/shard_map/all_gather | solution.py:462
  117.3 14.2 %attention.1 = (bf16[2,1024,256]{2,1,0:T(8,128)(2,1)}, bf16[2,512,256]{2,1,0:T(8,128)(2,1)S(1)}) custom-call(s32[2]{0:T(128)S(1)} %pad_add_fusion.s_ref, bf16[1024,2304]{1,0:T(8,128)(2,1)} %bitcast.109, bf16[3,2304,256]{2,1,0:T(8,128)(2,1)S(1)} %bitcast.110, f32[1024,256]{1,0:T(8,128)S(1)} %copy-done.16, f32[1024,256]{1,0:T(8,128)S(1)} %copy-done.15), custom_call_target="tpu_custom_call" | custom-call | flops 4697620480 | bytes 8257536 | tf_op jit(solution)/shard_map/attention/pallas_call | solution.py:386
  132.9 40.0 %collective-permute-done.8.refs_6_.refs_5_ = bf16[38,16,720]{2,1,0:T(8,128)(2,1)} collective-permute-done((bf16[38,16,720]{2,1,0:T(8,128)(2,1)}, bf16[38,16,720]{2,1,0:T(8,128)(2,1)}, u32[]{:S(2)}, u32[]{:S(2)}) %collective-permute-start.8) | collective-permute-done | bytes 875552 | tf_op jit(solution)/shard_map/ppermute | solution.py:17
  176.3 5.1 %project.1 = (f32[64,2304]{1,0:T(8,128)}, f32[64,2304]{1,0:T(8,128)}, bf16[64,2304]{1,0:T(8,128)(2,1)}, bf16[64,2304]{1,0:T(8,128)(2,1)}, bf16[64,2304]{1,0:T(8,...) custom-call(s32[1]{0:T(128)} %bitcast.22.chip_ref, ...), custom_call_target="tpu_custom_call" | custom-call | tf_op jit(solution)/shard_map/project/pallas_call | solution.py:225
  182.4 2.5 collective-permute-start.15
  185.0 4.7 %join_gate_up.1 = (bf16[144,16,720]{2,1,0:T(8,128)(2,1)S(1)}, bf16[144,16,720]{2,1,0:T(8,128)(2,1)S(1)}) custom-call(s32[1]{0:T(128)} %bitcast.2.me_ref, bf16[38,16,720]{2,1,0:T(8,128)(2,1)S(1)} %get-tuple-element.149.refs_1_.refs_0_, bf16[38,16,720]{2,1,0:T(8,128)(2,1)S(1)} %collective-permute-done.4.refs_2_.refs_1_, ...), custom_call_target="tpu_custom_call" | custom-call | tf_op jit(solution)/shard_map/join_gate_up/pallas_call | solution.py:125
  191.5 6.4 %collective-permute-done.14 = bf16[64,2304]{1,0:T(8,128)(2,1)S(1)} collective-permute-done((bf16[64,2304]{1,0:T(8,128)(2,1)}, bf16[64,2304]{1,0:T(8,128)(2,1)S(1)}, u32[]{:S(2)}, u32[]{:S(2)}) %collective-permute-start.14) | collective-permute-done | bytes 294944 | tf_op jit(solution)/shard_map/ppermute | solution.py:17
  206.4 6.6 %join_down.1 = bf16[144,16,720]{2,1,0:T(8,128)(2,1)S(1)} custom-call(s32[1]{0:T(128)} %bitcast.2.me_ref, bf16[4,8,4,16,720]{4,3,2,1,0:T(8,128)(2,1)S(1)} %bitcast.118, bf16[38,16,720]{2,1,0:T(8,128)(2,1)S(1)} %get-tuple-element.149.refs_1_.refs_0_, bf16[38,16,720]{2,1,0:T(8,128)(2,1)S(1)} %collective-permute-done.4.refs_2_.refs_1_, ...), custom_call_target="tpu_custom_call" | custom-call | tf_op jit(solution)/shard_map/join_down/pallas_call | solution.py:125
  215.8 6.3 %collective-permute-done.17 = bf16[64,2304]{1,0:T(8,128)(2,1)} collective-permute-done((bf16[64,2304]{1,0:T(8,128)(2,1)}, bf16[64,2304]{1,0:T(8,128)(2,1)}, u32[]{:S(2)}, u32[]{:S(2)}) %collective-permute-start.17) | collective-permute-done | bytes 294944 | tf_op jit(solution)/shard_map/ppermute | solution.py:17
  223.5 5.6 %copy.24 = bf16[2304,720]{0,1:T(8,128)(2,1)} copy(bf16[2304,720]{1,0:T(8,128)(2,1)} %bitcast.115) | data formatting | bytes 6635520 | tf_op jit(solution)/shard_map/optimization_barrier | solution.py:525
  235.2 11.4 %expert.2 = (bf16[256,2304]{1,0:T(8,128)(2,1)}, bf16[256,2304]{1,0:T(8,128)(2,1)}) custom-call(bf16[256,2304]{1,0:T(8,128)(2,1)} %bitcast.136, bf16[256,2304]{1,0:T(8,128)(2,1)} %bitcast.142, bf16[2304,720]{1,0:T(8,128)(2,1)} %bitcast.112, bf16[2304,720]{1,0:T(8,128)(2,1)} %bitcast.116, bf16[2304,720]{1,0:T(8,128)(2,1)} %bitcast.104), custom_call_target="tpu_custom_call" | custom-call | flops 5096079360 | bytes 9953280 | tf_op jit(solution)/shard_map/expert/pallas_call | solution.py:287
  255.9 11.3 %expert.3 = (bf16[256,2304]{1,0:T(8,128)(2,1)}, bf16[256,2304]{1,0:T(8,128)(2,1)}) custom-call(bf16[256,2304]{1,0:T(8,128)(2,1)} %bitcast.135, bf16[256,2304]{1,0:T(8,128)(2,1)} %bitcast.141, bf16[2304,720]{1,0:T(8,128)(2,1)} %bitcast.113, bf16[2304,720]{1,0:T(8,128)(2,1)} %bitcast.117, bf16[2304,720]{1,0:T(8,128)(2,1)} %bitcast.105), custom_call_target="tpu_custom_call" | custom-call | flops 5096079360 | bytes 9953280 | tf_op jit(solution)/shard_map/expert/pallas_call | solution.py:287
  270.8 2.4 add_convert_fusion.1
  278.0 5.6 %copy.25 = bf16[2304,720]{0,1:T(8,128)(2,1)} copy(bf16[2304,720]{1,0:T(8,128)(2,1)} %bitcast.114) | data formatting | bytes 6635520
  283.6 5.6 %copy.26 = bf16[2304,720]{0,1:T(8,128)(2,1)} copy(bf16[2304,720]{1,0:T(8,128)(2,1)} %bitcast.106) | data formatting | bytes 6635520
  (183 shorter events, 79.9 us)
Async XLA Ops:
  7.2 88.0 %all-gather.6.cloned.1.call-start = ((), (), s32[]{:S(2)}) async-start(), calls=%async_computation.2 | async-start | bytes 1474560 | tf_op jit(solution)/shard_map/all_gather | solution.py:486
  11.6 19.5 %all-to-all-start = ((bf16[8,3,72,256]{3,2,1,0:T(8,128)(2,1)}), bf16[8,3,72,256]{3,2,1,0:T(8,128)(2,1)S(1)}, u32[]{:S(2)}, u32[]{:S(2)}) async-start(bf16[8,3,72,256]{3,2,1,0:T(8,128)(2,1)} %split_heads.1), calls=%async_computation | async-start | bytes 1769472 | tf_op jit(solution)/shard_map/all_to_all | solution.py:455
  15.9 93.6 %all-gather.8.cloned.1.call-start = ((), (), s32[]{:S(2)}) async-start(), calls=%async_computation.3 | async-start | bytes 4423680 | tf_op jit(solution)/shard_map/all_gather | solution.py:462
  32.0 17.2 %collective-permute-start.2 = (bf16[128,2304]{1,0:T(8,128)(2,1)S(1)}, bf16[128,2304]{1,0:T(8,128)(2,1)S(1)}, u32[]{:S(2)}, u32[]{:S(2)}) collective-permute-start(bf16[128,2304]{1,0:T(8,128)(2,1)S(1)} %fusion.6), channel_id=1, source_target_pairs={{0,6},{1,7},{2,4},{3,5},{4,2},{5,3},{6,0},{7,1},{8,14},{9,15},{10,... | collective-permute-start | bytes 1769480 | tf_op jit(solution)/shard_map/ppermute | solution.py:17
  33.5 27.4 %collective-permute-start.1 = (bf16[128,2304]{1,0:T(8,128)(2,1)S(1)}, bf16[128,2304]{1,0:T(8,128)(2,1)S(1)}, u32[]{:S(2)}, u32[]{:S(2)}) collective-permute-start(bf16[128,2304]{1,0:T(8,128)(2,1)S(1)} %fusion.6), channel_id=1, source_target_pairs={{0,4},{1,5},{2,6},{3,7},{4,0},{5,1},{6,2},{7,3},{8,12},{9,13},{10,... | collective-permute-start | bytes 1769480 | tf_op jit(solution)/shard_map/ppermute | solution.py:17
  35.0 26.0 %collective-permute-start = (bf16[128,2304]{1,0:T(8,128)(2,1)S(1)}, bf16[128,2304]{1,0:T(8,128)(2,1)S(1)}, u32[]{:S(2)}, u32[]{:S(2)}) collective-permute-start(bf16[128,2304]{1,0:T(8,128)(2,1)S(1)} %fusion.6), channel_id=1, source_target_pairs={{0,2},{1,3},{2,0},{3,1},{4,6},{5,7},{6,4},{7,5},{8,10},{9,11},{10,... | collective-permute-start | bytes 1769480 | tf_op jit(solution)/shard_map/ppermute | solution.py:17
  62.8 25.5 %collective-permute-start.3 = (bf16[4,128,2304]{2,1,0:T(8,128)(2,1)}, bf16[4,128,2304]{2,1,0:T(8,128)(2,1)}, u32[]{:S(2)}, u32[]{:S(2)}) collective-permute-start(bf16[4,128,2304]{2,1,0:T(8,128)(2,1)} %pad_maximum_fusion), channel_id=1, source_target_pairs={{0,1},{1,0},{2,3},{3,2},{4,5},{5,4},{6,7},{7,6},{8,9},{9,8},{10,11... | collective-permute-start | bytes 7077896 | tf_op jit(solution)/shard_map/ppermute | solution.py:17
  63.0 17.6 %collective-permute-start.4 = (bf16[38,16,720]{2,1,0:T(8,128)(2,1)}, bf16[38,16,720]{2,1,0:T(8,128)(2,1)S(1)}, u32[]{:S(2)}, u32[]{:S(2)}) collective-permute-start(bf16[38,16,720]{2,1,0:T(8,128)(2,1)} %get-tuple-element.119), channel_id=1, source_target_pairs={{0,1},{1,0},{2,3},{3,2},{4,5},{5,4},{6,7},{7,6},{8,9},{9,8},{10,11... | collective-permute-start | bytes 2626568 | tf_op jit(solution)/shard_map/ppermute | solution.py:17
  63.4 23.8 %collective-permute-start.5 = (bf16[38,16,720]{2,1,0:T(8,128)(2,1)}, bf16[38,16,720]{2,1,0:T(8,128)(2,1)S(1)}, u32[]{:S(2)}, u32[]{:S(2)}) collective-permute-start(bf16[38,16,720]{2,1,0:T(8,128)(2,1)} %get-tuple-element.120), channel_id=1, source_target_pairs={{0,2},{1,3},{2,0},{3,1},{4,6},{5,7},{6,4},{7,5},{8,10},{9,11},{10,... | collective-permute-start | bytes 2626568 | tf_op jit(solution)/shard_map/ppermute | solution.py:17
  64.0 24.3 %collective-permute-start.6 = (bf16[38,16,720]{2,1,0:T(8,128)(2,1)}, bf16[38,16,720]{2,1,0:T(8,128)(2,1)}, u32[]{:S(2)}, u32[]{:S(2)}) collective-permute-start(bf16[38,16,720]{2,1,0:T(8,128)(2,1)} %get-tuple-element.121), channel_id=1, source_target_pairs={{0,4},{1,5},{2,6},{3,7},{4,0},{5,1},{6,2},{7,3},{8,12},{9,13},{10,... | collective-permute-start | bytes 2626568 | tf_op jit(solution)/shard_map/ppermute | solution.py:17
  69.5 25.7 %all-to-all-start.1 = ((bf16[8,64,720]{2,1,0:T(8,128)(2,1)}), bf16[8,64,720]{2,1,0:T(8,128)(2,1)}, u32[]{:S(2)}, u32[]{:S(2)}) async-start(bf16[8,64,720]{2,1,0:T(8,128)(2,1)} %copy-done.8), calls=%async_computation.1 | async-start | bytes 1572864 | tf_op jit(solution)/shard_map/all_to_all | solution.py:464
  74.3 130.3 %all-gather.10.cloned.1.call-start = ((), (), s32[]{:S(2)}) async-start(), calls=%async_computation.4 | async-start | bytes 3932160 | tf_op jit(solution)/shard_map/all_gather | solution.py:490
  109.5 23.4 %collective-permute-start.7 = (bf16[38,16,720]{2,1,0:T(8,128)(2,1)}, bf16[38,16,720]{2,1,0:T(8,128)(2,1)}, u32[]{:S(2)}, u32[]{:S(2)}) collective-permute-start(bf16[38,16,720]{2,1,0:T(8,128)(2,1)} %copy-done.20), channel_id=1, source_target_pairs={{0,3},{1,2},{2,1},{3,0},{4,7},{5,6},{6,5},{7,4},{8,11},{9,10},{10,... | collective-permute-start | bytes 2626568 | tf_op jit(solution)/shard_map/ppermute | solution.py:17
  110.5 62.5 %collective-permute-start.8 = (bf16[38,16,720]{2,1,0:T(8,128)(2,1)}, bf16[38,16,720]{2,1,0:T(8,128)(2,1)}, u32[]{:S(2)}, u32[]{:S(2)}) collective-permute-start(bf16[38,16,720]{2,1,0:T(8,128)(2,1)} %copy-done.19), channel_id=1, source_target_pairs={{0,5},{1,4},{2,7},{3,6},{4,1},{5,0},{6,3},{7,2},{8,13},{9,12},{10,... | collective-permute-start | bytes 2626568 | tf_op jit(solution)/shard_map/ppermute | solution.py:17
  111.3 64.2 %collective-permute-start.12 = (bf16[256,2304]{1,0:T(8,128)(2,1)}, bf16[256,2304]{1,0:T(8,128)(2,1)}, u32[]{:S(2)}, u32[]{:S(2)}) collective-permute-start(bf16[256,2304]{1,0:T(8,128)(2,1)} %all-gather.6.cloned.1.call-done.own_ref), channel_id=1, source_target_pairs={{0,1},{1,0},{2,3},{3,2},{4,5},{5,4},{6,7},{7,6},{8,9},{9,8},{10,11... | collective-permute-start | bytes 3538952 | tf_op jit(solution)/shard_map/ppermute | solution.py:17
  112.1 62.3 %collective-permute-start.10 = (bf16[38,16,720]{2,1,0:T(8,128)(2,1)}, bf16[38,16,720]{2,1,0:T(8,128)(2,1)}, u32[]{:S(2)}, u32[]{:S(2)}) collective-permute-start(bf16[38,16,720]{2,1,0:T(8,128)(2,1)} %copy-done.18), channel_id=1, source_target_pairs={{0,6},{1,7},{2,4},{3,5},{4,2},{5,3},{6,0},{7,1},{8,14},{9,15},{10,... | collective-permute-start | bytes 2626568 | tf_op jit(solution)/shard_map/ppermute | solution.py:17
  113.6 60.8 %collective-permute-start.11 = (bf16[38,16,720]{2,1,0:T(8,128)(2,1)}, bf16[38,16,720]{2,1,0:T(8,128)(2,1)}, u32[]{:S(2)}, u32[]{:S(2)}) collective-permute-start(bf16[38,16,720]{2,1,0:T(8,128)(2,1)} %copy-done.17), channel_id=1, source_target_pairs={{0,7},{1,6},{2,5},{3,4},{4,3},{5,2},{6,1},{7,0},{8,15},{9,14},{10,... | collective-permute-start | bytes 2626568 | tf_op jit(solution)/shard_map/ppermute | solution.py:17
  198.0 16.8 %collective-permute-start.16 = (bf16[64,2304]{1,0:T(8,128)(2,1)}, bf16[64,2304]{1,0:T(8,128)(2,1)}, u32[]{:S(2)}, u32[]{:S(2)}) collective-permute-start(bf16[64,2304]{1,0:T(8,128)(2,1)} %get-tuple-element.145), channel_id=1, source_target_pairs={{0,2},{1,3},{2,0},{3,1},{4,6},{5,7},{6,4},{7,5},{8,10},{9,11},{10,... | collective-permute-start | bytes 884744 | tf_op jit(solution)/shard_map/ppermute | solution.py:17
  199.2 22.9 %collective-permute-start.17 = (bf16[64,2304]{1,0:T(8,128)(2,1)}, bf16[64,2304]{1,0:T(8,128)(2,1)}, u32[]{:S(2)}, u32[]{:S(2)}) collective-permute-start(bf16[64,2304]{1,0:T(8,128)(2,1)} %get-tuple-element.146), channel_id=1, source_target_pairs={{0,4},{1,5},{2,6},{3,7},{4,0},{5,1},{6,2},{7,3},{8,12},{9,13},{10,... | collective-permute-start | bytes 884744 | tf_op jit(solution)/shard_map/ppermute | solution.py:17
  199.8 22.2 %collective-permute-start.18 = (bf16[64,2304]{1,0:T(8,128)(2,1)}, bf16[64,2304]{1,0:T(8,128)(2,1)}, u32[]{:S(2)}, u32[]{:S(2)}) collective-permute-start(bf16[64,2304]{1,0:T(8,128)(2,1)} %get-tuple-element.147), channel_id=1, source_target_pairs={{0,6},{1,7},{2,4},{3,5},{4,2},{5,3},{6,0},{7,1},{8,14},{9,15},{10,... | collective-permute-start | bytes 884744 | tf_op jit(solution)/shard_map/ppermute | solution.py:17
  201.9 27.2 %collective-permute-start.21 = (bf16[64,2304]{1,0:T(8,128)(2,1)S(1)}, bf16[64,2304]{1,0:T(8,128)(2,1)}, u32[]{:S(2)}, u32[]{:S(2)}) collective-permute-start(bf16[64,2304]{1,0:T(8,128)(2,1)S(1)} %fusion.9), channel_id=1, source_target_pairs={{0,6},{1,7},{2,4},{3,5},{4,2},{5,3},{6,0},{7,1},{8,14},{9,15},{10,... | collective-permute-start | bytes 884744 | tf_op jit(solution)/shard_map/ppermute | solution.py:17
  203.2 26.0 %collective-permute-start.20 = (bf16[64,2304]{1,0:T(8,128)(2,1)S(1)}, bf16[64,2304]{1,0:T(8,128)(2,1)}, u32[]{:S(2)}, u32[]{:S(2)}) collective-permute-start(bf16[64,2304]{1,0:T(8,128)(2,1)S(1)} %fusion.9), channel_id=1, source_target_pairs={{0,4},{1,5},{2,6},{3,7},{4,0},{5,1},{6,2},{7,3},{8,12},{9,13},{10,... | collective-permute-start | bytes 884744 | tf_op jit(solution)/shard_map/ppermute | solution.py:17
  230.6 16.0 %collective-permute-start.25 = (bf16[64,2304]{1,0:T(8,128)(2,1)S(1)}, bf16[64,2304]{1,0:T(8,128)(2,1)S(1)}, u32[]{:S(2)}, u32[]{:S(2)}) collective-permute-start(bf16[64,2304]{1,0:T(8,128)(2,1)S(1)} %fusion.12), channel_id=1, source_target_pairs={{0,6},{1,7},{2,4},{3,5},{4,2},{5,3},{6,0},{7,1},{8,14},{9,15},{10,... | collective-permute-start | bytes 884744 | tf_op jit(solution)/shard_map/ppermute | solution.py:17
  273.2 16.0 %collective-permute-start.33 = (bf16[64,2304]{1,0:T(8,128)(2,1)}, bf16[64,2304]{1,0:T(8,128)(2,1)S(1)}, u32[]{:S(2)}, u32[]{:S(2)}) collective-permute-start(bf16[64,2304]{1,0:T(8,128)(2,1)} %get-tuple-element.225), channel_id=1, source_target_pairs={{0,4},{1,5},{2,6},{3,7},{4,0},{5,1},{6,2},{7,3},{8,12},{9,13},{10,... | collective-permute-start | bytes 884744 | tf_op jit(solution)/shard_map/ppermute | solution.py:17
  (54 other events, 647.3 us)
Sparse Core Ops, SparseCore 0:
  9.6 31.0 all-gather.5
  42.2 67.2 all-gather.7
  111.1 62.1 all-gather.9

commit v9 on v8

--- a/solution.py
+++ b/solution.py
@@ -471,10 +471,13 @@
 
     first = [1, 2, 4][: size.bit_length() - 1]
     rest = [k for k in range(3, size) if k not in first]
+    rest = sorted(rest, key=lambda k: k % 2)
     early = [send(parts[k], size, k) for k in first]
-    late = list(lax.optimization_barrier((*[parts[k] for k in rest], *early)))
-    early = late[len(rest) :]
-    late = [send(block, size, k) for block, k in zip(late, rest)]
+    after = list(lax.optimization_barrier((*[parts[k] for k in rest], *early)))
+    early = after[len(rest) :] + [send(after[0], size, rest[0])]
+    late = list(lax.optimization_barrier((*after[1 : len(rest)], *early)))
+    early = late[len(rest) - 1 :]
+    late = [send(block, size, k) for block, k in zip(late, rest[1:])]
 
     half_dim = HEAD_DIM // 2
     inv_freq = jnp.power(

time: 305 us -> 292 us (0.957)
  waiting for transfers between devices: 110 us -> 95.4 us
    all_gather x1, waiting for transfers between devices: 14.3 us -> 0.01 us  [shards(): qkv_all = lax.all_gather(qkv_cols, 'dp', axis=0)]
    unnamed x78 -> x90, local copies, waits for them, and re-layouts: 31.1 us -> 34.1 us
  transfers between devices with their start and end apart: 40 -> 40, of which waited for: 16 -> 15; matrix products, arithmetic and copies ran while one was open for 12% -> 12% of each run, Pallas kernels for 23% -> 24%
where the time goes in v9:
time: 292 us; the launch traced here: 288 us
  waiting for transfers between devices  95.4 us (33%)
  Pallas kernels  68.2 us (23%)
  local copies, waits for them, and re-layouts  45.9 us (16%)
  starting transfers between devices  42.6 us (15%)
  other arithmetic  20.4 us (7%)
  between operations  15.5 us (5%)
    ppermute x35, waiting for transfers between devices, send(): return lax.ppermute(block, 'tensor', swap_pairs(size, step))  95.3 us
    unnamed x90, local copies, waits for them, and re-layouts  34.1 us
    ppermute x35, starting transfers between devices, send(): return lax.ppermute(block, 'tensor', swap_pairs(size, step))  32.8 us
    pallas_call x2, Pallas kernels, expert(): pl.pallas_call(kernel, out_shape=[jax.ShapeDtypeStruct((rows, model), jnp...  22.7 us
    pallas_call x1, Pallas kernels, attention(): pl.pallas_call(kernel, out_shape=(jax.ShapeDtypeStruct((2, seq, width), j...  14.3 us
    pallas_call x3, Pallas kernels, copy_rows(): pl.pallas_call(kernel, out_shape=[jax.ShapeDtypeStruct(shape, jnp.bfloat1...  13.9 us
    pallas_call x1, Pallas kernels, split_columns(): pl.pallas_call(kernel, out_shape=[jax.ShapeDtypeStruct(((2 * rows + tail)...  9.43 us
  transfers between devices with their start and end apart: 40, of which 15 were waited for; matrix products, arithmetic and copies ran while one was open for 12% of the time, Pallas kernels for 24%

profile of v9, /device:TPU:12, one launch (start us, length us, event | category | flops | bytes accessed | tf_op | source)
XLA Modules:
  0.0 288.3 jit_solution(13251688130935717540)
XLA Ops:
  9.1 2.5 split_heads.1
  11.6 4.4 %all-to-all-start = ((bf16[8,3,72,256]{3,2,1,0:T(8,128)(2,1)}), bf16[8,3,72,256]{3,2,1,0:T(8,128)(2,1)S(1)}, u32[]{:S(2)}, u32[]{:S(2)}) async-start(bf16[8,3,72,256]{3,2,1,0:T(8,128)(2,1)} %split_heads.1), calls=%async_computation | async-start | bytes 1769472 | tf_op jit(solution)/shard_map/all_to_all | solution.py:455
  17.3 9.4 %split_columns.1 = (bf16[38,16,720]{2,1,0:T(8,128)(2,1)S(1)}, bf16[38,16,720]{2,1,0:T(8,128)(2,1)}, bf16[38,16,720]{2,1,0:T(8,128)(2,1)S(1)}, bf16[38,16,720]{2,...) custom-call(s32[1]{0:T(128)} %bitcast.2.me_ref, ...), custom_call_target="tpu_custom_call" | custom-call | tf_op jit(solution)/shard_map/split_columns/pallas_call | solution.py:91
  36.1 13.6 %collective-permute-done.2 = bf16[128,2304]{1,0:T(8,128)(2,1)S(1)} collective-permute-done((bf16[128,2304]{1,0:T(8,128)(2,1)S(1)}, bf16[128,2304]{1,0:T(8,128)(2,1)S(1)}, u32[]{:S(2)}, u32[]{:S(2)}) %collective-permute-start.2) | collective-permute-done | bytes 589856 | tf_op jit(solution)/shard_map/ppermute | solution.py:17
  49.8 11.8 %collective-permute-done.1 = bf16[128,2304]{1,0:T(8,128)(2,1)S(1)} collective-permute-done((bf16[128,2304]{1,0:T(8,128)(2,1)S(1)}, bf16[128,2304]{1,0:T(8,128)(2,1)S(1)}, u32[]{:S(2)}, u32[]{:S(2)}) %collective-permute-start.1) | collective-permute-done | bytes 589856 | tf_op jit(solution)/shard_map/ppermute | solution.py:17
  65.9 3.3 %collective-permute-done.4.refs_2_.refs_1_ = bf16[38,16,720]{2,1,0:T(8,128)(2,1)S(1)} collective-permute-done((bf16[38,16,720]{2,1,0:T(8,128)(2,1)}, bf16[38,16,720]{2,1,0:T(8,128)(2,1)S(1)}, u32[]{:S(2)}, u32[]{:S(2)}) %collective-permute-start.4) | collective-permute-done | bytes 875552 | tf_op jit(solution)/shard_map/ppermute | solution.py:17
  69.2 17.4 %collective-permute-done.5.refs_3_.refs_2_ = bf16[38,16,720]{2,1,0:T(8,128)(2,1)S(1)} collective-permute-done((bf16[38,16,720]{2,1,0:T(8,128)(2,1)S(1)}, bf16[38,16,720]{2,1,0:T(8,128)(2,1)S(1)}, u32[]{:S(2)}, u32[]{:S(2)}) %collective-permute-start.5) | collective-permute-done | bytes 875552 | tf_op jit(solution)/shard_map/ppermute | solution.py:17
  89.4 2.9 %copy-done.2 = f32[288,5760]{1,0:T(8,128)S(1)} copy-done((f32[288,5760]{1,0:T(8,128)S(1)}, f32[288,5760]{1,0:T(8,128)}, u32[]{:S(2)}) %copy-start.2) | copy-done | bytes 6635544
  93.5 5.4 %all-to-all-start.1 = ((bf16[8,64,720]{2,1,0:T(8,128)(2,1)}), bf16[8,64,720]{2,1,0:T(8,128)(2,1)}, u32[]{:S(2)}, u32[]{:S(2)}) async-start(bf16[8,64,720]{2,1,0:T(8,128)(2,1)} %copy-done.11), calls=%async_computation.1 | async-start | bytes 1572864 | tf_op jit(solution)/shard_map/all_to_all | solution.py:464
  99.7 5.5 %multiply_sine_fusion = (f32[1024,256]{1,0:T(8,128)}, f32[1024,256]{1,0:T(8,128)}) fusion(f32[256]{0:T(256)S(1)} %mul.108, f32[1024]{0:T(1024)S(1)} %add_convert_fusion.6), kind=kLoop, calls=%fused_computation.1 | loop fusion | flops 262144 | bytes 2102272 | tf_op jit(solution)/shard_map/sin | solution.py:488
  105.2 7.7 %collective-permute-done.7.refs_7_.refs_6_ = bf16[38,16,720]{2,1,0:T(8,128)(2,1)} collective-permute-done((bf16[38,16,720]{2,1,0:T(8,128)(2,1)}, bf16[38,16,720]{2,1,0:T(8,128)(2,1)}, u32[]{:S(2)}, u32[]{:S(2)}) %collective-permute-start.7) | collective-permute-done | bytes 875552 | tf_op jit(solution)/shard_map/ppermute | solution.py:17
  125.9 14.3 %attention.1 = (bf16[2,1024,256]{2,1,0:T(8,128)(2,1)}, bf16[2,512,256]{2,1,0:T(8,128)(2,1)S(1)}) custom-call(s32[2]{0:T(128)S(1)} %pad_add_fusion.s_ref, bf16[1024,2304]{1,0:T(8,128)(2,1)} %bitcast.109, bf16[3,2304,256]{2,1,0:T(8,128)(2,1)S(1)} %bitcast.110, f32[1024,256]{1,0:T(8,128)S(1)} %copy-done.19, f32[1024,256]{1,0:T(8,128)S(1)} %copy-done.18), custom_call_target="tpu_custom_call" | custom-call | flops 4697620480 | bytes 8257536 | tf_op jit(solution)/shard_map/attention/pallas_call | solution.py:386
  140.2 2.5 collective-permute-done.8.refs_4_.refs_3_
  143.5 21.2 %collective-permute-done.10.refs_6_.refs_5_ = bf16[38,16,720]{2,1,0:T(8,128)(2,1)} collective-permute-done((bf16[38,16,720]{2,1,0:T(8,128)(2,1)}, bf16[38,16,720]{2,1,0:T(8,128)(2,1)}, u32[]{:S(2)}, u32[]{:S(2)}) %collective-permute-start.10) | collective-permute-done | bytes 875552 | tf_op jit(solution)/shard_map/ppermute | solution.py:17
  165.4 5.1 %project.1 = (f32[64,2304]{1,0:T(8,128)}, f32[64,2304]{1,0:T(8,128)}, bf16[64,2304]{1,0:T(8,128)(2,1)}, bf16[64,2304]{1,0:T(8,128)(2,1)}, bf16[64,2304]{1,0:T(8,...) custom-call(s32[1]{0:T(128)} %bitcast.22.chip_ref, ...), custom_call_target="tpu_custom_call" | custom-call | tf_op jit(solution)/shard_map/project/pallas_call | solution.py:225
  174.1 4.9 %join_gate_up.1 = (bf16[144,16,720]{2,1,0:T(8,128)(2,1)S(1)}, bf16[144,16,720]{2,1,0:T(8,128)(2,1)S(1)}) custom-call(s32[1]{0:T(128)} %bitcast.2.me_ref, bf16[38,16,720]{2,1,0:T(8,128)(2,1)S(1)} %get-tuple-element.163.refs_1_.refs_0_, bf16[38,16,720]{2,1,0:T(8,128)(2,1)S(1)} %collective-permute-done.4.refs_2_.refs_1_, ...), custom_call_target="tpu_custom_call" | custom-call | tf_op jit(solution)/shard_map/join_gate_up/pallas_call | solution.py:125
  180.8 6.0 %collective-permute-done.14 = bf16[64,2304]{1,0:T(8,128)(2,1)S(1)} collective-permute-done((bf16[64,2304]{1,0:T(8,128)(2,1)}, bf16[64,2304]{1,0:T(8,128)(2,1)S(1)}, u32[]{:S(2)}, u32[]{:S(2)}) %collective-permute-start.14) | collective-permute-done | bytes 294944 | tf_op jit(solution)/shard_map/ppermute | solution.py:17
  196.5 6.6 %join_down.1 = bf16[144,16,720]{2,1,0:T(8,128)(2,1)S(1)} custom-call(s32[1]{0:T(128)} %bitcast.2.me_ref, bf16[4,8,4,16,720]{4,3,2,1,0:T(8,128)(2,1)S(1)} %bitcast.118, bf16[38,16,720]{2,1,0:T(8,128)(2,1)S(1)} %get-tuple-element.163.refs_1_.refs_0_, bf16[38,16,720]{2,1,0:T(8,128)(2,1)S(1)} %collective-permute-done.4.refs_2_.refs_1_, ...), custom_call_target="tpu_custom_call" | custom-call | tf_op jit(solution)/shard_map/join_down/pallas_call | solution.py:125
  205.9 5.1 %collective-permute-done.17 = bf16[64,2304]{1,0:T(8,128)(2,1)} collective-permute-done((bf16[64,2304]{1,0:T(8,128)(2,1)}, bf16[64,2304]{1,0:T(8,128)(2,1)}, u32[]{:S(2)}, u32[]{:S(2)}) %collective-permute-start.17) | collective-permute-done | bytes 294944 | tf_op jit(solution)/shard_map/ppermute | solution.py:17
  212.4 5.6 %copy.24 = bf16[2304,720]{0,1:T(8,128)(2,1)} copy(bf16[2304,720]{1,0:T(8,128)(2,1)} %bitcast.115) | data formatting | bytes 6635520 | tf_op jit(solution)/shard_map/optimization_barrier | solution.py:528
  224.1 11.4 %expert.2 = (bf16[256,2304]{1,0:T(8,128)(2,1)}, bf16[256,2304]{1,0:T(8,128)(2,1)}) custom-call(bf16[256,2304]{1,0:T(8,128)(2,1)} %bitcast.136, bf16[256,2304]{1,0:T(8,128)(2,1)} %bitcast.142, bf16[2304,720]{1,0:T(8,128)(2,1)} %bitcast.112, bf16[2304,720]{1,0:T(8,128)(2,1)} %bitcast.116, bf16[2304,720]{1,0:T(8,128)(2,1)} %bitcast.104), custom_call_target="tpu_custom_call" | custom-call | flops 5096079360 | bytes 9953280 | tf_op jit(solution)/shard_map/expert/pallas_call | solution.py:287
  244.7 11.4 %expert.3 = (bf16[256,2304]{1,0:T(8,128)(2,1)}, bf16[256,2304]{1,0:T(8,128)(2,1)}) custom-call(bf16[256,2304]{1,0:T(8,128)(2,1)} %bitcast.135, bf16[256,2304]{1,0:T(8,128)(2,1)} %bitcast.141, bf16[2304,720]{1,0:T(8,128)(2,1)} %bitcast.113, bf16[2304,720]{1,0:T(8,128)(2,1)} %bitcast.117, bf16[2304,720]{1,0:T(8,128)(2,1)} %bitcast.105), custom_call_target="tpu_custom_call" | custom-call | flops 5096079360 | bytes 9953280 | tf_op jit(solution)/shard_map/expert/pallas_call | solution.py:287
  266.9 5.6 %copy.25 = bf16[2304,720]{0,1:T(8,128)(2,1)} copy(bf16[2304,720]{1,0:T(8,128)(2,1)} %bitcast.114) | data formatting | bytes 6635520
  272.5 5.6 %copy.26 = bf16[2304,720]{0,1:T(8,128)(2,1)} copy(bf16[2304,720]{1,0:T(8,128)(2,1)} %bitcast.106) | data formatting | bytes 6635520
  (195 shorter events, 83.6 us)
Async XLA Ops:
  7.2 112.1 %all-gather.6.cloned.1.call-start = ((), (), s32[]{:S(2)}) async-start(), calls=%async_computation.2 | async-start | bytes 1474560 | tf_op jit(solution)/shard_map/all_gather | solution.py:489
  11.6 20.1 %all-to-all-start = ((bf16[8,3,72,256]{3,2,1,0:T(8,128)(2,1)}), bf16[8,3,72,256]{3,2,1,0:T(8,128)(2,1)S(1)}, u32[]{:S(2)}, u32[]{:S(2)}) async-start(bf16[8,3,72,256]{3,2,1,0:T(8,128)(2,1)} %split_heads.1), calls=%async_computation | async-start | bytes 1769472 | tf_op jit(solution)/shard_map/all_to_all | solution.py:455
  15.9 103.4 %all-gather.8.cloned.1.call-start = ((), (), s32[]{:S(2)}) async-start(), calls=%async_computation.3 | async-start | bytes 4423680 | tf_op jit(solution)/shard_map/all_gather | solution.py:462
  32.6 17.2 %collective-permute-start.2 = (bf16[128,2304]{1,0:T(8,128)(2,1)S(1)}, bf16[128,2304]{1,0:T(8,128)(2,1)S(1)}, u32[]{:S(2)}, u32[]{:S(2)}) collective-permute-start(bf16[128,2304]{1,0:T(8,128)(2,1)S(1)} %fusion.6), channel_id=1, source_target_pairs={{0,6},{1,7},{2,4},{3,5},{4,2},{5,3},{6,0},{7,1},{8,14},{9,15},{10,... | collective-permute-start | bytes 1769480 | tf_op jit(solution)/shard_map/ppermute | solution.py:17
  34.1 27.4 %collective-permute-start.1 = (bf16[128,2304]{1,0:T(8,128)(2,1)S(1)}, bf16[128,2304]{1,0:T(8,128)(2,1)S(1)}, u32[]{:S(2)}, u32[]{:S(2)}) collective-permute-start(bf16[128,2304]{1,0:T(8,128)(2,1)S(1)} %fusion.6), channel_id=1, source_target_pairs={{0,4},{1,5},{2,6},{3,7},{4,0},{5,1},{6,2},{7,3},{8,12},{9,13},{10,... | collective-permute-start | bytes 1769480 | tf_op jit(solution)/shard_map/ppermute | solution.py:17
  35.6 26.0 %collective-permute-start = (bf16[128,2304]{1,0:T(8,128)(2,1)S(1)}, bf16[128,2304]{1,0:T(8,128)(2,1)S(1)}, u32[]{:S(2)}, u32[]{:S(2)}) collective-permute-start(bf16[128,2304]{1,0:T(8,128)(2,1)S(1)} %fusion.6), channel_id=1, source_target_pairs={{0,2},{1,3},{2,0},{3,1},{4,6},{5,7},{6,4},{7,5},{8,10},{9,11},{10,... | collective-permute-start | bytes 1769480 | tf_op jit(solution)/shard_map/ppermute | solution.py:17
  63.3 49.6 %collective-permute-start.3 = (bf16[4,128,2304]{2,1,0:T(8,128)(2,1)}, bf16[4,128,2304]{2,1,0:T(8,128)(2,1)}, u32[]{:S(2)}, u32[]{:S(2)}) collective-permute-start(bf16[4,128,2304]{2,1,0:T(8,128)(2,1)} %pad_maximum_fusion), channel_id=1, source_target_pairs={{0,1},{1,0},{2,3},{3,2},{4,5},{5,4},{6,7},{7,6},{8,9},{9,8},{10,11... | collective-permute-start | bytes 7077896 | tf_op jit(solution)/shard_map/ppermute | solution.py:17
  63.8 22.7 %collective-permute-start.5 = (bf16[38,16,720]{2,1,0:T(8,128)(2,1)S(1)}, bf16[38,16,720]{2,1,0:T(8,128)(2,1)S(1)}, u32[]{:S(2)}, u32[]{:S(2)}) collective-permute-start(bf16[38,16,720]{2,1,0:T(8,128)(2,1)S(1)} %copy-done.26), channel_id=1, source_target_pairs={{0,2},{1,3},{2,0},{3,1},{4,6},{5,7},{6,4},{7,5},{8,10},{9,11},{10,... | collective-permute-start | bytes 2626568 | tf_op jit(solution)/shard_map/ppermute | solution.py:17
  64.5 22.5 %collective-permute-start.6 = (bf16[38,16,720]{2,1,0:T(8,128)(2,1)S(1)}, bf16[38,16,720]{2,1,0:T(8,128)(2,1)S(1)}, u32[]{:S(2)}, u32[]{:S(2)}) collective-permute-start(bf16[38,16,720]{2,1,0:T(8,128)(2,1)S(1)} %copy-done.24), channel_id=1, source_target_pairs={{0,4},{1,5},{2,6},{3,7},{4,0},{5,1},{6,2},{7,3},{8,12},{9,13},{10,... | collective-permute-start | bytes 2626568 | tf_op jit(solution)/shard_map/ppermute | solution.py:17
  87.9 24.9 %collective-permute-start.7 = (bf16[38,16,720]{2,1,0:T(8,128)(2,1)}, bf16[38,16,720]{2,1,0:T(8,128)(2,1)}, u32[]{:S(2)}, u32[]{:S(2)}) collective-permute-start(bf16[38,16,720]{2,1,0:T(8,128)(2,1)} %get-tuple-element.135), channel_id=1, source_target_pairs={{0,6},{1,7},{2,4},{3,5},{4,2},{5,3},{6,0},{7,1},{8,14},{9,15},{10,... | collective-permute-start | bytes 2626568 | tf_op jit(solution)/shard_map/ppermute | solution.py:17
  93.5 25.8 %all-to-all-start.1 = ((bf16[8,64,720]{2,1,0:T(8,128)(2,1)}), bf16[8,64,720]{2,1,0:T(8,128)(2,1)}, u32[]{:S(2)}, u32[]{:S(2)}) async-start(bf16[8,64,720]{2,1,0:T(8,128)(2,1)} %copy-done.11), calls=%async_computation.1 | async-start | bytes 1572864 | tf_op jit(solution)/shard_map/all_to_all | solution.py:464
  99.0 94.4 %all-gather.10.cloned.1.call-start = ((), (), s32[]{:S(2)}) async-start(), calls=%async_computation.4 | async-start | bytes 3932160 | tf_op jit(solution)/shard_map/all_gather | solution.py:493
  119.4 23.4 %collective-permute-start.8 = (bf16[38,16,720]{2,1,0:T(8,128)(2,1)}, bf16[38,16,720]{2,1,0:T(8,128)(2,1)}, u32[]{:S(2)}, u32[]{:S(2)}) collective-permute-start(bf16[38,16,720]{2,1,0:T(8,128)(2,1)} %copy-done.22), channel_id=1, source_target_pairs={{0,3},{1,2},{2,1},{3,0},{4,7},{5,6},{6,5},{7,4},{8,11},{9,10},{10,... | collective-permute-start | bytes 2626568 | tf_op jit(solution)/shard_map/ppermute | solution.py:17
  120.2 44.4 %collective-permute-start.12 = (bf16[256,2304]{1,0:T(8,128)(2,1)}, bf16[256,2304]{1,0:T(8,128)(2,1)}, u32[]{:S(2)}, u32[]{:S(2)}) collective-permute-start(bf16[256,2304]{1,0:T(8,128)(2,1)} %all-gather.6.cloned.1.call-done.own_ref), channel_id=1, source_target_pairs={{0,1},{1,0},{2,3},{3,2},{4,5},{5,4},{6,7},{7,6},{8,9},{9,8},{10,11... | collective-permute-start | bytes 3538952 | tf_op jit(solution)/shard_map/ppermute | solution.py:17
  121.5 43.2 %collective-permute-start.10 = (bf16[38,16,720]{2,1,0:T(8,128)(2,1)}, bf16[38,16,720]{2,1,0:T(8,128)(2,1)}, u32[]{:S(2)}, u32[]{:S(2)}) collective-permute-start(bf16[38,16,720]{2,1,0:T(8,128)(2,1)} %copy-done.21), channel_id=1, source_target_pairs={{0,5},{1,4},{2,7},{3,6},{4,1},{5,0},{6,3},{7,2},{8,13},{9,12},{10,... | collective-permute-start | bytes 2626568 | tf_op jit(solution)/shard_map/ppermute | solution.py:17
  122.0 42.7 %collective-permute-start.11 = (bf16[38,16,720]{2,1,0:T(8,128)(2,1)}, bf16[38,16,720]{2,1,0:T(8,128)(2,1)}, u32[]{:S(2)}, u32[]{:S(2)}) collective-permute-start(bf16[38,16,720]{2,1,0:T(8,128)(2,1)} %copy-done.20), channel_id=1, source_target_pairs={{0,7},{1,6},{2,5},{3,4},{4,3},{5,2},{6,1},{7,0},{8,15},{9,14},{10,... | collective-permute-start | bytes 2626568 | tf_op jit(solution)/shard_map/ppermute | solution.py:17
  143.5 21.2 %collective-permute-start.9 = (bf16[512,256]{1,0:T(8,128)(2,1)S(1)}, bf16[512,256]{1,0:T(8,128)(2,1)S(1)}, u32[]{:S(2)}, u32[]{:S(2)}) collective-permute-start(bf16[512,256]{1,0:T(8,128)(2,1)S(1)} %get-tuple-element.249), channel_id=1, source_target_pairs={{0,1},{1,0},{2,3},{3,2},{4,5},{5,4},{6,7},{7,6},{8,9},{9,8},{10,11... | collective-permute-start | bytes 786440 | tf_op jit(solution)/shard_map/ppermute | solution.py:17
  186.9 17.9 %collective-permute-start.16 = (bf16[64,2304]{1,0:T(8,128)(2,1)}, bf16[64,2304]{1,0:T(8,128)(2,1)}, u32[]{:S(2)}, u32[]{:S(2)}) collective-permute-start(bf16[64,2304]{1,0:T(8,128)(2,1)} %get-tuple-element.159), channel_id=1, source_target_pairs={{0,2},{1,3},{2,0},{3,1},{4,6},{5,7},{6,4},{7,5},{8,10},{9,11},{10,... | collective-permute-start | bytes 884744 | tf_op jit(solution)/shard_map/ppermute | solution.py:17
  188.0 22.9 %collective-permute-start.17 = (bf16[64,2304]{1,0:T(8,128)(2,1)}, bf16[64,2304]{1,0:T(8,128)(2,1)}, u32[]{:S(2)}, u32[]{:S(2)}) collective-permute-start(bf16[64,2304]{1,0:T(8,128)(2,1)} %get-tuple-element.160), channel_id=1, source_target_pairs={{0,4},{1,5},{2,6},{3,7},{4,0},{5,1},{6,2},{7,3},{8,12},{9,13},{10,... | collective-permute-start | bytes 884744 | tf_op jit(solution)/shard_map/ppermute | solution.py:17
  188.8 22.1 %collective-permute-start.18 = (bf16[64,2304]{1,0:T(8,128)(2,1)}, bf16[64,2304]{1,0:T(8,128)(2,1)}, u32[]{:S(2)}, u32[]{:S(2)}) collective-permute-start(bf16[64,2304]{1,0:T(8,128)(2,1)} %get-tuple-element.161), channel_id=1, source_target_pairs={{0,6},{1,7},{2,4},{3,5},{4,2},{5,3},{6,0},{7,1},{8,14},{9,15},{10,... | collective-permute-start | bytes 884744 | tf_op jit(solution)/shard_map/ppermute | solution.py:17
  190.8 27.2 %collective-permute-start.21 = (bf16[64,2304]{1,0:T(8,128)(2,1)S(1)}, bf16[64,2304]{1,0:T(8,128)(2,1)}, u32[]{:S(2)}, u32[]{:S(2)}) collective-permute-start(bf16[64,2304]{1,0:T(8,128)(2,1)S(1)} %fusion.9), channel_id=1, source_target_pairs={{0,6},{1,7},{2,4},{3,5},{4,2},{5,3},{6,0},{7,1},{8,14},{9,15},{10,... | collective-permute-start | bytes 884744 | tf_op jit(solution)/shard_map/ppermute | solution.py:17
  192.1 25.9 %collective-permute-start.20 = (bf16[64,2304]{1,0:T(8,128)(2,1)S(1)}, bf16[64,2304]{1,0:T(8,128)(2,1)}, u32[]{:S(2)}, u32[]{:S(2)}) collective-permute-start(bf16[64,2304]{1,0:T(8,128)(2,1)S(1)} %fusion.9), channel_id=1, source_target_pairs={{0,4},{1,5},{2,6},{3,7},{4,0},{5,1},{6,2},{7,3},{8,12},{9,13},{10,... | collective-permute-start | bytes 884744 | tf_op jit(solution)/shard_map/ppermute | solution.py:17
  219.5 16.0 %collective-permute-start.25 = (bf16[64,2304]{1,0:T(8,128)(2,1)S(1)}, bf16[64,2304]{1,0:T(8,128)(2,1)S(1)}, u32[]{:S(2)}, u32[]{:S(2)}) collective-permute-start(bf16[64,2304]{1,0:T(8,128)(2,1)S(1)} %fusion.12), channel_id=1, source_target_pairs={{0,6},{1,7},{2,4},{3,5},{4,2},{5,3},{6,0},{7,1},{8,14},{9,15},{10,... | collective-permute-start | bytes 884744 | tf_op jit(solution)/shard_map/ppermute | solution.py:17
  262.1 16.0 %collective-permute-start.33 = (bf16[64,2304]{1,0:T(8,128)(2,1)}, bf16[64,2304]{1,0:T(8,128)(2,1)S(1)}, u32[]{:S(2)}, u32[]{:S(2)}) collective-permute-start(bf16[64,2304]{1,0:T(8,128)(2,1)} %get-tuple-element.239), channel_id=1, source_target_pairs={{0,4},{1,5},{2,6},{3,7},{4,0},{5,1},{6,2},{7,3},{8,12},{9,13},{10,... | collective-permute-start | bytes 884744 | tf_op jit(solution)/shard_map/ppermute | solution.py:17
  (60 other events, 643.9 us)
Sparse Core Ops, SparseCore 0:
  9.6 31.0 all-gather.5
  42.2 67.2 all-gather.7
  119.5 62.0 all-gather.9

commit v10 on v9

--- a/solution.py
+++ b/solution.py
@@ -90,8 +90,7 @@
 
     return pl.pallas_call(
         kernel,
-        out_shape=[jax.ShapeDtypeStruct(((2 * rows + tail) // 16, 16, part), jnp.bfloat16)]
-        * parts,
+        out_shape=[pltpu.HBM(((2 * rows + tail) // 16, 16, part), jnp.bfloat16)] * parts,
         grid_spec=pltpu.PrefetchScalarGridSpec(
             num_scalar_prefetch=1,
             grid=(rows // chunk,),
@@ -124,7 +123,7 @@
 
     return pl.pallas_call(
         kernel,
-        out_shape=[jax.ShapeDtypeStruct(shape, jnp.bfloat16) for shape in outs_shape],
+        out_shape=[pltpu.HBM(shape, jnp.bfloat16) for shape in outs_shape],
         grid_spec=pltpu.PrefetchScalarGridSpec(
             num_scalar_prefetch=1,
             grid=(1,),

time: 292 us -> 293 us (level)
  Pallas kernels: 68.2 us -> 74.4 us
  waiting for transfers between devices: 95.4 us -> 91.1 us
    pallas_call x4, Pallas kernels: 23.3 us -> 28.5 us  [the longest x3 21.1 us: copy_rows(): pl.pallas_call(kernel, out_shape=[pltpu.HBM(shape, jnp.bfloat16) for shap...]
    ppermute x35, waiting for transfers between devices: 95.3 us -> 91 us  [send(): return lax.ppermute(block, 'tensor', swap_pairs(size, step))]
  transfers between devices with their start and end apart: 40 -> 40, of which waited for: 15 -> 16; matrix products, arithmetic and copies ran while one was open for 12% -> 12% of each run, Pallas kernels for 24% -> 26%
where the time goes in v10:
time: 293 us; the launch traced here: 289 us
  waiting for transfers between devices  91.1 us (31%)
  Pallas kernels  74.4 us (25%)
  local copies, waits for them, and re-layouts  44.9 us (15%)
  starting transfers between devices  43 us (15%)
  other arithmetic  20.1 us (7%)
  between operations  15.5 us (5%)
    ppermute x35, waiting for transfers between devices, send(): return lax.ppermute(block, 'tensor', swap_pairs(size, step))  91 us
    unnamed x90, local copies, waits for them, and re-layouts  33 us
    ppermute x35, starting transfers between devices, send(): return lax.ppermute(block, 'tensor', swap_pairs(size, step))  33 us
    pallas_call x2, Pallas kernels, expert(): pl.pallas_call(kernel, out_shape=[jax.ShapeDtypeStruct((rows, model), jnp...  22.7 us
    pallas_call x3, Pallas kernels, copy_rows(): pl.pallas_call(kernel, out_shape=[pltpu.HBM(shape, jnp.bfloat16) for shap...  21.1 us
    pallas_call x1, Pallas kernels, attention(): pl.pallas_call(kernel, out_shape=(jax.ShapeDtypeStruct((2, seq, width), j...  14.3 us
    pallas_call x1, Pallas kernels, split_columns(): pl.pallas_call(kernel, out_shape=[pltpu.HBM(((2 * rows + tail) // 16, 16,...  7.46 us
  transfers between devices with their start and end apart: 40, of which 16 were waited for; matrix products, arithmetic and copies ran while one was open for 12% of the time, Pallas kernels for 26%

profile of v10, /device:TPU:12, one launch (start us, length us, event | category | flops | bytes accessed | tf_op | source)
XLA Modules:
  0.0 289.3 jit_solution(3697810139172267474)
XLA Ops:
  11.5 4.4 %all-to-all-start = ((bf16[8,3,72,256]{3,2,1,0:T(8,128)(2,1)}), bf16[8,3,72,256]{3,2,1,0:T(8,128)(2,1)S(1)}, u32[]{:S(2)}, u32[]{:S(2)}) async-start(bf16[8,3,72,256]{3,2,1,0:T(8,128)(2,1)} %split_heads.1), calls=%async_computation | async-start | bytes 1769472 | tf_op jit(solution)/shard_map/all_to_all | solution.py:454
  17.3 3.1 %copy-done.2 = f32[288,5760]{1,0:T(8,128)S(1)} copy-done((f32[288,5760]{1,0:T(8,128)S(1)}, f32[288,5760]{1,0:T(8,128)}, u32[]{:S(2)}) %copy-start.2) | copy-done | bytes 6635544
  20.4 2.9 copy-done.3
  23.3 7.5 %split_columns.1 = (bf16[38,16,720]{2,1,0:T(8,128)(2,1)}, bf16[38,16,720]{2,1,0:T(8,128)(2,1)}, bf16[38,16,720]{2,1,0:T(8,128)(2,1)}, bf16[38,16,720]{2,1,0:T(8,...) custom-call(s32[1]{0:T(128)} %bitcast.2.me_ref, ...), custom_call_target="tpu_custom_call" | custom-call | tf_op jit(solution)/shard_map/split_columns/pallas_call | solution.py:91
  35.5 13.6 %collective-permute-done.2 = bf16[128,2304]{1,0:T(8,128)(2,1)S(1)} collective-permute-done((bf16[128,2304]{1,0:T(8,128)(2,1)S(1)}, bf16[128,2304]{1,0:T(8,128)(2,1)S(1)}, u32[]{:S(2)}, u32[]{:S(2)}) %collective-permute-start.2) | collective-permute-done | bytes 589856 | tf_op jit(solution)/shard_map/ppermute | solution.py:17
  49.1 11.8 %collective-permute-done.1 = bf16[128,2304]{1,0:T(8,128)(2,1)S(1)} collective-permute-done((bf16[128,2304]{1,0:T(8,128)(2,1)S(1)}, bf16[128,2304]{1,0:T(8,128)(2,1)S(1)}, u32[]{:S(2)}, u32[]{:S(2)}) %collective-permute-start.1) | collective-permute-done | bytes 589856 | tf_op jit(solution)/shard_map/ppermute | solution.py:17
  68.3 18.1 %collective-permute-done.5.refs_3_.refs_2_ = bf16[38,16,720]{2,1,0:T(8,128)(2,1)S(1)} collective-permute-done((bf16[38,16,720]{2,1,0:T(8,128)(2,1)S(1)}, bf16[38,16,720]{2,1,0:T(8,128)(2,1)S(1)}, u32[]{:S(2)}, u32[]{:S(2)}) %collective-permute-start.5) | collective-permute-done | bytes 875552 | tf_op jit(solution)/shard_map/ppermute | solution.py:17
  89.1 2.9 %copy-done.1 = f32[288,5760]{1,0:T(8,128)S(1)} copy-done((f32[288,5760]{1,0:T(8,128)S(1)}, f32[288,5760]{1,0:T(8,128)}, u32[]{:S(2)}) %copy-start.1) | copy-done | bytes 6635544
  93.2 5.6 %all-to-all-start.1 = ((bf16[8,64,720]{2,1,0:T(8,128)(2,1)}), bf16[8,64,720]{2,1,0:T(8,128)(2,1)}, u32[]{:S(2)}, u32[]{:S(2)}) async-start(bf16[8,64,720]{2,1,0:T(8,128)(2,1)} %split_rows.1), calls=%async_computation.1 | async-start | bytes 1572864 | tf_op jit(solution)/shard_map/all_to_all | solution.py:463
  99.6 5.5 %multiply_sine_fusion = (f32[1024,256]{1,0:T(8,128)}, f32[1024,256]{1,0:T(8,128)}) fusion(f32[256]{0:T(256)S(1)} %mul.108, f32[1024]{0:T(1024)S(1)} %add_convert_fusion.6), kind=kLoop, calls=%fused_computation.1 | loop fusion | flops 262144 | bytes 2102272 | tf_op jit(solution)/shard_map/sin | solution.py:487
  105.1 7.5 %collective-permute-done.7.refs_7_.refs_6_ = bf16[38,16,720]{2,1,0:T(8,128)(2,1)} collective-permute-done((bf16[38,16,720]{2,1,0:T(8,128)(2,1)}, bf16[38,16,720]{2,1,0:T(8,128)(2,1)}, u32[]{:S(2)}, u32[]{:S(2)}) %collective-permute-start.7) | collective-permute-done | bytes 875552 | tf_op jit(solution)/shard_map/ppermute | solution.py:17
  114.3 4.6 %join_blocks.1 = bf16[64,16,2304]{2,1,0:T(8,128)(2,1)} custom-call(s32[1]{0:T(128)} %bitcast.2.me_ref, bf16[8,16,2304]{2,1,0:T(8,128)(2,1)S(1)} %bitcast.105, bf16[8,16,2304]{2,1,0:T(8,128)(2,1)S(1)} %bitcast.118, bf16[8,16,2304]{2,1,0:T(8,128)(2,1)S(1)} %bitcast.114, bf16[8,16,2304]{2,1,0:T(8,128)(2,1)S(1)} %bitcast.117, ...), custom_call_target="tpu_custom_call" | custom-call | tf_op jit(solution)/shard_map/join_blocks/pallas_call | solution.py:124
  125.6 14.3 %attention.1 = (bf16[2,1024,256]{2,1,0:T(8,128)(2,1)}, bf16[2,512,256]{2,1,0:T(8,128)(2,1)S(1)}) custom-call(s32[2]{0:T(128)S(1)} %pad_add_fusion.s_ref, bf16[1024,2304]{1,0:T(8,128)(2,1)} %bitcast.122, bf16[3,2304,256]{2,1,0:T(8,128)(2,1)S(1)} %bitcast.106, f32[1024,256]{1,0:T(8,128)S(1)} %copy-done.18, f32[1024,256]{1,0:T(8,128)S(1)} %copy-done.17), custom_call_target="tpu_custom_call" | custom-call | flops 4697620480 | bytes 8257536 | tf_op jit(solution)/shard_map/attention/pallas_call | solution.py:385
  143.3 21.2 %collective-permute-done.10.refs_6_.refs_5_ = bf16[38,16,720]{2,1,0:T(8,128)(2,1)} collective-permute-done((bf16[38,16,720]{2,1,0:T(8,128)(2,1)}, bf16[38,16,720]{2,1,0:T(8,128)(2,1)}, u32[]{:S(2)}, u32[]{:S(2)}) %collective-permute-start.10) | collective-permute-done | bytes 875552 | tf_op jit(solution)/shard_map/ppermute | solution.py:17
  165.3 5.2 %project.1 = (f32[64,2304]{1,0:T(8,128)}, f32[64,2304]{1,0:T(8,128)}, bf16[64,2304]{1,0:T(8,128)(2,1)}, bf16[64,2304]{1,0:T(8,128)(2,1)}, bf16[64,2304]{1,0:T(8,...) custom-call(s32[1]{0:T(128)} %bitcast.22.chip_ref, ...), custom_call_target="tpu_custom_call" | custom-call | tf_op jit(solution)/shard_map/project/pallas_call | solution.py:224
  175.2 8.0 %join_gate_up.1 = (bf16[144,16,720]{2,1,0:T(8,128)(2,1)}, bf16[144,16,720]{2,1,0:T(8,128)(2,1)}) custom-call(s32[1]{0:T(128)} %bitcast.2.me_ref, bf16[38,16,720]{2,1,0:T(8,128)(2,1)S(1)} %copy-done.4, bf16[38,16,720]{2,1,0:T(8,128)(2,1)S(1)} %collective-permute-done.4.refs_2_.refs_1_, bf16[38,16,720]{2,1,0:T(8,128)(2,1)S(1)} %collective-permute-done.5.refs_3_.refs_2_, ...), custom_call_target="tpu_custom_call" | custom-call | tf_op jit(solution)/shard_map/join_gate_up/pallas_call | solution.py:124
  183.3 3.3 %collective-permute-done.14 = bf16[64,2304]{1,0:T(8,128)(2,1)S(1)} collective-permute-done((bf16[64,2304]{1,0:T(8,128)(2,1)}, bf16[64,2304]{1,0:T(8,128)(2,1)S(1)}, u32[]{:S(2)}, u32[]{:S(2)}) %collective-permute-start.14) | collective-permute-done | bytes 294944 | tf_op jit(solution)/shard_map/ppermute | solution.py:17
  197.6 8.4 %join_down.1 = bf16[144,16,720]{2,1,0:T(8,128)(2,1)} custom-call(s32[1]{0:T(128)} %bitcast.2.me_ref, bf16[4,8,4,16,720]{4,3,2,1,0:T(8,128)(2,1)S(1)} %bitcast.108, bf16[38,16,720]{2,1,0:T(8,128)(2,1)S(1)} %copy-done.4, bf16[38,16,720]{2,1,0:T(8,128)(2,1)S(1)} %collective-permute-done.4.refs_2_.refs_1_, ...), custom_call_target="tpu_custom_call" | custom-call | tf_op jit(solution)/shard_map/join_down/pallas_call | solution.py:124
  207.0 3.9 %collective-permute-done.17 = bf16[64,2304]{1,0:T(8,128)(2,1)} collective-permute-done((bf16[64,2304]{1,0:T(8,128)(2,1)}, bf16[64,2304]{1,0:T(8,128)(2,1)}, u32[]{:S(2)}, u32[]{:S(2)}) %collective-permute-start.17) | collective-permute-done | bytes 294944 | tf_op jit(solution)/shard_map/ppermute | solution.py:17
  212.3 5.6 %copy.24 = bf16[2304,720]{0,1:T(8,128)(2,1)} copy(bf16[2304,720]{1,0:T(8,128)(2,1)} %bitcast.127) | data formatting | bytes 6635520 | tf_op jit(solution)/shard_map/optimization_barrier | solution.py:527
  224.0 11.4 %expert.2 = (bf16[256,2304]{1,0:T(8,128)(2,1)}, bf16[256,2304]{1,0:T(8,128)(2,1)}) custom-call(bf16[256,2304]{1,0:T(8,128)(2,1)} %bitcast.136, bf16[256,2304]{1,0:T(8,128)(2,1)} %bitcast.142, bf16[2304,720]{1,0:T(8,128)(2,1)} %bitcast.124, bf16[2304,720]{1,0:T(8,128)(2,1)} %bitcast.128, bf16[2304,720]{1,0:T(8,128)(2,1)} %bitcast.119), custom_call_target="tpu_custom_call" | custom-call | flops 5096079360 | bytes 9953280 | tf_op jit(solution)/shard_map/expert/pallas_call | solution.py:286
  244.7 11.3 %expert.3 = (bf16[256,2304]{1,0:T(8,128)(2,1)}, bf16[256,2304]{1,0:T(8,128)(2,1)}) custom-call(bf16[256,2304]{1,0:T(8,128)(2,1)} %bitcast.135, bf16[256,2304]{1,0:T(8,128)(2,1)} %bitcast.141, bf16[2304,720]{1,0:T(8,128)(2,1)} %bitcast.125, bf16[2304,720]{1,0:T(8,128)(2,1)} %bitcast.129, bf16[2304,720]{1,0:T(8,128)(2,1)} %bitcast.120), custom_call_target="tpu_custom_call" | custom-call | flops 5096079360 | bytes 9953280 | tf_op jit(solution)/shard_map/expert/pallas_call | solution.py:286
  268.0 5.6 %copy.25 = bf16[2304,720]{0,1:T(8,128)(2,1)} copy(bf16[2304,720]{1,0:T(8,128)(2,1)} %bitcast.126) | data formatting | bytes 6635520
  273.6 5.6 %copy.26 = bf16[2304,720]{0,1:T(8,128)(2,1)} copy(bf16[2304,720]{1,0:T(8,128)(2,1)} %bitcast.121) | data formatting | bytes 6635520
  (195 shorter events, 82.3 us)
Async XLA Ops:
  7.2 111.8 %all-gather.6.cloned.1.call-start = ((), (), s32[]{:S(2)}) async-start(), calls=%async_computation.2 | async-start | bytes 1474560 | tf_op jit(solution)/shard_map/all_gather | solution.py:488
  11.5 19.4 %all-to-all-start = ((bf16[8,3,72,256]{3,2,1,0:T(8,128)(2,1)}), bf16[8,3,72,256]{3,2,1,0:T(8,128)(2,1)S(1)}, u32[]{:S(2)}, u32[]{:S(2)}) async-start(bf16[8,3,72,256]{3,2,1,0:T(8,128)(2,1)} %split_heads.1), calls=%async_computation | async-start | bytes 1769472 | tf_op jit(solution)/shard_map/all_to_all | solution.py:454
  15.9 103.1 %all-gather.8.cloned.1.call-start = ((), (), s32[]{:S(2)}) async-start(), calls=%async_computation.3 | async-start | bytes 4423680 | tf_op jit(solution)/shard_map/all_gather | solution.py:461
  31.9 17.2 %collective-permute-start.2 = (bf16[128,2304]{1,0:T(8,128)(2,1)S(1)}, bf16[128,2304]{1,0:T(8,128)(2,1)S(1)}, u32[]{:S(2)}, u32[]{:S(2)}) collective-permute-start(bf16[128,2304]{1,0:T(8,128)(2,1)S(1)} %fusion.6), channel_id=1, source_target_pairs={{0,6},{1,7},{2,4},{3,5},{4,2},{5,3},{6,0},{7,1},{8,14},{9,15},{10,... | collective-permute-start | bytes 1769480 | tf_op jit(solution)/shard_map/ppermute | solution.py:17
  33.4 27.5 %collective-permute-start.1 = (bf16[128,2304]{1,0:T(8,128)(2,1)S(1)}, bf16[128,2304]{1,0:T(8,128)(2,1)S(1)}, u32[]{:S(2)}, u32[]{:S(2)}) collective-permute-start(bf16[128,2304]{1,0:T(8,128)(2,1)S(1)} %fusion.6), channel_id=1, source_target_pairs={{0,4},{1,5},{2,6},{3,7},{4,0},{5,1},{6,2},{7,3},{8,12},{9,13},{10,... | collective-permute-start | bytes 1769480 | tf_op jit(solution)/shard_map/ppermute | solution.py:17
  34.9 26.0 %collective-permute-start = (bf16[128,2304]{1,0:T(8,128)(2,1)S(1)}, bf16[128,2304]{1,0:T(8,128)(2,1)S(1)}, u32[]{:S(2)}, u32[]{:S(2)}) collective-permute-start(bf16[128,2304]{1,0:T(8,128)(2,1)S(1)} %fusion.6), channel_id=1, source_target_pairs={{0,2},{1,3},{2,0},{3,1},{4,6},{5,7},{6,4},{7,5},{8,10},{9,11},{10,... | collective-permute-start | bytes 1769480 | tf_op jit(solution)/shard_map/ppermute | solution.py:17
  62.7 49.9 %collective-permute-start.3 = (bf16[4,128,2304]{2,1,0:T(8,128)(2,1)}, bf16[4,128,2304]{2,1,0:T(8,128)(2,1)}, u32[]{:S(2)}, u32[]{:S(2)}) collective-permute-start(bf16[4,128,2304]{2,1,0:T(8,128)(2,1)} %pad_maximum_fusion), channel_id=1, source_target_pairs={{0,1},{1,0},{2,3},{3,2},{4,5},{5,4},{6,7},{7,6},{8,9},{9,8},{10,11... | collective-permute-start | bytes 7077896 | tf_op jit(solution)/shard_map/ppermute | solution.py:17
  63.7 22.7 %collective-permute-start.5 = (bf16[38,16,720]{2,1,0:T(8,128)(2,1)S(1)}, bf16[38,16,720]{2,1,0:T(8,128)(2,1)S(1)}, u32[]{:S(2)}, u32[]{:S(2)}) collective-permute-start(bf16[38,16,720]{2,1,0:T(8,128)(2,1)S(1)} %copy-done.42), channel_id=1, source_target_pairs={{0,2},{1,3},{2,0},{3,1},{4,6},{5,7},{6,4},{7,5},{8,10},{9,11},{10,... | collective-permute-start | bytes 2626568 | tf_op jit(solution)/shard_map/ppermute | solution.py:17
  64.3 22.3 %collective-permute-start.6 = (bf16[38,16,720]{2,1,0:T(8,128)(2,1)S(1)}, bf16[38,16,720]{2,1,0:T(8,128)(2,1)S(1)}, u32[]{:S(2)}, u32[]{:S(2)}) collective-permute-start(bf16[38,16,720]{2,1,0:T(8,128)(2,1)S(1)} %copy-done.41), channel_id=1, source_target_pairs={{0,4},{1,5},{2,6},{3,7},{4,0},{5,1},{6,2},{7,3},{8,12},{9,13},{10,... | collective-permute-start | bytes 2626568 | tf_op jit(solution)/shard_map/ppermute | solution.py:17
  87.6 24.9 %collective-permute-start.7 = (bf16[38,16,720]{2,1,0:T(8,128)(2,1)}, bf16[38,16,720]{2,1,0:T(8,128)(2,1)}, u32[]{:S(2)}, u32[]{:S(2)}) collective-permute-start(bf16[38,16,720]{2,1,0:T(8,128)(2,1)} %get-tuple-element.135), channel_id=1, source_target_pairs={{0,6},{1,7},{2,4},{3,5},{4,2},{5,3},{6,0},{7,1},{8,14},{9,15},{10,... | collective-permute-start | bytes 2626568 | tf_op jit(solution)/shard_map/ppermute | solution.py:17
  93.2 25.8 %all-to-all-start.1 = ((bf16[8,64,720]{2,1,0:T(8,128)(2,1)}), bf16[8,64,720]{2,1,0:T(8,128)(2,1)}, u32[]{:S(2)}, u32[]{:S(2)}) async-start(bf16[8,64,720]{2,1,0:T(8,128)(2,1)} %split_rows.1), calls=%async_computation.1 | async-start | bytes 1572864 | tf_op jit(solution)/shard_map/all_to_all | solution.py:463
  98.8 94.5 %all-gather.10.cloned.1.call-start = ((), (), s32[]{:S(2)}) async-start(), calls=%async_computation.4 | async-start | bytes 3932160 | tf_op jit(solution)/shard_map/all_gather | solution.py:492
  119.1 23.3 %collective-permute-start.8 = (bf16[38,16,720]{2,1,0:T(8,128)(2,1)}, bf16[38,16,720]{2,1,0:T(8,128)(2,1)S(1)}, u32[]{:S(2)}, u32[]{:S(2)}) collective-permute-start(bf16[38,16,720]{2,1,0:T(8,128)(2,1)} %get-tuple-element.145), channel_id=1, source_target_pairs={{0,3},{1,2},{2,1},{3,0},{4,7},{5,6},{6,5},{7,4},{8,11},{9,10},{10,... | collective-permute-start | bytes 2626568 | tf_op jit(solution)/shard_map/ppermute | solution.py:17
  120.2 44.4 %collective-permute-start.12 = (bf16[256,2304]{1,0:T(8,128)(2,1)}, bf16[256,2304]{1,0:T(8,128)(2,1)}, u32[]{:S(2)}, u32[]{:S(2)}) collective-permute-start(bf16[256,2304]{1,0:T(8,128)(2,1)} %all-gather.6.cloned.1.call-done.own_ref), channel_id=1, source_target_pairs={{0,1},{1,0},{2,3},{3,2},{4,5},{5,4},{6,7},{7,6},{8,9},{9,8},{10,11... | collective-permute-start | bytes 3538952 | tf_op jit(solution)/shard_map/ppermute | solution.py:17
  121.4 43.1 %collective-permute-start.10 = (bf16[38,16,720]{2,1,0:T(8,128)(2,1)}, bf16[38,16,720]{2,1,0:T(8,128)(2,1)}, u32[]{:S(2)}, u32[]{:S(2)}) collective-permute-start(bf16[38,16,720]{2,1,0:T(8,128)(2,1)} %get-tuple-element.147), channel_id=1, source_target_pairs={{0,5},{1,4},{2,7},{3,6},{4,1},{5,0},{6,3},{7,2},{8,13},{9,12},{10,... | collective-permute-start | bytes 2626568 | tf_op jit(solution)/shard_map/ppermute | solution.py:17
  121.7 42.8 %collective-permute-start.11 = (bf16[38,16,720]{2,1,0:T(8,128)(2,1)}, bf16[38,16,720]{2,1,0:T(8,128)(2,1)}, u32[]{:S(2)}, u32[]{:S(2)}) collective-permute-start(bf16[38,16,720]{2,1,0:T(8,128)(2,1)} %get-tuple-element.148), channel_id=1, source_target_pairs={{0,7},{1,6},{2,5},{3,4},{4,3},{5,2},{6,1},{7,0},{8,15},{9,14},{10,... | collective-permute-start | bytes 2626568 | tf_op jit(solution)/shard_map/ppermute | solution.py:17
  143.1 21.4 %collective-permute-start.9 = (bf16[512,256]{1,0:T(8,128)(2,1)S(1)}, bf16[512,256]{1,0:T(8,128)(2,1)S(1)}, u32[]{:S(2)}, u32[]{:S(2)}) collective-permute-start(bf16[512,256]{1,0:T(8,128)(2,1)S(1)} %get-tuple-element.249), channel_id=1, source_target_pairs={{0,1},{1,0},{2,3},{3,2},{4,5},{5,4},{6,7},{7,6},{8,9},{9,8},{10,11... | collective-permute-start | bytes 786440 | tf_op jit(solution)/shard_map/ppermute | solution.py:17
  186.7 19.3 %collective-permute-start.16 = (bf16[64,2304]{1,0:T(8,128)(2,1)}, bf16[64,2304]{1,0:T(8,128)(2,1)}, u32[]{:S(2)}, u32[]{:S(2)}) collective-permute-start(bf16[64,2304]{1,0:T(8,128)(2,1)} %get-tuple-element.159), channel_id=1, source_target_pairs={{0,2},{1,3},{2,0},{3,1},{4,6},{5,7},{6,4},{7,5},{8,10},{9,11},{10,... | collective-permute-start | bytes 884744 | tf_op jit(solution)/shard_map/ppermute | solution.py:17
  188.0 22.9 %collective-permute-start.17 = (bf16[64,2304]{1,0:T(8,128)(2,1)}, bf16[64,2304]{1,0:T(8,128)(2,1)}, u32[]{:S(2)}, u32[]{:S(2)}) collective-permute-start(bf16[64,2304]{1,0:T(8,128)(2,1)} %get-tuple-element.160), channel_id=1, source_target_pairs={{0,4},{1,5},{2,6},{3,7},{4,0},{5,1},{6,2},{7,3},{8,12},{9,13},{10,... | collective-permute-start | bytes 884744 | tf_op jit(solution)/shard_map/ppermute | solution.py:17
  188.6 22.3 %collective-permute-start.18 = (bf16[64,2304]{1,0:T(8,128)(2,1)}, bf16[64,2304]{1,0:T(8,128)(2,1)}, u32[]{:S(2)}, u32[]{:S(2)}) collective-permute-start(bf16[64,2304]{1,0:T(8,128)(2,1)} %get-tuple-element.161), channel_id=1, source_target_pairs={{0,6},{1,7},{2,4},{3,5},{4,2},{5,3},{6,0},{7,1},{8,14},{9,15},{10,... | collective-permute-start | bytes 884744 | tf_op jit(solution)/shard_map/ppermute | solution.py:17
  190.6 27.4 %collective-permute-start.21 = (bf16[64,2304]{1,0:T(8,128)(2,1)S(1)}, bf16[64,2304]{1,0:T(8,128)(2,1)}, u32[]{:S(2)}, u32[]{:S(2)}) collective-permute-start(bf16[64,2304]{1,0:T(8,128)(2,1)S(1)} %fusion.9), channel_id=1, source_target_pairs={{0,6},{1,7},{2,4},{3,5},{4,2},{5,3},{6,0},{7,1},{8,14},{9,15},{10,... | collective-permute-start | bytes 884744 | tf_op jit(solution)/shard_map/ppermute | solution.py:17
  191.9 26.1 %collective-permute-start.20 = (bf16[64,2304]{1,0:T(8,128)(2,1)S(1)}, bf16[64,2304]{1,0:T(8,128)(2,1)}, u32[]{:S(2)}, u32[]{:S(2)}) collective-permute-start(bf16[64,2304]{1,0:T(8,128)(2,1)S(1)} %fusion.9), channel_id=1, source_target_pairs={{0,4},{1,5},{2,6},{3,7},{4,0},{5,1},{6,2},{7,3},{8,12},{9,13},{10,... | collective-permute-start | bytes 884744 | tf_op jit(solution)/shard_map/ppermute | solution.py:17
  219.4 16.0 %collective-permute-start.25 = (bf16[64,2304]{1,0:T(8,128)(2,1)S(1)}, bf16[64,2304]{1,0:T(8,128)(2,1)S(1)}, u32[]{:S(2)}, u32[]{:S(2)}) collective-permute-start(bf16[64,2304]{1,0:T(8,128)(2,1)S(1)} %fusion.12), channel_id=1, source_target_pairs={{0,6},{1,7},{2,4},{3,5},{4,2},{5,3},{6,0},{7,1},{8,14},{9,15},{10,... | collective-permute-start | bytes 884744 | tf_op jit(solution)/shard_map/ppermute | solution.py:17
  263.2 16.0 %collective-permute-start.33 = (bf16[64,2304]{1,0:T(8,128)(2,1)}, bf16[64,2304]{1,0:T(8,128)(2,1)S(1)}, u32[]{:S(2)}, u32[]{:S(2)}) collective-permute-start(bf16[64,2304]{1,0:T(8,128)(2,1)} %get-tuple-element.239), channel_id=1, source_target_pairs={{0,4},{1,5},{2,6},{3,7},{4,0},{5,1},{6,2},{7,3},{8,12},{9,13},{10,... | collective-permute-start | bytes 884744 | tf_op jit(solution)/shard_map/ppermute | solution.py:17
  (60 other events, 646.2 us)
Sparse Core Ops, SparseCore 0:
  9.6 31.0 all-gather.5
  42.2 67.2 all-gather.7
  119.2 62.2 all-gather.9

commit v11 on v9

--- a/solution.py
+++ b/solution.py
@@ -460,14 +460,15 @@
     normed = rms_scale(tokens, attn_gain).astype(jnp.bfloat16)
     qkv_cols, normed, *parts = lax.optimization_barrier((qkv_cols, normed, *parts))
     qkv_all = lax.all_gather(qkv_cols, "dp", axis=0)
-    down_parts = split_rows(trainer_down, size, plane, part_rows)
-    down_cols = lax.all_to_all(down_parts, "tensor", 0, 0, tiled=True)
     same_core = [normed] + [send(normed, size, 2 * j) for j in range(1, chips)]
     other_core = send(jnp.stack(same_core), size, 1)
     blocks = []
     for j in range(chips):
         blocks += [same_core[j], other_core[j]]
     piece = join_blocks(blocks, me)
+    plane, piece = lax.optimization_barrier((plane, piece))
+    down_parts = split_rows(trainer_down, size, plane, part_rows)
+    down_cols = lax.all_to_all(down_parts, "tensor", 0, 0, tiled=True)
 
     first = [1, 2, 4][: size.bit_length() - 1]
     rest = [k for k in range(3, size) if k not in first]

time: 292 us -> 290 us (level)
  local copies, waits for them, and re-layouts: 45.9 us -> 40 us
  waiting for transfers between devices: 95.4 us -> 99.7 us
    all_to_all x1, waiting for transfers between devices: 0.04 us -> 6.34 us  [shards(): down_cols = lax.all_to_all(down_parts, 'tensor', 0, 0, tiled=True)]
    unnamed x90 -> x80, local copies, waits for them, and re-layouts: 34.1 us -> 28.1 us
  transfers between devices with their start and end apart: 40 -> 40, of which waited for: 15 -> 16; matrix products, arithmetic and copies ran while one was open for 12% -> 12% of each run, Pallas kernels for 24% -> 24%
where the time goes in v11:
time: 290 us; the launch traced here: 287 us
  waiting for transfers between devices  99.7 us (34%)
  Pallas kernels  68.3 us (24%)
  starting transfers between devices  42.8 us (15%)
  local copies, waits for them, and re-layouts  40 us (14%)
  other arithmetic  20.5 us (7%)
  between operations  15.5 us (5%)
    ppermute x35, waiting for transfers between devices, send(): return lax.ppermute(block, 'tensor', swap_pairs(size, step))  93.3 us
    ppermute x35, starting transfers between devices, send(): return lax.ppermute(block, 'tensor', swap_pairs(size, step))  32.7 us
    unnamed x80, local copies, waits for them, and re-layouts  28.1 us
    pallas_call x2, Pallas kernels, expert(): pl.pallas_call(kernel, out_shape=[jax.ShapeDtypeStruct((rows, model), jnp...  22.7 us
    pallas_call x1, Pallas kernels, attention(): pl.pallas_call(kernel, out_shape=(jax.ShapeDtypeStruct((2, seq, width), j...  14.3 us
    pallas_call x3, Pallas kernels, copy_rows(): pl.pallas_call(kernel, out_shape=[jax.ShapeDtypeStruct(shape, jnp.bfloat1...  13.7 us
    pallas_call x1, Pallas kernels, split_columns(): pl.pallas_call(kernel, out_shape=[jax.ShapeDtypeStruct(((2 * rows + tail)...  9.73 us
    all_to_all x1, waiting for transfers between devices, shards(): down_cols = lax.all_to_all(down_parts, 'tensor', 0, 0, tiled=True)  6.34 us
  transfers between devices with their start and end apart: 40, of which 16 were waited for; matrix products, arithmetic and copies ran while one was open for 12% of the time, Pallas kernels for 24%

profile of v11, /device:TPU:12, one launch (start us, length us, event | category | flops | bytes accessed | tf_op | source)
XLA Modules:
  0.0 287.0 jit_solution(8143469684317760775)
XLA Ops:
  9.1 2.5 split_heads.1
  11.6 4.4 %all-to-all-start = ((bf16[8,3,72,256]{3,2,1,0:T(8,128)(2,1)}), bf16[8,3,72,256]{3,2,1,0:T(8,128)(2,1)S(1)}, u32[]{:S(2)}, u32[]{:S(2)}) async-start(bf16[8,3,72,256]{3,2,1,0:T(8,128)(2,1)} %split_heads.1), calls=%async_computation | async-start | bytes 1769472 | tf_op jit(solution)/shard_map/all_to_all | solution.py:455
  17.3 9.7 %split_columns.1 = (bf16[38,16,720]{2,1,0:T(8,128)(2,1)S(1)}, bf16[38,16,720]{2,1,0:T(8,128)(2,1)}, bf16[38,16,720]{2,1,0:T(8,128)(2,1)}, bf16[38,16,720]{2,1,0:...) custom-call(s32[1]{0:T(128)} %bitcast.2.me_ref, ...), custom_call_target="tpu_custom_call" | custom-call | tf_op jit(solution)/shard_map/split_columns/pallas_call | solution.py:91
  35.5 13.6 %collective-permute-done.2 = bf16[128,2304]{1,0:T(8,128)(2,1)S(1)} collective-permute-done((bf16[128,2304]{1,0:T(8,128)(2,1)S(1)}, bf16[128,2304]{1,0:T(8,128)(2,1)S(1)}, u32[]{:S(2)}, u32[]{:S(2)}) %collective-permute-start.2) | collective-permute-done | bytes 589856 | tf_op jit(solution)/shard_map/ppermute | solution.py:17
  49.1 11.8 %collective-permute-done.1 = bf16[128,2304]{1,0:T(8,128)(2,1)S(1)} collective-permute-done((bf16[128,2304]{1,0:T(8,128)(2,1)S(1)}, bf16[128,2304]{1,0:T(8,128)(2,1)S(1)}, u32[]{:S(2)}, u32[]{:S(2)}) %collective-permute-start.1) | collective-permute-done | bytes 589856 | tf_op jit(solution)/shard_map/ppermute | solution.py:17
  65.3 3.3 %collective-permute-done.4.refs_2_.refs_1_ = bf16[38,16,720]{2,1,0:T(8,128)(2,1)S(1)} collective-permute-done((bf16[38,16,720]{2,1,0:T(8,128)(2,1)}, bf16[38,16,720]{2,1,0:T(8,128)(2,1)S(1)}, u32[]{:S(2)}, u32[]{:S(2)}) %collective-permute-start.4) | collective-permute-done | bytes 875552 | tf_op jit(solution)/shard_map/ppermute | solution.py:17
  68.6 17.6 %collective-permute-done.5.refs_3_.refs_2_ = bf16[38,16,720]{2,1,0:T(8,128)(2,1)S(1)} collective-permute-done((bf16[38,16,720]{2,1,0:T(8,128)(2,1)}, bf16[38,16,720]{2,1,0:T(8,128)(2,1)S(1)}, u32[]{:S(2)}, u32[]{:S(2)}) %collective-permute-start.5) | collective-permute-done | bytes 875552 | tf_op jit(solution)/shard_map/ppermute | solution.py:17
  95.7 5.7 %all-to-all-start.1 = ((bf16[8,64,720]{2,1,0:T(8,128)(2,1)}), bf16[8,64,720]{2,1,0:T(8,128)(2,1)}, u32[]{:S(2)}, u32[]{:S(2)}) async-start(bf16[8,64,720]{2,1,0:T(8,128)(2,1)} %copy-done.7), calls=%async_computation.1 | async-start | bytes 1572864 | tf_op jit(solution)/shard_map/all_to_all | solution.py:471
  102.2 5.5 %multiply_sine_fusion = (f32[1024,256]{1,0:T(8,128)}, f32[1024,256]{1,0:T(8,128)}) fusion(f32[256]{0:T(256)S(1)} %mul.108, f32[1024]{0:T(1024)S(1)} %add_convert_fusion.6), kind=kLoop, calls=%fused_computation.1 | loop fusion | flops 262144 | bytes 2102272 | tf_op jit(solution)/shard_map/sin | solution.py:489
  107.7 3.9 %collective-permute-done.7.refs_7_.refs_6_ = bf16[38,16,720]{2,1,0:T(8,128)(2,1)} collective-permute-done((bf16[38,16,720]{2,1,0:T(8,128)(2,1)}, bf16[38,16,720]{2,1,0:T(8,128)(2,1)}, u32[]{:S(2)}, u32[]{:S(2)}) %collective-permute-start.7) | collective-permute-done | bytes 875552 | tf_op jit(solution)/shard_map/ppermute | solution.py:17
  111.6 6.3 %all-to-all-done.1 = bf16[8,64,720]{2,1,0:T(8,128)(2,1)} async-done(((bf16[8,64,720]{2,1,0:T(8,128)(2,1)}), bf16[8,64,720]{2,1,0:T(8,128)(2,1)}, u32[]{:S(2)}, u32[]{:S(2)}) %all-to-all-start.1) | async-done | bytes 737312 | tf_op jit(solution)/shard_map/all_to_all | solution.py:471
  124.6 14.3 %attention.1 = (bf16[2,1024,256]{2,1,0:T(8,128)(2,1)}, bf16[2,512,256]{2,1,0:T(8,128)(2,1)S(1)}) custom-call(s32[2]{0:T(128)S(1)} %pad_add_fusion.s_ref, bf16[1024,2304]{1,0:T(8,128)(2,1)} %bitcast.111, bf16[3,2304,256]{2,1,0:T(8,128)(2,1)S(1)} %bitcast.112, f32[1024,256]{1,0:T(8,128)S(1)} %copy-done.15, f32[1024,256]{1,0:T(8,128)S(1)} %copy-done.14), custom_call_target="tpu_custom_call" | custom-call | flops 4697620480 | bytes 8257536 | tf_op jit(solution)/shard_map/attention/pallas_call | solution.py:386
  138.8 2.5 collective-permute-done.8.refs_4_.refs_3_
  142.1 21.2 %collective-permute-done.10.refs_6_.refs_5_ = bf16[38,16,720]{2,1,0:T(8,128)(2,1)} collective-permute-done((bf16[38,16,720]{2,1,0:T(8,128)(2,1)}, bf16[38,16,720]{2,1,0:T(8,128)(2,1)}, u32[]{:S(2)}, u32[]{:S(2)}) %collective-permute-start.10) | collective-permute-done | bytes 875552 | tf_op jit(solution)/shard_map/ppermute | solution.py:17
  164.1 5.1 %project.1 = (f32[64,2304]{1,0:T(8,128)}, f32[64,2304]{1,0:T(8,128)}, bf16[64,2304]{1,0:T(8,128)(2,1)}, bf16[64,2304]{1,0:T(8,128)(2,1)}, bf16[64,2304]{1,0:T(8,...) custom-call(s32[1]{0:T(128)} %bitcast.22.chip_ref, ...), custom_call_target="tpu_custom_call" | custom-call | tf_op jit(solution)/shard_map/project/pallas_call | solution.py:225
  172.8 4.7 %join_gate_up.1 = (bf16[144,16,720]{2,1,0:T(8,128)(2,1)S(1)}, bf16[144,16,720]{2,1,0:T(8,128)(2,1)S(1)}) custom-call(s32[1]{0:T(128)} %bitcast.2.me_ref, bf16[38,16,720]{2,1,0:T(8,128)(2,1)S(1)} %get-tuple-element.167.refs_1_.refs_0_, bf16[38,16,720]{2,1,0:T(8,128)(2,1)S(1)} %collective-permute-done.4.refs_2_.refs_1_, ...), custom_call_target="tpu_custom_call" | custom-call | tf_op jit(solution)/shard_map/join_gate_up/pallas_call | solution.py:125
  179.3 6.1 %collective-permute-done.14 = bf16[64,2304]{1,0:T(8,128)(2,1)S(1)} collective-permute-done((bf16[64,2304]{1,0:T(8,128)(2,1)}, bf16[64,2304]{1,0:T(8,128)(2,1)S(1)}, u32[]{:S(2)}, u32[]{:S(2)}) %collective-permute-start.14) | collective-permute-done | bytes 294944 | tf_op jit(solution)/shard_map/ppermute | solution.py:17
  194.0 6.6 %join_down.1 = bf16[144,16,720]{2,1,0:T(8,128)(2,1)S(1)} custom-call(s32[1]{0:T(128)} %bitcast.2.me_ref, bf16[4,8,4,16,720]{4,3,2,1,0:T(8,128)(2,1)S(1)} %bitcast.120, bf16[38,16,720]{2,1,0:T(8,128)(2,1)S(1)} %get-tuple-element.167.refs_1_.refs_0_, bf16[38,16,720]{2,1,0:T(8,128)(2,1)S(1)} %collective-permute-done.4.refs_2_.refs_1_, ...), custom_call_target="tpu_custom_call" | custom-call | tf_op jit(solution)/shard_map/join_down/pallas_call | solution.py:125
  203.3 6.3 %collective-permute-done.17 = bf16[64,2304]{1,0:T(8,128)(2,1)} collective-permute-done((bf16[64,2304]{1,0:T(8,128)(2,1)}, bf16[64,2304]{1,0:T(8,128)(2,1)}, u32[]{:S(2)}, u32[]{:S(2)}) %collective-permute-start.17) | collective-permute-done | bytes 294944 | tf_op jit(solution)/shard_map/ppermute | solution.py:17
  211.1 5.6 %copy.24 = bf16[2304,720]{0,1:T(8,128)(2,1)} copy(bf16[2304,720]{1,0:T(8,128)(2,1)} %bitcast.117) | data formatting | bytes 6635520 | tf_op jit(solution)/shard_map/optimization_barrier | solution.py:529
  222.7 11.4 %expert.2 = (bf16[256,2304]{1,0:T(8,128)(2,1)}, bf16[256,2304]{1,0:T(8,128)(2,1)}) custom-call(bf16[256,2304]{1,0:T(8,128)(2,1)} %bitcast.138, bf16[256,2304]{1,0:T(8,128)(2,1)} %bitcast.144, bf16[2304,720]{1,0:T(8,128)(2,1)} %bitcast.114, bf16[2304,720]{1,0:T(8,128)(2,1)} %bitcast.118, bf16[2304,720]{1,0:T(8,128)(2,1)} %bitcast.104), custom_call_target="tpu_custom_call" | custom-call | flops 5096079360 | bytes 9953280 | tf_op jit(solution)/shard_map/expert/pallas_call | solution.py:287
  243.4 11.4 %expert.3 = (bf16[256,2304]{1,0:T(8,128)(2,1)}, bf16[256,2304]{1,0:T(8,128)(2,1)}) custom-call(bf16[256,2304]{1,0:T(8,128)(2,1)} %bitcast.137, bf16[256,2304]{1,0:T(8,128)(2,1)} %bitcast.143, bf16[2304,720]{1,0:T(8,128)(2,1)} %bitcast.115, bf16[2304,720]{1,0:T(8,128)(2,1)} %bitcast.119, bf16[2304,720]{1,0:T(8,128)(2,1)} %bitcast.105), custom_call_target="tpu_custom_call" | custom-call | flops 5096079360 | bytes 9953280 | tf_op jit(solution)/shard_map/expert/pallas_call | solution.py:287
  265.5 5.6 %copy.25 = bf16[2304,720]{0,1:T(8,128)(2,1)} copy(bf16[2304,720]{1,0:T(8,128)(2,1)} %bitcast.116) | data formatting | bytes 6635520
  271.2 5.6 %copy.26 = bf16[2304,720]{0,1:T(8,128)(2,1)} copy(bf16[2304,720]{1,0:T(8,128)(2,1)} %bitcast.106) | data formatting | bytes 6635520
  (186 shorter events, 80.6 us)
Async XLA Ops:
  7.2 104.4 %all-gather.6.cloned.1.call-start = ((), (), s32[]{:S(2)}) async-start(), calls=%async_computation.2 | async-start | bytes 1474560 | tf_op jit(solution)/shard_map/all_gather | solution.py:490
  11.6 19.4 %all-to-all-start = ((bf16[8,3,72,256]{3,2,1,0:T(8,128)(2,1)}), bf16[8,3,72,256]{3,2,1,0:T(8,128)(2,1)S(1)}, u32[]{:S(2)}, u32[]{:S(2)}) async-start(bf16[8,3,72,256]{3,2,1,0:T(8,128)(2,1)} %split_heads.1), calls=%async_computation | async-start | bytes 1769472 | tf_op jit(solution)/shard_map/all_to_all | solution.py:455
  15.9 102.0 %all-gather.8.cloned.1.call-start = ((), (), s32[]{:S(2)}) async-start(), calls=%async_computation.3 | async-start | bytes 4423680 | tf_op jit(solution)/shard_map/all_gather | solution.py:462
  32.0 17.2 %collective-permute-start.2 = (bf16[128,2304]{1,0:T(8,128)(2,1)S(1)}, bf16[128,2304]{1,0:T(8,128)(2,1)S(1)}, u32[]{:S(2)}, u32[]{:S(2)}) collective-permute-start(bf16[128,2304]{1,0:T(8,128)(2,1)S(1)} %fusion.6), channel_id=1, source_target_pairs={{0,6},{1,7},{2,4},{3,5},{4,2},{5,3},{6,0},{7,1},{8,14},{9,15},{10,... | collective-permute-start | bytes 1769480 | tf_op jit(solution)/shard_map/ppermute | solution.py:17
  33.5 27.4 %collective-permute-start.1 = (bf16[128,2304]{1,0:T(8,128)(2,1)S(1)}, bf16[128,2304]{1,0:T(8,128)(2,1)S(1)}, u32[]{:S(2)}, u32[]{:S(2)}) collective-permute-start(bf16[128,2304]{1,0:T(8,128)(2,1)S(1)} %fusion.6), channel_id=1, source_target_pairs={{0,4},{1,5},{2,6},{3,7},{4,0},{5,1},{6,2},{7,3},{8,12},{9,13},{10,... | collective-permute-start | bytes 1769480 | tf_op jit(solution)/shard_map/ppermute | solution.py:17
  35.0 26.0 %collective-permute-start = (bf16[128,2304]{1,0:T(8,128)(2,1)S(1)}, bf16[128,2304]{1,0:T(8,128)(2,1)S(1)}, u32[]{:S(2)}, u32[]{:S(2)}) collective-permute-start(bf16[128,2304]{1,0:T(8,128)(2,1)S(1)} %fusion.6), channel_id=1, source_target_pairs={{0,2},{1,3},{2,0},{3,1},{4,6},{5,7},{6,4},{7,5},{8,10},{9,11},{10,... | collective-permute-start | bytes 1769480 | tf_op jit(solution)/shard_map/ppermute | solution.py:17
  62.7 25.3 %collective-permute-start.3 = (bf16[4,128,2304]{2,1,0:T(8,128)(2,1)}, bf16[4,128,2304]{2,1,0:T(8,128)(2,1)}, u32[]{:S(2)}, u32[]{:S(2)}) collective-permute-start(bf16[4,128,2304]{2,1,0:T(8,128)(2,1)} %pad_maximum_fusion), channel_id=1, source_target_pairs={{0,1},{1,0},{2,3},{3,2},{4,5},{5,4},{6,7},{7,6},{8,9},{9,8},{10,11... | collective-permute-start | bytes 7077896 | tf_op jit(solution)/shard_map/ppermute | solution.py:17
  63.3 22.9 %collective-permute-start.5 = (bf16[38,16,720]{2,1,0:T(8,128)(2,1)}, bf16[38,16,720]{2,1,0:T(8,128)(2,1)S(1)}, u32[]{:S(2)}, u32[]{:S(2)}) collective-permute-start(bf16[38,16,720]{2,1,0:T(8,128)(2,1)} %get-tuple-element.131), channel_id=1, source_target_pairs={{0,2},{1,3},{2,0},{3,1},{4,6},{5,7},{6,4},{7,5},{8,10},{9,11},{10,... | collective-permute-start | bytes 2626568 | tf_op jit(solution)/shard_map/ppermute | solution.py:17
  63.9 22.7 %collective-permute-start.6 = (bf16[38,16,720]{2,1,0:T(8,128)(2,1)}, bf16[38,16,720]{2,1,0:T(8,128)(2,1)}, u32[]{:S(2)}, u32[]{:S(2)}) collective-permute-start(bf16[38,16,720]{2,1,0:T(8,128)(2,1)} %get-tuple-element.132), channel_id=1, source_target_pairs={{0,4},{1,5},{2,6},{3,7},{4,0},{5,1},{6,2},{7,3},{8,12},{9,13},{10,... | collective-permute-start | bytes 2626568 | tf_op jit(solution)/shard_map/ppermute | solution.py:17
  86.7 24.9 %collective-permute-start.7 = (bf16[38,16,720]{2,1,0:T(8,128)(2,1)}, bf16[38,16,720]{2,1,0:T(8,128)(2,1)}, u32[]{:S(2)}, u32[]{:S(2)}) collective-permute-start(bf16[38,16,720]{2,1,0:T(8,128)(2,1)} %copy-done.19), channel_id=1, source_target_pairs={{0,6},{1,7},{2,4},{3,5},{4,2},{5,3},{6,0},{7,1},{8,14},{9,15},{10,... | collective-permute-start | bytes 2626568 | tf_op jit(solution)/shard_map/ppermute | solution.py:17
  95.7 22.2 %all-to-all-start.1 = ((bf16[8,64,720]{2,1,0:T(8,128)(2,1)}), bf16[8,64,720]{2,1,0:T(8,128)(2,1)}, u32[]{:S(2)}, u32[]{:S(2)}) async-start(bf16[8,64,720]{2,1,0:T(8,128)(2,1)} %copy-done.7), calls=%async_computation.1 | async-start | bytes 1572864 | tf_op jit(solution)/shard_map/all_to_all | solution.py:471
  101.4 90.7 %all-gather.10.cloned.1.call-start = ((), (), s32[]{:S(2)}) async-start(), calls=%async_computation.4 | async-start | bytes 3932160 | tf_op jit(solution)/shard_map/all_gather | solution.py:494
  118.0 23.4 %collective-permute-start.8 = (bf16[38,16,720]{2,1,0:T(8,128)(2,1)}, bf16[38,16,720]{2,1,0:T(8,128)(2,1)}, u32[]{:S(2)}, u32[]{:S(2)}) collective-permute-start(bf16[38,16,720]{2,1,0:T(8,128)(2,1)} %copy-done.18), channel_id=1, source_target_pairs={{0,3},{1,2},{2,1},{3,0},{4,7},{5,6},{6,5},{7,4},{8,11},{9,10},{10,... | collective-permute-start | bytes 2626568 | tf_op jit(solution)/shard_map/ppermute | solution.py:17
  119.1 44.3 %collective-permute-start.12 = (bf16[256,2304]{1,0:T(8,128)(2,1)}, bf16[256,2304]{1,0:T(8,128)(2,1)}, u32[]{:S(2)}, u32[]{:S(2)}) collective-permute-start(bf16[256,2304]{1,0:T(8,128)(2,1)} %all-gather.6.cloned.1.call-done.own_ref), channel_id=1, source_target_pairs={{0,1},{1,0},{2,3},{3,2},{4,5},{5,4},{6,7},{7,6},{8,9},{9,8},{10,11... | collective-permute-start | bytes 3538952 | tf_op jit(solution)/shard_map/ppermute | solution.py:17
  120.2 43.1 %collective-permute-start.10 = (bf16[38,16,720]{2,1,0:T(8,128)(2,1)}, bf16[38,16,720]{2,1,0:T(8,128)(2,1)}, u32[]{:S(2)}, u32[]{:S(2)}) collective-permute-start(bf16[38,16,720]{2,1,0:T(8,128)(2,1)} %copy-done.17), channel_id=1, source_target_pairs={{0,5},{1,4},{2,7},{3,6},{4,1},{5,0},{6,3},{7,2},{8,13},{9,12},{10,... | collective-permute-start | bytes 2626568 | tf_op jit(solution)/shard_map/ppermute | solution.py:17
  120.5 42.8 %collective-permute-start.11 = (bf16[38,16,720]{2,1,0:T(8,128)(2,1)}, bf16[38,16,720]{2,1,0:T(8,128)(2,1)}, u32[]{:S(2)}, u32[]{:S(2)}) collective-permute-start(bf16[38,16,720]{2,1,0:T(8,128)(2,1)} %copy-done.16), channel_id=1, source_target_pairs={{0,7},{1,6},{2,5},{3,4},{4,3},{5,2},{6,1},{7,0},{8,15},{9,14},{10,... | collective-permute-start | bytes 2626568 | tf_op jit(solution)/shard_map/ppermute | solution.py:17
  142.1 21.3 %collective-permute-start.9 = (bf16[512,256]{1,0:T(8,128)(2,1)S(1)}, bf16[512,256]{1,0:T(8,128)(2,1)S(1)}, u32[]{:S(2)}, u32[]{:S(2)}) collective-permute-start(bf16[512,256]{1,0:T(8,128)(2,1)S(1)} %get-tuple-element.253), channel_id=1, source_target_pairs={{0,1},{1,0},{2,3},{3,2},{4,5},{5,4},{6,7},{7,6},{8,9},{9,8},{10,11... | collective-permute-start | bytes 786440 | tf_op jit(solution)/shard_map/ppermute | solution.py:17
  185.6 16.8 %collective-permute-start.16 = (bf16[64,2304]{1,0:T(8,128)(2,1)}, bf16[64,2304]{1,0:T(8,128)(2,1)}, u32[]{:S(2)}, u32[]{:S(2)}) collective-permute-start(bf16[64,2304]{1,0:T(8,128)(2,1)} %get-tuple-element.163), channel_id=1, source_target_pairs={{0,2},{1,3},{2,0},{3,1},{4,6},{5,7},{6,4},{7,5},{8,10},{9,11},{10,... | collective-permute-start | bytes 884744 | tf_op jit(solution)/shard_map/ppermute | solution.py:17
  186.7 22.9 %collective-permute-start.17 = (bf16[64,2304]{1,0:T(8,128)(2,1)}, bf16[64,2304]{1,0:T(8,128)(2,1)}, u32[]{:S(2)}, u32[]{:S(2)}) collective-permute-start(bf16[64,2304]{1,0:T(8,128)(2,1)} %get-tuple-element.164), channel_id=1, source_target_pairs={{0,4},{1,5},{2,6},{3,7},{4,0},{5,1},{6,2},{7,3},{8,12},{9,13},{10,... | collective-permute-start | bytes 884744 | tf_op jit(solution)/shard_map/ppermute | solution.py:17
  187.4 22.2 %collective-permute-start.18 = (bf16[64,2304]{1,0:T(8,128)(2,1)}, bf16[64,2304]{1,0:T(8,128)(2,1)}, u32[]{:S(2)}, u32[]{:S(2)}) collective-permute-start(bf16[64,2304]{1,0:T(8,128)(2,1)} %get-tuple-element.165), channel_id=1, source_target_pairs={{0,6},{1,7},{2,4},{3,5},{4,2},{5,3},{6,0},{7,1},{8,14},{9,15},{10,... | collective-permute-start | bytes 884744 | tf_op jit(solution)/shard_map/ppermute | solution.py:17
  189.5 27.3 %collective-permute-start.21 = (bf16[64,2304]{1,0:T(8,128)(2,1)S(1)}, bf16[64,2304]{1,0:T(8,128)(2,1)}, u32[]{:S(2)}, u32[]{:S(2)}) collective-permute-start(bf16[64,2304]{1,0:T(8,128)(2,1)S(1)} %fusion.9), channel_id=1, source_target_pairs={{0,6},{1,7},{2,4},{3,5},{4,2},{5,3},{6,0},{7,1},{8,14},{9,15},{10,... | collective-permute-start | bytes 884744 | tf_op jit(solution)/shard_map/ppermute | solution.py:17
  190.7 26.0 %collective-permute-start.20 = (bf16[64,2304]{1,0:T(8,128)(2,1)S(1)}, bf16[64,2304]{1,0:T(8,128)(2,1)}, u32[]{:S(2)}, u32[]{:S(2)}) collective-permute-start(bf16[64,2304]{1,0:T(8,128)(2,1)S(1)} %fusion.9), channel_id=1, source_target_pairs={{0,4},{1,5},{2,6},{3,7},{4,0},{5,1},{6,2},{7,3},{8,12},{9,13},{10,... | collective-permute-start | bytes 884744 | tf_op jit(solution)/shard_map/ppermute | solution.py:17
  218.2 16.0 %collective-permute-start.25 = (bf16[64,2304]{1,0:T(8,128)(2,1)S(1)}, bf16[64,2304]{1,0:T(8,128)(2,1)S(1)}, u32[]{:S(2)}, u32[]{:S(2)}) collective-permute-start(bf16[64,2304]{1,0:T(8,128)(2,1)S(1)} %fusion.12), channel_id=1, source_target_pairs={{0,6},{1,7},{2,4},{3,5},{4,2},{5,3},{6,0},{7,1},{8,14},{9,15},{10,... | collective-permute-start | bytes 884744 | tf_op jit(solution)/shard_map/ppermute | solution.py:17
  260.8 16.0 %collective-permute-start.33 = (bf16[64,2304]{1,0:T(8,128)(2,1)}, bf16[64,2304]{1,0:T(8,128)(2,1)S(1)}, u32[]{:S(2)}, u32[]{:S(2)}) collective-permute-start(bf16[64,2304]{1,0:T(8,128)(2,1)} %get-tuple-element.243), channel_id=1, source_target_pairs={{0,4},{1,5},{2,6},{3,7},{4,0},{5,1},{6,2},{7,3},{8,12},{9,13},{10,... | collective-permute-start | bytes 884744 | tf_op jit(solution)/shard_map/ppermute | solution.py:17
  (55 other events, 686.9 us)
Sparse Core Ops, SparseCore 0:
  9.6 31.0 all-gather.5
  42.2 67.2 all-gather.7
  118.1 62.1 all-gather.9
